TPU v7x, 128 devices: a whole 4x4x4 slice. The times are simulated.
128 devices in a mesh: section: 4 (over z_lo, core), seq: 16 (over x, y), head: 2 (over z_hi).
Axes of the slice: x: 4, y: 4, z: 4 (z_hi: 2, z_lo: 2; z = z_hi * 2 + z_lo), core: 2. Of those that a mesh axis runs over, the one named last changes fastest.
Arguments:
- text_hidden: bfloat16 [16384, 4096], P('seq'), may hold values from -600 to 600
- norm_gain: float32 [4096], replicated, may hold values from 0.1 to 1.9
- image_features: bfloat16 [32768, 1024], P('seq'), may hold values from -6 to 6
- query_weight: bfloat16 [4096, 4096], P(None, ('section', 'head')), may hold values from -30 to 30
- key_weight: bfloat16 [1024, 1024], P(None, ('section', 'head')), may hold values from -0.75 to 0.75
- value_weight: bfloat16 [1024, 1024], P(None, ('section', 'head')), may hold values from -0.1875 to 0.1875
- output_weight: bfloat16 [4096, 4096], P(('section', 'head')), may hold values from -0.125 to 0.125
- selected: int32 [128, 16], P('seq'), may hold values from 0 to 511, as said below
Outputs:
- attn_output: bfloat16 [16384, 4096], P('seq', ('section', 'head'))
Inputs may be any that keep to these rules, and one draw needn't show every extreme that they name: `selected`: each row names 16 different image blocks. The tiles of one seq index together select at most 8 different blocks from the 32 blocks of any one seq index, and exactly 8 from some seq index.
All inputs are finite; a program needn't handle non-finite values.
Results may differ from a plain program's by a relative error of at most 0.0069.
The roundings to bfloat16 on the way count: a program that leaves them out, or rounds other values in their place, can miss the bound.
Values may be sent and summed in bfloat16 or wider, within the bound.
No kernel may reach another device: no remote copies, remote signals or barrier semaphores. Data moves between devices by JAX's collectives and lax.ppermute only.
A program may use at most 128 MiB of HBM per device.

v0:
```python
import jax
import jax.numpy as jnp
from jax import lax
from jax.sharding import PartitionSpec as P

HEADS = 32
KV_HEADS = 8
HEAD_DIM = 128
TILE = 128
BLOCK = 64
TOPK = 16


EPSILON = 1e-05


def joined_along(tiles, dim):
    dims = list(tiles.shape[1:])
    dims[dim] *= tiles.shape[0]
    return jnp.moveaxis(tiles, 0, dim).reshape(dims)


def copy_for_each(value, axis):
    peers = lax.axis_size(axis)
    return lax.all_to_all(
        jnp.broadcast_to(value[None], (peers, *value.shape)), axis, 0, 0, tiled=True
    )


def gather_directly(value, axis, dim):
    return joined_along(copy_for_each(value, axis), dim)


def in_one_piece(arrays, axis, split_dim, concat_dim, along):
    ends, at = ([], 0)
    for a in arrays[:-1]:
        at += a.shape[along]
        ends.append(at)
    both = jnp.concatenate(arrays, axis=along)
    return tuple(
        jnp.split(
            lax.all_to_all(both, axis, split_axis=split_dim, concat_axis=concat_dim, tiled=True),
            ends,
            axis=along,
        )
    )


def split_up(value, dim, peers):
    dims = value.shape
    tiles = value.reshape(*dims[:dim], peers, dims[dim] // peers, *dims[dim + 1 :])
    return jnp.moveaxis(tiles, dim, 0)


def summed_on_arrival(value, axis, dim):
    peers = lax.axis_size(axis)
    tiles = lax.all_to_all(split_up(value, dim, peers), axis, 0, 0, tiled=True)
    return jnp.sum(tiles.astype(jnp.float32), axis=0)


def rms_normed(text_hidden, norm_gain):
    as_float = text_hidden.astype(jnp.float32)
    inverse = lax.rsqrt(jnp.mean(as_float * as_float, axis=-1, keepdims=True) + EPSILON)
    return (as_float * inverse * norm_gain).astype(jnp.bfloat16)


def attend(queries, key_picked, value_picked):
    tile_count = key_picked.shape[0]
    pick_count = key_picked.shape[1]
    local_kv = key_picked.shape[-1] // HEAD_DIM
    group_size = HEADS // KV_HEADS
    query_tiles = queries.reshape(tile_count, TILE, local_kv, group_size, HEAD_DIM)
    key_tiles = key_picked.reshape(tile_count, pick_count * BLOCK, local_kv, HEAD_DIM)
    value_tiles = value_picked.reshape(tile_count, pick_count * BLOCK, local_kv, HEAD_DIM)
    scores = jnp.einsum(
        "ntkgd,nskd->nkgts", query_tiles, key_tiles, preferred_element_type=jnp.float32
    ) * HEAD_DIM ** (-0.5)
    largest = jnp.max(scores, axis=-1, keepdims=True)
    exponent = jnp.exp(scores - largest)
    weights = (exponent / jnp.sum(exponent, axis=-1, keepdims=True)).astype(jnp.bfloat16)
    attended = jnp.einsum(
        "nkgts,nskd->ntkgd", weights, value_tiles, preferred_element_type=jnp.float32
    )
    return attended.astype(jnp.bfloat16).reshape(
        tile_count * TILE, local_kv * group_size * HEAD_DIM
    )


def shards(
    text_hidden,
    norm_gain,
    image_features,
    query_weight,
    key_weight,
    value_weight,
    output_weight,
    selected,
):
    normed = rms_normed(text_hidden, norm_gain)
    key_rows = jnp.dot(image_features, key_weight, preferred_element_type=jnp.float32).astype(
        jnp.bfloat16
    )
    value_rows = jnp.dot(image_features, value_weight, preferred_element_type=jnp.float32).astype(
        jnp.bfloat16
    )
    queries = jnp.dot(normed, query_weight, preferred_element_type=jnp.float32).astype(jnp.bfloat16)
    width = key_rows.shape[1]
    seq_count = lax.axis_size("seq")
    tiles_dev = selected.shape[0]
    blocks_dev = key_rows.shape[0] // BLOCK
    slot_count = max(1, min(blocks_dev, tiles_dev * TOPK // seq_count))
    all_ids = gather_directly(selected, "seq", 0)
    local_ids = all_ids.reshape(seq_count, tiles_dev * TOPK) - lax.axis_index("seq") * blocks_dev
    block_range = jnp.arange(blocks_dev, dtype=jnp.int32)
    wanted = jnp.any(local_ids[:, :, None] == block_range[None, None, :], axis=1)
    wanted_rank = jnp.cumsum(wanted.astype(jnp.int32), axis=1) - 1
    slot_range = jnp.arange(slot_count, dtype=jnp.int32)
    placing = (wanted[:, None, :] & (wanted_rank[:, None, :] == slot_range[None, :, None])).astype(
        jnp.bfloat16
    )
    own_keys = key_rows.reshape(blocks_dev, BLOCK * width)
    own_values = value_rows.reshape(blocks_dev, BLOCK * width)
    outgoing_keys = jnp.einsum(
        "rcb,bx->rcx", placing, own_keys, preferred_element_type=jnp.float32
    ).astype(jnp.bfloat16)
    outgoing_values = jnp.einsum(
        "rcb,bx->rcx", placing, own_values, preferred_element_type=jnp.float32
    ).astype(jnp.bfloat16)
    incoming_keys, incoming_values = in_one_piece((outgoing_keys, outgoing_values), "seq", 0, 0, 1)
    all_blocks = jnp.arange(seq_count * blocks_dev, dtype=jnp.int32)
    mine = jnp.any(selected.reshape(-1)[:, None] == all_blocks[None, :], axis=0).reshape(
        seq_count, blocks_dev
    )
    my_rank = jnp.cumsum(mine.astype(jnp.int32), axis=1) - 1
    owner_base = jnp.arange(seq_count, dtype=jnp.int32)[:, None] * slot_count
    slot_table = (owner_base + my_rank).reshape(-1)
    matches = selected[:, :, None] == all_blocks[None, None, :]
    slot_index = jnp.sum(jnp.where(matches, slot_table[None, None, :], 0), axis=-1)
    key_picked = incoming_keys.reshape(seq_count * slot_count, BLOCK, width)[slot_index]
    value_picked = incoming_values.reshape(seq_count * slot_count, BLOCK, width)[slot_index]
    attended = attend(queries, key_picked, value_picked)
    head_partial = jnp.dot(attended, output_weight, preferred_element_type=jnp.float32)
    summed = summed_on_arrival(head_partial.astype(jnp.bfloat16), ("section", "head"), 1)
    return summed.astype(jnp.bfloat16)


def solution(mesh):
    in_specs = (
        P("seq", None),
        P(),
        P("seq", None),
        P(None, ("section", "head")),
        P(None, ("section", "head")),
        P(None, ("section", "head")),
        P(("section", "head"), None),
        P("seq", None),
    )
    out_specs = P("seq", ("section", "head"))
    return jax.shard_map(shards, mesh=mesh, in_specs=in_specs, out_specs=out_specs, check_vma=False)
```

profile of v0, /device:TPU:1, one launch (start us, length us, event | category | flops | bytes accessed | tf_op | source)
XLA Modules:
  0.0 240.7 jit_solution(10272385896619827413)
XLA Ops:
  0.0 0.7 broadcast_in_dim.10
  0.8 0.7 reshape.153
  1.4 7.6 %all-to-all-start = ((s32[16,1,128]{2,1,0:T(1,128)}), s32[16,1,128]{2,1,0:T(1,128)S(1)}, u32[]{:S(2)}, u32[]{:S(2)}) async-start(s32[16,1,128]{2,1,0:T(1,128)} %reshape.153), calls=%async_computation | async-start | bytes 16384 | tf_op jit(solution)/shard_map/all_to_all | solution.py:25
  9.0 0.0 copy-done
  9.0 0.0 copy-start.4
  9.1 3.6 %convolution_convert_fusion.4 = bf16[2048,128]{1,0:T(8,128)(2,1)S(1)} fusion(bf16[2048,1024]{1,0:T(8,128)(2,1)} %param.10, bf16[1024,128]{1,0:T(8,128)(2,1)S(1)} %copy-done), kind=kOutput, calls=%fused_computation.24 | convolution fusion | flops 537133056 | bytes 4980736 | tf_op jit(solution)/shard_map/dot_general | solution.py:100
  12.6 0.0 copy-done.7
  12.7 0.0 copy-done.4
  12.7 1.3 convolution_convert_fusion.3
  14.0 0.2 reshape.147
  14.2 0.2 reshape.148
  14.5 0.9 all-to-all-done
  15.4 0.5 broadcast.89
  15.9 0.7 reduce.3
  16.6 0.1 reshape.154
  16.7 0.1 sub.29
  16.7 0.4 fusion.25
  17.1 0.2 reduce_window_sum.17
  17.3 0.7 convolution_convert_fusion
  18.0 0.7 convolution_convert_fusion.1
  18.7 2.2 pad_maximum_fusion
  20.9 5.9 %all-to-all-start.1 = ((bf16[16,16,8192]{2,1,0:T(8,128)(2,1)}), bf16[16,16,8192]{2,1,0:T(8,128)(2,1)}, u32[]{:S(2)}, u32[]{:S(2)}) async-start(bf16[16,16,8192]{2,1,0:T(8,128)(2,1)} %pad_maximum_fusion), calls=%async_computation.1 | async-start | bytes 8388608 | tf_op jit(solution)/shard_map/all_to_all | solution.py:42
  26.9 0.1 eq.63
  27.0 0.1 fusion.26
  27.1 0.1 reshape.126
  27.2 0.2 reduce_window_sum.18
  27.4 0.1 add_add_fusion
  27.5 0.1 add.50
  27.5 0.3 select_reduce_fusion
  27.9 0.1 reshape.129
  27.9 5.2 %fusion = f32[1024]{0:T(1024)S(1)} fusion(bf16[1024,4096]{1,0:T(8,128)(2,1)} %param.8), kind=kLoop, calls=%fused_computation.4 | loop fusion | flops 12581888 | bytes 8392704 | tf_op jit(solution)/shard_map/reduce_sum | solution.py:63
  33.2 7.9 %fusion.15 = bf16[1024,512]{1,0:T(8,128)(2,1)S(1)} fusion(bf16[4096,512]{1,0:T(8,128)(2,1)S(1)} %copy-done.5, bf16[1024,4096]{1,0:T(8,128)(2,1)} %param.8, f32[4096]{0:T(1024)S(1)} %copy-done.8, f32[1024]{0:T(1024)S(1)} %add_rsqrt_fusion), kind=kOutput, calls=%fused_computation.28 | convolution fusion | flops 4312268800 | bytes 13651968 | tf_op jit(solution)/shard_map/dot_general | solution.py:106
  41.1 0.5 reshape.122
  41.6 37.1 %all-to-all-done.1 = bf16[16,16,8192]{2,1,0:T(8,128)(2,1)} async-done(((bf16[16,16,8192]{2,1,0:T(8,128)(2,1)}), bf16[16,16,8192]{2,1,0:T(8,128)(2,1)}, u32[]{:S(2)}, u32[]{:S(2)}) %all-to-all-start.1) | async-done | bytes 4194336 | tf_op jit(solution)/shard_map/all_to_all | solution.py:42
  78.8 2.6 %slice_bitcast_fusion = (bf16[16,8,64,128]{3,1,2,0:T(8,128)(2,1)S(1)}, bf16[16,8,64,128]{3,1,2,0:T(8,128)(2,1)S(1)}) fusion(bf16[16,16,8192]{2,1,0:T(8,128)(2,1)} %all-to-all-done.1), kind=kLoop, calls=%fused_computation.25 | loop fusion | bytes 8388608
  81.4 1.9 copy.32
  83.3 1.9 copy.31
  85.3 2.5 %gather_fusion.1 = bf16[128,64,128]{2,1,0:T(8,128)(2,1)S(1)} fusion(bf16[128,64,128]{2,1,0:T(8,128)(2,1)} %bitcast.77, s32[1024]{0:T(1024)S(1)} %pad_clamp_fusion), kind=kCustom, calls=%fused_computation.1 | custom fusion | bytes 4194816 | tf_op jit(solution)/shard_map/gather | solution.py:139
  87.8 3.8 %gather_fusion = bf16[128,64,128]{2,1,0:T(8,128)(2,1)} fusion(bf16[128,64,128]{2,1,0:T(8,128)(2,1)} %bitcast.78, s32[1024]{0:T(1024)S(1)} %pad_clamp_fusion), kind=kCustom, calls=%fused_computation | custom fusion | bytes 4194816 | tf_op jit(solution)/shard_map/gather | solution.py:140
  91.6 8.1 %bitcast_reduce_fusion = (f32[8,4,128]{2,1,0:T(4,128)S(1)}, f32[8,1024,128,4]{2,1,3,0:T(8,128)}) fusion(bf16[8,1024,128,1]{2,1,3,0:T(8,128)(2,1)S(1)} %bitcast.76, bf16[8,128,4,128]{3,2,1,0:T(4,128)(2,1)S(1)} %reshape.122), kind=kOutput, calls=%fused_computation.8 | convolution fusion | flops 1082126336 | bytes 19939328 | tf_op jit(solution)/shard_map/ntkgd,nskd->nkgts/dot_general | solution.py:75
  99.6 8.8 %fusion.4 = f32[8,4,128]{2,1,0:T(4,128)S(1)} fusion(f32[8,1024,128,4]{2,1,3,0:T(8,128)} %get-tuple-element.8, f32[8,4,128]{2,1,0:T(4,128)S(1)} %get-tuple-element.7), kind=kLoop, calls=%fused_computation.11 | loop fusion | flops 12578816 | bytes 16809984 | tf_op jit(solution)/shard_map/reduce_sum | solution.py:80
  108.4 0.0 copy-start.6
  108.4 8.0 %fusion.18 = bf16[8,128,1,4,128]{1,4,3,0,2:T(8,128)(2,1)S(1)} fusion(bf16[8,1024,128,1]{2,1,3,0:T(8,128)(2,1)S(1)} %bitcast.80, f32[8,4,128]{2,1,0:T(4,128)S(1)} %fusion.4, f32[8,4,128]{2,1,0:T(4,128)S(1)} %get-tuple-element.7, f32[8,1024,128,4]{2,1,3,0:T(8,128)} %get-tuple-element.8), kind=kOutput, calls=%fused_computation.29 | convolution fusion | flops 1091043328 | bytes 19955712 | tf_op jit(solution)/shard_map/nkgts,nskd->ntkgd/dot_general | solution.py:81
  116.4 0.7 copy.23
  117.1 6.8 %convolution_convert_fusion.2 = bf16[1024,4096]{1,0:T(8,128)(2,1)} fusion(bf16[512,4096]{1,0:T(8,128)(2,1)S(1)} %copy-done.6, bf16[64,8,8,128]{3,2,1,0:T(8,128)(2,1)S(1)} %bitcast.81), kind=kOutput, calls=%fused_computation.21 | convolution fusion | flops 4299161600 | bytes 13631488 | tf_op jit(solution)/shard_map/dot_general | solution.py:142
  123.9 7.4 %copy.43 = bf16[128,8,8,512]{3,2,0,1:T(8,128)(2,1)} copy(bf16[128,8,8,512]{3,2,1,0:T(8,128)(2,1)} %bitcast.79) | data formatting | bytes 16777216 | tf_op jit(solution)/shard_map/reshape | solution.py:51
  131.3 103.6 %all_to_all.15 = bf16[8,1024,512]{2,1,0:T(8,128)(2,1)} all-to-all(bf16[8,1024,512]{2,1,0:T(8,128)(2,1)} %bitcast.75), channel_id=1, replica_groups=mesh['section'=4,'seq'=16,'head'=2] {'section','head'}, dimensions={0} | all-to-all | bytes 16777216 | tf_op jit(solution)/shard_map/all_to_all | solution.py:57
  234.9 5.9 %reduce_sum.45 = bf16[1024,512]{1,0:T(8,128)(2,1)} reduce(bf16[8,1024,512]{2,1,0:T(8,128)(2,1)} %all_to_all.15, bf16[]{:T(256)} %constant.37.clone.1), dimensions={0}, to_apply=%region_8.9 | reduce | flops 3670016 | bytes 9437186 | tf_op jit(solution)/shard_map/reduce_sum | solution.py:58
  (21 shorter events, 0.1 us)
Async XLA Ops:
  0.0 9.0 %copy-start = (bf16[1024,128]{1,0:T(8,128)(2,1)S(1)}, bf16[1024,128]{1,0:T(8,128)(2,1)}, u32[]{:S(2)}) copy-start(bf16[1024,128]{1,0:T(8,128)(2,1)} %param.12) | copy-start | bytes 786436
  0.0 12.6 %copy-start.7 = (bf16[1024,128]{1,0:T(8,128)(2,1)S(1)}, bf16[1024,128]{1,0:T(8,128)(2,1)}, u32[]{:S(2)}) copy-start(bf16[1024,128]{1,0:T(8,128)(2,1)} %param.13) | copy-start | bytes 786436
  1.4 13.9 %all-to-all-start = ((s32[16,1,128]{2,1,0:T(1,128)}), s32[16,1,128]{2,1,0:T(1,128)S(1)}, u32[]{:S(2)}, u32[]{:S(2)}) async-start(s32[16,1,128]{2,1,0:T(1,128)} %reshape.153), calls=%async_computation | async-start | bytes 16384 | tf_op jit(solution)/shard_map/all_to_all | solution.py:25
  9.0 3.6 %copy-start.4 = (bf16[2048,1024]{1,0:T(8,128)(2,1)S(1)}, bf16[2048,1024]{1,0:T(8,128)(2,1)}, u32[]{:S(2)}) copy-start(bf16[2048,1024]{1,0:T(8,128)(2,1)} %param.10) | copy-start | bytes 12582916
  20.9 5.9 %copy-start.3 = (s32[8,16]{1,0:T(8,128)S(1)}, s32[8,16]{1,0:T(8,128)}, u32[]{:S(2)}) copy-start(s32[8,16]{1,0:T(8,128)} %param.15) | copy-start | bytes 1540
  20.9 57.8 %all-to-all-start.1 = ((bf16[16,16,8192]{2,1,0:T(8,128)(2,1)}), bf16[16,16,8192]{2,1,0:T(8,128)(2,1)}, u32[]{:S(2)}, u32[]{:S(2)}) async-start(bf16[16,16,8192]{2,1,0:T(8,128)(2,1)} %pad_maximum_fusion), calls=%async_computation.1 | async-start | bytes 8388608 | tf_op jit(solution)/shard_map/all_to_all | solution.py:42
  27.9 5.2 %copy-start.5 = (bf16[4096,512]{1,0:T(8,128)(2,1)S(1)}, bf16[4096,512]{1,0:T(8,128)(2,1)}, u32[]{:S(2)}) copy-start(bf16[4096,512]{1,0:T(8,128)(2,1)} %param.11) | copy-start | bytes 12582916
  27.9 5.3 %copy-start.8 = (f32[4096]{0:T(1024)S(1)}, f32[4096]{0:T(1024)}, u32[]{:S(2)}) copy-start(f32[4096]{0:T(1024)} %param.9) | copy-start | bytes 49156
  99.6 8.8 %copy-start.2 = (bf16[128,64,128]{2,1,0:T(8,128)(2,1)S(1)}, bf16[128,64,128]{2,1,0:T(8,128)(2,1)}, u32[]{:S(2)}) copy-start(bf16[128,64,128]{2,1,0:T(8,128)(2,1)} %gather_fusion) | copy-start | bytes 6291460
  108.4 8.7 %copy-start.6 = (bf16[512,4096]{1,0:T(8,128)(2,1)S(1)}, bf16[512,4096]{1,0:T(8,128)(2,1)}, u32[]{:S(2)}) copy-start(bf16[512,4096]{1,0:T(8,128)(2,1)} %param.14) | copy-start | bytes 12582916
  131.3 109.5 %copy-start.1 = (bf16[1024,128]{1,0:T(8,128)(2,1)S(1)}, bf16[1024,128]{1,0:T(8,128)(2,1)}, u32[]{:S(2)}) copy-start(bf16[1024,128]{1,0:T(8,128)(2,1)} %param.12) | copy-start | bytes 786436
where the time goes:
time: 244 us; the launch traced here: 241 us
  blocking collectives  104 us (43%)
  waiting for transfers between devices  38 us (16%)
  matrix products  37 us (15%)
  local copies, waits for them, and re-layouts  24.3 us (10%)
  other arithmetic  24 us (10%)
  starting transfers between devices  13.5 us (6%)
    all_to_all x1, blocking collectives, summed_on_arrival(): tiles = lax.all_to_all(split_up(value, dim, peers), axis, 0, 0, tiled=True)  104 us
    all_to_all x1, waiting for transfers between devices, in_one_piece(): lax.all_to_all(both, axis, split_axis=split_dim, concat_axis=concat_dim,...  37.1 us
    reduce_sum x1, other arithmetic, attend(): jnp.sum(exponent, axis=-1, keepdims=True)  8.76 us
    dot_general x1, matrix products, attend(): jnp.einsum('ntkgd,nskd->nkgts', query_tiles, key_tiles, preferred_element...  8.06 us
    dot_general x1, matrix products, attend(): jnp.einsum('nkgts,nskd->ntkgd', weights, value_tiles, preferred_element_t...  7.97 us
    dot_general x1, matrix products, shards(): jnp.dot(normed, query_weight, preferred_element_type=jnp.float32)  7.94 us
    all_to_all x1, starting transfers between devices, copy_for_each(): lax.all_to_all(jnp.broadcast_to(value[None], (peers, *value.shape)), axis...  7.58 us
    reshape x1, local copies, waits for them, and re-layouts, split_up(): value.reshape(*dims[:dim], peers, dims[dim] // peers, *dims[dim + 1:])  7.41 us
  transfers between devices with their start and end apart: 2, of which 2 were waited for; matrix products, arithmetic and copies ran while one was open for 8% of the time, Pallas kernels for 0%

commit v1 on v0

v1 whole, which is shorter than its diff:
```python
import functools

import jax
import jax.numpy as jnp
from jax import lax
from jax.experimental import pallas as pl
from jax.experimental.pallas import tpu as pltpu
from jax.sharding import PartitionSpec as P

HEADS = 32
KV_HEADS = 8
HEAD_DIM = 128
GROUP = HEADS // KV_HEADS
TILE = 128
BLOCK = 64
TOPK = 16
SIDE = 4
CAP = 8
PICKS = SIDE * SIDE * CAP
NOTE_ROWS = 16
EPSILON = 1e-05
SCALE = HEAD_DIM**-0.5

SECTION_HEAD = ("section", "head")
VMEM_WHOLE = pl.BlockSpec(memory_space=pltpu.VMEM)
SMEM_WHOLE = pl.BlockSpec(memory_space=pltpu.SMEM)


def along_seq(value, dx, dy):
    pairs = [
        (x * SIDE + y, (x + dx) % SIDE * SIDE + (y + dy) % SIDE)
        for x in range(SIDE)
        for y in range(SIDE)
    ]
    return lax.ppermute(value, "seq", pairs)


def column(z, core):
    return (z % 2) * 4 + core * 2 + z // 2


def along_z(value, place):
    pairs = []
    for z in range(4):
        for core in range(2):
            pairs.append((column(z, core), column(*place(z, core))))
    return lax.ppermute(value, SECTION_HEAD, pairs)


def to_near(value):
    return along_z(value, lambda z, core: (z ^ 1, core))


def to_far(value):
    return along_z(value, lambda z, core: (3 - z, core))


def to_core(value):
    return along_z(value, lambda z, core: (z, 1 - core))


def project_body(ids_ref, x_ref, wk_ref, wv_ref, k_ref, v_ref, slots_ref, w_ref):
    step = pl.program_id(0)
    rows = x_ref.shape[0]
    steps = pl.num_programs(0)
    blocks_dev = (k_ref.shape[0] - NOTE_ROWS) // BLOCK
    blocks = SIDE * SIDE * blocks_dev

    @pl.when(step == 0)
    def _():
        w_ref[:, :HEAD_DIM] = wk_ref[...]
        w_ref[:, HEAD_DIM:] = wv_ref[...]

    @pl.when(step == steps - 1)
    def _():
        ids = ids_ref[...]
        block = lax.broadcasted_iota(jnp.int32, (blocks, PICKS), 0)
        hit = (block == ids).astype(jnp.float32)
        wanted = jnp.broadcast_to(jnp.max(hit, axis=1, keepdims=True), (blocks, PICKS))
        one = lax.broadcasted_iota(jnp.int32, (blocks, blocks), 0)
        other = lax.broadcasted_iota(jnp.int32, (blocks, blocks), 1)
        before = (one // blocks_dev == other // blocks_dev) & (other < one)
        rank = jnp.dot(
            before.astype(jnp.float32).astype(jnp.bfloat16),
            wanted.astype(jnp.bfloat16),
            preferred_element_type=jnp.float32,
        )
        owner = block // blocks_dev
        slot = (owner * CAP).astype(jnp.float32) + rank
        slots = jnp.sum(hit * slot, axis=0, keepdims=True)
        slots_ref[...] = jnp.broadcast_to(slots, slots_ref.shape).astype(jnp.int32)
        place = lax.broadcasted_iota(jnp.int32, (blocks, PICKS), 1).astype(jnp.float32)
        local = (block % blocks_dev).astype(jnp.float32)
        asked = jnp.sum(
            jnp.where(slot == place, wanted * local, 0.0), axis=0, keepdims=True
        )
        note = jnp.broadcast_to(asked, (NOTE_ROWS, PICKS)).astype(jnp.bfloat16)
        k_ref[rows * steps :, :] = note
        v_ref[rows * steps :, :] = note

    both = jnp.dot(x_ref[...], w_ref[...], preferred_element_type=jnp.float32)
    at = pl.ds(pl.multiple_of(step * rows, rows), rows)
    k_ref[at, :] = both[:, :HEAD_DIM].astype(jnp.bfloat16)
    v_ref[at, :] = both[:, HEAD_DIM:].astype(jnp.bfloat16)


def project(image_features, key_weight, value_weight, ids):
    rows, enc = image_features.shape
    steps = 4
    out = jax.ShapeDtypeStruct((rows + NOTE_ROWS, HEAD_DIM), jnp.bfloat16)
    whole = lambda shape: pl.BlockSpec(shape, lambda i: (0,) * len(shape))
    return pl.pallas_call(
        project_body,
        grid=(steps,),
        in_specs=[
            whole((1, PICKS)),
            pl.BlockSpec((rows // steps, enc), lambda i: (i, 0)),
            whole((enc, HEAD_DIM)),
            whole((enc, HEAD_DIM)),
        ],
        out_specs=[
            whole((rows + NOTE_ROWS, HEAD_DIM)),
            whole((rows + NOTE_ROWS, HEAD_DIM)),
            whole((8, PICKS)),
        ],
        out_shape=[out, out, jax.ShapeDtypeStruct((8, PICKS), jnp.int32)],
        scratch_shapes=[pltpu.VMEM((enc, 2 * HEAD_DIM), jnp.bfloat16)],
        compiler_params=pltpu.CompilerParams(vmem_limit_bytes=40 << 20),
        cost_estimate=pl.CostEstimate(
            flops=4 * rows * enc * HEAD_DIM, bytes_accessed=2 * rows * enc, transcendentals=0
        ),
        name="project",
    )(ids, image_features, key_weight, value_weight)


def pack_body(ask_ref, place_ref, own, plus, two_low, two_high, minus, out0, out1, out2, out3):
    me, base, stride = place_ref[0], place_ref[1], place_ref[2]
    half = two_low.shape[0] // BLOCK
    for dest, out in enumerate((out0, out1, out2, out3)):
        for away in range(SIDE):
            first = base + ((me + away) & (SIDE - 1)) * stride
            for slot in range(CAP):
                block = ask_ref[dest, first + slot]

                def rows(ref, index):
                    return ref[pl.ds(pl.multiple_of(index * BLOCK, BLOCK), BLOCK), :]

                if away == 0:
                    value = rows(own, block)
                elif away == 1:
                    value = rows(plus, block)
                elif away == 3:
                    value = rows(minus, block)
                else:
                    value = jnp.where(
                        block < half,
                        rows(two_low, jnp.minimum(block, half - 1)),
                        rows(two_high, jnp.maximum(block - half, 0)),
                    )
                out[(away * CAP + slot) * BLOCK : (away * CAP + slot + 1) * BLOCK, :] = value


def pack(ask, place, own, plus, two_low, two_high, minus):
    out = jax.ShapeDtypeStruct((SIDE * CAP * BLOCK, HEAD_DIM), jnp.bfloat16)
    return pl.pallas_call(
        pack_body,
        in_specs=[SMEM_WHOLE, SMEM_WHOLE] + [VMEM_WHOLE] * 5,
        out_specs=[VMEM_WHOLE] * SIDE,
        out_shape=[out] * SIDE,
        compiler_params=pltpu.CompilerParams(vmem_limit_bytes=24 << 20),
        name="pack",
    )(ask, place, own, plus, two_low, two_high, minus)


def attend_body(first_tile, slots_ref, place_ref, q_ref, k_ref, v_ref, o_ref, kt, vt):
    my_x, my_y = place_ref[0], place_ref[1]
    for tile in range(q_ref.shape[0] // TILE):
        for pick in range(TOPK):
            slot = slots_ref[0, (first_tile + tile) * TOPK + pick]
            owner, rank = slot >> 3, slot & (CAP - 1)
            away_x = ((owner >> 2) - my_x) & (SIDE - 1)
            away_y = ((owner & 3) - my_y) & (SIDE - 1)
            k_at = (away_y * SIDE + away_x) * CAP + rank
            v_at = (away_x * SIDE + away_y) * CAP + rank
            to = slice(pick * BLOCK, (pick + 1) * BLOCK)
            kt[tile % 2, to, :] = k_ref[pl.ds(pl.multiple_of(k_at * BLOCK, BLOCK), BLOCK), :]
            vt[tile % 2, to, :] = v_ref[pl.ds(pl.multiple_of(v_at * BLOCK, BLOCK), BLOCK), :]
        keys, values = kt[tile % 2], vt[tile % 2]
        rows = slice(tile * TILE, (tile + 1) * TILE)
        for head in range(GROUP):
            columns = slice(head * HEAD_DIM, (head + 1) * HEAD_DIM)
            scores = lax.dot_general(
                q_ref[rows, columns], keys, (((1,), (1,)), ((), ())),
                preferred_element_type=jnp.float32,
            ) * SCALE
            exponent = jnp.exp(scores - jnp.max(scores, axis=-1, keepdims=True))
            total = jnp.sum(exponent, axis=-1, keepdims=True)
            weights = (exponent * (1.0 / total)).astype(jnp.bfloat16)
            mixed = jnp.dot(weights, values, preferred_element_type=jnp.float32)
            o_ref[rows, columns] = mixed.astype(jnp.bfloat16)


def attend(first_tile, tiles, slots, place, queries, keys, values):
    width = queries.shape[1]
    rows = tiles * TILE
    return pl.pallas_call(
        functools.partial(attend_body, first_tile),
        in_specs=[SMEM_WHOLE, SMEM_WHOLE] + [VMEM_WHOLE] * 3,
        out_specs=VMEM_WHOLE,
        out_shape=jax.ShapeDtypeStruct((rows, width), jnp.bfloat16),
        scratch_shapes=[pltpu.VMEM((2, TOPK * BLOCK, HEAD_DIM), jnp.bfloat16)] * 2,
        compiler_params=pltpu.CompilerParams(vmem_limit_bytes=32 << 20),
        cost_estimate=pl.CostEstimate(
            flops=4 * rows * GROUP * TOPK * BLOCK * HEAD_DIM,
            bytes_accessed=4 * rows * width,
            transcendentals=rows * GROUP * TOPK * BLOCK,
        ),
        name="attend",
    )(slots, place, queries, keys, values)


def rms_normed(text_hidden, norm_gain):
    as_float = text_hidden.astype(jnp.float32)
    inverse = lax.rsqrt(jnp.mean(as_float * as_float, axis=-1, keepdims=True) + EPSILON)
    return (as_float * inverse * norm_gain).astype(jnp.bfloat16)


def spread(value, dx, dy):
    half = (value.shape[0] - NOTE_ROWS) // 2
    minus = along_seq(value, dx, dy)
    plus = along_seq(value, -dx, -dy)
    low = along_seq(minus[:half], dx, dy)
    high = along_seq(plus[half:], -dx, -dy)
    return plus, low, high, minus


def asks(own, plus, high, minus):
    rows = own.shape[0] - NOTE_ROWS
    at = high.shape[0] - NOTE_ROWS
    return jnp.concatenate(
        [own[rows : rows + 1], plus[rows : rows + 1], high[at : at + 1], minus[rows : rows + 1]]
    ).astype(jnp.int32)


def columns_of(weight, places):
    width = weight.shape[1] // 8
    return [lax.dynamic_slice_in_dim(weight, p * width, width, 1) for p in places]


def shards(
    text_hidden,
    norm_gain,
    image_features,
    query_weight,
    key_weight,
    value_weight,
    output_weight,
    selected,
):
    seq = lax.axis_index("seq")
    my_x, my_y = seq // SIDE, seq % SIDE
    section, z_hi = lax.axis_index("section"), lax.axis_index("head")
    z, core = z_hi * 2 + section // 2, section % 2

    k_own, v_own, slots = project(
        image_features, key_weight, value_weight, selected.reshape(1, PICKS)
    )
    k_plus, k_low, k_high, k_minus = spread(k_own, 1, 0)
    v_plus, v_low, v_high, v_minus = spread(v_own, 0, 1)

    def wanted_columns(z):
        return [
            column(z, core), column(3 - z, core), column(z, 1 - core), column(3 - z, 1 - core)
        ]

    own_weight = columns_of(output_weight, wanted_columns(z))
    near_weight = to_near(
        jnp.concatenate(columns_of(output_weight, wanted_columns(z ^ 1)), axis=1)
    )
    keep_own = jnp.concatenate(own_weight[:2], axis=1)
    give_own = jnp.concatenate(own_weight[2:], axis=1)
    kept = keep_own.shape[1]
    keep_near, give_near = near_weight[:, :kept], near_weight[:, kept:]

    normed = rms_normed(text_hidden, norm_gain)
    queries = jnp.dot(normed, query_weight, preferred_element_type=jnp.float32).astype(jnp.bfloat16)

    k_place = jnp.stack([my_x, my_y * CAP, SIDE * CAP + 0 * my_x])
    v_place = jnp.stack([my_y, my_x * (SIDE * CAP), CAP + 0 * my_y])
    k_out = pack(
        asks(v_own, v_plus, v_high, v_minus), k_place, k_own, k_plus, k_low, k_high, k_minus
    )
    v_out = pack(
        asks(k_own, k_plus, k_high, k_minus), v_place, v_own, v_plus, v_low, v_high, v_minus
    )
    keys = jnp.concatenate(
        [
            k_out[0],
            along_seq(k_out[3], 0, -1),
            along_seq(k_out[2], 0, 2),
            along_seq(k_out[1], 0, 1),
        ]
    )
    values = jnp.concatenate(
        [
            v_out[0],
            along_seq(v_out[3], -1, 0),
            along_seq(v_out[2], 2, 0),
            along_seq(v_out[1], 1, 0),
        ]
    )

    place = jnp.stack([my_x, my_y])
    tiles_dev = selected.shape[0]
    per = 2
    outs = []
    half = output_weight.shape[1] // 8

    def product(a, b):
        return jnp.dot(a, b, preferred_element_type=jnp.float32)

    for first in range(0, tiles_dev, per):
        rows = slice(first * TILE, (first + per) * TILE)
        mine = attend(first, per, slots, place, queries[rows], keys, values)
        near = to_near(mine)
        give = (product(mine, give_own) + product(near, give_near)).astype(jnp.bfloat16)
        got = to_core(give)
        keep = product(mine, keep_own) + product(near, keep_near)
        keep = keep + got.astype(jnp.float32)
        far = to_far(keep[:, half:].astype(jnp.bfloat16))
        outs.append((keep[:, :half] + far.astype(jnp.float32)).astype(jnp.bfloat16))
    return jnp.concatenate(outs, axis=0)


def solution(mesh):
    in_specs = (
        P("seq", None),
        P(),
        P("seq", None),
        P(None, ("section", "head")),
        P(None, ("section", "head")),
        P(None, ("section", "head")),
        P(("section", "head"), None),
        P("seq", None),
    )
    out_specs = P("seq", ("section", "head"))
    return jax.shard_map(shards, mesh=mesh, in_specs=in_specs, out_specs=out_specs, check_vma=False)
```

time: 244 us -> 151 us (0.62)
  the two profiles are of different devices: /device:TPU:1 before, /device:TPU:2 now
where the time goes in v1:
time: 151 us; the launch traced here: 150 us
  waiting for transfers between devices  45.8 us (30%)
  starting transfers between devices  37.2 us (25%)
  Pallas kernels  24.4 us (16%)
  matrix products  22.6 us (15%)
  local copies, waits for them, and re-layouts  14.9 us (10%)
  other arithmetic  4.91 us (3%)
    ppermute x14, waiting for transfers between devices, along_seq(): return lax.ppermute(value, 'seq', pairs)  27.3 us
    ppermute x14, starting transfers between devices, along_seq(): return lax.ppermute(value, 'seq', pairs)  22.6 us
    ppermute x13, waiting for transfers between devices, along_z(): return lax.ppermute(value, SECTION_HEAD, pairs)  18.5 us
    pallas_call x4, Pallas kernels, attend(): pl.pallas_call(functools.partial(attend_body, first_tile), in_specs=[SMEM...  17.8 us
    dot_general x16, matrix products, product(): return jnp.dot(a, b, preferred_element_type=jnp.float32)  17 us
    ppermute x13, starting transfers between devices, along_z(): return lax.ppermute(value, SECTION_HEAD, pairs)  14.6 us
    dot_general x1, matrix products, shards(): jnp.dot(normed, query_weight, preferred_element_type=jnp.float32)  5.55 us
    unnamed x26, local copies, waits for them, and re-layouts  4.46 us
  transfers between devices with their start and end apart: 27, of which 10 were waited for; matrix products, arithmetic and copies ran while one was open for 24% of the time, Pallas kernels for 14%

profile of v1, /device:TPU:2, one launch (start us, length us, event | category | flops | bytes accessed | tf_op | source)
XLA Modules:
  0.0 150.2 jit_solution(4669813840883790229)
XLA Ops:
  0.8 2.2 %copy-done = bf16[2048,1024]{1,0:T(8,128)(2,1)S(1)} copy-done((bf16[2048,1024]{1,0:T(8,128)(2,1)S(1)}, bf16[2048,1024]{1,0:T(8,128)(2,1)}, u32[]{:S(2)}) %copy-start) | copy-done | bytes 4194328
  3.0 0.9 copy-done.1
  4.9 3.4 %project.1 = (bf16[2064,128]{1,0:T(8,128)(2,1)}, bf16[2064,128]{1,0:T(8,128)(2,1)}, s32[8,128]{1,0:T(8,128)S(1)}) custom-call(s32[1,128]{1,0:T(1,128)S(1)} %reshape.12.ids_ref, bf16[2048,1024]{1,0:T(8,128)(2,1)S(1)} %copy-done, bf16[1024,128]{1,0:T(8,128)(2,1)S(1)} %copy-done.1, bf16[1024,128]{1,0:T(8,128)(2,1)S(1)} %copy-done.2), custom_call_target="tpu_custom_call" | custom-call | flops 1073741824 | bytes 4194304 | tf_op jit(solution)/shard_map/project/pallas_call | solution.py:112
  8.2 1.6 %collective-permute-start.2 = (bf16[2064,128]{1,0:T(8,128)(2,1)}, bf16[2064,128]{1,0:T(8,128)(2,1)S(1)}, u32[]{:S(2)}, u32[]{:S(2)}) collective-permute-start(bf16[2064,128]{1,0:T(8,128)(2,1)} %get-tuple-element.17.own), channel_id=1, source_target_pairs={{0,2},{2,4},{4,6},{6,0},{8,10},{10,12},{12,14},{14,8},{16,18},{18,... | collective-permute-start | bytes 1585160 | tf_op jit(solution)/shard_map/ppermute | solution.py:35
  9.8 1.7 %collective-permute-start = (bf16[2064,128]{1,0:T(8,128)(2,1)}, bf16[2064,128]{1,0:T(8,128)(2,1)S(1)}, u32[]{:S(2)}, u32[]{:S(2)}) collective-permute-start(bf16[2064,128]{1,0:T(8,128)(2,1)} %get-tuple-element.17.own), channel_id=1, source_target_pairs={{0,6},{2,0},{4,2},{6,4},{8,14},{10,8},{12,10},{14,12},{16,22},{18,... | collective-permute-start | bytes 1585160 | tf_op jit(solution)/shard_map/ppermute | solution.py:35
  11.5 1.5 collective-permute-start.4
  13.5 3.9 %constant_dynamic-slice_fusion.7 = (bf16[512,512]{1,0:T(8,128)(2,1)}, bf16[512,512]{1,0:T(8,128)(2,1)S(1)}, bf16[512,512]{1,0:T(8,128)(2,1)S(1)}, bf16[512,512]{...) fusion(bf16[512,4096]{1,0:T(8,128)(2,1)} %param.14, ...), kind=kLoop, calls=%fused_computation.73 | loop fusion | bytes 8388640 | tf_op jit(solution)/shard_map/dynamic_slice | solution.py:247
  17.3 1.6 %pad_maximum_fusion = bf16[512,2048]{1,0:T(8,128)(2,1)} fusion(bf16[512,512]{1,0:T(8,128)(2,1)S(1)} %get-tuple-element.28, bf16[512,512]{1,0:T(8,128)(2,1)S(1)} %get-tuple-element.29, bf16[512,512]{1,0:T(8,128)(2,1)S(1)} %get-tuple-element.30, bf16[512,512]{1,0:T(8,128)(2,1)S(1)} %get-tuple-element.31), kind=kLoop, calls=%fused_computation.8 | loop fusion | flops 8388608 | bytes 4194304 | tf_op jit(solution)/shard_map/concatenate | solution.py:278
  19.0 1.9 %collective-permute-start.15 = (bf16[512,2048]{1,0:T(8,128)(2,1)}, bf16[512,2048]{1,0:T(8,128)(2,1)}, u32[]{:S(2)}, u32[]{:S(2)}) collective-permute-start(bf16[512,2048]{1,0:T(8,128)(2,1)} %pad_maximum_fusion), channel_id=1, source_target_pairs={{0,64},{32,96},{64,0},{96,32},{1,65},{33,97},{65,1},{97,33},{2,66}... | collective-permute-start | bytes 6291464 | tf_op jit(solution)/shard_map/ppermute | solution.py:47
  20.9 1.7 %fusion = f32[1024]{0:T(1024)S(1)} fusion(bf16[1024,4096]{1,0:T(8,128)(2,1)S(1)} %copy-done.7), kind=kLoop, calls=%fused_computation.2 | loop fusion | flops 12581888 | bytes 8392704 | tf_op jit(solution)/shard_map/reduce_sum | solution.py:224
  22.6 5.6 %fusion.7 = bf16[1024,512]{1,0:T(8,128)(2,1)} fusion(bf16[4096,512]{1,0:T(8,128)(2,1)S(1)} %copy-done.8, bf16[1024,4096]{1,0:T(8,128)(2,1)S(1)} %copy-done.7, f32[4096]{0:T(1024)S(1)} %copy-done.9, f32[1024]{0:T(1024)S(1)} %add_rsqrt_fusion), kind=kOutput, calls=%fused_computation.9 | convolution fusion | flops 4312268800 | bytes 13651968 | tf_op jit(solution)/shard_map/dot_general | solution.py:286
  28.2 1.3 fusion.38
  30.2 1.8 %collective-permute-start.6 = (bf16[1040,128]{1,0:T(8,128)(2,1)}, bf16[1040,128]{1,0:T(8,128)(2,1)S(1)}, u32[]{:S(2)}, u32[]{:S(2)}) collective-permute-start(bf16[1040,128]{1,0:T(8,128)(2,1)} %slice.114), channel_id=1, source_target_pairs={{0,24},{2,26},{4,28},{6,30},{8,0},{10,2},{12,4},{14,6},{16,8},{18,... | collective-permute-start | bytes 798728 | tf_op jit(solution)/shard_map/ppermute | solution.py:35
  33.9 2.9 %collective-permute-start.1 = (bf16[1040,128]{1,0:T(8,128)(2,1)}, bf16[1040,128]{1,0:T(8,128)(2,1)}, u32[]{:S(2)}, u32[]{:S(2)}) collective-permute-start(bf16[1040,128]{1,0:T(8,128)(2,1)} %slice.110), channel_id=1, source_target_pairs={{0,6},{2,0},{4,2},{6,4},{8,14},{10,8},{12,10},{14,12},{16,22},{18,... | collective-permute-start | bytes 798728 | tf_op jit(solution)/shard_map/ppermute | solution.py:35
  38.7 2.1 %collective-permute-done.10.two_low = bf16[1024,128]{1,0:T(8,128)(2,1)} collective-permute-done((bf16[1024,128]{1,0:T(8,128)(2,1)}, bf16[1024,128]{1,0:T(8,128)(2,1)}, u32[]{:S(2)}, u32[]{:S(2)}) %collective-permute-start.10) | collective-permute-done | bytes 262176 | tf_op jit(solution)/shard_map/ppermute | solution.py:35
  41.0 1.7 %pack.3 = (bf16[2048,128]{1,0:T(8,128)(2,1)S(1)}, bf16[2048,128]{1,0:T(8,128)(2,1)S(1)}, bf16[2048,128]{1,0:T(8,128)(2,1)S(1)}, bf16[2048,128]{1,0:T(8,128)(2,1)S(1)}) custom-call(s32[4,128]{1,0:T(4,128)S(1)} %maximum_convert_fusion.1.ask_ref, s32[3]{0:T(128)S(1)} %pad_add_fusion.2.place_ref, bf16[2064,128]{1,0:T(8,128)(2,1)} %get-tuple-element.17.own, ...), custom_call_target="tpu_custom_call" | custom-call | tf_op jit(solution)/shard_map/pack/pallas_call | solution.py:165
  42.7 1.6 %collective-permute-start.11 = (bf16[2048,128]{1,0:T(8,128)(2,1)S(1)}, bf16[2048,128]{1,0:T(8,128)(2,1)S(1)}, u32[]{:S(2)}, u32[]{:S(2)}) collective-permute-start(bf16[2048,128]{1,0:T(8,128)(2,1)S(1)} %get-tuple-element.24), channel_id=1, source_target_pairs={{0,24},{2,26},{4,28},{6,30},{8,0},{10,2},{12,4},{14,6},{16,8},{18,... | collective-permute-start | bytes 1572872 | tf_op jit(solution)/shard_map/ppermute | solution.py:35
  44.5 2.1 %collective-permute-start.13 = (bf16[2048,128]{1,0:T(8,128)(2,1)S(1)}, bf16[2048,128]{1,0:T(8,128)(2,1)S(1)}, u32[]{:S(2)}, u32[]{:S(2)}) collective-permute-start(bf16[2048,128]{1,0:T(8,128)(2,1)S(1)} %get-tuple-element.26), channel_id=1, source_target_pairs={{0,8},{2,10},{4,12},{6,14},{8,16},{10,18},{12,20},{14,22},{16,24},... | collective-permute-start | bytes 1572872 | tf_op jit(solution)/shard_map/ppermute | solution.py:35
  47.3 1.6 %pack.2 = (bf16[2048,128]{1,0:T(8,128)(2,1)S(1)}, bf16[2048,128]{1,0:T(8,128)(2,1)S(1)}, bf16[2048,128]{1,0:T(8,128)(2,1)S(1)}, bf16[2048,128]{1,0:T(8,128)(2,1)S(1)}) custom-call(s32[4,128]{1,0:T(4,128)S(1)} %maximum_convert_fusion.ask_ref, s32[3]{0:T(128)S(1)} %pad_add_fusion.1.place_ref, bf16[2064,128]{1,0:T(8,128)(2,1)} %get-tuple-element.18.own, ...), custom_call_target="tpu_custom_call" | custom-call | tf_op jit(solution)/shard_map/pack/pallas_call | solution.py:165
  48.9 3.8 %collective-permute-start.7 = (bf16[2048,128]{1,0:T(8,128)(2,1)S(1)}, bf16[2048,128]{1,0:T(8,128)(2,1)S(1)}, u32[]{:S(2)}, u32[]{:S(2)}) collective-permute-start(bf16[2048,128]{1,0:T(8,128)(2,1)S(1)} %get-tuple-element.20), channel_id=1, source_target_pairs={{0,6},{2,0},{4,2},{6,4},{8,14},{10,8},{12,10},{14,12},{16,22},{18,... | collective-permute-start | bytes 1572872 | tf_op jit(solution)/shard_map/ppermute | solution.py:35
  52.7 12.2 %collective-permute-done.11 = bf16[2048,128]{1,0:T(8,128)(2,1)S(1)} collective-permute-done((bf16[2048,128]{1,0:T(8,128)(2,1)S(1)}, bf16[2048,128]{1,0:T(8,128)(2,1)S(1)}, u32[]{:S(2)}, u32[]{:S(2)}) %collective-permute-start.11) | collective-permute-done | bytes 524320 | tf_op jit(solution)/shard_map/ppermute | solution.py:35
  64.9 2.5 %collective-permute-start.8 = (bf16[2048,128]{1,0:T(8,128)(2,1)S(1)}, bf16[2048,128]{1,0:T(8,128)(2,1)S(1)}, u32[]{:S(2)}, u32[]{:S(2)}) collective-permute-start(bf16[2048,128]{1,0:T(8,128)(2,1)S(1)} %get-tuple-element.21), channel_id=1, source_target_pairs={{0,4},{2,6},{4,0},{6,2},{8,12},{10,14},{12,8},{14,10},{16,20},{18,... | collective-permute-start | bytes 1572872 | tf_op jit(solution)/shard_map/ppermute | solution.py:35
  67.4 1.9 %collective-permute-start.9 = (bf16[2048,128]{1,0:T(8,128)(2,1)S(1)}, bf16[2048,128]{1,0:T(8,128)(2,1)S(1)}, u32[]{:S(2)}, u32[]{:S(2)}) collective-permute-start(bf16[2048,128]{1,0:T(8,128)(2,1)S(1)} %get-tuple-element.22), channel_id=1, source_target_pairs={{0,2},{2,4},{4,6},{6,0},{8,10},{10,12},{12,14},{14,8},{16,18},{18,... | collective-permute-start | bytes 1572872 | tf_op jit(solution)/shard_map/ppermute | solution.py:35
  69.6 7.7 %collective-permute-done.8 = bf16[2048,128]{1,0:T(8,128)(2,1)S(1)} collective-permute-done((bf16[2048,128]{1,0:T(8,128)(2,1)S(1)}, bf16[2048,128]{1,0:T(8,128)(2,1)S(1)}, u32[]{:S(2)}, u32[]{:S(2)}) %collective-permute-start.8) | collective-permute-done | bytes 524320 | tf_op jit(solution)/shard_map/ppermute | solution.py:35
  77.4 5.0 %collective-permute-done.9 = bf16[2048,128]{1,0:T(8,128)(2,1)S(1)} collective-permute-done((bf16[2048,128]{1,0:T(8,128)(2,1)S(1)}, bf16[2048,128]{1,0:T(8,128)(2,1)S(1)}, u32[]{:S(2)}, u32[]{:S(2)}) %collective-permute-start.9) | collective-permute-done | bytes 524320 | tf_op jit(solution)/shard_map/ppermute | solution.py:35
  82.5 4.5 %attend.5 = bf16[256,512]{1,0:T(8,128)(2,1)S(1)} custom-call(s32[8,128]{1,0:T(8,128)S(1)} %get-tuple-element.16.slots_ref, s32[2]{0:T(128)S(1)} %pad_add_fusion.place_ref, bf16[256,512]{1,0:T(8,128)(2,1)S(1)} %get-tuple-element.38.q_ref, bf16[8192,128]{1,0:T(8,128)(2,1)S(1)} %constant_dynamic-update-slice_fusion.k_ref, ...), custom_call_target="tpu_custom_call" | custom-call | flops 536870912 | bytes 524288 | tf_op jit(solution)/shard_map/attend/pallas_call | solution.py:206
  86.9 1.1 collective-permute-start.18
  88.0 4.4 %attend.4 = bf16[256,512]{1,0:T(8,128)(2,1)S(1)} custom-call(s32[8,128]{1,0:T(8,128)S(1)} %get-tuple-element.16.slots_ref, s32[2]{0:T(128)S(1)} %pad_add_fusion.place_ref, bf16[256,512]{1,0:T(8,128)(2,1)S(1)} %get-tuple-element.35.q_ref, bf16[8192,128]{1,0:T(8,128)(2,1)S(1)} %constant_dynamic-update-slice_fusion.k_ref, ...), custom_call_target="tpu_custom_call" | custom-call | flops 536870912 | bytes 524288 | tf_op jit(solution)/shard_map/attend/pallas_call | solution.py:206
  92.5 1.1 collective-permute-start.14
  93.6 4.4 %attend.6 = bf16[256,512]{1,0:T(8,128)(2,1)S(1)} custom-call(s32[8,128]{1,0:T(8,128)S(1)} %get-tuple-element.16.slots_ref, s32[2]{0:T(128)S(1)} %pad_add_fusion.place_ref, bf16[256,512]{1,0:T(8,128)(2,1)S(1)} %get-tuple-element.37.q_ref, bf16[8192,128]{1,0:T(8,128)(2,1)S(1)} %constant_dynamic-update-slice_fusion.k_ref, ...), custom_call_target="tpu_custom_call" | custom-call | flops 536870912 | bytes 524288 | tf_op jit(solution)/shard_map/attend/pallas_call | solution.py:206
  98.0 1.3 collective-permute-start.21
  99.3 4.4 %attend.7 = bf16[256,512]{1,0:T(8,128)(2,1)S(1)} custom-call(s32[8,128]{1,0:T(8,128)S(1)} %get-tuple-element.16.slots_ref, s32[2]{0:T(128)S(1)} %pad_add_fusion.place_ref, bf16[256,512]{1,0:T(8,128)(2,1)S(1)} %get-tuple-element.36.q_ref, bf16[8192,128]{1,0:T(8,128)(2,1)S(1)} %constant_dynamic-update-slice_fusion.k_ref, ...), custom_call_target="tpu_custom_call" | custom-call | flops 536870912 | bytes 524288 | tf_op jit(solution)/shard_map/attend/pallas_call | solution.py:206
  103.8 1.1 collective-permute-start.24
  104.9 1.7 %fusion.22 = f32[256,1024]{1,0:T(8,128)S(1)} fusion(bf16[256,512]{1,0:T(8,128)(2,1)S(1)} %collective-permute-done.18, bf16[512,2048]{1,0:T(8,128)(2,1)} %collective-permute-done.15), kind=kOutput, calls=%fused_computation.33 | convolution fusion | flops 268435456 | bytes 2359296 | tf_op jit(solution)/shard_map/dot_general | solution.py:320
  107.2 1.7 %fusion.20 = f32[256,1024]{1,0:T(8,128)S(1)} fusion(bf16[256,512]{1,0:T(8,128)(2,1)S(1)} %collective-permute-done.21, bf16[512,2048]{1,0:T(8,128)(2,1)} %collective-permute-done.15), kind=kOutput, calls=%fused_computation.31 | convolution fusion | flops 268435456 | bytes 2359296 | tf_op jit(solution)/shard_map/dot_general | solution.py:320
  110.3 1.7 %fusion.18 = f32[256,1024]{1,0:T(8,128)S(1)} fusion(bf16[256,512]{1,0:T(8,128)(2,1)S(1)} %collective-permute-done.24, bf16[512,2048]{1,0:T(8,128)(2,1)} %collective-permute-done.15), kind=kOutput, calls=%fused_computation.29 | convolution fusion | flops 268435456 | bytes 2359296 | tf_op jit(solution)/shard_map/dot_general | solution.py:320
  112.5 1.7 %fusion.24 = f32[256,1024]{1,0:T(8,128)S(1)} fusion(bf16[256,512]{1,0:T(8,128)(2,1)S(1)} %collective-permute-done.14, bf16[512,2048]{1,0:T(8,128)(2,1)} %collective-permute-done.15), kind=kOutput, calls=%fused_computation.35 | convolution fusion | flops 268435456 | bytes 2359296 | tf_op jit(solution)/shard_map/dot_general | solution.py:320
  115.2 1.7 %fusion.30 = f32[256,1024]{1,0:T(8,128)S(1)} fusion(bf16[256,512]{1,0:T(8,128)(2,1)S(1)} %collective-permute-done.18, bf16[512,2048]{1,0:T(8,128)(2,1)} %collective-permute-done.15), kind=kOutput, calls=%fused_computation.41 | convolution fusion | flops 268435456 | bytes 2359296 | tf_op jit(solution)/shard_map/dot_general | solution.py:320
  116.9 1.7 %fusion.28 = f32[256,1024]{1,0:T(8,128)S(1)} fusion(bf16[256,512]{1,0:T(8,128)(2,1)S(1)} %collective-permute-done.21, bf16[512,2048]{1,0:T(8,128)(2,1)} %collective-permute-done.15), kind=kOutput, calls=%fused_computation.39 | convolution fusion | flops 268435456 | bytes 2359296 | tf_op jit(solution)/shard_map/dot_general | solution.py:320
  118.6 1.8 %fusion.26 = f32[256,1024]{1,0:T(8,128)S(1)} fusion(bf16[256,512]{1,0:T(8,128)(2,1)S(1)} %collective-permute-done.24, bf16[512,2048]{1,0:T(8,128)(2,1)} %collective-permute-done.15), kind=kOutput, calls=%fused_computation.37 | convolution fusion | flops 268435456 | bytes 2359296 | tf_op jit(solution)/shard_map/dot_general | solution.py:320
  120.4 1.7 %fusion.32 = f32[256,1024]{1,0:T(8,128)S(1)} fusion(bf16[256,512]{1,0:T(8,128)(2,1)S(1)} %collective-permute-done.14, bf16[512,2048]{1,0:T(8,128)(2,1)} %collective-permute-done.15), kind=kOutput, calls=%fused_computation.43 | convolution fusion | flops 268435456 | bytes 2359296 | tf_op jit(solution)/shard_map/dot_general | solution.py:320
  122.6 3.2 %collective-permute-start.20 = (bf16[256,512]{1,0:T(8,128)(2,1)S(1)}, bf16[256,512]{1,0:T(8,128)(2,1)S(1)}, u32[]{:S(2)}, u32[]{:S(2)}) collective-permute-start(bf16[256,512]{1,0:T(8,128)(2,1)S(1)} %slice.166), channel_id=1, source_target_pairs={{0,65},{32,97},{64,1},{96,33},{1,64},{33,96},{65,0},{97,32},{2,67}... | collective-permute-start | bytes 786440 | tf_op jit(solution)/shard_map/ppermute | solution.py:47
  126.9 3.2 %collective-permute-start.26 = (bf16[256,512]{1,0:T(8,128)(2,1)S(1)}, bf16[256,512]{1,0:T(8,128)(2,1)S(1)}, u32[]{:S(2)}, u32[]{:S(2)}) collective-permute-start(bf16[256,512]{1,0:T(8,128)(2,1)S(1)} %slice.164), channel_id=1, source_target_pairs={{0,65},{32,97},{64,1},{96,33},{1,64},{33,96},{65,0},{97,32},{2,67}... | collective-permute-start | bytes 786440 | tf_op jit(solution)/shard_map/ppermute | solution.py:47
  130.8 2.2 %collective-permute-done.20 = bf16[256,512]{1,0:T(8,128)(2,1)S(1)} collective-permute-done((bf16[256,512]{1,0:T(8,128)(2,1)S(1)}, bf16[256,512]{1,0:T(8,128)(2,1)S(1)}, u32[]{:S(2)}, u32[]{:S(2)}) %collective-permute-start.20) | collective-permute-done | bytes 262176 | tf_op jit(solution)/shard_map/ppermute | solution.py:47
  133.1 5.5 %collective-permute-done.23 = bf16[256,512]{1,0:T(8,128)(2,1)S(1)} collective-permute-done((bf16[256,512]{1,0:T(8,128)(2,1)S(1)}, bf16[256,512]{1,0:T(8,128)(2,1)S(1)}, u32[]{:S(2)}, u32[]{:S(2)}) %collective-permute-start.23) | collective-permute-done | bytes 262176 | tf_op jit(solution)/shard_map/ppermute | solution.py:47
  138.7 5.5 %collective-permute-done.26 = bf16[256,512]{1,0:T(8,128)(2,1)S(1)} collective-permute-done((bf16[256,512]{1,0:T(8,128)(2,1)S(1)}, bf16[256,512]{1,0:T(8,128)(2,1)S(1)}, u32[]{:S(2)}, u32[]{:S(2)}) %collective-permute-start.26) | collective-permute-done | bytes 262176 | tf_op jit(solution)/shard_map/ppermute | solution.py:47
  144.3 4.8 %collective-permute-done.17 = bf16[256,512]{1,0:T(8,128)(2,1)S(1)} collective-permute-done((bf16[256,512]{1,0:T(8,128)(2,1)S(1)}, bf16[256,512]{1,0:T(8,128)(2,1)S(1)}, u32[]{:S(2)}, u32[]{:S(2)}) %collective-permute-start.17) | collective-permute-done | bytes 262176 | tf_op jit(solution)/shard_map/ppermute | solution.py:47
  149.2 1.0 pad_maximum_fusion.3
  (90 shorter events, 14.5 us)
Async XLA Ops:
  0.8 2.2 %copy-start = (bf16[2048,1024]{1,0:T(8,128)(2,1)S(1)}, bf16[2048,1024]{1,0:T(8,128)(2,1)}, u32[]{:S(2)}) copy-start(bf16[2048,1024]{1,0:T(8,128)(2,1)} %x_ref.1) | copy-start | bytes 12582916
  3.0 0.9 copy-start.1
  3.9 0.9 copy-start.2
  8.2 23.8 %collective-permute-start.2 = (bf16[2064,128]{1,0:T(8,128)(2,1)}, bf16[2064,128]{1,0:T(8,128)(2,1)S(1)}, u32[]{:S(2)}, u32[]{:S(2)}) collective-permute-start(bf16[2064,128]{1,0:T(8,128)(2,1)} %get-tuple-element.17.own), channel_id=1, source_target_pairs={{0,2},{2,4},{4,6},{6,0},{8,10},{10,12},{12,14},{14,8},{16,18},{18,... | collective-permute-start | bytes 1585160 | tf_op jit(solution)/shard_map/ppermute | solution.py:35
  9.8 23.3 %collective-permute-start = (bf16[2064,128]{1,0:T(8,128)(2,1)}, bf16[2064,128]{1,0:T(8,128)(2,1)S(1)}, u32[]{:S(2)}, u32[]{:S(2)}) collective-permute-start(bf16[2064,128]{1,0:T(8,128)(2,1)} %get-tuple-element.17.own), channel_id=1, source_target_pairs={{0,6},{2,0},{4,2},{6,4},{8,14},{10,8},{12,10},{14,12},{16,22},{18,... | collective-permute-start | bytes 1585160 | tf_op jit(solution)/shard_map/ppermute | solution.py:35
  11.5 25.4 %collective-permute-start.4 = (bf16[2064,128]{1,0:T(8,128)(2,1)}, bf16[2064,128]{1,0:T(8,128)(2,1)S(1)}, u32[]{:S(2)}, u32[]{:S(2)}) collective-permute-start(bf16[2064,128]{1,0:T(8,128)(2,1)} %get-tuple-element.18.own), channel_id=1, source_target_pairs={{0,8},{2,10},{4,12},{6,14},{8,16},{10,18},{12,20},{14,22},{16,24},... | collective-permute-start | bytes 1585160 | tf_op jit(solution)/shard_map/ppermute | solution.py:35
  12.9 16.5 %collective-permute-start.3 = (bf16[2064,128]{1,0:T(8,128)(2,1)}, bf16[2064,128]{1,0:T(8,128)(2,1)S(1)}, u32[]{:S(2)}, u32[]{:S(2)}) collective-permute-start(bf16[2064,128]{1,0:T(8,128)(2,1)} %get-tuple-element.18.own), channel_id=1, source_target_pairs={{0,24},{2,26},{4,28},{6,30},{8,0},{10,2},{12,4},{14,6},{16,8},{18,... | collective-permute-start | bytes 1585160 | tf_op jit(solution)/shard_map/ppermute | solution.py:35
  13.5 7.4 %copy-start.7 = (bf16[1024,4096]{1,0:T(8,128)(2,1)S(1)}, bf16[1024,4096]{1,0:T(8,128)(2,1)}, u32[]{:S(2)}) copy-start(bf16[1024,4096]{1,0:T(8,128)(2,1)} %param.8) | copy-start | bytes 25165828
  19.0 3.6 %copy-start.8 = (bf16[4096,512]{1,0:T(8,128)(2,1)S(1)}, bf16[4096,512]{1,0:T(8,128)(2,1)}, u32[]{:S(2)}) copy-start(bf16[4096,512]{1,0:T(8,128)(2,1)} %param.11) | copy-start | bytes 12582916
  19.0 3.6 %copy-start.9 = (f32[4096]{0:T(1024)S(1)}, f32[4096]{0:T(1024)}, u32[]{:S(2)}) copy-start(f32[4096]{0:T(1024)} %param.9) | copy-start | bytes 49156
  19.0 85.9 %collective-permute-start.15 = (bf16[512,2048]{1,0:T(8,128)(2,1)}, bf16[512,2048]{1,0:T(8,128)(2,1)}, u32[]{:S(2)}, u32[]{:S(2)}) collective-permute-start(bf16[512,2048]{1,0:T(8,128)(2,1)} %pad_maximum_fusion), channel_id=1, source_target_pairs={{0,64},{32,96},{64,0},{96,32},{1,65},{33,97},{65,1},{97,33},{2,66}... | collective-permute-start | bytes 6291464 | tf_op jit(solution)/shard_map/ppermute | solution.py:47
  30.2 8.4 %collective-permute-start.6 = (bf16[1040,128]{1,0:T(8,128)(2,1)}, bf16[1040,128]{1,0:T(8,128)(2,1)S(1)}, u32[]{:S(2)}, u32[]{:S(2)}) collective-permute-start(bf16[1040,128]{1,0:T(8,128)(2,1)} %slice.114), channel_id=1, source_target_pairs={{0,24},{2,26},{4,28},{6,30},{8,0},{10,2},{12,4},{14,6},{16,8},{18,... | collective-permute-start | bytes 798728 | tf_op jit(solution)/shard_map/ppermute | solution.py:35
  32.8 7.9 %collective-permute-start.10 = (bf16[1024,128]{1,0:T(8,128)(2,1)}, bf16[1024,128]{1,0:T(8,128)(2,1)}, u32[]{:S(2)}, u32[]{:S(2)}) collective-permute-start(bf16[1024,128]{1,0:T(8,128)(2,1)} %slice.118), channel_id=1, source_target_pairs={{0,2},{2,4},{4,6},{6,0},{8,10},{10,12},{12,14},{14,8},{16,18},{18,... | collective-permute-start | bytes 786440 | tf_op jit(solution)/shard_map/ppermute | solution.py:35
  33.9 7.1 %collective-permute-start.1 = (bf16[1040,128]{1,0:T(8,128)(2,1)}, bf16[1040,128]{1,0:T(8,128)(2,1)}, u32[]{:S(2)}, u32[]{:S(2)}) collective-permute-start(bf16[1040,128]{1,0:T(8,128)(2,1)} %slice.110), channel_id=1, source_target_pairs={{0,6},{2,0},{4,2},{6,4},{8,14},{10,8},{12,10},{14,12},{16,22},{18,... | collective-permute-start | bytes 798728 | tf_op jit(solution)/shard_map/ppermute | solution.py:35
  36.8 10.4 %collective-permute-start.5 = (bf16[1024,128]{1,0:T(8,128)(2,1)S(1)}, bf16[1024,128]{1,0:T(8,128)(2,1)S(1)}, u32[]{:S(2)}, u32[]{:S(2)}) collective-permute-start(bf16[1024,128]{1,0:T(8,128)(2,1)S(1)} %slice.113), channel_id=1, source_target_pairs={{0,8},{2,10},{4,12},{6,14},{8,16},{10,18},{12,20},{14,22},{16,24},... | collective-permute-start | bytes 786440 | tf_op jit(solution)/shard_map/ppermute | solution.py:35
  42.7 22.2 %collective-permute-start.11 = (bf16[2048,128]{1,0:T(8,128)(2,1)S(1)}, bf16[2048,128]{1,0:T(8,128)(2,1)S(1)}, u32[]{:S(2)}, u32[]{:S(2)}) collective-permute-start(bf16[2048,128]{1,0:T(8,128)(2,1)S(1)} %get-tuple-element.24), channel_id=1, source_target_pairs={{0,24},{2,26},{4,28},{6,30},{8,0},{10,2},{12,4},{14,6},{16,8},{18,... | collective-permute-start | bytes 1572872 | tf_op jit(solution)/shard_map/ppermute | solution.py:35
  44.3 23.1 %collective-permute-start.12 = (bf16[2048,128]{1,0:T(8,128)(2,1)S(1)}, bf16[2048,128]{1,0:T(8,128)(2,1)S(1)}, u32[]{:S(2)}, u32[]{:S(2)}) collective-permute-start(bf16[2048,128]{1,0:T(8,128)(2,1)S(1)} %get-tuple-element.25), channel_id=1, source_target_pairs={{0,16},{2,18},{4,20},{6,22},{8,24},{10,26},{12,28},{14,30},{16,0},... | collective-permute-start | bytes 1572872 | tf_op jit(solution)/shard_map/ppermute | solution.py:35
  44.5 24.9 %collective-permute-start.13 = (bf16[2048,128]{1,0:T(8,128)(2,1)S(1)}, bf16[2048,128]{1,0:T(8,128)(2,1)S(1)}, u32[]{:S(2)}, u32[]{:S(2)}) collective-permute-start(bf16[2048,128]{1,0:T(8,128)(2,1)S(1)} %get-tuple-element.26), channel_id=1, source_target_pairs={{0,8},{2,10},{4,12},{6,14},{8,16},{10,18},{12,20},{14,22},{16,24},... | collective-permute-start | bytes 1572872 | tf_op jit(solution)/shard_map/ppermute | solution.py:35
  48.9 20.6 %collective-permute-start.7 = (bf16[2048,128]{1,0:T(8,128)(2,1)S(1)}, bf16[2048,128]{1,0:T(8,128)(2,1)S(1)}, u32[]{:S(2)}, u32[]{:S(2)}) collective-permute-start(bf16[2048,128]{1,0:T(8,128)(2,1)S(1)} %get-tuple-element.20), channel_id=1, source_target_pairs={{0,6},{2,0},{4,2},{6,4},{8,14},{10,8},{12,10},{14,12},{16,22},{18,... | collective-permute-start | bytes 1572872 | tf_op jit(solution)/shard_map/ppermute | solution.py:35
  64.9 12.4 %collective-permute-start.8 = (bf16[2048,128]{1,0:T(8,128)(2,1)S(1)}, bf16[2048,128]{1,0:T(8,128)(2,1)S(1)}, u32[]{:S(2)}, u32[]{:S(2)}) collective-permute-start(bf16[2048,128]{1,0:T(8,128)(2,1)S(1)} %get-tuple-element.21), channel_id=1, source_target_pairs={{0,4},{2,6},{4,0},{6,2},{8,12},{10,14},{12,8},{14,10},{16,20},{18,... | collective-permute-start | bytes 1572872 | tf_op jit(solution)/shard_map/ppermute | solution.py:35
  67.4 15.0 %collective-permute-start.9 = (bf16[2048,128]{1,0:T(8,128)(2,1)S(1)}, bf16[2048,128]{1,0:T(8,128)(2,1)S(1)}, u32[]{:S(2)}, u32[]{:S(2)}) collective-permute-start(bf16[2048,128]{1,0:T(8,128)(2,1)S(1)} %get-tuple-element.22), channel_id=1, source_target_pairs={{0,2},{2,4},{4,6},{6,0},{8,10},{10,12},{12,14},{14,8},{16,18},{18,... | collective-permute-start | bytes 1572872 | tf_op jit(solution)/shard_map/ppermute | solution.py:35
  86.9 18.0 %collective-permute-start.18 = (bf16[256,512]{1,0:T(8,128)(2,1)S(1)}, bf16[256,512]{1,0:T(8,128)(2,1)S(1)}, u32[]{:S(2)}, u32[]{:S(2)}) collective-permute-start(bf16[256,512]{1,0:T(8,128)(2,1)S(1)} %attend.5), channel_id=1, source_target_pairs={{0,64},{32,96},{64,0},{96,32},{1,65},{33,97},{65,1},{97,33},{2,66}... | collective-permute-start | bytes 786440 | tf_op jit(solution)/shard_map/ppermute | solution.py:47
  92.5 20.0 %collective-permute-start.14 = (bf16[256,512]{1,0:T(8,128)(2,1)S(1)}, bf16[256,512]{1,0:T(8,128)(2,1)S(1)}, u32[]{:S(2)}, u32[]{:S(2)}) collective-permute-start(bf16[256,512]{1,0:T(8,128)(2,1)S(1)} %attend.4), channel_id=1, source_target_pairs={{0,64},{32,96},{64,0},{96,32},{1,65},{33,97},{65,1},{97,33},{2,66}... | collective-permute-start | bytes 786440 | tf_op jit(solution)/shard_map/ppermute | solution.py:47
  98.0 9.1 %collective-permute-start.21 = (bf16[256,512]{1,0:T(8,128)(2,1)S(1)}, bf16[256,512]{1,0:T(8,128)(2,1)S(1)}, u32[]{:S(2)}, u32[]{:S(2)}) collective-permute-start(bf16[256,512]{1,0:T(8,128)(2,1)S(1)} %attend.6), channel_id=1, source_target_pairs={{0,64},{32,96},{64,0},{96,32},{1,65},{33,97},{65,1},{97,33},{2,66}... | collective-permute-start | bytes 786440 | tf_op jit(solution)/shard_map/ppermute | solution.py:47
  103.8 2.8 %copy-start.5 = (bf16[512,512]{1,0:T(8,128)(2,1)S(1)}, bf16[512,512]{1,0:T(8,128)(2,1)}, u32[]{:S(2)}) copy-start(bf16[512,512]{1,0:T(8,128)(2,1)} %get-tuple-element.33) | copy-start | bytes 1572868
  103.8 2.8 %copy-start.6 = (bf16[512,512]{1,0:T(8,128)(2,1)S(1)}, bf16[512,512]{1,0:T(8,128)(2,1)}, u32[]{:S(2)}) copy-start(bf16[512,512]{1,0:T(8,128)(2,1)} %get-tuple-element.34) | copy-start | bytes 1572868
  103.8 6.5 %collective-permute-start.24 = (bf16[256,512]{1,0:T(8,128)(2,1)S(1)}, bf16[256,512]{1,0:T(8,128)(2,1)S(1)}, u32[]{:S(2)}, u32[]{:S(2)}) collective-permute-start(bf16[256,512]{1,0:T(8,128)(2,1)S(1)} %attend.7), channel_id=1, source_target_pairs={{0,64},{32,96},{64,0},{96,32},{1,65},{33,97},{65,1},{97,33},{2,66}... | collective-permute-start | bytes 786440 | tf_op jit(solution)/shard_map/ppermute | solution.py:47
  107.1 15.0 %collective-permute-start.19 = (bf16[256,1024]{1,0:T(8,128)(2,1)S(1)}, bf16[256,1024]{1,0:T(8,128)(2,1)S(1)}, u32[]{:S(2)}, u32[]{:S(2)}) collective-permute-start(bf16[256,1024]{1,0:T(8,128)(2,1)S(1)} %fusion.15), channel_id=1, source_target_pairs={{0,32},{32,0},{64,96},{96,64},{1,33},{33,1},{65,97},{97,65},{2,34}... | collective-permute-start | bytes 1572872 | tf_op jit(solution)/shard_map/ppermute | solution.py:47
  109.3 16.5 %collective-permute-start.22 = (bf16[256,1024]{1,0:T(8,128)(2,1)S(1)}, bf16[256,1024]{1,0:T(8,128)(2,1)S(1)}, u32[]{:S(2)}, u32[]{:S(2)}) collective-permute-start(bf16[256,1024]{1,0:T(8,128)(2,1)S(1)} %fusion.16), channel_id=1, source_target_pairs={{0,32},{32,0},{64,96},{96,64},{1,33},{33,1},{65,97},{97,65},{2,34}... | collective-permute-start | bytes 1572872 | tf_op jit(solution)/shard_map/ppermute | solution.py:47
  112.4 14.1 %collective-permute-start.25 = (bf16[256,1024]{1,0:T(8,128)(2,1)S(1)}, bf16[256,1024]{1,0:T(8,128)(2,1)S(1)}, u32[]{:S(2)}, u32[]{:S(2)}) collective-permute-start(bf16[256,1024]{1,0:T(8,128)(2,1)S(1)} %fusion.17), channel_id=1, source_target_pairs={{0,32},{32,0},{64,96},{96,64},{1,33},{33,1},{65,97},{97,65},{2,34}... | collective-permute-start | bytes 1572872 | tf_op jit(solution)/shard_map/ppermute | solution.py:47
  114.6 15.6 %collective-permute-start.16 = (bf16[256,1024]{1,0:T(8,128)(2,1)S(1)}, bf16[256,1024]{1,0:T(8,128)(2,1)S(1)}, u32[]{:S(2)}, u32[]{:S(2)}) collective-permute-start(bf16[256,1024]{1,0:T(8,128)(2,1)S(1)} %fusion.14), channel_id=1, source_target_pairs={{0,32},{32,0},{64,96},{96,64},{1,33},{33,1},{65,97},{97,65},{2,34}... | collective-permute-start | bytes 1572872 | tf_op jit(solution)/shard_map/ppermute | solution.py:47
  118.6 3.5 %copy-start.3 = (bf16[512,512]{1,0:T(8,128)(2,1)S(1)}, bf16[512,512]{1,0:T(8,128)(2,1)}, u32[]{:S(2)}) copy-start(bf16[512,512]{1,0:T(8,128)(2,1)} %get-tuple-element.27) | copy-start | bytes 1572868
  118.6 3.5 %copy-start.4 = (bf16[512,512]{1,0:T(8,128)(2,1)S(1)}, bf16[512,512]{1,0:T(8,128)(2,1)}, u32[]{:S(2)}) copy-start(bf16[512,512]{1,0:T(8,128)(2,1)} %get-tuple-element.32) | copy-start | bytes 1572868
  122.6 10.4 %collective-permute-start.20 = (bf16[256,512]{1,0:T(8,128)(2,1)S(1)}, bf16[256,512]{1,0:T(8,128)(2,1)S(1)}, u32[]{:S(2)}, u32[]{:S(2)}) collective-permute-start(bf16[256,512]{1,0:T(8,128)(2,1)S(1)} %slice.166), channel_id=1, source_target_pairs={{0,65},{32,97},{64,1},{96,33},{1,64},{33,96},{65,0},{97,32},{2,67}... | collective-permute-start | bytes 786440 | tf_op jit(solution)/shard_map/ppermute | solution.py:47
  126.3 12.3 %collective-permute-start.23 = (bf16[256,512]{1,0:T(8,128)(2,1)S(1)}, bf16[256,512]{1,0:T(8,128)(2,1)S(1)}, u32[]{:S(2)}, u32[]{:S(2)}) collective-permute-start(bf16[256,512]{1,0:T(8,128)(2,1)S(1)} %slice.165), channel_id=1, source_target_pairs={{0,65},{32,97},{64,1},{96,33},{1,64},{33,96},{65,0},{97,32},{2,67}... | collective-permute-start | bytes 786440 | tf_op jit(solution)/shard_map/ppermute | solution.py:47
  126.9 17.3 %collective-permute-start.26 = (bf16[256,512]{1,0:T(8,128)(2,1)S(1)}, bf16[256,512]{1,0:T(8,128)(2,1)S(1)}, u32[]{:S(2)}, u32[]{:S(2)}) collective-permute-start(bf16[256,512]{1,0:T(8,128)(2,1)S(1)} %slice.164), channel_id=1, source_target_pairs={{0,65},{32,97},{64,1},{96,33},{1,64},{33,96},{65,0},{97,32},{2,67}... | collective-permute-start | bytes 786440 | tf_op jit(solution)/shard_map/ppermute | solution.py:47
  130.7 18.5 %collective-permute-start.17 = (bf16[256,512]{1,0:T(8,128)(2,1)S(1)}, bf16[256,512]{1,0:T(8,128)(2,1)S(1)}, u32[]{:S(2)}, u32[]{:S(2)}) collective-permute-start(bf16[256,512]{1,0:T(8,128)(2,1)S(1)} %slice.167), channel_id=1, source_target_pairs={{0,65},{32,97},{64,1},{96,33},{1,64},{33,96},{65,0},{97,32},{2,67}... | collective-permute-start | bytes 786440 | tf_op jit(solution)/shard_map/ppermute | solution.py:47

commit v2 on v1

v2 whole, which is shorter than its diff:
```python
import functools

import jax
import jax.numpy as jnp
from jax import lax
from jax.experimental import pallas as pl
from jax.experimental.pallas import tpu as pltpu
from jax.sharding import PartitionSpec as P

HEADS = 32
KV_HEADS = 8
HEAD_DIM = 128
GROUP = HEADS // KV_HEADS
TILE = 128
BLOCK = 64
TOPK = 16
SIDE = 4
CAP = 8
PICKS = SIDE * SIDE * CAP
NOTE_ROWS = 16
EPSILON = 1e-05
NEAR_PIECES = (128, 128, 192, 64)
CHUNKS = (2, 2, 2, 2)
AHEAD = 4
SCALE = HEAD_DIM**-0.5
LOG2_E = 1.4426950408889634

SECTION_HEAD = ("section", "head")
SMALL = pl.CostEstimate(flops=1, bytes_accessed=1, transcendentals=0)
VMEM_WHOLE = pl.BlockSpec(memory_space=pltpu.VMEM)
HBM_WHOLE = pl.BlockSpec(memory_space=pltpu.HBM)
SMEM_WHOLE = pl.BlockSpec(memory_space=pltpu.SMEM)


def along_seq(value, dx, dy):
    pairs = [
        (x * SIDE + y, (x + dx) % SIDE * SIDE + (y + dy) % SIDE)
        for x in range(SIDE)
        for y in range(SIDE)
    ]
    return lax.ppermute(value, "seq", pairs)


def column(z, core):
    return (z % 2) * 4 + core * 2 + z // 2


def along_z(value, place):
    pairs = []
    for z in range(4):
        for core in range(2):
            pairs.append((column(z, core), column(*place(z, core))))
    return lax.ppermute(value, SECTION_HEAD, pairs)


def to_near(value):
    return along_z(value, lambda z, core: (z ^ 1, core))


def to_far(value):
    return along_z(value, lambda z, core: (3 - z, core))


def to_core(value):
    return along_z(value, lambda z, core: (z, 1 - core))


def project_body(
    selected_ref, places_ref, x_ref, wk_ref, wv_ref, wo_ref, k_ref, v_ref, slots_ref, *rest
):
    piece_refs, (w_ref, sem) = rest[:-2], rest[-2:]
    step = pl.program_id(0)

    def copies():
        width = wo_ref.shape[1] // 8
        found, at = [], 0
        for index, piece in enumerate(piece_refs):
            for group in range(4):
                start = pl.multiple_of(places_ref[group] * width, width)
                found.append(
                    pltpu.make_async_copy(
                        wo_ref.at[pl.ds(at, piece.shape[0]), pl.ds(start, width)],
                        piece.at[:, pl.ds(group * width, width)],
                        sem.at[index * 4 + group],
                    )
                )
            at += piece.shape[0]
        return found

    rows = x_ref.shape[0]
    steps = pl.num_programs(0)
    blocks_dev = (k_ref.shape[0] - NOTE_ROWS) // BLOCK
    blocks = SIDE * SIDE * blocks_dev

    @pl.when(step == 0)
    def _():
        w_ref[:, :HEAD_DIM] = wk_ref[...]
        w_ref[:, HEAD_DIM:] = wv_ref[...]
        for copy in copies():
            copy.start()

    @pl.when(step == steps - 1)
    def _():
        picked = selected_ref[...]
        tiles, per_tile = picked.shape
        source = lax.broadcasted_iota(jnp.int32, (per_tile, PICKS), 0)
        place = lax.broadcasted_iota(jnp.int32, (per_tile, PICKS), 1)
        repeat = (place % per_tile == source).astype(jnp.float32).astype(jnp.bfloat16)

        def repeated(part):
            part = part.astype(jnp.float32).astype(jnp.bfloat16)
            return jnp.dot(part, repeat, preferred_element_type=jnp.float32)

        wide = repeated(picked // blocks_dev) * blocks_dev + repeated(picked % blocks_dev)
        tile = lax.broadcasted_iota(jnp.int32, (tiles, PICKS), 0)
        at = lax.broadcasted_iota(jnp.int32, (tiles, PICKS), 1)
        ids = jnp.sum(jnp.where(at // per_tile == tile, wide, 0.0), axis=0, keepdims=True)

        block = lax.broadcasted_iota(jnp.int32, (blocks, PICKS), 0)
        hit = (block == ids.astype(jnp.int32)).astype(jnp.float32)
        wanted = jnp.broadcast_to(jnp.max(hit, axis=1, keepdims=True), (blocks, PICKS))
        one = lax.broadcasted_iota(jnp.int32, (blocks, blocks), 0)
        other = lax.broadcasted_iota(jnp.int32, (blocks, blocks), 1)
        before = (one // blocks_dev == other // blocks_dev) & (other < one)
        rank = jnp.dot(
            before.astype(jnp.float32).astype(jnp.bfloat16),
            wanted.astype(jnp.bfloat16),
            preferred_element_type=jnp.float32,
        )
        owner = block // blocks_dev
        slot = (owner * CAP).astype(jnp.float32) + rank
        slots = jnp.sum(hit * slot, axis=0, keepdims=True)
        slots_ref[...] = jnp.broadcast_to(slots, slots_ref.shape).astype(jnp.int32)
        place = lax.broadcasted_iota(jnp.int32, (blocks, PICKS), 1).astype(jnp.float32)
        local = (block % blocks_dev).astype(jnp.float32)
        asked = jnp.sum(
            jnp.where(slot == place, wanted * local, 0.0), axis=0, keepdims=True
        )
        note = jnp.broadcast_to(asked, (NOTE_ROWS, PICKS)).astype(jnp.bfloat16)
        k_ref[rows * steps :, :] = note
        v_ref[rows * steps :, :] = note

    both = jnp.dot(x_ref[...], w_ref[...], preferred_element_type=jnp.float32)
    at = pl.ds(pl.multiple_of(step * rows, rows), rows)
    k_ref[at, :] = both[:, :HEAD_DIM].astype(jnp.bfloat16)
    v_ref[at, :] = both[:, HEAD_DIM:].astype(jnp.bfloat16)

    @pl.when(step == steps - 1)
    def _():
        for copy in copies():
            copy.wait()


def in_hbm(value):
    return pltpu.with_memory_space_constraint(value, pltpu.HBM)


def project(image_features, key_weight, value_weight, selected, places, output_weight):
    rows, enc = image_features.shape
    steps = 4
    out = jax.ShapeDtypeStruct((rows + NOTE_ROWS, HEAD_DIM), jnp.bfloat16)
    whole = lambda shape: pl.BlockSpec(shape, lambda i: (0,) * len(shape))
    return pl.pallas_call(
        project_body,
        grid=(steps,),
        in_specs=[
            whole(selected.shape),
            SMEM_WHOLE,
            pl.BlockSpec((rows // steps, enc), lambda i: (i, 0)),
            whole((enc, HEAD_DIM)),
            whole((enc, HEAD_DIM)),
            HBM_WHOLE,
        ],
        out_specs=[
            whole((rows + NOTE_ROWS, HEAD_DIM)),
            whole((rows + NOTE_ROWS, HEAD_DIM)),
            whole((8, PICKS)),
            *[HBM_WHOLE for _ in NEAR_PIECES],
        ],
        out_shape=[
            out,
            out,
            jax.ShapeDtypeStruct((8, PICKS), jnp.int32),
            *[
                jax.ShapeDtypeStruct((rows, output_weight.shape[1] // 2), output_weight.dtype)
                for rows in NEAR_PIECES
            ],
        ],
        scratch_shapes=[
            pltpu.VMEM((enc, 2 * HEAD_DIM), jnp.bfloat16),
            pltpu.SemaphoreType.DMA((4 * len(NEAR_PIECES),)),
        ],
        compiler_params=pltpu.CompilerParams(vmem_limit_bytes=40 << 20),
        cost_estimate=SMALL,
        name="project",
    )(
        selected,
        places,
        in_hbm(image_features),
        in_hbm(key_weight),
        in_hbm(value_weight),
        in_hbm(output_weight),
    )


def pack_one(ask, me, base, stride, own, plus, two, minus, here, up, down):
    chunk = SIDE * CAP * BLOCK

    def rows(ref, index):
        return ref[pl.ds(pl.multiple_of(index * BLOCK, BLOCK), BLOCK), :]

    for dest in range(SIDE):
        for away in range(SIDE):
            first = base + ((me + away) & (SIDE - 1)) * stride
            for slot in range(CAP):
                block = ask[dest, first + slot]
                value = rows((own, plus, two, minus)[away], block)
                at = (away * CAP + slot) * BLOCK
                if dest == 0:
                    here[at : at + BLOCK, :] = value
                elif dest == 1:
                    up[at : at + BLOCK, :] = value
                elif dest == 3:
                    down[at : at + BLOCK, :] = value
                elif at < chunk // 2:
                    up[chunk + at : chunk + at + BLOCK, :] = value
                else:
                    down[chunk // 2 + at : chunk // 2 + at + BLOCK, :] = value


def pack_body(place_ref, *refs):
    k_in, v_in, k_out, v_out = refs[:4], refs[4:8], refs[8:11], refs[11:14]
    note_ref, ask_ref, sem = refs[14:]

    def note(ring):
        last = lambda ref: ref[ref.shape[0] - NOTE_ROWS :, :].astype(jnp.float32)[:1]
        return jnp.concatenate([last(ref) for ref in ring], axis=0)

    notes = jnp.concatenate([note(v_in), note(k_in)], axis=0)
    note_ref[...] = notes.astype(jnp.int32)
    copy = pltpu.make_async_copy(note_ref, ask_ref, sem)
    copy.start()
    copy.wait()
    my_x, my_y = place_ref[0], place_ref[1]
    pack_one(ask_ref, my_x, my_y * CAP, SIDE * CAP, *k_in, *k_out)
    pack_one(ask_ref.at[SIDE:], my_y, my_x * (SIDE * CAP), CAP, *v_in, *v_out)


def pack(place, k_in, v_in):
    chunk = SIDE * CAP * BLOCK
    outs = [
        jax.ShapeDtypeStruct((rows, HEAD_DIM), jnp.bfloat16)
        for rows in (chunk, chunk + chunk // 2, chunk + chunk // 2)
    ]
    out = pl.pallas_call(
        pack_body,
        in_specs=[SMEM_WHOLE] + [VMEM_WHOLE] * 8,
        out_specs=[VMEM_WHOLE] * 6,
        out_shape=outs + outs,
        scratch_shapes=[
            pltpu.VMEM((2 * SIDE, PICKS), jnp.int32),
            pltpu.SMEM((2 * SIDE, PICKS), jnp.int32),
            pltpu.SemaphoreType.DMA,
        ],
        compiler_params=pltpu.CompilerParams(vmem_limit_bytes=32 << 20),
        cost_estimate=SMALL,
        name="pack",
    )(place, *k_in, *v_in)
    return out[:3], out[3:]


def attend_body(first_tile, slots_ref, place_ref, q_ref, k_ref, v_ref, o_ref, kt, vt):
    my_x, my_y = place_ref[0], place_ref[1]
    for tile in range(o_ref.shape[0] // TILE):
        for pick in range(TOPK):
            slot = slots_ref[0, (first_tile + tile) * TOPK + pick]
            owner, rank = slot >> 3, slot & (CAP - 1)
            away_x = ((owner >> 2) - my_x) & (SIDE - 1)
            away_y = ((owner & 3) - my_y) & (SIDE - 1)
            k_at = (away_y * SIDE + away_x) * CAP + rank
            v_at = (away_x * SIDE + away_y) * CAP + rank
            to = slice(pick * BLOCK, (pick + 1) * BLOCK)
            kt[tile % 2, to, :] = k_ref[pl.ds(pl.multiple_of(k_at * BLOCK, BLOCK), BLOCK), :]
            vt[tile % 2, to, :] = v_ref[pl.ds(pl.multiple_of(v_at * BLOCK, BLOCK), BLOCK), :]
        rows = slice(tile * TILE, (tile + 1) * TILE)
        asking = slice((first_tile + tile) * TILE, (first_tile + tile + 1) * TILE)
        heads = [slice(h * HEAD_DIM, (h + 1) * HEAD_DIM) for h in range(GROUP)]
        stacked = jnp.concatenate([q_ref[asking, columns] for columns in heads], axis=0)
        scores = lax.dot_general(
            stacked, kt[tile % 2], (((1,), (1,)), ((), ())), preferred_element_type=jnp.float32
        )
        largest = jnp.max(scores, axis=-1, keepdims=True)
        exponent = jnp.exp2((scores - largest) * (SCALE * LOG2_E))
        total = jnp.sum(exponent, axis=-1, keepdims=True)
        weights = (exponent * (1.0 / total)).astype(jnp.bfloat16)
        mixed = jnp.dot(weights, vt[tile % 2], preferred_element_type=jnp.float32)
        mixed = mixed.astype(jnp.bfloat16)
        for h, columns in enumerate(heads):
            o_ref[rows, columns] = mixed[h * TILE : (h + 1) * TILE]


def attend(first_tile, tiles, slots, place, queries, keys, values):
    width = queries.shape[1]
    rows = tiles * TILE
    return pl.pallas_call(
        functools.partial(attend_body, first_tile),
        in_specs=[SMEM_WHOLE, SMEM_WHOLE] + [VMEM_WHOLE] * 3,
        out_specs=VMEM_WHOLE,
        out_shape=jax.ShapeDtypeStruct((rows, width), jnp.bfloat16),
        scratch_shapes=[pltpu.VMEM((2, TOPK * BLOCK, HEAD_DIM), jnp.bfloat16)] * 2,
        compiler_params=pltpu.CompilerParams(vmem_limit_bytes=32 << 20),
        cost_estimate=SMALL,
        name="attend",
    )(slots, place, queries, keys, values)


def pick_body(places_ref, w_ref, *out_refs):
    at = 0
    for ref in out_refs:
        ref[...] = w_ref[at : at + ref.shape[0], :]
        at += ref.shape[0]


def pick(places, weight, pieces):
    depth, width = weight.shape[0], weight.shape[1] // 8
    return pl.pallas_call(
        pick_body,
        grid_spec=pltpu.PrefetchScalarGridSpec(
            num_scalar_prefetch=1,
            grid=(4,),
            in_specs=[pl.BlockSpec((depth, width), lambda i, places: (0, places[i]))],
            out_specs=[pl.BlockSpec((rows, width), lambda i, places: (0, i)) for rows in pieces],
        ),
        out_shape=[jax.ShapeDtypeStruct((rows, 4 * width), weight.dtype) for rows in pieces],
        compiler_params=pltpu.CompilerParams(vmem_limit_bytes=8 << 20),
        cost_estimate=SMALL,
        name="pick",
    )(places, in_hbm(weight))


def multiply_body(mine_ref, near_ref, w_ref, *out_refs):
    left = jnp.concatenate([mine_ref[...], near_ref[...]], axis=1)
    width = w_ref.shape[1] // len(out_refs)
    for group, out_ref in enumerate(out_refs):
        columns = slice(group * width, (group + 1) * width)
        product = jnp.dot(left, w_ref[:, columns], preferred_element_type=jnp.float32)
        out_ref[...] = product.astype(out_ref.dtype)


def multiply(mine, near, weight):
    shape = (mine.shape[0], weight.shape[1] // 4)
    give = jax.ShapeDtypeStruct(shape, jnp.bfloat16)
    keep = jax.ShapeDtypeStruct(shape, jnp.float32)
    return pl.pallas_call(
        multiply_body,
        in_specs=[VMEM_WHOLE] * 3,
        out_specs=[VMEM_WHOLE] * 4,
        out_shape=[give, give, keep, keep],
        compiler_params=pltpu.CompilerParams(vmem_limit_bytes=24 << 20),
        cost_estimate=SMALL,
        name="multiply",
    )(mine, near, weight)


def rms_normed(text_hidden, norm_gain):
    as_float = text_hidden.astype(jnp.float32)
    inverse = lax.rsqrt(jnp.mean(as_float * as_float, axis=-1, keepdims=True) + EPSILON)
    return (as_float * inverse * norm_gain).astype(jnp.bfloat16)


def after(value, other):
    return lax.optimization_barrier((value, other))[0]


def spread(value, dx, dy, hold=lambda part: part):
    minus = along_seq(value, dx, dy)
    plus = along_seq(value, -dx, -dy)
    return value, plus, along_seq(hold(minus), dx, dy), minus


def exchange(packed, dx, dy, hold=lambda part: part):
    here, up, down = packed
    chunk = here.shape[0]
    minus = along_seq(up, dx, dy)
    plus = along_seq(down, -dx, -dy)
    low = along_seq(minus[chunk:], dx, dy)
    high = along_seq(hold(plus)[chunk:], -dx, -dy)
    return jnp.concatenate([here, plus[:chunk], low, high, minus[:chunk]])


def shards(
    text_hidden,
    norm_gain,
    image_features,
    query_weight,
    key_weight,
    value_weight,
    output_weight,
    selected,
):
    seq = lax.axis_index("seq")
    my_x, my_y = seq // SIDE, seq % SIDE
    section, z_hi = lax.axis_index("section"), lax.axis_index("head")
    z, core = z_hi * 2 + section // 2, section % 2

    place = jnp.stack([my_x, my_y])

    def wanted_columns(z):
        return jnp.stack(
            [column(3 - z, 1 - core), column(z, 1 - core), column(3 - z, core), column(z, core)]
        )

    k_own, v_own, slots, *pieces = project(
        image_features, key_weight, value_weight, selected, wanted_columns(z ^ 1), output_weight
    )
    near_weight = [to_near(piece) for piece in pieces]
    k_ring = spread(k_own, 1, 0)
    v_ring = spread(v_own, 0, 1, lambda part: after(part, near_weight[0]))
    k_out, v_out = pack(after(place, near_weight[1]), k_ring, v_ring)
    keys = exchange(k_out, 0, 1)
    values = exchange(v_out, 1, 0, lambda part: after(part, near_weight[2]))

    text_hidden = after(text_hidden, k_out[0])
    normed = rms_normed(text_hidden, norm_gain)
    queries = jnp.dot(normed, query_weight, preferred_element_type=jnp.float32).astype(jnp.bfloat16)
    own_weight = pick(
        wanted_columns(z), after(output_weight, k_out[0]), (output_weight.shape[0],)
    )
    weight = jnp.concatenate([*own_weight, *near_weight])

    starts = [sum(CHUNKS[:index]) for index in range(len(CHUNKS))]
    mine, near, sent, outs = [], [], [], []

    def attended(slots):
        index = len(mine)
        part = attend(starts[index], CHUNKS[index], slots, place, queries, keys, values)
        mine.append(part)
        near.append(to_near(part))
        return after(slots, part)

    while len(mine) < AHEAD:
        slots = attended(slots)
    weight = after(weight, mine[-1])
    last = len(CHUNKS) - 1
    for index in range(len(CHUNKS)):
        if index >= 2:
            weight = after(weight, sent[index - 2])
        if index >= 3:
            weight = after(weight, outs[index - 3])
        give_far, give_own, keep_far, keep_own = multiply(mine[index], near[index], weight)
        weight = after(weight, give_far)
        if len(mine) < len(CHUNKS):
            slots = attended(after(slots, give_far))
            weight = after(weight, mine[-1])
        got_far, got_own = to_core(give_far), to_core(give_own)
        if index >= 2 and index == last:
            got_far = after(got_far, outs[index - 2])
        send = (keep_far + got_far.astype(jnp.float32)).astype(jnp.bfloat16)
        far = to_far(send)
        sent.append(send)
        total = keep_own + got_own.astype(jnp.float32) + far.astype(jnp.float32)
        outs.append(total.astype(jnp.bfloat16))
    return jnp.concatenate(outs, axis=0)


def solution(mesh):
    in_specs = (
        P("seq", None),
        P(),
        P("seq", None),
        P(None, ("section", "head")),
        P(None, ("section", "head")),
        P(None, ("section", "head")),
        P(("section", "head"), None),
        P("seq", None),
    )
    out_specs = P("seq", ("section", "head"))
    return jax.shard_map(shards, mesh=mesh, in_specs=in_specs, out_specs=out_specs, check_vma=False)
```

time: 151 us -> 144 us (0.954)
  the two profiles are of different devices: /device:TPU:2 before, /device:TPU:1 now
where the time goes in v2:
time: 144 us; the launch traced here: 143 us
  starting transfers between devices  47.3 us (33%)
  Pallas kernels  41.2 us (29%)
  waiting for transfers between devices  37.1 us (26%)
  other arithmetic  7.2 us (5%)
  local copies, waits for them, and re-layouts  5.15 us (4%)
  matrix products  4.57 us (3%)
    ppermute x20, starting transfers between devices, along_z(): return lax.ppermute(value, SECTION_HEAD, pairs)  30 us
    ppermute x20, waiting for transfers between devices, along_z(): return lax.ppermute(value, SECTION_HEAD, pairs)  29.1 us
    pallas_call x1, Pallas kernels, project(): pl.pallas_call(project_body, grid=(steps,), in_specs=[whole(selected.shap...  18.6 us
    ppermute x14, starting transfers between devices, along_seq(): return lax.ppermute(value, 'seq', pairs)  17.2 us
    pallas_call x4, Pallas kernels, attend(): pl.pallas_call(functools.partial(attend_body, first_tile), in_specs=[SMEM...  11.7 us
    ppermute x14, waiting for transfers between devices, along_seq(): return lax.ppermute(value, 'seq', pairs)  8 us
    reduce_sum x1, other arithmetic, rms_normed(): jnp.mean(as_float * as_float, axis=-1, keepdims=True) + EPSILON  5.22 us
    pallas_call x4, Pallas kernels, multiply(): pl.pallas_call(multiply_body, in_specs=[VMEM_WHOLE] * 3, out_specs=[VMEM_...  4.98 us
  transfers between devices with their start and end apart: 34, of which 10 were waited for; matrix products, arithmetic and copies ran while one was open for 9% of the time, Pallas kernels for 16%

profile of v2, /device:TPU:1, one launch (start us, length us, event | category | flops | bytes accessed | tf_op | source)
XLA Modules:
  0.0 142.9 jit_solution(8234687406732872786)
XLA Ops:
  0.8 18.6 %project.1 = (bf16[2064,128]{1,0:T(8,128)(2,1)S(1)}, bf16[2064,128]{1,0:T(8,128)(2,1)S(1)}, s32[8,128]{1,0:T(8,128)S(1)}, bf16[128,2048]{1,0:T(8,128)(2,1)S(1)},...) custom-call(s32[8,16]{1,0:T(8,128)S(1)} %copy-done, ...), custom_call_target="tpu_custom_call" | custom-call | flops 1 | bytes 1 | tf_op jit(solution)/shard_map/project/pallas_call | solution.py:163
  19.4 0.9 copy-done.1
  20.2 2.1 %collective-permute-start.5 = (bf16[2064,128]{1,0:T(8,128)(2,1)S(1)}, bf16[2064,128]{1,0:T(8,128)(2,1)S(1)}, u32[]{:S(2)}, u32[]{:S(2)}) collective-permute-start(bf16[2064,128]{1,0:T(8,128)(2,1)S(1)} %get-tuple-element.54.refs_4_), channel_id=1, source_target_pairs={{0,2},{2,4},{4,6},{6,0},{8,10},{10,12},{12,14},{14,8},{16,18},{18,... | collective-permute-start | bytes 1585160 | tf_op jit(solution)/shard_map/ppermute | solution.py:41
  22.4 1.2 collective-permute-start.2
  23.6 1.6 %collective-permute-start.6 = (bf16[128,2048]{1,0:T(8,128)(2,1)S(1)}, bf16[128,2048]{1,0:T(8,128)(2,1)S(1)}, u32[]{:S(2)}, u32[]{:S(2)}) collective-permute-start(bf16[128,2048]{1,0:T(8,128)(2,1)S(1)} %get-tuple-element.55), channel_id=1, source_target_pairs={{0,64},{32,96},{64,0},{96,32},{1,65},{33,97},{65,1},{97,33},{2,66}... | collective-permute-start | bytes 1572872 | tf_op jit(solution)/shard_map/ppermute | solution.py:53
  25.2 1.5 %collective-permute-start.1 = (bf16[2064,128]{1,0:T(8,128)(2,1)S(1)}, bf16[2064,128]{1,0:T(8,128)(2,1)S(1)}, u32[]{:S(2)}, u32[]{:S(2)}) collective-permute-start(bf16[2064,128]{1,0:T(8,128)(2,1)S(1)} %get-tuple-element.53.refs_0_), channel_id=1, source_target_pairs={{0,24},{2,26},{4,28},{6,30},{8,0},{10,2},{12,4},{14,6},{16,8},{18,... | collective-permute-start | bytes 1585160 | tf_op jit(solution)/shard_map/ppermute | solution.py:41
  26.7 1.4 %collective-permute-start.4 = (bf16[2064,128]{1,0:T(8,128)(2,1)S(1)}, bf16[2064,128]{1,0:T(8,128)(2,1)S(1)}, u32[]{:S(2)}, u32[]{:S(2)}) collective-permute-start(bf16[2064,128]{1,0:T(8,128)(2,1)S(1)} %get-tuple-element.54.refs_4_), channel_id=1, source_target_pairs={{0,6},{2,0},{4,2},{6,4},{8,14},{10,8},{12,10},{14,12},{16,22},{18,... | collective-permute-start | bytes 1585160 | tf_op jit(solution)/shard_map/ppermute | solution.py:41
  28.1 8.0 %collective-permute-done.6 = bf16[128,2048]{1,0:T(8,128)(2,1)S(1)} collective-permute-done((bf16[128,2048]{1,0:T(8,128)(2,1)S(1)}, bf16[128,2048]{1,0:T(8,128)(2,1)S(1)}, u32[]{:S(2)}, u32[]{:S(2)}) %collective-permute-start.6) | collective-permute-done | bytes 524320 | tf_op jit(solution)/shard_map/ppermute | solution.py:53
  36.1 0.8 copy-done.2
  36.9 1.2 collective-permute-start.3
  38.1 1.3 collective-permute-start.7
  39.4 1.3 collective-permute-start
  40.9 9.7 %collective-permute-done = bf16[128,2048]{1,0:T(8,128)(2,1)} collective-permute-done((bf16[128,2048]{1,0:T(8,128)(2,1)}, bf16[128,2048]{1,0:T(8,128)(2,1)}, u32[]{:S(2)}, u32[]{:S(2)}) %collective-permute-start) | collective-permute-done | bytes 524320 | tf_op jit(solution)/shard_map/ppermute | solution.py:53
  50.6 1.1 collective-permute-start.15
  51.8 2.6 %pack.1 = (bf16[2048,128]{1,0:T(8,128)(2,1)S(1)}, bf16[3072,128]{1,0:T(8,128)(2,1)S(1)}, bf16[3072,128]{1,0:T(8,128)(2,1)S(1)}, bf16[2048,128]{1,0:T(8,128)(2,1)...) custom-call(s32[2]{0:T(128)S(1)} %pad_add_fusion.1.place_ref, ...), custom_call_target="tpu_custom_call" | custom-call | flops 1 | bytes 1 | tf_op jit(solution)/shard_map/pack/pallas_call | solution.py:255
  54.4 5.2 %fusion = f32[1024]{0:T(1024)S(1)} fusion(bf16[1024,4096]{1,0:T(8,128)(2,1)} %param.8), kind=kLoop, calls=%fused_computation.2 | loop fusion | flops 12581888 | bytes 8392704 | tf_op jit(solution)/shard_map/reduce_sum | solution.py:367
  59.7 1.4 %collective-permute-start.8 = (bf16[3072,128]{1,0:T(8,128)(2,1)S(1)}, bf16[3072,128]{1,0:T(8,128)(2,1)S(1)}, u32[]{:S(2)}, u32[]{:S(2)}) collective-permute-start(bf16[3072,128]{1,0:T(8,128)(2,1)S(1)} %get-tuple-element.59), channel_id=1, source_target_pairs={{0,6},{2,0},{4,2},{6,4},{8,14},{10,8},{12,10},{14,12},{16,22},{18,... | collective-permute-start | bytes 2359304 | tf_op jit(solution)/shard_map/ppermute | solution.py:41
  61.2 1.5 %collective-permute-start.12 = (bf16[3072,128]{1,0:T(8,128)(2,1)S(1)}, bf16[3072,128]{1,0:T(8,128)(2,1)S(1)}, u32[]{:S(2)}, u32[]{:S(2)}) collective-permute-start(bf16[3072,128]{1,0:T(8,128)(2,1)S(1)} %get-tuple-element.62), channel_id=1, source_target_pairs={{0,24},{2,26},{4,28},{6,30},{8,0},{10,2},{12,4},{14,6},{16,8},{18,... | collective-permute-start | bytes 2359304 | tf_op jit(solution)/shard_map/ppermute | solution.py:41
  62.7 3.3 %pick.1 = bf16[512,2048]{1,0:T(8,128)(2,1)S(1)} custom-call(s32[4]{0:T(128)S(1)} %pad_add_fusion.2.places_ref, bf16[512,4096]{1,0:T(8,128)(2,1)} %w_ref), custom_call_target="tpu_custom_call" | custom-call | flops 1 | bytes 1 | tf_op jit(solution)/shard_map/pick/pallas_call | solution.py:326
  66.0 4.6 %fusion.7.q_ref = bf16[1024,512]{1,0:T(8,128)(2,1)S(1)} fusion(bf16[4096,512]{1,0:T(8,128)(2,1)S(1)} %copy-done.4, bf16[1024,4096]{1,0:T(8,128)(2,1)S(1)} %bitcast.12, f32[4096]{0:T(1024)S(1)} %copy-done.5, f32[1024]{0:T(1024)S(1)} %add_rsqrt_fusion), kind=kOutput, calls=%fused_computation.8 | convolution fusion | flops 4312268800 | bytes 13651968 | tf_op jit(solution)/shard_map/dot_general | solution.py:425
  70.8 0.9 copy-done.3
  71.7 1.1 constant_dynamic-update-slice_fusion.8
  72.9 4.2 %collective-permute-done.9 = bf16[3072,128]{1,0:T(8,128)(2,1)S(1)} collective-permute-done((bf16[3072,128]{1,0:T(8,128)(2,1)S(1)}, bf16[3072,128]{1,0:T(8,128)(2,1)S(1)}, u32[]{:S(2)}, u32[]{:S(2)}) %collective-permute-start.9) | collective-permute-done | bytes 786464 | tf_op jit(solution)/shard_map/ppermute | solution.py:41
  78.0 2.6 %collective-permute-start.11 = (bf16[1024,128]{1,0:T(8,128)(2,1)S(1)}, bf16[1024,128]{1,0:T(8,128)(2,1)S(1)}, u32[]{:S(2)}, u32[]{:S(2)}) collective-permute-start(bf16[1024,128]{1,0:T(8,128)(2,1)S(1)} %slice.34), channel_id=1, source_target_pairs={{0,6},{2,0},{4,2},{6,4},{8,14},{10,8},{12,10},{14,12},{16,22},{18,... | collective-permute-start | bytes 786440 | tf_op jit(solution)/shard_map/ppermute | solution.py:41
  80.6 1.0 collective-permute-start.14
  81.6 1.8 %collective-permute-start.16 = (bf16[1024,128]{1,0:T(8,128)(2,1)S(1)}, bf16[1024,128]{1,0:T(8,128)(2,1)S(1)}, u32[]{:S(2)}, u32[]{:S(2)}) collective-permute-start(bf16[1024,128]{1,0:T(8,128)(2,1)S(1)} %slice.30), channel_id=1, source_target_pairs={{0,24},{2,26},{4,28},{6,30},{8,0},{10,2},{12,4},{14,6},{16,8},{18,... | collective-permute-start | bytes 786440 | tf_op jit(solution)/shard_map/ppermute | solution.py:41
  83.6 0.8 collective-permute-done.10
  84.6 2.8 %collective-permute-done.14 = bf16[1024,128]{1,0:T(8,128)(2,1)S(1)} collective-permute-done((bf16[1024,128]{1,0:T(8,128)(2,1)S(1)}, bf16[1024,128]{1,0:T(8,128)(2,1)S(1)}, u32[]{:S(2)}, u32[]{:S(2)}) %collective-permute-start.14) | collective-permute-done | bytes 262176 | tf_op jit(solution)/shard_map/ppermute | solution.py:41
  87.6 2.9 %attend.4.mine_ref = bf16[256,512]{1,0:T(8,128)(2,1)S(1)} custom-call(s32[8,128]{1,0:T(8,128)S(1)} %get-tuple-element.70.slots_ref, s32[2]{0:T(128)S(1)} %pad_add_fusion.1.place_ref, bf16[1024,512]{1,0:T(8,128)(2,1)S(1)} %fusion.7.q_ref, bf16[8192,128]{1,0:T(8,128)(2,1)S(1)} %slice_dynamic-update-slice_fusion.2.k_ref, ...), custom_call_target="tpu_custom_call" | custom-call | flops 1 | bytes 1 | tf_op jit(solution)/shard_map/attend/pallas_call | solution.py:305
  91.2 2.9 %attend.5.mine_ref = bf16[256,512]{1,0:T(8,128)(2,1)S(1)} custom-call(s32[8,128]{1,0:T(8,128)S(1)} %get-tuple-element.70.slots_ref, s32[2]{0:T(128)S(1)} %pad_add_fusion.1.place_ref, bf16[1024,512]{1,0:T(8,128)(2,1)S(1)} %fusion.7.q_ref, bf16[8192,128]{1,0:T(8,128)(2,1)S(1)} %slice_dynamic-update-slice_fusion.2.k_ref, ...), custom_call_target="tpu_custom_call" | custom-call | flops 1 | bytes 1 | tf_op jit(solution)/shard_map/attend/pallas_call | solution.py:305
  94.2 1.3 collective-permute-start.22
  95.4 2.9 %attend.6.mine_ref = bf16[256,512]{1,0:T(8,128)(2,1)S(1)} custom-call(s32[8,128]{1,0:T(8,128)S(1)} %get-tuple-element.70.slots_ref, s32[2]{0:T(128)S(1)} %pad_add_fusion.1.place_ref, bf16[1024,512]{1,0:T(8,128)(2,1)S(1)} %fusion.7.q_ref, bf16[8192,128]{1,0:T(8,128)(2,1)S(1)} %slice_dynamic-update-slice_fusion.2.k_ref, ...), custom_call_target="tpu_custom_call" | custom-call | flops 1 | bytes 1 | tf_op jit(solution)/shard_map/attend/pallas_call | solution.py:305
  98.4 2.9 %attend.7.mine_ref = bf16[256,512]{1,0:T(8,128)(2,1)S(1)} custom-call(s32[8,128]{1,0:T(8,128)S(1)} %get-tuple-element.70.slots_ref, s32[2]{0:T(128)S(1)} %pad_add_fusion.1.place_ref, bf16[1024,512]{1,0:T(8,128)(2,1)S(1)} %fusion.7.q_ref, bf16[8192,128]{1,0:T(8,128)(2,1)S(1)} %slice_dynamic-update-slice_fusion.2.k_ref, ...), custom_call_target="tpu_custom_call" | custom-call | flops 1 | bytes 1 | tf_op jit(solution)/shard_map/attend/pallas_call | solution.py:305
  101.3 1.2 multiply.10
  102.6 9.0 %collective-permute-start.20 = (bf16[256,512]{1,0:T(8,128)(2,1)S(1)}, bf16[256,512]{1,0:T(8,128)(2,1)S(1)}, u32[]{:S(2)}, u32[]{:S(2)}) collective-permute-start(bf16[256,512]{1,0:T(8,128)(2,1)S(1)} %get-tuple-element.75), channel_id=1, source_target_pairs={{0,32},{32,0},{64,96},{96,64},{1,33},{33,1},{65,97},{97,65},{2,34}... | collective-permute-start | bytes 786440 | tf_op jit(solution)/shard_map/ppermute | solution.py:53
  111.5 1.2 multiply.11
  113.5 3.7 %collective-permute-start.21 = (bf16[256,512]{1,0:T(8,128)(2,1)S(1)}, bf16[256,512]{1,0:T(8,128)(2,1)S(1)}, u32[]{:S(2)}, u32[]{:S(2)}) collective-permute-start(bf16[256,512]{1,0:T(8,128)(2,1)S(1)} %add_convert_fusion.7), channel_id=1, source_target_pairs={{0,65},{32,97},{64,1},{96,33},{1,64},{33,96},{65,0},{97,32},{2,67}... | collective-permute-start | bytes 786440 | tf_op jit(solution)/shard_map/ppermute | solution.py:53
  117.1 2.3 %collective-permute-done.26.near_ref = bf16[256,512]{1,0:T(8,128)(2,1)S(1)} collective-permute-done((bf16[256,512]{1,0:T(8,128)(2,1)S(1)}, bf16[256,512]{1,0:T(8,128)(2,1)S(1)}, u32[]{:S(2)}, u32[]{:S(2)}) %collective-permute-start.26) | collective-permute-done | bytes 262176 | tf_op jit(solution)/shard_map/ppermute | solution.py:53
  119.4 0.9 collective-permute-start.23
  120.3 1.2 multiply.12
  121.7 2.8 %collective-permute-start.25 = (bf16[256,512]{1,0:T(8,128)(2,1)S(1)}, bf16[256,512]{1,0:T(8,128)(2,1)S(1)}, u32[]{:S(2)}, u32[]{:S(2)}) collective-permute-start(bf16[256,512]{1,0:T(8,128)(2,1)S(1)} %add_convert_fusion.5), channel_id=1, source_target_pairs={{0,65},{32,97},{64,1},{96,33},{1,64},{33,96},{65,0},{97,32},{2,67}... | collective-permute-start | bytes 786440 | tf_op jit(solution)/shard_map/ppermute | solution.py:53
  124.5 0.8 collective-permute-start.27
  125.4 1.2 multiply.13
  127.4 2.3 %collective-permute-start.29 = (bf16[256,512]{1,0:T(8,128)(2,1)S(1)}, bf16[256,512]{1,0:T(8,128)(2,1)S(1)}, u32[]{:S(2)}, u32[]{:S(2)}) collective-permute-start(bf16[256,512]{1,0:T(8,128)(2,1)S(1)} %add_convert_fusion.3), channel_id=1, source_target_pairs={{0,65},{32,97},{64,1},{96,33},{1,64},{33,96},{65,0},{97,32},{2,67}... | collective-permute-start | bytes 786440 | tf_op jit(solution)/shard_map/ppermute | solution.py:53
  130.6 2.7 %collective-permute-start.33 = (bf16[256,512]{1,0:T(8,128)(2,1)S(1)}, bf16[256,512]{1,0:T(8,128)(2,1)S(1)}, u32[]{:S(2)}, u32[]{:S(2)}) collective-permute-start(bf16[256,512]{1,0:T(8,128)(2,1)S(1)} %add_convert_fusion.1), channel_id=1, source_target_pairs={{0,65},{32,97},{64,1},{96,33},{1,64},{33,96},{65,0},{97,32},{2,67}... | collective-permute-start | bytes 786440 | tf_op jit(solution)/shard_map/ppermute | solution.py:53
  133.4 2.8 %collective-permute-done.29 = bf16[256,512]{1,0:T(8,128)(2,1)S(1)} collective-permute-done((bf16[256,512]{1,0:T(8,128)(2,1)S(1)}, bf16[256,512]{1,0:T(8,128)(2,1)S(1)}, u32[]{:S(2)}, u32[]{:S(2)}) %collective-permute-start.29) | collective-permute-done | bytes 262176 | tf_op jit(solution)/shard_map/ppermute | solution.py:53
  136.3 5.5 %collective-permute-done.33 = bf16[256,512]{1,0:T(8,128)(2,1)S(1)} collective-permute-done((bf16[256,512]{1,0:T(8,128)(2,1)S(1)}, bf16[256,512]{1,0:T(8,128)(2,1)S(1)}, u32[]{:S(2)}, u32[]{:S(2)}) %collective-permute-start.33) | collective-permute-done | bytes 262176 | tf_op jit(solution)/shard_map/ppermute | solution.py:53
  141.9 1.0 pad_maximum_fusion
  (81 shorter events, 6.2 us)
Async XLA Ops:
  0.1 0.7 copy-start
  19.4 0.9 copy-start.1
  20.2 15.9 %collective-permute-start.5 = (bf16[2064,128]{1,0:T(8,128)(2,1)S(1)}, bf16[2064,128]{1,0:T(8,128)(2,1)S(1)}, u32[]{:S(2)}, u32[]{:S(2)}) collective-permute-start(bf16[2064,128]{1,0:T(8,128)(2,1)S(1)} %get-tuple-element.54.refs_4_), channel_id=1, source_target_pairs={{0,2},{2,4},{4,6},{6,0},{8,10},{10,12},{12,14},{14,8},{16,18},{18,... | collective-permute-start | bytes 1585160 | tf_op jit(solution)/shard_map/ppermute | solution.py:41
  22.4 13.8 %collective-permute-start.2 = (bf16[2064,128]{1,0:T(8,128)(2,1)S(1)}, bf16[2064,128]{1,0:T(8,128)(2,1)S(1)}, u32[]{:S(2)}, u32[]{:S(2)}) collective-permute-start(bf16[2064,128]{1,0:T(8,128)(2,1)S(1)} %get-tuple-element.53.refs_0_), channel_id=1, source_target_pairs={{0,8},{2,10},{4,12},{6,14},{8,16},{10,18},{12,20},{14,22},{16,24},... | collective-permute-start | bytes 1585160 | tf_op jit(solution)/shard_map/ppermute | solution.py:41
  23.6 12.5 %collective-permute-start.6 = (bf16[128,2048]{1,0:T(8,128)(2,1)S(1)}, bf16[128,2048]{1,0:T(8,128)(2,1)S(1)}, u32[]{:S(2)}, u32[]{:S(2)}) collective-permute-start(bf16[128,2048]{1,0:T(8,128)(2,1)S(1)} %get-tuple-element.55), channel_id=1, source_target_pairs={{0,64},{32,96},{64,0},{96,32},{1,65},{33,97},{65,1},{97,33},{2,66}... | collective-permute-start | bytes 1572872 | tf_op jit(solution)/shard_map/ppermute | solution.py:53
  25.2 26.5 %collective-permute-start.1 = (bf16[2064,128]{1,0:T(8,128)(2,1)S(1)}, bf16[2064,128]{1,0:T(8,128)(2,1)S(1)}, u32[]{:S(2)}, u32[]{:S(2)}) collective-permute-start(bf16[2064,128]{1,0:T(8,128)(2,1)S(1)} %get-tuple-element.53.refs_0_), channel_id=1, source_target_pairs={{0,24},{2,26},{4,28},{6,30},{8,0},{10,2},{12,4},{14,6},{16,8},{18,... | collective-permute-start | bytes 1585160 | tf_op jit(solution)/shard_map/ppermute | solution.py:41
  26.7 25.1 %collective-permute-start.4 = (bf16[2064,128]{1,0:T(8,128)(2,1)S(1)}, bf16[2064,128]{1,0:T(8,128)(2,1)S(1)}, u32[]{:S(2)}, u32[]{:S(2)}) collective-permute-start(bf16[2064,128]{1,0:T(8,128)(2,1)S(1)} %get-tuple-element.54.refs_4_), channel_id=1, source_target_pairs={{0,6},{2,0},{4,2},{6,4},{8,14},{10,8},{12,10},{14,12},{16,22},{18,... | collective-permute-start | bytes 1585160 | tf_op jit(solution)/shard_map/ppermute | solution.py:41
  36.1 0.8 copy-start.2
  36.9 14.8 %collective-permute-start.3 = (bf16[2064,128]{1,0:T(8,128)(2,1)S(1)}, bf16[2064,128]{1,0:T(8,128)(2,1)}, u32[]{:S(2)}, u32[]{:S(2)}) collective-permute-start(bf16[2064,128]{1,0:T(8,128)(2,1)S(1)} %collective-permute-done.2.refs_3_), channel_id=1, source_target_pairs={{0,8},{2,10},{4,12},{6,14},{8,16},{10,18},{12,20},{14,22},{16,24},... | collective-permute-start | bytes 1585160 | tf_op jit(solution)/shard_map/ppermute | solution.py:41
  38.1 13.6 %collective-permute-start.7 = (bf16[2064,128]{1,0:T(8,128)(2,1)S(1)}, bf16[2064,128]{1,0:T(8,128)(2,1)}, u32[]{:S(2)}, u32[]{:S(2)}) collective-permute-start(bf16[2064,128]{1,0:T(8,128)(2,1)S(1)} %collective-permute-done.5.refs_7_), channel_id=1, source_target_pairs={{0,2},{2,4},{4,6},{6,0},{8,10},{10,12},{12,14},{14,8},{16,18},{18,... | collective-permute-start | bytes 1585160 | tf_op jit(solution)/shard_map/ppermute | solution.py:41
  39.4 11.2 %collective-permute-start = (bf16[128,2048]{1,0:T(8,128)(2,1)}, bf16[128,2048]{1,0:T(8,128)(2,1)}, u32[]{:S(2)}, u32[]{:S(2)}) collective-permute-start(bf16[128,2048]{1,0:T(8,128)(2,1)} %get-tuple-element.51), channel_id=1, source_target_pairs={{0,64},{32,96},{64,0},{96,32},{1,65},{33,97},{65,1},{97,33},{2,66}... | collective-permute-start | bytes 1572872 | tf_op jit(solution)/shard_map/ppermute | solution.py:53
  50.6 30.0 %collective-permute-start.15 = (bf16[192,2048]{1,0:T(8,128)(2,1)}, bf16[192,2048]{1,0:T(8,128)(2,1)S(1)}, u32[]{:S(2)}, u32[]{:S(2)}) collective-permute-start(bf16[192,2048]{1,0:T(8,128)(2,1)} %copy-done.1), channel_id=1, source_target_pairs={{0,64},{32,96},{64,0},{96,32},{1,65},{33,97},{65,1},{97,33},{2,66}... | collective-permute-start | bytes 2359304 | tf_op jit(solution)/shard_map/ppermute | solution.py:53
  51.8 14.2 %slice-start = ((s8[8388608]{0:T(1024)(128)(4,1)}), s8[4194304]{0:T(1024)(128)(4,1)S(1)}, s32[]{:S(2)}) async-start(s8[8388608]{0:T(1024)(128)(4,1)} %bitcast.11), calls=%async_computation | async-start | bytes 8388608
  54.4 11.6 %slice-start.1 = ((s8[8388608]{0:T(1024)(128)(4,1)}), s8[4194304]{0:T(1024)(128)(4,1)S(1)}, s32[]{:S(2)}) async-start(s8[8388608]{0:T(1024)(128)(4,1)} %bitcast.11), calls=%async_computation.1 | async-start | bytes 8388608
  59.7 18.0 %collective-permute-start.8 = (bf16[3072,128]{1,0:T(8,128)(2,1)S(1)}, bf16[3072,128]{1,0:T(8,128)(2,1)S(1)}, u32[]{:S(2)}, u32[]{:S(2)}) collective-permute-start(bf16[3072,128]{1,0:T(8,128)(2,1)S(1)} %get-tuple-element.59), channel_id=1, source_target_pairs={{0,6},{2,0},{4,2},{6,4},{8,14},{10,8},{12,10},{14,12},{16,22},{18,... | collective-permute-start | bytes 2359304 | tf_op jit(solution)/shard_map/ppermute | solution.py:41
  61.1 15.9 %collective-permute-start.9 = (bf16[3072,128]{1,0:T(8,128)(2,1)S(1)}, bf16[3072,128]{1,0:T(8,128)(2,1)S(1)}, u32[]{:S(2)}, u32[]{:S(2)}) collective-permute-start(bf16[3072,128]{1,0:T(8,128)(2,1)S(1)} %get-tuple-element.60), channel_id=1, source_target_pairs={{0,2},{2,4},{4,6},{6,0},{8,10},{10,12},{12,14},{14,8},{16,18},{18,... | collective-permute-start | bytes 2359304 | tf_op jit(solution)/shard_map/ppermute | solution.py:41
  61.2 20.4 %collective-permute-start.12 = (bf16[3072,128]{1,0:T(8,128)(2,1)S(1)}, bf16[3072,128]{1,0:T(8,128)(2,1)S(1)}, u32[]{:S(2)}, u32[]{:S(2)}) collective-permute-start(bf16[3072,128]{1,0:T(8,128)(2,1)S(1)} %get-tuple-element.62), channel_id=1, source_target_pairs={{0,24},{2,26},{4,28},{6,30},{8,0},{10,2},{12,4},{14,6},{16,8},{18,... | collective-permute-start | bytes 2359304 | tf_op jit(solution)/shard_map/ppermute | solution.py:41
  62.7 3.3 %copy-start.4 = (bf16[4096,512]{1,0:T(8,128)(2,1)S(1)}, bf16[4096,512]{1,0:T(8,128)(2,1)}, u32[]{:S(2)}) copy-start(bf16[4096,512]{1,0:T(8,128)(2,1)} %param.11) | copy-start | bytes 12582916
  62.7 3.3 %copy-start.5 = (f32[4096]{0:T(1024)S(1)}, f32[4096]{0:T(1024)}, u32[]{:S(2)}) copy-start(f32[4096]{0:T(1024)} %param.9) | copy-start | bytes 49156
  62.7 15.3 %collective-permute-start.13 = (bf16[3072,128]{1,0:T(8,128)(2,1)S(1)}, bf16[3072,128]{1,0:T(8,128)(2,1)S(1)}, u32[]{:S(2)}, u32[]{:S(2)}) collective-permute-start(bf16[3072,128]{1,0:T(8,128)(2,1)S(1)} %get-tuple-element.63), channel_id=1, source_target_pairs={{0,8},{2,10},{4,12},{6,14},{8,16},{10,18},{12,20},{14,22},{16,24},... | collective-permute-start | bytes 2359304 | tf_op jit(solution)/shard_map/ppermute | solution.py:41
  70.6 1.0 copy-start.3
  77.0 14.2 %collective-permute-start.18 = (bf16[64,2048]{1,0:T(8,128)(2,1)S(1)}, bf16[64,2048]{1,0:T(8,128)(2,1)S(1)}, u32[]{:S(2)}, u32[]{:S(2)}) collective-permute-start(bf16[64,2048]{1,0:T(8,128)(2,1)S(1)} %get-tuple-element.67), channel_id=1, source_target_pairs={{0,64},{32,96},{64,0},{96,32},{1,65},{33,97},{65,1},{97,33},{2,66}... | collective-permute-start | bytes 786440 | tf_op jit(solution)/shard_map/ppermute | solution.py:53
  77.7 6.7 %collective-permute-start.10 = (bf16[1024,128]{1,0:T(8,128)(2,1)S(1)}, bf16[1024,128]{1,0:T(8,128)(2,1)S(1)}, u32[]{:S(2)}, u32[]{:S(2)}) collective-permute-start(bf16[1024,128]{1,0:T(8,128)(2,1)S(1)} %slice.33), channel_id=1, source_target_pairs={{0,2},{2,4},{4,6},{6,0},{8,10},{10,12},{12,14},{14,8},{16,18},{18,... | collective-permute-start | bytes 786440 | tf_op jit(solution)/shard_map/ppermute | solution.py:41
  78.0 6.4 %collective-permute-start.11 = (bf16[1024,128]{1,0:T(8,128)(2,1)S(1)}, bf16[1024,128]{1,0:T(8,128)(2,1)S(1)}, u32[]{:S(2)}, u32[]{:S(2)}) collective-permute-start(bf16[1024,128]{1,0:T(8,128)(2,1)S(1)} %slice.34), channel_id=1, source_target_pairs={{0,6},{2,0},{4,2},{6,4},{8,14},{10,8},{12,10},{14,12},{16,22},{18,... | collective-permute-start | bytes 786440 | tf_op jit(solution)/shard_map/ppermute | solution.py:41
  80.6 6.8 %collective-permute-start.14 = (bf16[1024,128]{1,0:T(8,128)(2,1)S(1)}, bf16[1024,128]{1,0:T(8,128)(2,1)S(1)}, u32[]{:S(2)}, u32[]{:S(2)}) collective-permute-start(bf16[1024,128]{1,0:T(8,128)(2,1)S(1)} %slice.37), channel_id=1, source_target_pairs={{0,8},{2,10},{4,12},{6,14},{8,16},{10,18},{12,20},{14,22},{16,24},... | collective-permute-start | bytes 786440 | tf_op jit(solution)/shard_map/ppermute | solution.py:41
  81.6 5.8 %collective-permute-start.16 = (bf16[1024,128]{1,0:T(8,128)(2,1)S(1)}, bf16[1024,128]{1,0:T(8,128)(2,1)S(1)}, u32[]{:S(2)}, u32[]{:S(2)}) collective-permute-start(bf16[1024,128]{1,0:T(8,128)(2,1)S(1)} %slice.30), channel_id=1, source_target_pairs={{0,24},{2,26},{4,28},{6,30},{8,0},{10,2},{12,4},{14,6},{16,8},{18,... | collective-permute-start | bytes 786440 | tf_op jit(solution)/shard_map/ppermute | solution.py:41
  90.5 10.8 %collective-permute-start.17 = (bf16[256,512]{1,0:T(8,128)(2,1)S(1)}, bf16[256,512]{1,0:T(8,128)(2,1)S(1)}, u32[]{:S(2)}, u32[]{:S(2)}) collective-permute-start(bf16[256,512]{1,0:T(8,128)(2,1)S(1)} %attend.4.mine_ref), channel_id=1, source_target_pairs={{0,64},{32,96},{64,0},{96,32},{1,65},{33,97},{65,1},{97,33},{2,66}... | collective-permute-start | bytes 786440 | tf_op jit(solution)/shard_map/ppermute | solution.py:53
  94.2 17.4 %collective-permute-start.22 = (bf16[256,512]{1,0:T(8,128)(2,1)S(1)}, bf16[256,512]{1,0:T(8,128)(2,1)S(1)}, u32[]{:S(2)}, u32[]{:S(2)}) collective-permute-start(bf16[256,512]{1,0:T(8,128)(2,1)S(1)} %attend.5.mine_ref), channel_id=1, source_target_pairs={{0,64},{32,96},{64,0},{96,32},{1,65},{33,97},{65,1},{97,33},{2,66}... | collective-permute-start | bytes 786440 | tf_op jit(solution)/shard_map/ppermute | solution.py:53
  102.6 10.8 %collective-permute-start.20 = (bf16[256,512]{1,0:T(8,128)(2,1)S(1)}, bf16[256,512]{1,0:T(8,128)(2,1)S(1)}, u32[]{:S(2)}, u32[]{:S(2)}) collective-permute-start(bf16[256,512]{1,0:T(8,128)(2,1)S(1)} %get-tuple-element.75), channel_id=1, source_target_pairs={{0,32},{32,0},{64,96},{96,64},{1,33},{33,1},{65,97},{97,65},{2,34}... | collective-permute-start | bytes 786440 | tf_op jit(solution)/shard_map/ppermute | solution.py:53
  111.5 7.9 %collective-permute-start.26 = (bf16[256,512]{1,0:T(8,128)(2,1)S(1)}, bf16[256,512]{1,0:T(8,128)(2,1)S(1)}, u32[]{:S(2)}, u32[]{:S(2)}) collective-permute-start(bf16[256,512]{1,0:T(8,128)(2,1)S(1)} %attend.6.mine_ref), channel_id=1, source_target_pairs={{0,64},{32,96},{64,0},{96,32},{1,65},{33,97},{65,1},{97,33},{2,66}... | collective-permute-start | bytes 786440 | tf_op jit(solution)/shard_map/ppermute | solution.py:53
  112.8 8.7 %collective-permute-start.24 = (bf16[256,512]{1,0:T(8,128)(2,1)S(1)}, bf16[256,512]{1,0:T(8,128)(2,1)S(1)}, u32[]{:S(2)}, u32[]{:S(2)}) collective-permute-start(bf16[256,512]{1,0:T(8,128)(2,1)S(1)} %get-tuple-element.80), channel_id=1, source_target_pairs={{0,32},{32,0},{64,96},{96,64},{1,33},{33,1},{65,97},{97,65},{2,34}... | collective-permute-start | bytes 786440 | tf_op jit(solution)/shard_map/ppermute | solution.py:53
  113.2 8.5 %collective-permute-start.19 = (bf16[256,512]{1,0:T(8,128)(2,1)S(1)}, bf16[256,512]{1,0:T(8,128)(2,1)S(1)}, u32[]{:S(2)}, u32[]{:S(2)}) collective-permute-start(bf16[256,512]{1,0:T(8,128)(2,1)S(1)} %get-tuple-element.73), channel_id=1, source_target_pairs={{0,32},{32,0},{64,96},{96,64},{1,33},{33,1},{65,97},{97,65},{2,34}... | collective-permute-start | bytes 786440 | tf_op jit(solution)/shard_map/ppermute | solution.py:53
  113.5 11.0 %collective-permute-start.21 = (bf16[256,512]{1,0:T(8,128)(2,1)S(1)}, bf16[256,512]{1,0:T(8,128)(2,1)S(1)}, u32[]{:S(2)}, u32[]{:S(2)}) collective-permute-start(bf16[256,512]{1,0:T(8,128)(2,1)S(1)} %add_convert_fusion.7), channel_id=1, source_target_pairs={{0,65},{32,97},{64,1},{96,33},{1,64},{33,96},{65,0},{97,32},{2,67}... | collective-permute-start | bytes 786440 | tf_op jit(solution)/shard_map/ppermute | solution.py:53
  117.1 8.2 %collective-permute-start.30 = (bf16[256,512]{1,0:T(8,128)(2,1)S(1)}, bf16[256,512]{1,0:T(8,128)(2,1)S(1)}, u32[]{:S(2)}, u32[]{:S(2)}) collective-permute-start(bf16[256,512]{1,0:T(8,128)(2,1)S(1)} %attend.7.mine_ref), channel_id=1, source_target_pairs={{0,64},{32,96},{64,0},{96,32},{1,65},{33,97},{65,1},{97,33},{2,66}... | collective-permute-start | bytes 786440 | tf_op jit(solution)/shard_map/ppermute | solution.py:53
  119.4 8.0 %collective-permute-start.23 = (bf16[256,512]{1,0:T(8,128)(2,1)S(1)}, bf16[256,512]{1,0:T(8,128)(2,1)S(1)}, u32[]{:S(2)}, u32[]{:S(2)}) collective-permute-start(bf16[256,512]{1,0:T(8,128)(2,1)S(1)} %get-tuple-element.78), channel_id=1, source_target_pairs={{0,32},{32,0},{64,96},{96,64},{1,33},{33,1},{65,97},{97,65},{2,34}... | collective-permute-start | bytes 786440 | tf_op jit(solution)/shard_map/ppermute | solution.py:53
  121.5 5.7 %collective-permute-start.28 = (bf16[256,512]{1,0:T(8,128)(2,1)S(1)}, bf16[256,512]{1,0:T(8,128)(2,1)S(1)}, u32[]{:S(2)}, u32[]{:S(2)}) collective-permute-start(bf16[256,512]{1,0:T(8,128)(2,1)S(1)} %get-tuple-element.86), channel_id=1, source_target_pairs={{0,32},{32,0},{64,96},{96,64},{1,33},{33,1},{65,97},{97,65},{2,34}... | collective-permute-start | bytes 786440 | tf_op jit(solution)/shard_map/ppermute | solution.py:53
  121.7 8.7 %collective-permute-start.25 = (bf16[256,512]{1,0:T(8,128)(2,1)S(1)}, bf16[256,512]{1,0:T(8,128)(2,1)S(1)}, u32[]{:S(2)}, u32[]{:S(2)}) collective-permute-start(bf16[256,512]{1,0:T(8,128)(2,1)S(1)} %add_convert_fusion.5), channel_id=1, source_target_pairs={{0,65},{32,97},{64,1},{96,33},{1,64},{33,96},{65,0},{97,32},{2,67}... | collective-permute-start | bytes 786440 | tf_op jit(solution)/shard_map/ppermute | solution.py:53
  124.5 8.9 %collective-permute-start.27 = (bf16[256,512]{1,0:T(8,128)(2,1)S(1)}, bf16[256,512]{1,0:T(8,128)(2,1)S(1)}, u32[]{:S(2)}, u32[]{:S(2)}) collective-permute-start(bf16[256,512]{1,0:T(8,128)(2,1)S(1)} %get-tuple-element.84), channel_id=1, source_target_pairs={{0,32},{32,0},{64,96},{96,64},{1,33},{33,1},{65,97},{97,65},{2,34}... | collective-permute-start | bytes 786440 | tf_op jit(solution)/shard_map/ppermute | solution.py:53
  126.6 3.9 %collective-permute-start.32 = (bf16[256,512]{1,0:T(8,128)(2,1)S(1)}, bf16[256,512]{1,0:T(8,128)(2,1)S(1)}, u32[]{:S(2)}, u32[]{:S(2)}) collective-permute-start(bf16[256,512]{1,0:T(8,128)(2,1)S(1)} %get-tuple-element.93), channel_id=1, source_target_pairs={{0,32},{32,0},{64,96},{96,64},{1,33},{33,1},{65,97},{97,65},{2,34}... | collective-permute-start | bytes 786440 | tf_op jit(solution)/shard_map/ppermute | solution.py:53
  127.2 9.1 %collective-permute-start.31 = (bf16[256,512]{1,0:T(8,128)(2,1)S(1)}, bf16[256,512]{1,0:T(8,128)(2,1)S(1)}, u32[]{:S(2)}, u32[]{:S(2)}) collective-permute-start(bf16[256,512]{1,0:T(8,128)(2,1)S(1)} %get-tuple-element.91), channel_id=1, source_target_pairs={{0,32},{32,0},{64,96},{96,64},{1,33},{33,1},{65,97},{97,65},{2,34}... | collective-permute-start | bytes 786440 | tf_op jit(solution)/shard_map/ppermute | solution.py:53
  127.4 8.8 %collective-permute-start.29 = (bf16[256,512]{1,0:T(8,128)(2,1)S(1)}, bf16[256,512]{1,0:T(8,128)(2,1)S(1)}, u32[]{:S(2)}, u32[]{:S(2)}) collective-permute-start(bf16[256,512]{1,0:T(8,128)(2,1)S(1)} %add_convert_fusion.3), channel_id=1, source_target_pairs={{0,65},{32,97},{64,1},{96,33},{1,64},{33,96},{65,0},{97,32},{2,67}... | collective-permute-start | bytes 786440 | tf_op jit(solution)/shard_map/ppermute | solution.py:53
  130.6 11.2 %collective-permute-start.33 = (bf16[256,512]{1,0:T(8,128)(2,1)S(1)}, bf16[256,512]{1,0:T(8,128)(2,1)S(1)}, u32[]{:S(2)}, u32[]{:S(2)}) collective-permute-start(bf16[256,512]{1,0:T(8,128)(2,1)S(1)} %add_convert_fusion.1), channel_id=1, source_target_pairs={{0,65},{32,97},{64,1},{96,33},{1,64},{33,96},{65,0},{97,32},{2,67}... | collective-permute-start | bytes 786440 | tf_op jit(solution)/shard_map/ppermute | solution.py:53

commit v3 on v2

--- a/solution.py
+++ b/solution.py
@@ -19,16 +19,15 @@
 PICKS = SIDE * SIDE * CAP
 NOTE_ROWS = 16
 EPSILON = 1e-05
-NEAR_PIECES = (128, 128, 192, 64)
+NEAR_PIECES = (128, 128, 128, 128)
 CHUNKS = (2, 2, 2, 2)
-AHEAD = 4
+AHEAD = 3
 SCALE = HEAD_DIM**-0.5
 LOG2_E = 1.4426950408889634
 
 SECTION_HEAD = ("section", "head")
 SMALL = pl.CostEstimate(flops=1, bytes_accessed=1, transcendentals=0)
 VMEM_WHOLE = pl.BlockSpec(memory_space=pltpu.VMEM)
-HBM_WHOLE = pl.BlockSpec(memory_space=pltpu.HBM)
 SMEM_WHOLE = pl.BlockSpec(memory_space=pltpu.SMEM)
 
 
@@ -66,26 +65,15 @@
 
 
 def project_body(
-    selected_ref, places_ref, x_ref, wk_ref, wv_ref, wo_ref, k_ref, v_ref, slots_ref, *rest
+    places_ref, selected_ref, x_ref, wk_ref, wv_ref, wo_ref, k_ref, v_ref, slots_ref, *rest
 ):
-    piece_refs, (w_ref, sem) = rest[:-2], rest[-2:]
+    piece_refs, w_ref = rest[:-1], rest[-1]
     step = pl.program_id(0)
 
-    def copies():
-        width = wo_ref.shape[1] // 8
-        found, at = [], 0
-        for index, piece in enumerate(piece_refs):
-            for group in range(4):
-                start = pl.multiple_of(places_ref[group] * width, width)
-                found.append(
-                    pltpu.make_async_copy(
-                        wo_ref.at[pl.ds(at, piece.shape[0]), pl.ds(start, width)],
-                        piece.at[:, pl.ds(group * width, width)],
-                        sem.at[index * 4 + group],
-                    )
-                )
-            at += piece.shape[0]
-        return found
+    at = 0
+    for piece in piece_refs:
+        piece[...] = wo_ref[at : at + piece.shape[0], :]
+        at += piece.shape[0]
 
     rows = x_ref.shape[0]
     steps = pl.num_programs(0)
@@ -96,9 +84,6 @@
     def _():
         w_ref[:, :HEAD_DIM] = wk_ref[...]
         w_ref[:, HEAD_DIM:] = wv_ref[...]
-        for copy in copies():
-            copy.start()
-
     @pl.when(step == steps - 1)
     def _():
         picked = selected_ref[...]
@@ -145,11 +130,6 @@
     k_ref[at, :] = both[:, :HEAD_DIM].astype(jnp.bfloat16)
     v_ref[at, :] = both[:, HEAD_DIM:].astype(jnp.bfloat16)
 
-    @pl.when(step == steps - 1)
-    def _():
-        for copy in copies():
-            copy.wait()
-
 
 def in_hbm(value):
     return pltpu.with_memory_space_constraint(value, pltpu.HBM)
@@ -159,43 +139,43 @@
     rows, enc = image_features.shape
     steps = 4
     out = jax.ShapeDtypeStruct((rows + NOTE_ROWS, HEAD_DIM), jnp.bfloat16)
-    whole = lambda shape: pl.BlockSpec(shape, lambda i: (0,) * len(shape))
+    whole = lambda shape: pl.BlockSpec(shape, lambda i, places: (0,) * len(shape))
+    depth, width = output_weight.shape[0], output_weight.shape[1] // 8
     return pl.pallas_call(
         project_body,
-        grid=(steps,),
-        in_specs=[
-            whole(selected.shape),
-            SMEM_WHOLE,
-            pl.BlockSpec((rows // steps, enc), lambda i: (i, 0)),
-            whole((enc, HEAD_DIM)),
-            whole((enc, HEAD_DIM)),
-            HBM_WHOLE,
-        ],
-        out_specs=[
-            whole((rows + NOTE_ROWS, HEAD_DIM)),
-            whole((rows + NOTE_ROWS, HEAD_DIM)),
-            whole((8, PICKS)),
-            *[HBM_WHOLE for _ in NEAR_PIECES],
-        ],
+        grid_spec=pltpu.PrefetchScalarGridSpec(
+            num_scalar_prefetch=1,
+            grid=(steps,),
+            in_specs=[
+                whole(selected.shape),
+                pl.BlockSpec((rows // steps, enc), lambda i, places: (i, 0)),
+                whole((enc, HEAD_DIM)),
+                whole((enc, HEAD_DIM)),
+                pl.BlockSpec((depth, width), lambda i, places: (0, places[i])),
+            ],
+            out_specs=[
+                whole((rows + NOTE_ROWS, HEAD_DIM)),
+                whole((rows + NOTE_ROWS, HEAD_DIM)),
+                whole((8, PICKS)),
+                *[pl.BlockSpec((part, width), lambda i, places: (0, i)) for part in NEAR_PIECES],
+            ],
+            scratch_shapes=[pltpu.VMEM((enc, 2 * HEAD_DIM), jnp.bfloat16)],
+        ),
         out_shape=[
             out,
             out,
             jax.ShapeDtypeStruct((8, PICKS), jnp.int32),
             *[
-                jax.ShapeDtypeStruct((rows, output_weight.shape[1] // 2), output_weight.dtype)
-                for rows in NEAR_PIECES
+                jax.ShapeDtypeStruct((part, steps * width), output_weight.dtype)
+                for part in NEAR_PIECES
             ],
-        ],
-        scratch_shapes=[
-            pltpu.VMEM((enc, 2 * HEAD_DIM), jnp.bfloat16),
-            pltpu.SemaphoreType.DMA((4 * len(NEAR_PIECES),)),
         ],
         compiler_params=pltpu.CompilerParams(vmem_limit_bytes=40 << 20),
         cost_estimate=SMALL,
         name="project",
     )(
+        places,
         selected,
-        places,
         in_hbm(image_features),
         in_hbm(key_weight),
         in_hbm(value_weight),
@@ -203,34 +183,19 @@
     )
 
 
-def pack_one(ask, me, base, stride, own, plus, two, minus, here, up, down):
-    chunk = SIDE * CAP * BLOCK
-
-    def rows(ref, index):
-        return ref[pl.ds(pl.multiple_of(index * BLOCK, BLOCK), BLOCK), :]
-
-    for dest in range(SIDE):
-        for away in range(SIDE):
+def pack_one(ask, me, base, stride, ring, outs):
+    for dest, out in enumerate(outs):
+        for away, ref in enumerate(ring):
             first = base + ((me + away) & (SIDE - 1)) * stride
             for slot in range(CAP):
-                block = ask[dest, first + slot]
-                value = rows((own, plus, two, minus)[away], block)
+                block = pl.multiple_of(ask[dest, first + slot] * BLOCK, BLOCK)
                 at = (away * CAP + slot) * BLOCK
-                if dest == 0:
-                    here[at : at + BLOCK, :] = value
-                elif dest == 1:
-                    up[at : at + BLOCK, :] = value
-                elif dest == 3:
-                    down[at : at + BLOCK, :] = value
-                elif at < chunk // 2:
-                    up[chunk + at : chunk + at + BLOCK, :] = value
-                else:
-                    down[chunk // 2 + at : chunk // 2 + at + BLOCK, :] = value
+                out[at : at + BLOCK, :] = ref[pl.ds(block, BLOCK), :]
 
 
 def pack_body(place_ref, *refs):
-    k_in, v_in, k_out, v_out = refs[:4], refs[4:8], refs[8:11], refs[11:14]
-    note_ref, ask_ref, sem = refs[14:]
+    k_in, v_in, k_out, v_out = refs[:4], refs[4:8], refs[8:12], refs[12:16]
+    note_ref, ask_ref, sem = refs[16:]
 
     def note(ring):
         last = lambda ref: ref[ref.shape[0] - NOTE_ROWS :, :].astype(jnp.float32)[:1]
@@ -242,20 +207,16 @@
     copy.start()
     copy.wait()
     my_x, my_y = place_ref[0], place_ref[1]
-    pack_one(ask_ref, my_x, my_y * CAP, SIDE * CAP, *k_in, *k_out)
-    pack_one(ask_ref.at[SIDE:], my_y, my_x * (SIDE * CAP), CAP, *v_in, *v_out)
+    pack_one(ask_ref, my_x, my_y * CAP, SIDE * CAP, k_in, k_out)
+    pack_one(ask_ref.at[SIDE:], my_y, my_x * (SIDE * CAP), CAP, v_in, v_out)
 
 
 def pack(place, k_in, v_in):
-    chunk = SIDE * CAP * BLOCK
-    outs = [
-        jax.ShapeDtypeStruct((rows, HEAD_DIM), jnp.bfloat16)
-        for rows in (chunk, chunk + chunk // 2, chunk + chunk // 2)
-    ]
+    outs = [jax.ShapeDtypeStruct((SIDE * CAP * BLOCK, HEAD_DIM), jnp.bfloat16)] * SIDE
     out = pl.pallas_call(
         pack_body,
         in_specs=[SMEM_WHOLE] + [VMEM_WHOLE] * 8,
-        out_specs=[VMEM_WHOLE] * 6,
+        out_specs=[VMEM_WHOLE] * 8,
         out_shape=outs + outs,
         scratch_shapes=[
             pltpu.VMEM((2 * SIDE, PICKS), jnp.int32),
@@ -266,7 +227,7 @@
         cost_estimate=SMALL,
         name="pack",
     )(place, *k_in, *v_in)
-    return out[:3], out[3:]
+    return out[:4], out[4:]
 
 
 def attend_body(first_tile, slots_ref, place_ref, q_ref, k_ref, v_ref, o_ref, kt, vt):
@@ -375,17 +336,16 @@
 def spread(value, dx, dy, hold=lambda part: part):
     minus = along_seq(value, dx, dy)
     plus = along_seq(value, -dx, -dy)
-    return value, plus, along_seq(hold(minus), dx, dy), minus
+    two = along_seq(hold(after(value, minus)), 2 * dx, 2 * dy)
+    return value, plus, two, minus
 
 
 def exchange(packed, dx, dy, hold=lambda part: part):
-    here, up, down = packed
-    chunk = here.shape[0]
+    here, up, across, down = packed
     minus = along_seq(up, dx, dy)
     plus = along_seq(down, -dx, -dy)
-    low = along_seq(minus[chunk:], dx, dy)
-    high = along_seq(hold(plus)[chunk:], -dx, -dy)
-    return jnp.concatenate([here, plus[:chunk], low, high, minus[:chunk]])
+    two = along_seq(hold(after(across, minus)), 2 * dx, 2 * dy)
+    return jnp.concatenate([here, plus, two, minus])
 
 
 def shards(
@@ -413,16 +373,18 @@
     k_own, v_own, slots, *pieces = project(
         image_features, key_weight, value_weight, selected, wanted_columns(z ^ 1), output_weight
     )
-    near_weight = [to_near(piece) for piece in pieces]
+    near_weight = []
+    for piece in pieces:
+        near_weight.append(to_near(after(piece, near_weight[-1]) if near_weight else piece))
     k_ring = spread(k_own, 1, 0)
     v_ring = spread(v_own, 0, 1, lambda part: after(part, near_weight[0]))
-    k_out, v_out = pack(after(place, near_weight[1]), k_ring, v_ring)
+
+    normed = rms_normed(after(text_hidden, k_own), norm_gain)
+    queries = jnp.dot(normed, query_weight, preferred_element_type=jnp.float32).astype(jnp.bfloat16)
+
+    k_out, v_out = pack(after(after(place, near_weight[1]), queries), k_ring, v_ring)
     keys = exchange(k_out, 0, 1)
     values = exchange(v_out, 1, 0, lambda part: after(part, near_weight[2]))
-
-    text_hidden = after(text_hidden, k_out[0])
-    normed = rms_normed(text_hidden, norm_gain)
-    queries = jnp.dot(normed, query_weight, preferred_element_type=jnp.float32).astype(jnp.bfloat16)
     own_weight = pick(
         wanted_columns(z), after(output_weight, k_out[0]), (output_weight.shape[0],)
     )

time: 144 us -> 131 us (0.910)
  Pallas kernels: 41.2 us -> 29.8 us
  other arithmetic: 7.2 us -> 3.69 us
  local copies, waits for them, and re-layouts: 5.15 us -> 6.77 us
  waiting for transfers between devices: 37.1 us -> 38.7 us
    pallas_call x1, Pallas kernels: 18.6 us -> 7.05 us  [project(): pl.pallas_call(project_body, grid_spec=pltpu.PrefetchScalarGridSpec(num_s...]
    ppermute x14 -> x12, waiting for transfers between devices: 8 us -> 16.3 us  [along_seq(): return lax.ppermute(value, 'seq', pairs)]
    ppermute x20, waiting for transfers between devices: 29.1 us -> 22.4 us  [along_z(): return lax.ppermute(value, SECTION_HEAD, pairs)]
    reduce_sum x1, other arithmetic: 5.22 us -> 1.69 us  [rms_normed(): jnp.mean(as_float * as_float, axis=-1, keepdims=True) + EPSILON]
    ppermute x14 -> x12, starting transfers between devices: 17.2 us -> 13.8 us  [along_seq(): return lax.ppermute(value, 'seq', pairs)]
    ppermute x20, starting transfers between devices: 30 us -> 33 us  [along_z(): return lax.ppermute(value, SECTION_HEAD, pairs)]
    unnamed x27 -> x32, local copies, waits for them, and re-layouts: 4.92 us -> 6.59 us
  transfers between devices with their start and end apart: 34 -> 32, of which waited for: 10 -> 11; matrix products, arithmetic and copies ran while one was open for 9% -> 7% of each run, Pallas kernels for 16% -> 17%
where the time goes in v3:
time: 131 us
  starting transfers between devices  46.9 us (36%)
  waiting for transfers between devices  38.7 us (30%)
  Pallas kernels  29.8 us (23%)
  local copies, waits for them, and re-layouts  6.77 us (5%)
  matrix products  4.56 us (3%)
  other arithmetic  3.69 us (3%)
    ppermute x20, starting transfers between devices, along_z(): return lax.ppermute(value, SECTION_HEAD, pairs)  33 us
    ppermute x20, waiting for transfers between devices, along_z(): return lax.ppermute(value, SECTION_HEAD, pairs)  22.4 us
    ppermute x12, waiting for transfers between devices, along_seq(): return lax.ppermute(value, 'seq', pairs)  16.3 us
    ppermute x12, starting transfers between devices, along_seq(): return lax.ppermute(value, 'seq', pairs)  13.8 us
    pallas_call x4, Pallas kernels, attend(): pl.pallas_call(functools.partial(attend_body, first_tile), in_specs=[SMEM...  11.9 us
    pallas_call x1, Pallas kernels, project(): pl.pallas_call(project_body, grid_spec=pltpu.PrefetchScalarGridSpec(num_s...  7.05 us
    unnamed x32, local copies, waits for them, and re-layouts  6.59 us
    pallas_call x4, Pallas kernels, multiply(): pl.pallas_call(multiply_body, in_specs=[VMEM_WHOLE] * 3, out_specs=[VMEM_...  5.18 us
  transfers between devices with their start and end apart: 32, of which 11 were waited for; matrix products, arithmetic and copies ran while one was open for 7% of the time, Pallas kernels for 17%

profile of v3, /device:TPU:1, one launch (start us, length us, event | category | flops | bytes accessed | tf_op | source)
XLA Modules:
  0.0 130.8 jit_solution(12980795868053816502)
XLA Ops:
  0.8 7.0 %project.1 = (bf16[2064,128]{1,0:T(8,128)(2,1)S(1)}, bf16[2064,128]{1,0:T(8,128)(2,1)S(1)}, s32[8,128]{1,0:T(8,128)S(1)}, bf16[128,2048]{1,0:T(8,128)(2,1)S(1)},...) custom-call(s32[4]{0:T(128)S(1)} %pad_add_fusion.places_ref, ...), custom_call_target="tpu_custom_call" | custom-call | flops 1 | bytes 1 | tf_op jit(solution)/shard_map/project/pallas_call | solution.py:144
  9.4 2.1 %collective-permute-start.6 = (bf16[2064,128]{1,0:T(8,128)(2,1)S(1)}, bf16[2064,128]{1,0:T(8,128)(2,1)S(1)}, u32[]{:S(2)}, u32[]{:S(2)}) collective-permute-start(bf16[2064,128]{1,0:T(8,128)(2,1)S(1)} %get-tuple-element.73.refs_4_), channel_id=1, source_target_pairs={{0,2},{2,4},{4,6},{6,0},{8,10},{10,12},{12,14},{14,8},{16,18},{18,... | collective-permute-start | bytes 1585160 | tf_op jit(solution)/shard_map/ppermute | solution.py:40
  11.6 1.4 %collective-permute-start.5 = (bf16[2064,128]{1,0:T(8,128)(2,1)S(1)}, bf16[2064,128]{1,0:T(8,128)(2,1)S(1)}, u32[]{:S(2)}, u32[]{:S(2)}) collective-permute-start(bf16[2064,128]{1,0:T(8,128)(2,1)S(1)} %get-tuple-element.73.refs_4_), channel_id=1, source_target_pairs={{0,6},{2,0},{4,2},{6,4},{8,14},{10,8},{12,10},{14,12},{16,22},{18,... | collective-permute-start | bytes 1585160 | tf_op jit(solution)/shard_map/ppermute | solution.py:40
  13.0 1.2 collective-permute-start.3
  14.2 1.5 %collective-permute-start.2 = (bf16[2064,128]{1,0:T(8,128)(2,1)S(1)}, bf16[2064,128]{1,0:T(8,128)(2,1)}, u32[]{:S(2)}, u32[]{:S(2)}) collective-permute-start(bf16[2064,128]{1,0:T(8,128)(2,1)S(1)} %get-tuple-element.70.refs_0_), channel_id=1, source_target_pairs={{0,24},{2,26},{4,28},{6,30},{8,0},{10,2},{12,4},{14,6},{16,8},{18,... | collective-permute-start | bytes 1585160 | tf_op jit(solution)/shard_map/ppermute | solution.py:40
  15.7 1.6 %collective-permute-start = (bf16[128,2048]{1,0:T(8,128)(2,1)S(1)}, bf16[128,2048]{1,0:T(8,128)(2,1)S(1)}, u32[]{:S(2)}, u32[]{:S(2)}) collective-permute-start(bf16[128,2048]{1,0:T(8,128)(2,1)S(1)} %get-tuple-element.66), channel_id=1, source_target_pairs={{0,64},{32,96},{64,0},{96,32},{1,65},{33,97},{65,1},{97,33},{2,66}... | collective-permute-start | bytes 1572872 | tf_op jit(solution)/shard_map/ppermute | solution.py:52
  17.3 1.7 %fusion = f32[1024]{0:T(1024)S(1)} fusion(bf16[1024,4096]{1,0:T(8,128)(2,1)S(1)} %copy-done.6), kind=kLoop, calls=%fused_computation.2 | loop fusion | flops 12581888 | bytes 8392704 | tf_op jit(solution)/shard_map/reduce_sum | solution.py:328
  19.0 8.9 %collective-permute-done = bf16[128,2048]{1,0:T(8,128)(2,1)S(1)} collective-permute-done((bf16[128,2048]{1,0:T(8,128)(2,1)S(1)}, bf16[128,2048]{1,0:T(8,128)(2,1)S(1)}, u32[]{:S(2)}, u32[]{:S(2)}) %collective-permute-start) | collective-permute-done | bytes 524320 | tf_op jit(solution)/shard_map/ppermute | solution.py:52
  27.9 1.2 collective-permute-start.1
  29.1 1.6 %collective-permute-start.7 = (bf16[2064,128]{1,0:T(8,128)(2,1)S(1)}, bf16[2064,128]{1,0:T(8,128)(2,1)}, u32[]{:S(2)}, u32[]{:S(2)}) collective-permute-start(bf16[2064,128]{1,0:T(8,128)(2,1)S(1)} %get-tuple-element.73.refs_4_), channel_id=1, source_target_pairs={{0,4},{2,6},{4,0},{6,2},{8,12},{10,14},{12,8},{14,10},{16,20},{18,... | collective-permute-start | bytes 1585160 | tf_op jit(solution)/shard_map/ppermute | solution.py:40
  31.5 1.5 %collective-permute-start.4 = (bf16[2064,128]{1,0:T(8,128)(2,1)S(1)}, bf16[2064,128]{1,0:T(8,128)(2,1)}, u32[]{:S(2)}, u32[]{:S(2)}) collective-permute-start(bf16[2064,128]{1,0:T(8,128)(2,1)S(1)} %get-tuple-element.70.refs_0_), channel_id=1, source_target_pairs={{0,16},{2,18},{4,20},{6,22},{8,24},{10,26},{12,28},{14,30},{16,0},... | collective-permute-start | bytes 1585160 | tf_op jit(solution)/shard_map/ppermute | solution.py:40
  33.0 4.6 %fusion.7.q_ref = bf16[1024,512]{1,0:T(8,128)(2,1)S(1)} fusion(bf16[4096,512]{1,0:T(8,128)(2,1)S(1)} %copy-done.9, bf16[1024,4096]{1,0:T(8,128)(2,1)S(1)} %copy-done.6, f32[4096]{0:T(1024)S(1)} %copy-done.10, f32[1024]{0:T(1024)S(1)} %add_rsqrt_fusion), kind=kOutput, calls=%fused_computation.8 | convolution fusion | flops 4312268800 | bytes 13651968 | tf_op jit(solution)/shard_map/dot_general | solution.py:383
  37.8 1.5 %collective-permute-done.1 = bf16[128,2048]{1,0:T(8,128)(2,1)} collective-permute-done((bf16[128,2048]{1,0:T(8,128)(2,1)}, bf16[128,2048]{1,0:T(8,128)(2,1)}, u32[]{:S(2)}, u32[]{:S(2)}) %collective-permute-start.1) | collective-permute-done | bytes 524320 | tf_op jit(solution)/shard_map/ppermute | solution.py:52
  39.4 0.9 collective-permute-start.13
  40.3 1.1 collective-permute-done.7.refs_6_
  41.4 2.0 %collective-permute-done.4.refs_2_ = bf16[2064,128]{1,0:T(8,128)(2,1)} collective-permute-done((bf16[2064,128]{1,0:T(8,128)(2,1)S(1)}, bf16[2064,128]{1,0:T(8,128)(2,1)}, u32[]{:S(2)}, u32[]{:S(2)}) %collective-permute-start.4) | collective-permute-done | bytes 528416 | tf_op jit(solution)/shard_map/ppermute | solution.py:40
  43.5 1.0 copy-done.1
  44.5 2.6 %pack.1 = (bf16[2048,128]{1,0:T(8,128)(2,1)S(1)}, bf16[2048,128]{1,0:T(8,128)(2,1)S(1)}, bf16[2048,128]{1,0:T(8,128)(2,1)S(1)}, bf16[2048,128]{1,0:T(8,128)(2,1)...) custom-call(s32[2]{0:T(128)S(1)} %pad_add_fusion.1.place_ref, ...), custom_call_target="tpu_custom_call" | custom-call | flops 1 | bytes 1 | tf_op jit(solution)/shard_map/pack/pallas_call | solution.py:216
  47.1 0.8 collective-permute-start.8
  48.7 1.3 collective-permute-start.11
  50.1 3.0 %pick.1 = bf16[512,2048]{1,0:T(8,128)(2,1)S(1)} custom-call(s32[4]{0:T(128)S(1)} %pad_add_fusion.2.places_ref, bf16[512,4096]{1,0:T(8,128)(2,1)} %w_ref), custom_call_target="tpu_custom_call" | custom-call | flops 1 | bytes 1 | tf_op jit(solution)/shard_map/pick/pallas_call | solution.py:287
  54.3 5.4 %collective-permute-done.12 = bf16[2048,128]{1,0:T(8,128)(2,1)S(1)} collective-permute-done((bf16[2048,128]{1,0:T(8,128)(2,1)S(1)}, bf16[2048,128]{1,0:T(8,128)(2,1)S(1)}, u32[]{:S(2)}, u32[]{:S(2)}) %collective-permute-start.12) | collective-permute-done | bytes 524320 | tf_op jit(solution)/shard_map/ppermute | solution.py:40
  59.6 1.1 constant_dynamic-update-slice_fusion.10
  61.3 1.5 %collective-permute-start.10 = (bf16[2048,128]{1,0:T(8,128)(2,1)S(1)}, bf16[2048,128]{1,0:T(8,128)(2,1)S(1)}, u32[]{:S(2)}, u32[]{:S(2)}) collective-permute-start(bf16[2048,128]{1,0:T(8,128)(2,1)S(1)} %get-tuple-element.78), channel_id=1, source_target_pairs={{0,4},{2,6},{4,0},{6,2},{8,12},{10,14},{12,8},{14,10},{16,20},{18,... | collective-permute-start | bytes 1572872 | tf_op jit(solution)/shard_map/ppermute | solution.py:40
  63.0 6.6 %collective-permute-done.14 = bf16[2048,128]{1,0:T(8,128)(2,1)S(1)} collective-permute-done((bf16[2048,128]{1,0:T(8,128)(2,1)S(1)}, bf16[2048,128]{1,0:T(8,128)(2,1)S(1)}, u32[]{:S(2)}, u32[]{:S(2)}) %collective-permute-start.14) | collective-permute-done | bytes 524320 | tf_op jit(solution)/shard_map/ppermute | solution.py:40
  69.7 1.2 collective-permute-done.10
  71.0 3.0 %attend.4.mine_ref = bf16[256,512]{1,0:T(8,128)(2,1)S(1)} custom-call(s32[8,128]{1,0:T(8,128)S(1)} %get-tuple-element.99.slots_ref, s32[2]{0:T(128)S(1)} %pad_add_fusion.1.place_ref, bf16[1024,512]{1,0:T(8,128)(2,1)S(1)} %fusion.7.q_ref, bf16[8192,128]{1,0:T(8,128)(2,1)S(1)} %constant_dynamic-update-slice_fusion.k_ref, ...), custom_call_target="tpu_custom_call" | custom-call | flops 1 | bytes 1 | tf_op jit(solution)/shard_map/attend/pallas_call | solution.py:266
  74.0 1.0 collective-permute-start.15
  75.1 3.0 %attend.5.mine_ref = bf16[256,512]{1,0:T(8,128)(2,1)S(1)} custom-call(s32[8,128]{1,0:T(8,128)S(1)} %get-tuple-element.99.slots_ref, s32[2]{0:T(128)S(1)} %pad_add_fusion.1.place_ref, bf16[1024,512]{1,0:T(8,128)(2,1)S(1)} %fusion.7.q_ref, bf16[8192,128]{1,0:T(8,128)(2,1)S(1)} %constant_dynamic-update-slice_fusion.k_ref, ...), custom_call_target="tpu_custom_call" | custom-call | flops 1 | bytes 1 | tf_op jit(solution)/shard_map/attend/pallas_call | solution.py:266
  78.7 3.0 %attend.6.mine_ref = bf16[256,512]{1,0:T(8,128)(2,1)S(1)} custom-call(s32[8,128]{1,0:T(8,128)S(1)} %get-tuple-element.99.slots_ref, s32[2]{0:T(128)S(1)} %pad_add_fusion.1.place_ref, bf16[1024,512]{1,0:T(8,128)(2,1)S(1)} %fusion.7.q_ref, bf16[8192,128]{1,0:T(8,128)(2,1)S(1)} %constant_dynamic-update-slice_fusion.k_ref, ...), custom_call_target="tpu_custom_call" | custom-call | flops 1 | bytes 1 | tf_op jit(solution)/shard_map/attend/pallas_call | solution.py:266
  82.5 1.3 multiply.10
  83.8 12.6 %collective-permute-start.18 = (bf16[256,512]{1,0:T(8,128)(2,1)S(1)}, bf16[256,512]{1,0:T(8,128)(2,1)S(1)}, u32[]{:S(2)}, u32[]{:S(2)}) collective-permute-start(bf16[256,512]{1,0:T(8,128)(2,1)S(1)} %get-tuple-element.96), channel_id=1, source_target_pairs={{0,32},{32,0},{64,96},{96,64},{1,33},{33,1},{65,97},{97,65},{2,34}... | collective-permute-start | bytes 786440 | tf_op jit(solution)/shard_map/ppermute | solution.py:52
  96.4 1.1 collective-permute-start.24
  97.5 3.0 %attend.7.mine_ref = bf16[256,512]{1,0:T(8,128)(2,1)S(1)} custom-call(s32[8,128]{1,0:T(8,128)S(1)} %get-tuple-element.99.slots_ref, s32[2]{0:T(128)S(1)} %pad_add_fusion.1.place_ref, bf16[1024,512]{1,0:T(8,128)(2,1)S(1)} %fusion.7.q_ref, bf16[8192,128]{1,0:T(8,128)(2,1)S(1)} %constant_dynamic-update-slice_fusion.k_ref, ...), custom_call_target="tpu_custom_call" | custom-call | flops 1 | bytes 1 | tf_op jit(solution)/shard_map/attend/pallas_call | solution.py:266
  100.5 1.3 multiply.11
  102.7 2.3 %collective-permute-start.19 = (bf16[256,512]{1,0:T(8,128)(2,1)S(1)}, bf16[256,512]{1,0:T(8,128)(2,1)S(1)}, u32[]{:S(2)}, u32[]{:S(2)}) collective-permute-start(bf16[256,512]{1,0:T(8,128)(2,1)S(1)} %add_convert_fusion.7), channel_id=1, source_target_pairs={{0,65},{32,97},{64,1},{96,33},{1,64},{33,96},{65,0},{97,32},{2,67}... | collective-permute-start | bytes 786440 | tf_op jit(solution)/shard_map/ppermute | solution.py:52
  105.7 1.0 collective-permute-start.21
  106.7 1.3 multiply.12
  108.2 1.7 %collective-permute-start.23 = (bf16[256,512]{1,0:T(8,128)(2,1)S(1)}, bf16[256,512]{1,0:T(8,128)(2,1)S(1)}, u32[]{:S(2)}, u32[]{:S(2)}) collective-permute-start(bf16[256,512]{1,0:T(8,128)(2,1)S(1)} %add_convert_fusion.5), channel_id=1, source_target_pairs={{0,65},{32,97},{64,1},{96,33},{1,64},{33,96},{65,0},{97,32},{2,67}... | collective-permute-start | bytes 786440 | tf_op jit(solution)/shard_map/ppermute | solution.py:52
  109.9 1.5 %collective-permute-done.19 = bf16[256,512]{1,0:T(8,128)(2,1)S(1)} collective-permute-done((bf16[256,512]{1,0:T(8,128)(2,1)S(1)}, bf16[256,512]{1,0:T(8,128)(2,1)S(1)}, u32[]{:S(2)}, u32[]{:S(2)}) %collective-permute-start.19) | collective-permute-done | bytes 262176 | tf_op jit(solution)/shard_map/ppermute | solution.py:52
  111.4 1.3 collective-permute-start.25
  112.8 1.3 multiply.13
  114.1 1.0 collective-permute-start.29
  115.3 2.5 %collective-permute-start.27 = (bf16[256,512]{1,0:T(8,128)(2,1)S(1)}, bf16[256,512]{1,0:T(8,128)(2,1)S(1)}, u32[]{:S(2)}, u32[]{:S(2)}) collective-permute-start(bf16[256,512]{1,0:T(8,128)(2,1)S(1)} %add_convert_fusion.3), channel_id=1, source_target_pairs={{0,65},{32,97},{64,1},{96,33},{1,64},{33,96},{65,0},{97,32},{2,67}... | collective-permute-start | bytes 786440 | tf_op jit(solution)/shard_map/ppermute | solution.py:52
  118.0 1.9 %collective-permute-start.31 = (bf16[256,512]{1,0:T(8,128)(2,1)S(1)}, bf16[256,512]{1,0:T(8,128)(2,1)S(1)}, u32[]{:S(2)}, u32[]{:S(2)}) collective-permute-start(bf16[256,512]{1,0:T(8,128)(2,1)S(1)} %add_convert_fusion.1), channel_id=1, source_target_pairs={{0,65},{32,97},{64,1},{96,33},{1,64},{33,96},{65,0},{97,32},{2,67}... | collective-permute-start | bytes 786440 | tf_op jit(solution)/shard_map/ppermute | solution.py:52
  119.8 4.2 %collective-permute-done.27 = bf16[256,512]{1,0:T(8,128)(2,1)S(1)} collective-permute-done((bf16[256,512]{1,0:T(8,128)(2,1)S(1)}, bf16[256,512]{1,0:T(8,128)(2,1)S(1)}, u32[]{:S(2)}, u32[]{:S(2)}) %collective-permute-start.27) | collective-permute-done | bytes 262176 | tf_op jit(solution)/shard_map/ppermute | solution.py:52
  124.2 5.5 %collective-permute-done.31 = bf16[256,512]{1,0:T(8,128)(2,1)S(1)} collective-permute-done((bf16[256,512]{1,0:T(8,128)(2,1)S(1)}, bf16[256,512]{1,0:T(8,128)(2,1)S(1)}, u32[]{:S(2)}, u32[]{:S(2)}) %collective-permute-start.31) | collective-permute-done | bytes 262176 | tf_op jit(solution)/shard_map/ppermute | solution.py:52
  129.8 1.0 pad_maximum_fusion
  (77 shorter events, 10.2 us)
Async XLA Ops:
  0.1 0.7 copy-start.2
  0.8 16.6 %copy-start.6 = (bf16[1024,4096]{1,0:T(8,128)(2,1)S(1)}, bf16[1024,4096]{1,0:T(8,128)(2,1)}, u32[]{:S(2)}) copy-start(bf16[1024,4096]{1,0:T(8,128)(2,1)} %param.8) | copy-start | bytes 25165828
  7.8 0.8 copy-start.3
  8.6 0.8 copy-start.5
  9.4 19.7 %collective-permute-start.6 = (bf16[2064,128]{1,0:T(8,128)(2,1)S(1)}, bf16[2064,128]{1,0:T(8,128)(2,1)S(1)}, u32[]{:S(2)}, u32[]{:S(2)}) collective-permute-start(bf16[2064,128]{1,0:T(8,128)(2,1)S(1)} %get-tuple-element.73.refs_4_), channel_id=1, source_target_pairs={{0,2},{2,4},{4,6},{6,0},{8,10},{10,12},{12,14},{14,8},{16,18},{18,... | collective-permute-start | bytes 1585160 | tf_op jit(solution)/shard_map/ppermute | solution.py:40
  11.6 28.7 %collective-permute-start.5 = (bf16[2064,128]{1,0:T(8,128)(2,1)S(1)}, bf16[2064,128]{1,0:T(8,128)(2,1)S(1)}, u32[]{:S(2)}, u32[]{:S(2)}) collective-permute-start(bf16[2064,128]{1,0:T(8,128)(2,1)S(1)} %get-tuple-element.73.refs_4_), channel_id=1, source_target_pairs={{0,6},{2,0},{4,2},{6,4},{8,14},{10,8},{12,10},{14,12},{16,22},{18,... | collective-permute-start | bytes 1585160 | tf_op jit(solution)/shard_map/ppermute | solution.py:40
  13.0 17.7 %collective-permute-start.3 = (bf16[2064,128]{1,0:T(8,128)(2,1)S(1)}, bf16[2064,128]{1,0:T(8,128)(2,1)S(1)}, u32[]{:S(2)}, u32[]{:S(2)}) collective-permute-start(bf16[2064,128]{1,0:T(8,128)(2,1)S(1)} %get-tuple-element.70.refs_0_), channel_id=1, source_target_pairs={{0,8},{2,10},{4,12},{6,14},{8,16},{10,18},{12,20},{14,22},{16,24},... | collective-permute-start | bytes 1585160 | tf_op jit(solution)/shard_map/ppermute | solution.py:40
  14.2 26.1 %collective-permute-start.2 = (bf16[2064,128]{1,0:T(8,128)(2,1)S(1)}, bf16[2064,128]{1,0:T(8,128)(2,1)}, u32[]{:S(2)}, u32[]{:S(2)}) collective-permute-start(bf16[2064,128]{1,0:T(8,128)(2,1)S(1)} %get-tuple-element.70.refs_0_), channel_id=1, source_target_pairs={{0,24},{2,26},{4,28},{6,30},{8,0},{10,2},{12,4},{14,6},{16,8},{18,... | collective-permute-start | bytes 1585160 | tf_op jit(solution)/shard_map/ppermute | solution.py:40
  15.7 17.4 %copy-start.9 = (bf16[4096,512]{1,0:T(8,128)(2,1)S(1)}, bf16[4096,512]{1,0:T(8,128)(2,1)}, u32[]{:S(2)}) copy-start(bf16[4096,512]{1,0:T(8,128)(2,1)} %param.11) | copy-start | bytes 12582916
  15.7 17.4 %copy-start.10 = (f32[4096]{0:T(1024)S(1)}, f32[4096]{0:T(1024)}, u32[]{:S(2)}) copy-start(f32[4096]{0:T(1024)} %param.9) | copy-start | bytes 49156
  15.7 12.2 %collective-permute-start = (bf16[128,2048]{1,0:T(8,128)(2,1)S(1)}, bf16[128,2048]{1,0:T(8,128)(2,1)S(1)}, u32[]{:S(2)}, u32[]{:S(2)}) collective-permute-start(bf16[128,2048]{1,0:T(8,128)(2,1)S(1)} %get-tuple-element.66), channel_id=1, source_target_pairs={{0,64},{32,96},{64,0},{96,32},{1,65},{33,97},{65,1},{97,33},{2,66}... | collective-permute-start | bytes 1572872 | tf_op jit(solution)/shard_map/ppermute | solution.py:52
  27.9 2.8 %copy-start.7 = (bf16[128,2048]{1,0:T(8,128)(2,1)}, bf16[128,2048]{1,0:T(8,128)(2,1)S(1)}, u32[]{:S(2)}) copy-start(bf16[128,2048]{1,0:T(8,128)(2,1)S(1)} %collective-permute-done) | copy-start | bytes 1572868
  27.9 11.4 %collective-permute-start.1 = (bf16[128,2048]{1,0:T(8,128)(2,1)}, bf16[128,2048]{1,0:T(8,128)(2,1)}, u32[]{:S(2)}, u32[]{:S(2)}) collective-permute-start(bf16[128,2048]{1,0:T(8,128)(2,1)} %get-tuple-element.67), channel_id=1, source_target_pairs={{0,64},{32,96},{64,0},{96,32},{1,65},{33,97},{65,1},{97,33},{2,66}... | collective-permute-start | bytes 1572872 | tf_op jit(solution)/shard_map/ppermute | solution.py:52
  29.1 12.3 %collective-permute-start.7 = (bf16[2064,128]{1,0:T(8,128)(2,1)S(1)}, bf16[2064,128]{1,0:T(8,128)(2,1)}, u32[]{:S(2)}, u32[]{:S(2)}) collective-permute-start(bf16[2064,128]{1,0:T(8,128)(2,1)S(1)} %get-tuple-element.73.refs_4_), channel_id=1, source_target_pairs={{0,4},{2,6},{4,0},{6,2},{8,12},{10,14},{12,8},{14,10},{16,20},{18,... | collective-permute-start | bytes 1585160 | tf_op jit(solution)/shard_map/ppermute | solution.py:40
  30.7 0.8 copy-start
  31.5 11.9 %collective-permute-start.4 = (bf16[2064,128]{1,0:T(8,128)(2,1)S(1)}, bf16[2064,128]{1,0:T(8,128)(2,1)}, u32[]{:S(2)}, u32[]{:S(2)}) collective-permute-start(bf16[2064,128]{1,0:T(8,128)(2,1)S(1)} %get-tuple-element.70.refs_0_), channel_id=1, source_target_pairs={{0,16},{2,18},{4,20},{6,22},{8,24},{10,26},{12,28},{14,30},{16,0},... | collective-permute-start | bytes 1585160 | tf_op jit(solution)/shard_map/ppermute | solution.py:40
  39.4 20.3 %collective-permute-start.13 = (bf16[128,2048]{1,0:T(8,128)(2,1)}, bf16[128,2048]{1,0:T(8,128)(2,1)S(1)}, u32[]{:S(2)}, u32[]{:S(2)}) collective-permute-start(bf16[128,2048]{1,0:T(8,128)(2,1)} %copy-done.5), channel_id=1, source_target_pairs={{0,64},{32,96},{64,0},{96,32},{1,65},{33,97},{65,1},{97,33},{2,66}... | collective-permute-start | bytes 1572872 | tf_op jit(solution)/shard_map/ppermute | solution.py:52
  43.5 1.0 copy-start.1
  47.1 15.8 %collective-permute-start.8 = (bf16[2048,128]{1,0:T(8,128)(2,1)S(1)}, bf16[2048,128]{1,0:T(8,128)(2,1)S(1)}, u32[]{:S(2)}, u32[]{:S(2)}) collective-permute-start(bf16[2048,128]{1,0:T(8,128)(2,1)S(1)} %get-tuple-element.75), channel_id=1, source_target_pairs={{0,6},{2,0},{4,2},{6,4},{8,14},{10,8},{12,10},{14,12},{16,22},{18,... | collective-permute-start | bytes 1572872 | tf_op jit(solution)/shard_map/ppermute | solution.py:40
  48.0 13.4 %collective-permute-start.9 = (bf16[2048,128]{1,0:T(8,128)(2,1)S(1)}, bf16[2048,128]{1,0:T(8,128)(2,1)S(1)}, u32[]{:S(2)}, u32[]{:S(2)}) collective-permute-start(bf16[2048,128]{1,0:T(8,128)(2,1)S(1)} %get-tuple-element.77), channel_id=1, source_target_pairs={{0,2},{2,4},{4,6},{6,0},{8,10},{10,12},{12,14},{14,8},{16,18},{18,... | collective-permute-start | bytes 1572872 | tf_op jit(solution)/shard_map/ppermute | solution.py:40
  48.7 14.2 %collective-permute-start.11 = (bf16[2048,128]{1,0:T(8,128)(2,1)S(1)}, bf16[2048,128]{1,0:T(8,128)(2,1)S(1)}, u32[]{:S(2)}, u32[]{:S(2)}) collective-permute-start(bf16[2048,128]{1,0:T(8,128)(2,1)S(1)} %get-tuple-element.80), channel_id=1, source_target_pairs={{0,24},{2,26},{4,28},{6,30},{8,0},{10,2},{12,4},{14,6},{16,8},{18,... | collective-permute-start | bytes 1572872 | tf_op jit(solution)/shard_map/ppermute | solution.py:40
  49.9 9.7 %collective-permute-start.12 = (bf16[2048,128]{1,0:T(8,128)(2,1)S(1)}, bf16[2048,128]{1,0:T(8,128)(2,1)S(1)}, u32[]{:S(2)}, u32[]{:S(2)}) collective-permute-start(bf16[2048,128]{1,0:T(8,128)(2,1)S(1)} %get-tuple-element.82), channel_id=1, source_target_pairs={{0,8},{2,10},{4,12},{6,14},{8,16},{10,18},{12,20},{14,22},{16,24},... | collective-permute-start | bytes 1572872 | tf_op jit(solution)/shard_map/ppermute | solution.py:40
  53.2 1.0 copy-start.8
  53.2 7.5 %copy-start.4 = (bf16[128,2048]{1,0:T(8,128)(2,1)S(1)}, bf16[128,2048]{1,0:T(8,128)(2,1)}, u32[]{:S(2)}) copy-start(bf16[128,2048]{1,0:T(8,128)(2,1)} %copy-done.3) | copy-start | bytes 1572868
  59.6 9.9 %collective-permute-start.14 = (bf16[2048,128]{1,0:T(8,128)(2,1)S(1)}, bf16[2048,128]{1,0:T(8,128)(2,1)S(1)}, u32[]{:S(2)}, u32[]{:S(2)}) collective-permute-start(bf16[2048,128]{1,0:T(8,128)(2,1)S(1)} %get-tuple-element.86), channel_id=1, source_target_pairs={{0,16},{2,18},{4,20},{6,22},{8,24},{10,26},{12,28},{14,30},{16,0},... | collective-permute-start | bytes 1572872 | tf_op jit(solution)/shard_map/ppermute | solution.py:40
  60.7 17.9 %collective-permute-start.16 = (bf16[128,2048]{1,0:T(8,128)(2,1)S(1)}, bf16[128,2048]{1,0:T(8,128)(2,1)S(1)}, u32[]{:S(2)}, u32[]{:S(2)}) collective-permute-start(bf16[128,2048]{1,0:T(8,128)(2,1)S(1)} %copy-done.4), channel_id=1, source_target_pairs={{0,64},{32,96},{64,0},{96,32},{1,65},{33,97},{65,1},{97,33},{2,66}... | collective-permute-start | bytes 1572872 | tf_op jit(solution)/shard_map/ppermute | solution.py:52
  61.3 9.5 %collective-permute-start.10 = (bf16[2048,128]{1,0:T(8,128)(2,1)S(1)}, bf16[2048,128]{1,0:T(8,128)(2,1)S(1)}, u32[]{:S(2)}, u32[]{:S(2)}) collective-permute-start(bf16[2048,128]{1,0:T(8,128)(2,1)S(1)} %get-tuple-element.78), channel_id=1, source_target_pairs={{0,4},{2,6},{4,0},{6,2},{8,12},{10,14},{12,8},{14,10},{16,20},{18,... | collective-permute-start | bytes 1572872 | tf_op jit(solution)/shard_map/ppermute | solution.py:40
  74.0 8.5 %collective-permute-start.15 = (bf16[256,512]{1,0:T(8,128)(2,1)S(1)}, bf16[256,512]{1,0:T(8,128)(2,1)S(1)}, u32[]{:S(2)}, u32[]{:S(2)}) collective-permute-start(bf16[256,512]{1,0:T(8,128)(2,1)S(1)} %attend.4.mine_ref), channel_id=1, source_target_pairs={{0,64},{32,96},{64,0},{96,32},{1,65},{33,97},{65,1},{97,33},{2,66}... | collective-permute-start | bytes 786440 | tf_op jit(solution)/shard_map/ppermute | solution.py:52
  78.1 22.4 %collective-permute-start.20 = (bf16[256,512]{1,0:T(8,128)(2,1)S(1)}, bf16[256,512]{1,0:T(8,128)(2,1)S(1)}, u32[]{:S(2)}, u32[]{:S(2)}) collective-permute-start(bf16[256,512]{1,0:T(8,128)(2,1)S(1)} %attend.5.mine_ref), channel_id=1, source_target_pairs={{0,64},{32,96},{64,0},{96,32},{1,65},{33,97},{65,1},{97,33},{2,66}... | collective-permute-start | bytes 786440 | tf_op jit(solution)/shard_map/ppermute | solution.py:52
  83.8 18.8 %collective-permute-start.18 = (bf16[256,512]{1,0:T(8,128)(2,1)S(1)}, bf16[256,512]{1,0:T(8,128)(2,1)S(1)}, u32[]{:S(2)}, u32[]{:S(2)}) collective-permute-start(bf16[256,512]{1,0:T(8,128)(2,1)S(1)} %get-tuple-element.96), channel_id=1, source_target_pairs={{0,32},{32,0},{64,96},{96,64},{1,33},{33,1},{65,97},{97,65},{2,34}... | collective-permute-start | bytes 786440 | tf_op jit(solution)/shard_map/ppermute | solution.py:52
  96.4 9.3 %collective-permute-start.24 = (bf16[256,512]{1,0:T(8,128)(2,1)S(1)}, bf16[256,512]{1,0:T(8,128)(2,1)S(1)}, u32[]{:S(2)}, u32[]{:S(2)}) collective-permute-start(bf16[256,512]{1,0:T(8,128)(2,1)S(1)} %attend.6.mine_ref), channel_id=1, source_target_pairs={{0,64},{32,96},{64,0},{96,32},{1,65},{33,97},{65,1},{97,33},{2,66}... | collective-permute-start | bytes 786440 | tf_op jit(solution)/shard_map/ppermute | solution.py:52
  101.8 6.2 %collective-permute-start.22 = (bf16[256,512]{1,0:T(8,128)(2,1)S(1)}, bf16[256,512]{1,0:T(8,128)(2,1)S(1)}, u32[]{:S(2)}, u32[]{:S(2)}) collective-permute-start(bf16[256,512]{1,0:T(8,128)(2,1)S(1)} %get-tuple-element.104), channel_id=1, source_target_pairs={{0,32},{32,0},{64,96},{96,64},{1,33},{33,1},{65,97},{97,65},{2,34}... | collective-permute-start | bytes 786440 | tf_op jit(solution)/shard_map/ppermute | solution.py:52
  102.5 5.7 %collective-permute-start.17 = (bf16[256,512]{1,0:T(8,128)(2,1)S(1)}, bf16[256,512]{1,0:T(8,128)(2,1)S(1)}, u32[]{:S(2)}, u32[]{:S(2)}) collective-permute-start(bf16[256,512]{1,0:T(8,128)(2,1)S(1)} %get-tuple-element.94), channel_id=1, source_target_pairs={{0,32},{32,0},{64,96},{96,64},{1,33},{33,1},{65,97},{97,65},{2,34}... | collective-permute-start | bytes 786440 | tf_op jit(solution)/shard_map/ppermute | solution.py:52
  102.7 8.8 %collective-permute-start.19 = (bf16[256,512]{1,0:T(8,128)(2,1)S(1)}, bf16[256,512]{1,0:T(8,128)(2,1)S(1)}, u32[]{:S(2)}, u32[]{:S(2)}) collective-permute-start(bf16[256,512]{1,0:T(8,128)(2,1)S(1)} %add_convert_fusion.7), channel_id=1, source_target_pairs={{0,65},{32,97},{64,1},{96,33},{1,64},{33,96},{65,0},{97,32},{2,67}... | collective-permute-start | bytes 786440 | tf_op jit(solution)/shard_map/ppermute | solution.py:52
  105.0 7.8 %collective-permute-start.28 = (bf16[256,512]{1,0:T(8,128)(2,1)S(1)}, bf16[256,512]{1,0:T(8,128)(2,1)S(1)}, u32[]{:S(2)}, u32[]{:S(2)}) collective-permute-start(bf16[256,512]{1,0:T(8,128)(2,1)S(1)} %attend.7.mine_ref), channel_id=1, source_target_pairs={{0,64},{32,96},{64,0},{96,32},{1,65},{33,97},{65,1},{97,33},{2,66}... | collective-permute-start | bytes 786440 | tf_op jit(solution)/shard_map/ppermute | solution.py:52
  105.7 9.5 %collective-permute-start.21 = (bf16[256,512]{1,0:T(8,128)(2,1)S(1)}, bf16[256,512]{1,0:T(8,128)(2,1)S(1)}, u32[]{:S(2)}, u32[]{:S(2)}) collective-permute-start(bf16[256,512]{1,0:T(8,128)(2,1)S(1)} %get-tuple-element.102), channel_id=1, source_target_pairs={{0,32},{32,0},{64,96},{96,64},{1,33},{33,1},{65,97},{97,65},{2,34}... | collective-permute-start | bytes 786440 | tf_op jit(solution)/shard_map/ppermute | solution.py:52
  108.0 7.1 %collective-permute-start.26 = (bf16[256,512]{1,0:T(8,128)(2,1)S(1)}, bf16[256,512]{1,0:T(8,128)(2,1)S(1)}, u32[]{:S(2)}, u32[]{:S(2)}) collective-permute-start(bf16[256,512]{1,0:T(8,128)(2,1)S(1)} %get-tuple-element.110), channel_id=1, source_target_pairs={{0,32},{32,0},{64,96},{96,64},{1,33},{33,1},{65,97},{97,65},{2,34}... | collective-permute-start | bytes 786440 | tf_op jit(solution)/shard_map/ppermute | solution.py:52
  108.2 9.5 %collective-permute-start.23 = (bf16[256,512]{1,0:T(8,128)(2,1)S(1)}, bf16[256,512]{1,0:T(8,128)(2,1)S(1)}, u32[]{:S(2)}, u32[]{:S(2)}) collective-permute-start(bf16[256,512]{1,0:T(8,128)(2,1)S(1)} %add_convert_fusion.5), channel_id=1, source_target_pairs={{0,65},{32,97},{64,1},{96,33},{1,64},{33,96},{65,0},{97,32},{2,67}... | collective-permute-start | bytes 786440 | tf_op jit(solution)/shard_map/ppermute | solution.py:52
  111.4 8.4 %collective-permute-start.25 = (bf16[256,512]{1,0:T(8,128)(2,1)S(1)}, bf16[256,512]{1,0:T(8,128)(2,1)S(1)}, u32[]{:S(2)}, u32[]{:S(2)}) collective-permute-start(bf16[256,512]{1,0:T(8,128)(2,1)S(1)} %get-tuple-element.108), channel_id=1, source_target_pairs={{0,32},{32,0},{64,96},{96,64},{1,33},{33,1},{65,97},{97,65},{2,34}... | collective-permute-start | bytes 786440 | tf_op jit(solution)/shard_map/ppermute | solution.py:52
  114.1 10.0 %collective-permute-start.29 = (bf16[256,512]{1,0:T(8,128)(2,1)S(1)}, bf16[256,512]{1,0:T(8,128)(2,1)S(1)}, u32[]{:S(2)}, u32[]{:S(2)}) collective-permute-start(bf16[256,512]{1,0:T(8,128)(2,1)S(1)} %get-tuple-element.115), channel_id=1, source_target_pairs={{0,32},{32,0},{64,96},{96,64},{1,33},{33,1},{65,97},{97,65},{2,34}... | collective-permute-start | bytes 786440 | tf_op jit(solution)/shard_map/ppermute | solution.py:52
  115.1 2.8 %collective-permute-start.30 = (bf16[256,512]{1,0:T(8,128)(2,1)S(1)}, bf16[256,512]{1,0:T(8,128)(2,1)S(1)}, u32[]{:S(2)}, u32[]{:S(2)}) collective-permute-start(bf16[256,512]{1,0:T(8,128)(2,1)S(1)} %get-tuple-element.117), channel_id=1, source_target_pairs={{0,32},{32,0},{64,96},{96,64},{1,33},{33,1},{65,97},{97,65},{2,34}... | collective-permute-start | bytes 786440 | tf_op jit(solution)/shard_map/ppermute | solution.py:52
  115.3 8.8 %collective-permute-start.27 = (bf16[256,512]{1,0:T(8,128)(2,1)S(1)}, bf16[256,512]{1,0:T(8,128)(2,1)S(1)}, u32[]{:S(2)}, u32[]{:S(2)}) collective-permute-start(bf16[256,512]{1,0:T(8,128)(2,1)S(1)} %add_convert_fusion.3), channel_id=1, source_target_pairs={{0,65},{32,97},{64,1},{96,33},{1,64},{33,96},{65,0},{97,32},{2,67}... | collective-permute-start | bytes 786440 | tf_op jit(solution)/shard_map/ppermute | solution.py:52
  118.0 11.7 %collective-permute-start.31 = (bf16[256,512]{1,0:T(8,128)(2,1)S(1)}, bf16[256,512]{1,0:T(8,128)(2,1)S(1)}, u32[]{:S(2)}, u32[]{:S(2)}) collective-permute-start(bf16[256,512]{1,0:T(8,128)(2,1)S(1)} %add_convert_fusion.1), channel_id=1, source_target_pairs={{0,65},{32,97},{64,1},{96,33},{1,64},{33,96},{65,0},{97,32},{2,67}... | collective-permute-start | bytes 786440 | tf_op jit(solution)/shard_map/ppermute | solution.py:52

commit v4 on v3

--- a/solution.py
+++ b/solution.py
@@ -19,9 +19,12 @@
 PICKS = SIDE * SIDE * CAP
 NOTE_ROWS = 16
 EPSILON = 1e-05
-NEAR_PIECES = (128, 128, 128, 128)
+NEAR_PIECES = (160, 192, 160)
 CHUNKS = (2, 2, 2, 2)
 AHEAD = 3
+LAG = 2
+FIN = 3
+GOT = 2
 SCALE = HEAD_DIM**-0.5
 LOG2_E = 1.4426950408889634
 
@@ -64,17 +67,8 @@
     return along_z(value, lambda z, core: (z, 1 - core))
 
 
-def project_body(
-    places_ref, selected_ref, x_ref, wk_ref, wv_ref, wo_ref, k_ref, v_ref, slots_ref, *rest
-):
-    piece_refs, w_ref = rest[:-1], rest[-1]
+def project_body(selected_ref, x_ref, wk_ref, wv_ref, k_ref, v_ref, slots_ref, w_ref):
     step = pl.program_id(0)
-
-    at = 0
-    for piece in piece_refs:
-        piece[...] = wo_ref[at : at + piece.shape[0], :]
-        at += piece.shape[0]
-
     rows = x_ref.shape[0]
     steps = pl.num_programs(0)
     blocks_dev = (k_ref.shape[0] - NOTE_ROWS) // BLOCK
@@ -135,52 +129,31 @@
     return pltpu.with_memory_space_constraint(value, pltpu.HBM)
 
 
-def project(image_features, key_weight, value_weight, selected, places, output_weight):
+def project(image_features, key_weight, value_weight, selected):
     rows, enc = image_features.shape
     steps = 4
     out = jax.ShapeDtypeStruct((rows + NOTE_ROWS, HEAD_DIM), jnp.bfloat16)
-    whole = lambda shape: pl.BlockSpec(shape, lambda i, places: (0,) * len(shape))
-    depth, width = output_weight.shape[0], output_weight.shape[1] // 8
+    whole = lambda shape: pl.BlockSpec(shape, lambda i: (0,) * len(shape))
     return pl.pallas_call(
         project_body,
-        grid_spec=pltpu.PrefetchScalarGridSpec(
-            num_scalar_prefetch=1,
-            grid=(steps,),
-            in_specs=[
-                whole(selected.shape),
-                pl.BlockSpec((rows // steps, enc), lambda i, places: (i, 0)),
-                whole((enc, HEAD_DIM)),
-                whole((enc, HEAD_DIM)),
-                pl.BlockSpec((depth, width), lambda i, places: (0, places[i])),
-            ],
-            out_specs=[
-                whole((rows + NOTE_ROWS, HEAD_DIM)),
-                whole((rows + NOTE_ROWS, HEAD_DIM)),
-                whole((8, PICKS)),
-                *[pl.BlockSpec((part, width), lambda i, places: (0, i)) for part in NEAR_PIECES],
-            ],
-            scratch_shapes=[pltpu.VMEM((enc, 2 * HEAD_DIM), jnp.bfloat16)],
-        ),
-        out_shape=[
-            out,
-            out,
-            jax.ShapeDtypeStruct((8, PICKS), jnp.int32),
-            *[
-                jax.ShapeDtypeStruct((part, steps * width), output_weight.dtype)
-                for part in NEAR_PIECES
-            ],
+        grid=(steps,),
+        in_specs=[
+            whole(selected.shape),
+            pl.BlockSpec((rows // steps, enc), lambda i: (i, 0)),
+            whole((enc, HEAD_DIM)),
+            whole((enc, HEAD_DIM)),
         ],
+        out_specs=[
+            whole((rows + NOTE_ROWS, HEAD_DIM)),
+            whole((rows + NOTE_ROWS, HEAD_DIM)),
+            whole((8, PICKS)),
+        ],
+        out_shape=[out, out, jax.ShapeDtypeStruct((8, PICKS), jnp.int32)],
+        scratch_shapes=[pltpu.VMEM((enc, 2 * HEAD_DIM), jnp.bfloat16)],
         compiler_params=pltpu.CompilerParams(vmem_limit_bytes=40 << 20),
         cost_estimate=SMALL,
         name="project",
-    )(
-        places,
-        selected,
-        in_hbm(image_features),
-        in_hbm(key_weight),
-        in_hbm(value_weight),
-        in_hbm(output_weight),
-    )
+    )(selected, in_hbm(image_features), in_hbm(key_weight), in_hbm(value_weight))
 
 
 def pack_one(ask, me, base, stride, ring, outs):
@@ -370,21 +343,21 @@
             [column(3 - z, 1 - core), column(z, 1 - core), column(3 - z, core), column(z, core)]
         )
 
-    k_own, v_own, slots, *pieces = project(
-        image_features, key_weight, value_weight, selected, wanted_columns(z ^ 1), output_weight
-    )
+    k_own, v_own, slots = project(image_features, key_weight, value_weight, selected)
+    pieces = pick(wanted_columns(z ^ 1), after(output_weight, k_own), NEAR_PIECES)
     near_weight = []
     for piece in pieces:
-        near_weight.append(to_near(after(piece, near_weight[-1]) if near_weight else piece))
+        hold = near_weight[-1] if near_weight else text_hidden
+        near_weight.append(to_near(after(piece, hold)))
     k_ring = spread(k_own, 1, 0)
-    v_ring = spread(v_own, 0, 1, lambda part: after(part, near_weight[0]))
+    v_ring = spread(v_own, 0, 1)
 
     normed = rms_normed(after(text_hidden, k_own), norm_gain)
     queries = jnp.dot(normed, query_weight, preferred_element_type=jnp.float32).astype(jnp.bfloat16)
 
-    k_out, v_out = pack(after(after(place, near_weight[1]), queries), k_ring, v_ring)
+    k_out, v_out = pack(after(after(place, near_weight[0]), queries), k_ring, v_ring)
     keys = exchange(k_out, 0, 1)
-    values = exchange(v_out, 1, 0, lambda part: after(part, near_weight[2]))
+    values = exchange(v_out, 1, 0, lambda part: after(part, near_weight[1]))
     own_weight = pick(
         wanted_columns(z), after(output_weight, k_out[0]), (output_weight.shape[0],)
     )
@@ -405,18 +378,18 @@
     weight = after(weight, mine[-1])
     last = len(CHUNKS) - 1
     for index in range(len(CHUNKS)):
-        if index >= 2:
-            weight = after(weight, sent[index - 2])
-        if index >= 3:
-            weight = after(weight, outs[index - 3])
+        if index >= LAG:
+            weight = after(weight, sent[index - LAG])
+        if FIN and index >= FIN:
+            weight = after(weight, outs[index - FIN])
         give_far, give_own, keep_far, keep_own = multiply(mine[index], near[index], weight)
         weight = after(weight, give_far)
         if len(mine) < len(CHUNKS):
             slots = attended(after(slots, give_far))
             weight = after(weight, mine[-1])
         got_far, got_own = to_core(give_far), to_core(give_own)
-        if index >= 2 and index == last:
-            got_far = after(got_far, outs[index - 2])
+        if GOT and index >= GOT:
+            got_far = after(got_far, outs[index - GOT])
         send = (keep_far + got_far.astype(jnp.float32)).astype(jnp.bfloat16)
         far = to_far(send)
         sent.append(send)

time: 131 us -> 137 us (1.046)
  other arithmetic: 3.69 us -> 13.7 us
  waiting for transfers between devices: 38.7 us -> 32.1 us
  starting transfers between devices: 46.9 us -> 40.6 us
  local copies, waits for them, and re-layouts: 6.77 us -> 12.4 us
  Pallas kernels: 29.8 us -> 32.4 us
    ppermute x20 -> x19, starting transfers between devices: 33 us -> 23.5 us  [along_z(): return lax.ppermute(value, SECTION_HEAD, pairs)]
    concatenate x0 -> x1, other arithmetic: none -> 5.92 us  [shards(): weight = jnp.concatenate([*own_weight, *near_weight])]
    unnamed x32 -> x42, local copies, waits for them, and re-layouts: 6.59 us -> 12.2 us
    ppermute x20 -> x19, waiting for transfers between devices: 22.4 us -> 17.3 us  [along_z(): return lax.ppermute(value, SECTION_HEAD, pairs)]
    pallas_call x1 -> x2, Pallas kernels: 3.02 us -> 7.42 us  [pick(): pl.pallas_call(pick_body, grid_spec=pltpu.PrefetchScalarGridSpec(num_scal...]
    reduce_sum x1, other arithmetic: 1.69 us -> 5.74 us  [rms_normed(): jnp.mean(as_float * as_float, axis=-1, keepdims=True) + EPSILON]
    ppermute x12, starting transfers between devices: 13.8 us -> 17 us  [along_seq(): return lax.ppermute(value, 'seq', pairs)]
    pallas_call x1, Pallas kernels: 7.05 us -> 4.68 us  [project(): pl.pallas_call(project_body, grid=(steps,), in_specs=[whole(selected.shap...]
  transfers between devices with their start and end apart: 32 -> 31, of which waited for: 11 -> 9; matrix products, arithmetic and copies ran while one was open for 7% -> 14% of each run, Pallas kernels for 17% -> 20%
where the time goes in v4:
time: 137 us; the launch traced here: 136 us
  starting transfers between devices  40.6 us (30%)
  Pallas kernels  32.4 us (24%)
  waiting for transfers between devices  32.1 us (23%)
  other arithmetic  13.7 us (10%)
  local copies, waits for them, and re-layouts  12.4 us (9%)
  matrix products  4.57 us (3%)
    ppermute x19, starting transfers between devices, along_z(): return lax.ppermute(value, SECTION_HEAD, pairs)  23.5 us
    ppermute x19, waiting for transfers between devices, along_z(): return lax.ppermute(value, SECTION_HEAD, pairs)  17.3 us
    ppermute x12, starting transfers between devices, along_seq(): return lax.ppermute(value, 'seq', pairs)  17 us
    ppermute x12, waiting for transfers between devices, along_seq(): return lax.ppermute(value, 'seq', pairs)  14.9 us
    unnamed x42, local copies, waits for them, and re-layouts  12.2 us
    pallas_call x4, Pallas kernels, attend(): pl.pallas_call(functools.partial(attend_body, first_tile), in_specs=[SMEM...  11.9 us
    pallas_call x2, Pallas kernels, pick(): pl.pallas_call(pick_body, grid_spec=pltpu.PrefetchScalarGridSpec(num_scal...  7.42 us
    concatenate x1, other arithmetic, shards(): weight = jnp.concatenate([*own_weight, *near_weight])  5.92 us
  transfers between devices with their start and end apart: 31, of which 9 were waited for; matrix products, arithmetic and copies ran while one was open for 14% of the time, Pallas kernels for 20%

profile of v4, /device:TPU:1, one launch (start us, length us, event | category | flops | bytes accessed | tf_op | source)
XLA Modules:
  0.0 136.1 jit_solution(15920925647266489078)
XLA Ops:
  0.7 4.7 %project.1 = (bf16[2064,128]{1,0:T(8,128)(2,1)S(1)}, bf16[2064,128]{1,0:T(8,128)(2,1)S(1)}, s32[8,128]{1,0:T(8,128)S(1)}) custom-call(s32[8,16]{1,0:T(8,128)S(1)} %copy-done.4, bf16[2048,1024]{1,0:T(8,128)(2,1)} %x_ref.1, bf16[1024,128]{1,0:T(8,128)(2,1)} %wk_ref.1, bf16[1024,128]{1,0:T(8,128)(2,1)} %wv_ref.1), custom_call_target="tpu_custom_call" | custom-call | flops 1 | bytes 1 | tf_op jit(solution)/shard_map/project/pallas_call | solution.py:137
  5.4 2.2 %collective-permute-start.5 = (bf16[2064,128]{1,0:T(8,128)(2,1)S(1)}, bf16[2064,128]{1,0:T(8,128)(2,1)S(1)}, u32[]{:S(2)}, u32[]{:S(2)}) collective-permute-start(bf16[2064,128]{1,0:T(8,128)(2,1)S(1)} %get-tuple-element.72.refs_4_), channel_id=1, source_target_pairs={{0,2},{2,4},{4,6},{6,0},{8,10},{10,12},{12,14},{14,8},{16,18},{18,... | collective-permute-start | bytes 1585160 | tf_op jit(solution)/shard_map/ppermute | solution.py:43
  7.6 1.5 %collective-permute-start.4 = (bf16[2064,128]{1,0:T(8,128)(2,1)S(1)}, bf16[2064,128]{1,0:T(8,128)(2,1)S(1)}, u32[]{:S(2)}, u32[]{:S(2)}) collective-permute-start(bf16[2064,128]{1,0:T(8,128)(2,1)S(1)} %get-tuple-element.72.refs_4_), channel_id=1, source_target_pairs={{0,6},{2,0},{4,2},{6,4},{8,14},{10,8},{12,10},{14,12},{16,22},{18,... | collective-permute-start | bytes 1585160 | tf_op jit(solution)/shard_map/ppermute | solution.py:43
  9.1 1.2 collective-permute-start.2
  10.3 1.5 %collective-permute-start.1 = (bf16[2064,128]{1,0:T(8,128)(2,1)S(1)}, bf16[2064,128]{1,0:T(8,128)(2,1)}, u32[]{:S(2)}, u32[]{:S(2)}) collective-permute-start(bf16[2064,128]{1,0:T(8,128)(2,1)S(1)} %get-tuple-element.70.refs_0_), channel_id=1, source_target_pairs={{0,24},{2,26},{4,28},{6,30},{8,0},{10,2},{12,4},{14,6},{16,8},{18,... | collective-permute-start | bytes 1585160 | tf_op jit(solution)/shard_map/ppermute | solution.py:43
  11.8 4.4 %pick.2 = (bf16[160,2048]{1,0:T(8,128)(2,1)S(1)}, bf16[192,2048]{1,0:T(8,128)(2,1)}, bf16[160,2048]{1,0:T(8,128)(2,1)S(1)}) custom-call(s32[4]{0:T(128)S(1)} %pad_add_fusion.1.places_ref, bf16[512,4096]{1,0:T(8,128)(2,1)} %w_ref.1), custom_call_target="tpu_custom_call" | custom-call | flops 1 | bytes 1 | tf_op jit(solution)/shard_map/pick/pallas_call | solution.py:260
  17.1 1.6 %collective-permute-start = (bf16[160,2048]{1,0:T(8,128)(2,1)S(1)}, bf16[160,2048]{1,0:T(8,128)(2,1)S(1)}, u32[]{:S(2)}, u32[]{:S(2)}) collective-permute-start(bf16[160,2048]{1,0:T(8,128)(2,1)S(1)} %get-tuple-element.67), channel_id=1, source_target_pairs={{0,64},{32,96},{64,0},{96,32},{1,65},{33,97},{65,1},{97,33},{2,66}... | collective-permute-start | bytes 1966088 | tf_op jit(solution)/shard_map/ppermute | solution.py:55
  18.7 5.7 %fusion = f32[1024]{0:T(1024)S(1)} fusion(bf16[1024,4096]{1,0:T(8,128)(2,1)} %param.8), kind=kLoop, calls=%fused_computation.2 | loop fusion | flops 12581888 | bytes 8392704 | tf_op jit(solution)/shard_map/reduce_sum | solution.py:301
  24.5 1.6 %collective-permute-start.6 = (bf16[2064,128]{1,0:T(8,128)(2,1)S(1)}, bf16[2064,128]{1,0:T(8,128)(2,1)}, u32[]{:S(2)}, u32[]{:S(2)}) collective-permute-start(bf16[2064,128]{1,0:T(8,128)(2,1)S(1)} %get-tuple-element.72.refs_4_), channel_id=1, source_target_pairs={{0,4},{2,6},{4,0},{6,2},{8,12},{10,14},{12,8},{14,10},{16,20},{18,... | collective-permute-start | bytes 1585160 | tf_op jit(solution)/shard_map/ppermute | solution.py:43
  26.9 1.5 %collective-permute-start.3 = (bf16[2064,128]{1,0:T(8,128)(2,1)S(1)}, bf16[2064,128]{1,0:T(8,128)(2,1)}, u32[]{:S(2)}, u32[]{:S(2)}) collective-permute-start(bf16[2064,128]{1,0:T(8,128)(2,1)S(1)} %get-tuple-element.70.refs_0_), channel_id=1, source_target_pairs={{0,16},{2,18},{4,20},{6,22},{8,24},{10,26},{12,28},{14,30},{16,0},... | collective-permute-start | bytes 1585160 | tf_op jit(solution)/shard_map/ppermute | solution.py:43
  28.5 3.7 %collective-permute-done = bf16[160,2048]{1,0:T(8,128)(2,1)S(1)} collective-permute-done((bf16[160,2048]{1,0:T(8,128)(2,1)S(1)}, bf16[160,2048]{1,0:T(8,128)(2,1)S(1)}, u32[]{:S(2)}, u32[]{:S(2)}) %collective-permute-start) | collective-permute-done | bytes 655392 | tf_op jit(solution)/shard_map/ppermute | solution.py:55
  32.2 0.8 copy-done.14
  33.0 1.2 collective-permute-start.12
  34.2 4.6 %fusion.7.q_ref = bf16[1024,512]{1,0:T(8,128)(2,1)S(1)} fusion(bf16[4096,512]{1,0:T(8,128)(2,1)S(1)} %copy-done.16, bf16[1024,4096]{1,0:T(8,128)(2,1)S(1)} %copy-done.13, f32[4096]{0:T(1024)S(1)} %copy-done.17, f32[1024]{0:T(1024)S(1)} %add_rsqrt_fusion), kind=kOutput, calls=%fused_computation.9 | convolution fusion | flops 4312268800 | bytes 13651968 | tf_op jit(solution)/shard_map/dot_general | solution.py:356
  38.9 1.0 collective-permute-done.3.refs_2_
  39.9 1.0 copy-done.1
  40.9 3.4 %pack.1 = (bf16[2048,128]{1,0:T(8,128)(2,1)S(1)}, bf16[2048,128]{1,0:T(8,128)(2,1)S(1)}, bf16[2048,128]{1,0:T(8,128)(2,1)S(1)}, bf16[2048,128]{1,0:T(8,128)(2,1)...) custom-call(s32[2]{0:T(128)S(1)} %pad_add_fusion.place_ref, ...), custom_call_target="tpu_custom_call" | custom-call | flops 1 | bytes 1 | tf_op jit(solution)/shard_map/pack/pallas_call | solution.py:189
  50.4 2.7 %collective-permute-start.10 = (bf16[2048,128]{1,0:T(8,128)(2,1)}, bf16[2048,128]{1,0:T(8,128)(2,1)S(1)}, u32[]{:S(2)}, u32[]{:S(2)}) collective-permute-start(bf16[2048,128]{1,0:T(8,128)(2,1)} %copy-done.11), channel_id=1, source_target_pairs={{0,24},{2,26},{4,28},{6,30},{8,0},{10,2},{12,4},{14,6},{16,8},{18,... | collective-permute-start | bytes 1572872 | tf_op jit(solution)/shard_map/ppermute | solution.py:43
  53.1 2.3 %collective-permute-start.7 = (bf16[2048,128]{1,0:T(8,128)(2,1)}, bf16[2048,128]{1,0:T(8,128)(2,1)S(1)}, u32[]{:S(2)}, u32[]{:S(2)}) collective-permute-start(bf16[2048,128]{1,0:T(8,128)(2,1)} %copy-done.10), channel_id=1, source_target_pairs={{0,6},{2,0},{4,2},{6,4},{8,14},{10,8},{12,10},{14,12},{16,22},{18,... | collective-permute-start | bytes 1572872 | tf_op jit(solution)/shard_map/ppermute | solution.py:43
  55.4 1.1 constant_dynamic-update-slice_fusion.7
  56.5 5.3 %collective-permute-done.11 = bf16[2048,128]{1,0:T(8,128)(2,1)S(1)} collective-permute-done((bf16[2048,128]{1,0:T(8,128)(2,1)}, bf16[2048,128]{1,0:T(8,128)(2,1)S(1)}, u32[]{:S(2)}, u32[]{:S(2)}) %collective-permute-start.11) | collective-permute-done | bytes 524320 | tf_op jit(solution)/shard_map/ppermute | solution.py:43
  62.1 1.1 constant_dynamic-update-slice_fusion.3
  63.2 3.0 %pick.3 = bf16[512,2048]{1,0:T(8,128)(2,1)S(1)} custom-call(s32[4]{0:T(128)S(1)} %pad_add_fusion.2.places_ref, bf16[512,4096]{1,0:T(8,128)(2,1)} %w_ref.1), custom_call_target="tpu_custom_call" | custom-call | flops 1 | bytes 1 | tf_op jit(solution)/shard_map/pick/pallas_call | solution.py:260
  66.3 1.8 %collective-permute-start.9 = (bf16[2048,128]{1,0:T(8,128)(2,1)S(1)}, bf16[2048,128]{1,0:T(8,128)(2,1)S(1)}, u32[]{:S(2)}, u32[]{:S(2)}) collective-permute-start(bf16[2048,128]{1,0:T(8,128)(2,1)S(1)} %copy-done.8), channel_id=1, source_target_pairs={{0,4},{2,6},{4,0},{6,2},{8,12},{10,14},{12,8},{14,10},{16,20},{18,... | collective-permute-start | bytes 1572872 | tf_op jit(solution)/shard_map/ppermute | solution.py:43
  68.3 4.6 %collective-permute-done.13 = bf16[2048,128]{1,0:T(8,128)(2,1)S(1)} collective-permute-done((bf16[2048,128]{1,0:T(8,128)(2,1)}, bf16[2048,128]{1,0:T(8,128)(2,1)S(1)}, u32[]{:S(2)}, u32[]{:S(2)}) %collective-permute-start.13) | collective-permute-done | bytes 524320 | tf_op jit(solution)/shard_map/ppermute | solution.py:43
  73.1 4.0 %collective-permute-done.9 = bf16[2048,128]{1,0:T(8,128)(2,1)S(1)} collective-permute-done((bf16[2048,128]{1,0:T(8,128)(2,1)S(1)}, bf16[2048,128]{1,0:T(8,128)(2,1)S(1)}, u32[]{:S(2)}, u32[]{:S(2)}) %collective-permute-start.9) | collective-permute-done | bytes 524320 | tf_op jit(solution)/shard_map/ppermute | solution.py:43
  77.2 3.0 %attend.4.mine_ref = bf16[256,512]{1,0:T(8,128)(2,1)S(1)} custom-call(s32[8,128]{1,0:T(8,128)S(1)} %get-tuple-element.98.slots_ref, s32[2]{0:T(128)S(1)} %pad_add_fusion.place_ref, bf16[1024,512]{1,0:T(8,128)(2,1)S(1)} %fusion.7.q_ref, bf16[8192,128]{1,0:T(8,128)(2,1)S(1)} %constant_dynamic-update-slice_fusion.k_ref, ...), custom_call_target="tpu_custom_call" | custom-call | flops 1 | bytes 1 | tf_op jit(solution)/shard_map/attend/pallas_call | solution.py:239
  80.2 1.2 collective-permute-start.14
  81.3 3.0 %attend.5.mine_ref = bf16[256,512]{1,0:T(8,128)(2,1)S(1)} custom-call(s32[8,128]{1,0:T(8,128)S(1)} %get-tuple-element.98.slots_ref, s32[2]{0:T(128)S(1)} %pad_add_fusion.place_ref, bf16[1024,512]{1,0:T(8,128)(2,1)S(1)} %fusion.7.q_ref, bf16[8192,128]{1,0:T(8,128)(2,1)S(1)} %constant_dynamic-update-slice_fusion.k_ref, ...), custom_call_target="tpu_custom_call" | custom-call | flops 1 | bytes 1 | tf_op jit(solution)/shard_map/attend/pallas_call | solution.py:239
  84.8 5.9 %pad_maximum_fusion.w_ref = bf16[1024,2048]{1,0:T(8,128)(2,1)S(1)} fusion(bf16[160,2048]{1,0:T(8,128)(2,1)S(1)} %collective-permute-done.15, bf16[192,2048]{1,0:T(8,128)(2,1)} %collective-permute-done.12, bf16[160,2048]{1,0:T(8,128)(2,1)S(1)} %copy-done.15, bf16[512,2048]{1,0:T(8,128)(2,1)S(1)} %pick.3), kind=kLoop, calls=%fused_computation.8 | loop fusion | flops 16777216 | bytes 8388608 | tf_op jit(solution)/shard_map/concatenate | solution.py:364
  90.7 3.0 %attend.6.mine_ref = bf16[256,512]{1,0:T(8,128)(2,1)S(1)} custom-call(s32[8,128]{1,0:T(8,128)S(1)} %get-tuple-element.98.slots_ref, s32[2]{0:T(128)S(1)} %pad_add_fusion.place_ref, bf16[1024,512]{1,0:T(8,128)(2,1)S(1)} %fusion.7.q_ref, bf16[8192,128]{1,0:T(8,128)(2,1)S(1)} %constant_dynamic-update-slice_fusion.k_ref, ...), custom_call_target="tpu_custom_call" | custom-call | flops 1 | bytes 1 | tf_op jit(solution)/shard_map/attend/pallas_call | solution.py:239
  93.7 1.2 multiply.10
  95.0 5.8 %collective-permute-start.17 = (bf16[256,512]{1,0:T(8,128)(2,1)S(1)}, bf16[256,512]{1,0:T(8,128)(2,1)S(1)}, u32[]{:S(2)}, u32[]{:S(2)}) collective-permute-start(bf16[256,512]{1,0:T(8,128)(2,1)S(1)} %get-tuple-element.95), channel_id=1, source_target_pairs={{0,32},{32,0},{64,96},{96,64},{1,33},{33,1},{65,97},{97,65},{2,34}... | collective-permute-start | bytes 786440 | tf_op jit(solution)/shard_map/ppermute | solution.py:55
  100.8 1.4 collective-permute-start.23
  102.2 3.0 %attend.7.mine_ref = bf16[256,512]{1,0:T(8,128)(2,1)S(1)} custom-call(s32[8,128]{1,0:T(8,128)S(1)} %get-tuple-element.98.slots_ref, s32[2]{0:T(128)S(1)} %pad_add_fusion.place_ref, bf16[1024,512]{1,0:T(8,128)(2,1)S(1)} %fusion.7.q_ref, bf16[8192,128]{1,0:T(8,128)(2,1)S(1)} %constant_dynamic-update-slice_fusion.k_ref, ...), custom_call_target="tpu_custom_call" | custom-call | flops 1 | bytes 1 | tf_op jit(solution)/shard_map/attend/pallas_call | solution.py:239
  105.2 1.2 multiply.11
  107.3 1.6 %collective-permute-start.18 = (bf16[256,512]{1,0:T(8,128)(2,1)S(1)}, bf16[256,512]{1,0:T(8,128)(2,1)S(1)}, u32[]{:S(2)}, u32[]{:S(2)}) collective-permute-start(bf16[256,512]{1,0:T(8,128)(2,1)S(1)} %add_convert_fusion.7), channel_id=1, source_target_pairs={{0,65},{32,97},{64,1},{96,33},{1,64},{33,96},{65,0},{97,32},{2,67}... | collective-permute-start | bytes 786440 | tf_op jit(solution)/shard_map/ppermute | solution.py:55
  109.6 1.0 collective-permute-start.20
  110.6 1.2 multiply.12
  112.0 1.8 %collective-permute-start.22 = (bf16[256,512]{1,0:T(8,128)(2,1)S(1)}, bf16[256,512]{1,0:T(8,128)(2,1)S(1)}, u32[]{:S(2)}, u32[]{:S(2)}) collective-permute-start(bf16[256,512]{1,0:T(8,128)(2,1)S(1)} %add_convert_fusion.5), channel_id=1, source_target_pairs={{0,65},{32,97},{64,1},{96,33},{1,64},{33,96},{65,0},{97,32},{2,67}... | collective-permute-start | bytes 786440 | tf_op jit(solution)/shard_map/ppermute | solution.py:55
  113.8 2.2 %collective-permute-done.18 = bf16[256,512]{1,0:T(8,128)(2,1)S(1)} collective-permute-done((bf16[256,512]{1,0:T(8,128)(2,1)S(1)}, bf16[256,512]{1,0:T(8,128)(2,1)S(1)}, u32[]{:S(2)}, u32[]{:S(2)}) %collective-permute-start.18) | collective-permute-done | bytes 262176 | tf_op jit(solution)/shard_map/ppermute | solution.py:55
  116.0 2.1 %collective-permute-start.24 = (bf16[256,512]{1,0:T(8,128)(2,1)S(1)}, bf16[256,512]{1,0:T(8,128)(2,1)S(1)}, u32[]{:S(2)}, u32[]{:S(2)}) collective-permute-start(bf16[256,512]{1,0:T(8,128)(2,1)S(1)} %get-tuple-element.107), channel_id=1, source_target_pairs={{0,32},{32,0},{64,96},{96,64},{1,33},{33,1},{65,97},{97,65},{2,34}... | collective-permute-start | bytes 786440 | tf_op jit(solution)/shard_map/ppermute | solution.py:55
  118.2 1.2 multiply.13
  120.2 1.3 collective-permute-start.26
  121.8 1.8 %collective-permute-start.30 = (bf16[256,512]{1,0:T(8,128)(2,1)S(1)}, bf16[256,512]{1,0:T(8,128)(2,1)S(1)}, u32[]{:S(2)}, u32[]{:S(2)}) collective-permute-start(bf16[256,512]{1,0:T(8,128)(2,1)S(1)} %add_convert_fusion.1), channel_id=1, source_target_pairs={{0,65},{32,97},{64,1},{96,33},{1,64},{33,96},{65,0},{97,32},{2,67}... | collective-permute-start | bytes 786440 | tf_op jit(solution)/shard_map/ppermute | solution.py:55
  123.7 5.6 %collective-permute-done.26 = bf16[256,512]{1,0:T(8,128)(2,1)S(1)} collective-permute-done((bf16[256,512]{1,0:T(8,128)(2,1)S(1)}, bf16[256,512]{1,0:T(8,128)(2,1)S(1)}, u32[]{:S(2)}, u32[]{:S(2)}) %collective-permute-start.26) | collective-permute-done | bytes 262176 | tf_op jit(solution)/shard_map/ppermute | solution.py:55
  129.5 5.5 %collective-permute-done.30 = bf16[256,512]{1,0:T(8,128)(2,1)S(1)} collective-permute-done((bf16[256,512]{1,0:T(8,128)(2,1)S(1)}, bf16[256,512]{1,0:T(8,128)(2,1)S(1)}, u32[]{:S(2)}, u32[]{:S(2)}) %collective-permute-start.30) | collective-permute-done | bytes 262176 | tf_op jit(solution)/shard_map/ppermute | solution.py:55
  135.1 1.0 pad_maximum_fusion.1
  (86 shorter events, 13.0 us)
Async XLA Ops:
  5.4 19.1 %collective-permute-start.5 = (bf16[2064,128]{1,0:T(8,128)(2,1)S(1)}, bf16[2064,128]{1,0:T(8,128)(2,1)S(1)}, u32[]{:S(2)}, u32[]{:S(2)}) collective-permute-start(bf16[2064,128]{1,0:T(8,128)(2,1)S(1)} %get-tuple-element.72.refs_4_), channel_id=1, source_target_pairs={{0,2},{2,4},{4,6},{6,0},{8,10},{10,12},{12,14},{14,8},{16,18},{18,... | collective-permute-start | bytes 1585160 | tf_op jit(solution)/shard_map/ppermute | solution.py:43
  7.6 31.4 %collective-permute-start.4 = (bf16[2064,128]{1,0:T(8,128)(2,1)S(1)}, bf16[2064,128]{1,0:T(8,128)(2,1)S(1)}, u32[]{:S(2)}, u32[]{:S(2)}) collective-permute-start(bf16[2064,128]{1,0:T(8,128)(2,1)S(1)} %get-tuple-element.72.refs_4_), channel_id=1, source_target_pairs={{0,6},{2,0},{4,2},{6,4},{8,14},{10,8},{12,10},{14,12},{16,22},{18,... | collective-permute-start | bytes 1585160 | tf_op jit(solution)/shard_map/ppermute | solution.py:43
  9.1 17.0 %collective-permute-start.2 = (bf16[2064,128]{1,0:T(8,128)(2,1)S(1)}, bf16[2064,128]{1,0:T(8,128)(2,1)S(1)}, u32[]{:S(2)}, u32[]{:S(2)}) collective-permute-start(bf16[2064,128]{1,0:T(8,128)(2,1)S(1)} %get-tuple-element.70.refs_0_), channel_id=1, source_target_pairs={{0,8},{2,10},{4,12},{6,14},{8,16},{10,18},{12,20},{14,22},{16,24},... | collective-permute-start | bytes 1585160 | tf_op jit(solution)/shard_map/ppermute | solution.py:43
  10.3 28.6 %collective-permute-start.1 = (bf16[2064,128]{1,0:T(8,128)(2,1)S(1)}, bf16[2064,128]{1,0:T(8,128)(2,1)}, u32[]{:S(2)}, u32[]{:S(2)}) collective-permute-start(bf16[2064,128]{1,0:T(8,128)(2,1)S(1)} %get-tuple-element.70.refs_0_), channel_id=1, source_target_pairs={{0,24},{2,26},{4,28},{6,30},{8,0},{10,2},{12,4},{14,6},{16,8},{18,... | collective-permute-start | bytes 1585160 | tf_op jit(solution)/shard_map/ppermute | solution.py:43
  11.8 22.4 %copy-start.16 = (bf16[4096,512]{1,0:T(8,128)(2,1)S(1)}, bf16[4096,512]{1,0:T(8,128)(2,1)}, u32[]{:S(2)}) copy-start(bf16[4096,512]{1,0:T(8,128)(2,1)} %param.11) | copy-start | bytes 12582916
  11.8 22.4 %copy-start.17 = (f32[4096]{0:T(1024)S(1)}, f32[4096]{0:T(1024)}, u32[]{:S(2)}) copy-start(f32[4096]{0:T(1024)} %param.9) | copy-start | bytes 49156
  16.2 0.8 copy-start.5
  17.1 17.2 %copy-start.13 = (bf16[1024,4096]{1,0:T(8,128)(2,1)S(1)}, bf16[1024,4096]{1,0:T(8,128)(2,1)}, u32[]{:S(2)}) copy-start(bf16[1024,4096]{1,0:T(8,128)(2,1)} %param.8) | copy-start | bytes 25165828
  17.1 15.1 %collective-permute-start = (bf16[160,2048]{1,0:T(8,128)(2,1)S(1)}, bf16[160,2048]{1,0:T(8,128)(2,1)S(1)}, u32[]{:S(2)}, u32[]{:S(2)}) collective-permute-start(bf16[160,2048]{1,0:T(8,128)(2,1)S(1)} %get-tuple-element.67), channel_id=1, source_target_pairs={{0,64},{32,96},{64,0},{96,32},{1,65},{33,97},{65,1},{97,33},{2,66}... | collective-permute-start | bytes 1966088 | tf_op jit(solution)/shard_map/ppermute | solution.py:55
  24.5 14.4 %collective-permute-start.6 = (bf16[2064,128]{1,0:T(8,128)(2,1)S(1)}, bf16[2064,128]{1,0:T(8,128)(2,1)}, u32[]{:S(2)}, u32[]{:S(2)}) collective-permute-start(bf16[2064,128]{1,0:T(8,128)(2,1)S(1)} %get-tuple-element.72.refs_4_), channel_id=1, source_target_pairs={{0,4},{2,6},{4,0},{6,2},{8,12},{10,14},{12,8},{14,10},{16,20},{18,... | collective-permute-start | bytes 1585160 | tf_op jit(solution)/shard_map/ppermute | solution.py:43
  26.1 0.8 copy-start
  26.9 13.0 %collective-permute-start.3 = (bf16[2064,128]{1,0:T(8,128)(2,1)S(1)}, bf16[2064,128]{1,0:T(8,128)(2,1)}, u32[]{:S(2)}, u32[]{:S(2)}) collective-permute-start(bf16[2064,128]{1,0:T(8,128)(2,1)S(1)} %get-tuple-element.70.refs_0_), channel_id=1, source_target_pairs={{0,16},{2,18},{4,20},{6,22},{8,24},{10,26},{12,28},{14,30},{16,0},... | collective-permute-start | bytes 1585160 | tf_op jit(solution)/shard_map/ppermute | solution.py:43
  32.2 0.8 copy-start.14
  33.0 28.7 %collective-permute-start.12 = (bf16[192,2048]{1,0:T(8,128)(2,1)}, bf16[192,2048]{1,0:T(8,128)(2,1)}, u32[]{:S(2)}, u32[]{:S(2)}) collective-permute-start(bf16[192,2048]{1,0:T(8,128)(2,1)} %get-tuple-element.84), channel_id=1, source_target_pairs={{0,64},{32,96},{64,0},{96,32},{1,65},{33,97},{65,1},{97,33},{2,66}... | collective-permute-start | bytes 2359304 | tf_op jit(solution)/shard_map/ppermute | solution.py:55
  39.9 1.0 copy-start.1
  44.4 0.8 copy-start.2
  45.2 0.8 copy-start.3
  46.0 0.8 copy-start.7
  46.8 0.8 copy-start.9
  47.6 0.8 copy-start.10
  48.4 0.8 copy-start.11
  49.2 0.8 copy-start.12
  50.0 11.8 %collective-permute-start.11 = (bf16[2048,128]{1,0:T(8,128)(2,1)}, bf16[2048,128]{1,0:T(8,128)(2,1)S(1)}, u32[]{:S(2)}, u32[]{:S(2)}) collective-permute-start(bf16[2048,128]{1,0:T(8,128)(2,1)} %get-tuple-element.81), channel_id=1, source_target_pairs={{0,8},{2,10},{4,12},{6,14},{8,16},{10,18},{12,20},{14,22},{16,24},... | collective-permute-start | bytes 1572872 | tf_op jit(solution)/shard_map/ppermute | solution.py:43
  50.0 16.3 %collective-permute-start.8 = (bf16[2048,128]{1,0:T(8,128)(2,1)}, bf16[2048,128]{1,0:T(8,128)(2,1)S(1)}, u32[]{:S(2)}, u32[]{:S(2)}) collective-permute-start(bf16[2048,128]{1,0:T(8,128)(2,1)} %copy-done.12), channel_id=1, source_target_pairs={{0,2},{2,4},{4,6},{6,0},{8,10},{10,12},{12,14},{14,8},{16,18},{18,... | collective-permute-start | bytes 1572872 | tf_op jit(solution)/shard_map/ppermute | solution.py:43
  50.4 17.7 %collective-permute-start.10 = (bf16[2048,128]{1,0:T(8,128)(2,1)}, bf16[2048,128]{1,0:T(8,128)(2,1)S(1)}, u32[]{:S(2)}, u32[]{:S(2)}) collective-permute-start(bf16[2048,128]{1,0:T(8,128)(2,1)} %copy-done.11), channel_id=1, source_target_pairs={{0,24},{2,26},{4,28},{6,30},{8,0},{10,2},{12,4},{14,6},{16,8},{18,... | collective-permute-start | bytes 1572872 | tf_op jit(solution)/shard_map/ppermute | solution.py:43
  53.1 15.0 %collective-permute-start.7 = (bf16[2048,128]{1,0:T(8,128)(2,1)}, bf16[2048,128]{1,0:T(8,128)(2,1)S(1)}, u32[]{:S(2)}, u32[]{:S(2)}) collective-permute-start(bf16[2048,128]{1,0:T(8,128)(2,1)} %copy-done.10), channel_id=1, source_target_pairs={{0,6},{2,0},{4,2},{6,4},{8,14},{10,8},{12,10},{14,12},{16,22},{18,... | collective-permute-start | bytes 1572872 | tf_op jit(solution)/shard_map/ppermute | solution.py:43
  61.8 11.1 %collective-permute-start.13 = (bf16[2048,128]{1,0:T(8,128)(2,1)}, bf16[2048,128]{1,0:T(8,128)(2,1)S(1)}, u32[]{:S(2)}, u32[]{:S(2)}) collective-permute-start(bf16[2048,128]{1,0:T(8,128)(2,1)} %copy-done.9), channel_id=1, source_target_pairs={{0,16},{2,18},{4,20},{6,22},{8,24},{10,26},{12,28},{14,30},{16,0},... | collective-permute-start | bytes 1572872 | tf_op jit(solution)/shard_map/ppermute | solution.py:43
  63.2 3.0 %copy-start.6 = (bf16[160,2048]{1,0:T(8,128)(2,1)S(1)}, bf16[160,2048]{1,0:T(8,128)(2,1)}, u32[]{:S(2)}) copy-start(bf16[160,2048]{1,0:T(8,128)(2,1)} %copy-done.5) | copy-start | bytes 1966084
  63.2 3.2 %copy-start.8 = (bf16[2048,128]{1,0:T(8,128)(2,1)S(1)}, bf16[2048,128]{1,0:T(8,128)(2,1)}, u32[]{:S(2)}) copy-start(bf16[2048,128]{1,0:T(8,128)(2,1)} %copy-done.7) | copy-start | bytes 1572868
  66.2 18.6 %collective-permute-start.15 = (bf16[160,2048]{1,0:T(8,128)(2,1)S(1)}, bf16[160,2048]{1,0:T(8,128)(2,1)S(1)}, u32[]{:S(2)}, u32[]{:S(2)}) collective-permute-start(bf16[160,2048]{1,0:T(8,128)(2,1)S(1)} %copy-done.6), channel_id=1, source_target_pairs={{0,64},{32,96},{64,0},{96,32},{1,65},{33,97},{65,1},{97,33},{2,66}... | collective-permute-start | bytes 1966088 | tf_op jit(solution)/shard_map/ppermute | solution.py:55
  66.3 10.7 %collective-permute-start.9 = (bf16[2048,128]{1,0:T(8,128)(2,1)S(1)}, bf16[2048,128]{1,0:T(8,128)(2,1)S(1)}, u32[]{:S(2)}, u32[]{:S(2)}) collective-permute-start(bf16[2048,128]{1,0:T(8,128)(2,1)S(1)} %copy-done.8), channel_id=1, source_target_pairs={{0,4},{2,6},{4,0},{6,2},{8,12},{10,14},{12,8},{14,10},{16,20},{18,... | collective-permute-start | bytes 1572872 | tf_op jit(solution)/shard_map/ppermute | solution.py:43
  80.2 4.6 %copy-start.15 = (bf16[160,2048]{1,0:T(8,128)(2,1)S(1)}, bf16[160,2048]{1,0:T(8,128)(2,1)}, u32[]{:S(2)}) copy-start(bf16[160,2048]{1,0:T(8,128)(2,1)} %copy-done.14) | copy-start | bytes 1966084
  80.2 13.5 %collective-permute-start.14 = (bf16[256,512]{1,0:T(8,128)(2,1)S(1)}, bf16[256,512]{1,0:T(8,128)(2,1)S(1)}, u32[]{:S(2)}, u32[]{:S(2)}) collective-permute-start(bf16[256,512]{1,0:T(8,128)(2,1)S(1)} %attend.4.mine_ref), channel_id=1, source_target_pairs={{0,64},{32,96},{64,0},{96,32},{1,65},{33,97},{65,1},{97,33},{2,66}... | collective-permute-start | bytes 786440 | tf_op jit(solution)/shard_map/ppermute | solution.py:55
  84.3 20.8 %collective-permute-start.19 = (bf16[256,512]{1,0:T(8,128)(2,1)S(1)}, bf16[256,512]{1,0:T(8,128)(2,1)S(1)}, u32[]{:S(2)}, u32[]{:S(2)}) collective-permute-start(bf16[256,512]{1,0:T(8,128)(2,1)S(1)} %attend.5.mine_ref), channel_id=1, source_target_pairs={{0,64},{32,96},{64,0},{96,32},{1,65},{33,97},{65,1},{97,33},{2,66}... | collective-permute-start | bytes 786440 | tf_op jit(solution)/shard_map/ppermute | solution.py:55
  95.0 12.2 %collective-permute-start.17 = (bf16[256,512]{1,0:T(8,128)(2,1)S(1)}, bf16[256,512]{1,0:T(8,128)(2,1)S(1)}, u32[]{:S(2)}, u32[]{:S(2)}) collective-permute-start(bf16[256,512]{1,0:T(8,128)(2,1)S(1)} %get-tuple-element.95), channel_id=1, source_target_pairs={{0,32},{32,0},{64,96},{96,64},{1,33},{33,1},{65,97},{97,65},{2,34}... | collective-permute-start | bytes 786440 | tf_op jit(solution)/shard_map/ppermute | solution.py:55
  100.8 8.8 %collective-permute-start.23 = (bf16[256,512]{1,0:T(8,128)(2,1)S(1)}, bf16[256,512]{1,0:T(8,128)(2,1)S(1)}, u32[]{:S(2)}, u32[]{:S(2)}) collective-permute-start(bf16[256,512]{1,0:T(8,128)(2,1)S(1)} %attend.6.mine_ref), channel_id=1, source_target_pairs={{0,64},{32,96},{64,0},{96,32},{1,65},{33,97},{65,1},{97,33},{2,66}... | collective-permute-start | bytes 786440 | tf_op jit(solution)/shard_map/ppermute | solution.py:55
  106.4 5.4 %collective-permute-start.21 = (bf16[256,512]{1,0:T(8,128)(2,1)S(1)}, bf16[256,512]{1,0:T(8,128)(2,1)S(1)}, u32[]{:S(2)}, u32[]{:S(2)}) collective-permute-start(bf16[256,512]{1,0:T(8,128)(2,1)S(1)} %get-tuple-element.103), channel_id=1, source_target_pairs={{0,32},{32,0},{64,96},{96,64},{1,33},{33,1},{65,97},{97,65},{2,34}... | collective-permute-start | bytes 786440 | tf_op jit(solution)/shard_map/ppermute | solution.py:55
  107.1 4.9 %collective-permute-start.16 = (bf16[256,512]{1,0:T(8,128)(2,1)S(1)}, bf16[256,512]{1,0:T(8,128)(2,1)S(1)}, u32[]{:S(2)}, u32[]{:S(2)}) collective-permute-start(bf16[256,512]{1,0:T(8,128)(2,1)S(1)} %get-tuple-element.93), channel_id=1, source_target_pairs={{0,32},{32,0},{64,96},{96,64},{1,33},{33,1},{65,97},{97,65},{2,34}... | collective-permute-start | bytes 786440 | tf_op jit(solution)/shard_map/ppermute | solution.py:55
  107.3 8.8 %collective-permute-start.18 = (bf16[256,512]{1,0:T(8,128)(2,1)S(1)}, bf16[256,512]{1,0:T(8,128)(2,1)S(1)}, u32[]{:S(2)}, u32[]{:S(2)}) collective-permute-start(bf16[256,512]{1,0:T(8,128)(2,1)S(1)} %add_convert_fusion.7), channel_id=1, source_target_pairs={{0,65},{32,97},{64,1},{96,33},{1,64},{33,96},{65,0},{97,32},{2,67}... | collective-permute-start | bytes 786440 | tf_op jit(solution)/shard_map/ppermute | solution.py:55
  108.8 9.4 %collective-permute-start.27 = (bf16[256,512]{1,0:T(8,128)(2,1)S(1)}, bf16[256,512]{1,0:T(8,128)(2,1)S(1)}, u32[]{:S(2)}, u32[]{:S(2)}) collective-permute-start(bf16[256,512]{1,0:T(8,128)(2,1)S(1)} %attend.7.mine_ref), channel_id=1, source_target_pairs={{0,64},{32,96},{64,0},{96,32},{1,65},{33,97},{65,1},{97,33},{2,66}... | collective-permute-start | bytes 786440 | tf_op jit(solution)/shard_map/ppermute | solution.py:55
  109.6 10.6 %collective-permute-start.20 = (bf16[256,512]{1,0:T(8,128)(2,1)S(1)}, bf16[256,512]{1,0:T(8,128)(2,1)S(1)}, u32[]{:S(2)}, u32[]{:S(2)}) collective-permute-start(bf16[256,512]{1,0:T(8,128)(2,1)S(1)} %get-tuple-element.101), channel_id=1, source_target_pairs={{0,32},{32,0},{64,96},{96,64},{1,33},{33,1},{65,97},{97,65},{2,34}... | collective-permute-start | bytes 786440 | tf_op jit(solution)/shard_map/ppermute | solution.py:55
  111.8 7.8 %collective-permute-start.25 = (bf16[256,512]{1,0:T(8,128)(2,1)S(1)}, bf16[256,512]{1,0:T(8,128)(2,1)S(1)}, u32[]{:S(2)}, u32[]{:S(2)}) collective-permute-start(bf16[256,512]{1,0:T(8,128)(2,1)S(1)} %get-tuple-element.109), channel_id=1, source_target_pairs={{0,32},{32,0},{64,96},{96,64},{1,33},{33,1},{65,97},{97,65},{2,34}... | collective-permute-start | bytes 786440 | tf_op jit(solution)/shard_map/ppermute | solution.py:55
  112.0 9.6 %collective-permute-start.22 = (bf16[256,512]{1,0:T(8,128)(2,1)S(1)}, bf16[256,512]{1,0:T(8,128)(2,1)S(1)}, u32[]{:S(2)}, u32[]{:S(2)}) collective-permute-start(bf16[256,512]{1,0:T(8,128)(2,1)S(1)} %add_convert_fusion.5), channel_id=1, source_target_pairs={{0,65},{32,97},{64,1},{96,33},{1,64},{33,96},{65,0},{97,32},{2,67}... | collective-permute-start | bytes 786440 | tf_op jit(solution)/shard_map/ppermute | solution.py:55
  116.0 7.7 %collective-permute-start.24 = (bf16[256,512]{1,0:T(8,128)(2,1)S(1)}, bf16[256,512]{1,0:T(8,128)(2,1)S(1)}, u32[]{:S(2)}, u32[]{:S(2)}) collective-permute-start(bf16[256,512]{1,0:T(8,128)(2,1)S(1)} %get-tuple-element.107), channel_id=1, source_target_pairs={{0,32},{32,0},{64,96},{96,64},{1,33},{33,1},{65,97},{97,65},{2,34}... | collective-permute-start | bytes 786440 | tf_op jit(solution)/shard_map/ppermute | solution.py:55
  119.5 10.0 %collective-permute-start.28 = (bf16[256,512]{1,0:T(8,128)(2,1)S(1)}, bf16[256,512]{1,0:T(8,128)(2,1)S(1)}, u32[]{:S(2)}, u32[]{:S(2)}) collective-permute-start(bf16[256,512]{1,0:T(8,128)(2,1)S(1)} %get-tuple-element.115), channel_id=1, source_target_pairs={{0,32},{32,0},{64,96},{96,64},{1,33},{33,1},{65,97},{97,65},{2,34}... | collective-permute-start | bytes 786440 | tf_op jit(solution)/shard_map/ppermute | solution.py:55
  119.6 2.2 %collective-permute-start.29 = (bf16[256,512]{1,0:T(8,128)(2,1)S(1)}, bf16[256,512]{1,0:T(8,128)(2,1)S(1)}, u32[]{:S(2)}, u32[]{:S(2)}) collective-permute-start(bf16[256,512]{1,0:T(8,128)(2,1)S(1)} %get-tuple-element.117), channel_id=1, source_target_pairs={{0,32},{32,0},{64,96},{96,64},{1,33},{33,1},{65,97},{97,65},{2,34}... | collective-permute-start | bytes 786440 | tf_op jit(solution)/shard_map/ppermute | solution.py:55
  120.2 9.2 %collective-permute-start.26 = (bf16[256,512]{1,0:T(8,128)(2,1)S(1)}, bf16[256,512]{1,0:T(8,128)(2,1)S(1)}, u32[]{:S(2)}, u32[]{:S(2)}) collective-permute-start(bf16[256,512]{1,0:T(8,128)(2,1)S(1)} %add_convert_fusion.3), channel_id=1, source_target_pairs={{0,65},{32,97},{64,1},{96,33},{1,64},{33,96},{65,0},{97,32},{2,67}... | collective-permute-start | bytes 786440 | tf_op jit(solution)/shard_map/ppermute | solution.py:55
  121.8 13.1 %collective-permute-start.30 = (bf16[256,512]{1,0:T(8,128)(2,1)S(1)}, bf16[256,512]{1,0:T(8,128)(2,1)S(1)}, u32[]{:S(2)}, u32[]{:S(2)}) collective-permute-start(bf16[256,512]{1,0:T(8,128)(2,1)S(1)} %add_convert_fusion.1), channel_id=1, source_target_pairs={{0,65},{32,97},{64,1},{96,33},{1,64},{33,96},{65,0},{97,32},{2,67}... | collective-permute-start | bytes 786440 | tf_op jit(solution)/shard_map/ppermute | solution.py:55
  (1 other events, 0.7 us)

commit v5 on v4

--- a/solution.py
+++ b/solution.py
@@ -19,12 +19,10 @@
 PICKS = SIDE * SIDE * CAP
 NOTE_ROWS = 16
 EPSILON = 1e-05
-NEAR_PIECES = (160, 192, 160)
+NEAR_PIECES = (64, 160, 160, 128)
 CHUNKS = (2, 2, 2, 2)
 AHEAD = 3
 LAG = 2
-FIN = 3
-GOT = 2
 SCALE = HEAD_DIM**-0.5
 LOG2_E = 1.4426950408889634
 
@@ -296,10 +294,31 @@
     )(mine, near, weight)
 
 
-def rms_normed(text_hidden, norm_gain):
-    as_float = text_hidden.astype(jnp.float32)
-    inverse = lax.rsqrt(jnp.mean(as_float * as_float, axis=-1, keepdims=True) + EPSILON)
-    return (as_float * inverse * norm_gain).astype(jnp.bfloat16)
+def ask_body(x_ref, gain_ref, w_ref, o_ref):
+    as_float = x_ref[...].astype(jnp.float32)
+    mean = jnp.mean(as_float * as_float, axis=-1, keepdims=True)
+    normed = (as_float * lax.rsqrt(mean + EPSILON) * gain_ref[...]).astype(jnp.bfloat16)
+    product = jnp.dot(normed, w_ref[...], preferred_element_type=jnp.float32)
+    o_ref[...] = product.astype(jnp.bfloat16)
+
+
+def queries_of(text_hidden, norm_gain, query_weight):
+    (rows, depth), width = text_hidden.shape, query_weight.shape[1]
+    steps = 4
+    return pl.pallas_call(
+        ask_body,
+        grid=(steps,),
+        in_specs=[
+            pl.BlockSpec((rows // steps, depth), lambda i: (i, 0)),
+            pl.BlockSpec((1, depth), lambda i: (0, 0)),
+            pl.BlockSpec((depth, width), lambda i: (0, 0)),
+        ],
+        out_specs=pl.BlockSpec((rows // steps, width), lambda i: (i, 0)),
+        out_shape=jax.ShapeDtypeStruct((rows, width), jnp.bfloat16),
+        compiler_params=pltpu.CompilerParams(vmem_limit_bytes=32 << 20),
+        cost_estimate=SMALL,
+        name="ask",
+    )(in_hbm(text_hidden), norm_gain.reshape(1, depth), in_hbm(query_weight))
 
 
 def after(value, other):
@@ -345,15 +364,13 @@
 
     k_own, v_own, slots = project(image_features, key_weight, value_weight, selected)
     pieces = pick(wanted_columns(z ^ 1), after(output_weight, k_own), NEAR_PIECES)
+    k_ring = spread(k_own, 1, 0, lambda part: after(part, pieces[0]))
+    v_ring = spread(v_own, 0, 1)
     near_weight = []
     for piece in pieces:
-        hold = near_weight[-1] if near_weight else text_hidden
-        near_weight.append(to_near(after(piece, hold)))
-    k_ring = spread(k_own, 1, 0)
-    v_ring = spread(v_own, 0, 1)
-
-    normed = rms_normed(after(text_hidden, k_own), norm_gain)
-    queries = jnp.dot(normed, query_weight, preferred_element_type=jnp.float32).astype(jnp.bfloat16)
+        near_weight.append(to_near(after(piece, near_weight[-1] if near_weight else k_ring[3])))
+
+    queries = queries_of(after(text_hidden, k_own), norm_gain, query_weight)
 
     k_out, v_out = pack(after(after(place, near_weight[0]), queries), k_ring, v_ring)
     keys = exchange(k_out, 0, 1)
@@ -380,16 +397,16 @@
     for index in range(len(CHUNKS)):
         if index >= LAG:
             weight = after(weight, sent[index - LAG])
-        if FIN and index >= FIN:
-            weight = after(weight, outs[index - FIN])
+        if index >= 3:
+            weight = after(weight, outs[index - 3])
         give_far, give_own, keep_far, keep_own = multiply(mine[index], near[index], weight)
         weight = after(weight, give_far)
         if len(mine) < len(CHUNKS):
             slots = attended(after(slots, give_far))
             weight = after(weight, mine[-1])
         got_far, got_own = to_core(give_far), to_core(give_own)
-        if GOT and index >= GOT:
-            got_far = after(got_far, outs[index - GOT])
+        if index >= 2 and index == last:
+            got_far = after(got_far, outs[index - 2])
         send = (keep_far + got_far.astype(jnp.float32)).astype(jnp.bfloat16)
         far = to_far(send)
         sent.append(send)

time: 137 us -> 124 us (0.905)
  other arithmetic: 13.7 us -> 2.04 us
  Pallas kernels: 32.4 us -> 40.2 us
  local copies, waits for them, and re-layouts: 12.4 us -> 5.04 us
  matrix products: 4.57 us -> 0 us
  waiting for transfers between devices: 32.1 us -> 35.1 us
    ppermute x19 -> x20, waiting for transfers between devices: 17.3 us -> 29 us  [along_z(): return lax.ppermute(value, SECTION_HEAD, pairs)]
    pallas_call x0 -> x1, Pallas kernels: none -> 9.63 us  [queries_of(): pl.pallas_call(ask_body, grid=(steps,), in_specs=[pl.BlockSpec((rows // s...]
    ppermute x12, waiting for transfers between devices: 14.9 us -> 6.12 us  [along_seq(): return lax.ppermute(value, 'seq', pairs)]
    unnamed x42 -> x24, local copies, waits for them, and re-layouts: 12.2 us -> 4.86 us
    concatenate x1 -> x0, other arithmetic: 5.92 us -> none  [shards(): weight = jnp.concatenate([*own_weight, *near_weight])]
    reduce_sum x1 -> x0, other arithmetic: 5.74 us -> none  [rms_normed(): jnp.mean(as_float * as_float, axis=-1, keepdims=True) + EPSILON]
    dot_general x1 -> x0, matrix products: 4.57 us -> none  [shards(): jnp.dot(normed, query_weight, preferred_element_type=jnp.float32)]
    ppermute x12, starting transfers between devices: 17 us -> 15.3 us  [along_seq(): return lax.ppermute(value, 'seq', pairs)]
  transfers between devices with their start and end apart: 31 -> 32, of which waited for: 9 -> 9; matrix products, arithmetic and copies ran while one was open for 14% -> 2% of each run, Pallas kernels for 20% -> 29%
where the time goes in v5:
time: 124 us; the launch traced here: 123 us
  starting transfers between devices  40.5 us (33%)
  Pallas kernels  40.2 us (32%)
  waiting for transfers between devices  35.1 us (28%)
  local copies, waits for them, and re-layouts  5.04 us (4%)
  other arithmetic  2.04 us (2%)
    ppermute x20, waiting for transfers between devices, along_z(): return lax.ppermute(value, SECTION_HEAD, pairs)  29 us
    ppermute x20, starting transfers between devices, along_z(): return lax.ppermute(value, SECTION_HEAD, pairs)  25.1 us
    ppermute x12, starting transfers between devices, along_seq(): return lax.ppermute(value, 'seq', pairs)  15.3 us
    pallas_call x4, Pallas kernels, attend(): pl.pallas_call(functools.partial(attend_body, first_tile), in_specs=[SMEM...  11.9 us
    pallas_call x1, Pallas kernels, queries_of(): pl.pallas_call(ask_body, grid=(steps,), in_specs=[pl.BlockSpec((rows // s...  9.63 us
    ppermute x12, waiting for transfers between devices, along_seq(): return lax.ppermute(value, 'seq', pairs)  6.12 us
    pallas_call x2, Pallas kernels, pick(): pl.pallas_call(pick_body, grid_spec=pltpu.PrefetchScalarGridSpec(num_scal...  6.04 us
    pallas_call x4, Pallas kernels, multiply(): pl.pallas_call(multiply_body, in_specs=[VMEM_WHOLE] * 3, out_specs=[VMEM_...  5.19 us
  transfers between devices with their start and end apart: 32, of which 9 were waited for; matrix products, arithmetic and copies ran while one was open for 2% of the time, Pallas kernels for 29%

profile of v5, /device:TPU:1, one launch (start us, length us, event | category | flops | bytes accessed | tf_op | source)
XLA Modules:
  0.0 123.4 jit_solution(962225972943070965)
XLA Ops:
  0.0 0.7 copy-done.1
  0.7 4.7 %project.1 = (bf16[2064,128]{1,0:T(8,128)(2,1)S(1)}, bf16[2064,128]{1,0:T(8,128)(2,1)S(1)}, s32[8,128]{1,0:T(8,128)S(1)}) custom-call(s32[8,16]{1,0:T(8,128)S(1)} %copy-done.1, bf16[2048,1024]{1,0:T(8,128)(2,1)} %x_ref.1, bf16[1024,128]{1,0:T(8,128)(2,1)} %wk_ref.1, bf16[1024,128]{1,0:T(8,128)(2,1)} %wv_ref.1), custom_call_target="tpu_custom_call" | custom-call | flops 1 | bytes 1 | tf_op jit(solution)/shard_map/project/pallas_call | solution.py:135
  5.4 2.2 %collective-permute-start.5 = (bf16[2064,128]{1,0:T(8,128)(2,1)S(1)}, bf16[2064,128]{1,0:T(8,128)(2,1)S(1)}, u32[]{:S(2)}, u32[]{:S(2)}) collective-permute-start(bf16[2064,128]{1,0:T(8,128)(2,1)S(1)} %get-tuple-element.75.refs_4_), channel_id=1, source_target_pairs={{0,2},{2,4},{4,6},{6,0},{8,10},{10,12},{12,14},{14,8},{16,18},{18,... | collective-permute-start | bytes 1585160 | tf_op jit(solution)/shard_map/ppermute | solution.py:41
  7.6 1.2 collective-permute-start
  8.8 1.5 %collective-permute-start.4 = (bf16[2064,128]{1,0:T(8,128)(2,1)S(1)}, bf16[2064,128]{1,0:T(8,128)(2,1)}, u32[]{:S(2)}, u32[]{:S(2)}) collective-permute-start(bf16[2064,128]{1,0:T(8,128)(2,1)S(1)} %get-tuple-element.75.refs_4_), channel_id=1, source_target_pairs={{0,6},{2,0},{4,2},{6,4},{8,14},{10,8},{12,10},{14,12},{16,22},{18,... | collective-permute-start | bytes 1585160 | tf_op jit(solution)/shard_map/ppermute | solution.py:41
  10.3 1.5 %collective-permute-start.2 = (bf16[2064,128]{1,0:T(8,128)(2,1)S(1)}, bf16[2064,128]{1,0:T(8,128)(2,1)}, u32[]{:S(2)}, u32[]{:S(2)}) collective-permute-start(bf16[2064,128]{1,0:T(8,128)(2,1)S(1)} %get-tuple-element.73.refs_0_), channel_id=1, source_target_pairs={{0,24},{2,26},{4,28},{6,30},{8,0},{10,2},{12,4},{14,6},{16,8},{18,... | collective-permute-start | bytes 1585160 | tf_op jit(solution)/shard_map/ppermute | solution.py:41
  11.8 3.0 %pick.2 = (bf16[64,2048]{1,0:T(8,128)(2,1)S(1)}, bf16[160,2048]{1,0:T(8,128)(2,1)S(1)}, bf16[160,2048]{1,0:T(8,128)(2,1)S(1)}, bf16[128,2048]{1,0:T(8,128)(2,1)S(1)}) custom-call(s32[4]{0:T(128)S(1)} %pad_add_fusion.1.places_ref, bf16[512,4096]{1,0:T(8,128)(2,1)} %w_ref.3), custom_call_target="tpu_custom_call" | custom-call | flops 1 | bytes 1 | tf_op jit(solution)/shard_map/pick/pallas_call | solution.py:258
  14.9 0.8 copy-done.2
  15.7 0.8 copy-done.4
  16.5 0.8 copy-done.5
  17.3 3.3 %collective-permute-done.5.refs_7_ = bf16[2064,128]{1,0:T(8,128)(2,1)S(1)} collective-permute-done((bf16[2064,128]{1,0:T(8,128)(2,1)S(1)}, bf16[2064,128]{1,0:T(8,128)(2,1)S(1)}, u32[]{:S(2)}, u32[]{:S(2)}) %collective-permute-start.5) | collective-permute-done | bytes 528416 | tf_op jit(solution)/shard_map/ppermute | solution.py:41
  20.6 1.6 %collective-permute-start.6 = (bf16[2064,128]{1,0:T(8,128)(2,1)S(1)}, bf16[2064,128]{1,0:T(8,128)(2,1)}, u32[]{:S(2)}, u32[]{:S(2)}) collective-permute-start(bf16[2064,128]{1,0:T(8,128)(2,1)S(1)} %get-tuple-element.75.refs_4_), channel_id=1, source_target_pairs={{0,4},{2,6},{4,0},{6,2},{8,12},{10,14},{12,8},{14,10},{16,20},{18,... | collective-permute-start | bytes 1585160 | tf_op jit(solution)/shard_map/ppermute | solution.py:41
  22.2 2.7 %collective-permute-start.3 = (bf16[2064,128]{1,0:T(8,128)(2,1)S(1)}, bf16[2064,128]{1,0:T(8,128)(2,1)}, u32[]{:S(2)}, u32[]{:S(2)}) collective-permute-start(bf16[2064,128]{1,0:T(8,128)(2,1)S(1)} %get-tuple-element.73.refs_0_), channel_id=1, source_target_pairs={{0,16},{2,18},{4,20},{6,22},{8,24},{10,26},{12,28},{14,30},{16,0},... | collective-permute-start | bytes 1585160 | tf_op jit(solution)/shard_map/ppermute | solution.py:41
  24.9 1.6 %collective-permute-start.1 = (bf16[64,2048]{1,0:T(8,128)(2,1)S(1)}, bf16[64,2048]{1,0:T(8,128)(2,1)}, u32[]{:S(2)}, u32[]{:S(2)}) collective-permute-start(bf16[64,2048]{1,0:T(8,128)(2,1)S(1)} %get-tuple-element.69), channel_id=1, source_target_pairs={{0,64},{32,96},{64,0},{96,32},{1,65},{33,97},{65,1},{97,33},{2,66}... | collective-permute-start | bytes 786440 | tf_op jit(solution)/shard_map/ppermute | solution.py:53
  26.6 9.6 %ask.1.q_ref = bf16[1024,512]{1,0:T(8,128)(2,1)S(1)} custom-call(bf16[1024,4096]{1,0:T(8,128)(2,1)} %x_ref.2, f32[1,4096]{1,0:T(1,128)S(1)} %bitcast.11, bf16[4096,512]{1,0:T(8,128)(2,1)} %w_ref.1), custom_call_target="tpu_custom_call" | custom-call | flops 1 | bytes 1 | tf_op jit(solution)/shard_map/ask/pallas_call | solution.py:308
  36.5 2.8 %pack.1 = (bf16[2048,128]{1,0:T(8,128)(2,1)S(1)}, bf16[2048,128]{1,0:T(8,128)(2,1)S(1)}, bf16[2048,128]{1,0:T(8,128)(2,1)S(1)}, bf16[2048,128]{1,0:T(8,128)(2,1)...) custom-call(s32[2]{0:T(128)S(1)} %pad_add_fusion.place_ref, ...), custom_call_target="tpu_custom_call" | custom-call | flops 1 | bytes 1 | tf_op jit(solution)/shard_map/pack/pallas_call | solution.py:187
  39.4 0.8 collective-permute-start.7
  40.2 0.7 collective-permute-start.8
  40.9 1.5 %collective-permute-start.10 = (bf16[2048,128]{1,0:T(8,128)(2,1)S(1)}, bf16[2048,128]{1,0:T(8,128)(2,1)S(1)}, u32[]{:S(2)}, u32[]{:S(2)}) collective-permute-start(bf16[2048,128]{1,0:T(8,128)(2,1)S(1)} %get-tuple-element.82), channel_id=1, source_target_pairs={{0,24},{2,26},{4,28},{6,30},{8,0},{10,2},{12,4},{14,6},{16,8},{18,... | collective-permute-start | bytes 1572872 | tf_op jit(solution)/shard_map/ppermute | solution.py:41
  42.4 3.0 %pick.3 = bf16[512,2048]{1,0:T(8,128)(2,1)S(1)} custom-call(s32[4]{0:T(128)S(1)} %pad_add_fusion.2.places_ref, bf16[512,4096]{1,0:T(8,128)(2,1)} %w_ref.3), custom_call_target="tpu_custom_call" | custom-call | flops 1 | bytes 1 | tf_op jit(solution)/shard_map/pick/pallas_call | solution.py:258
  45.8 1.0 constant_dynamic-update-slice_fusion.11
  46.8 3.8 %collective-permute-done.12 = bf16[160,2048]{1,0:T(8,128)(2,1)S(1)} collective-permute-done((bf16[160,2048]{1,0:T(8,128)(2,1)}, bf16[160,2048]{1,0:T(8,128)(2,1)S(1)}, u32[]{:S(2)}, u32[]{:S(2)}) %collective-permute-start.12) | collective-permute-done | bytes 655392 | tf_op jit(solution)/shard_map/ppermute | solution.py:53
  50.8 2.8 %collective-permute-done.11 = bf16[2048,128]{1,0:T(8,128)(2,1)S(1)} collective-permute-done((bf16[2048,128]{1,0:T(8,128)(2,1)S(1)}, bf16[2048,128]{1,0:T(8,128)(2,1)S(1)}, u32[]{:S(2)}, u32[]{:S(2)}) %collective-permute-start.11) | collective-permute-done | bytes 524320 | tf_op jit(solution)/shard_map/ppermute | solution.py:41
  53.7 1.6 %collective-permute-start.9 = (bf16[2048,128]{1,0:T(8,128)(2,1)S(1)}, bf16[2048,128]{1,0:T(8,128)(2,1)S(1)}, u32[]{:S(2)}, u32[]{:S(2)}) collective-permute-start(bf16[2048,128]{1,0:T(8,128)(2,1)S(1)} %get-tuple-element.80), channel_id=1, source_target_pairs={{0,4},{2,6},{4,0},{6,2},{8,12},{10,14},{12,8},{14,10},{16,20},{18,... | collective-permute-start | bytes 1572872 | tf_op jit(solution)/shard_map/ppermute | solution.py:41
  55.4 8.4 %collective-permute-done.15 = bf16[160,2048]{1,0:T(8,128)(2,1)S(1)} collective-permute-done((bf16[160,2048]{1,0:T(8,128)(2,1)S(1)}, bf16[160,2048]{1,0:T(8,128)(2,1)S(1)}, u32[]{:S(2)}, u32[]{:S(2)}) %collective-permute-start.15) | collective-permute-done | bytes 655392 | tf_op jit(solution)/shard_map/ppermute | solution.py:53
  64.4 3.0 %attend.4.mine_ref = bf16[256,512]{1,0:T(8,128)(2,1)S(1)} custom-call(s32[8,128]{1,0:T(8,128)S(1)} %get-tuple-element.103.slots_ref, s32[2]{0:T(128)S(1)} %pad_add_fusion.place_ref, bf16[1024,512]{1,0:T(8,128)(2,1)S(1)} %ask.1.q_ref, bf16[8192,128]{1,0:T(8,128)(2,1)S(1)} %constant_dynamic-update-slice_fusion.k_ref, ...), custom_call_target="tpu_custom_call" | custom-call | flops 1 | bytes 1 | tf_op jit(solution)/shard_map/attend/pallas_call | solution.py:237
  67.4 1.9 %collective-permute-start.14 = (bf16[256,512]{1,0:T(8,128)(2,1)S(1)}, bf16[256,512]{1,0:T(8,128)(2,1)S(1)}, u32[]{:S(2)}, u32[]{:S(2)}) collective-permute-start(bf16[256,512]{1,0:T(8,128)(2,1)S(1)} %attend.4.mine_ref), channel_id=1, source_target_pairs={{0,64},{32,96},{64,0},{96,32},{1,65},{33,97},{65,1},{97,33},{2,66}... | collective-permute-start | bytes 786440 | tf_op jit(solution)/shard_map/ppermute | solution.py:53
  69.3 3.0 %attend.5.mine_ref = bf16[256,512]{1,0:T(8,128)(2,1)S(1)} custom-call(s32[8,128]{1,0:T(8,128)S(1)} %get-tuple-element.103.slots_ref, s32[2]{0:T(128)S(1)} %pad_add_fusion.place_ref, bf16[1024,512]{1,0:T(8,128)(2,1)S(1)} %ask.1.q_ref, bf16[8192,128]{1,0:T(8,128)(2,1)S(1)} %constant_dynamic-update-slice_fusion.k_ref, ...), custom_call_target="tpu_custom_call" | custom-call | flops 1 | bytes 1 | tf_op jit(solution)/shard_map/attend/pallas_call | solution.py:237
  72.4 3.0 %attend.6.mine_ref = bf16[256,512]{1,0:T(8,128)(2,1)S(1)} custom-call(s32[8,128]{1,0:T(8,128)S(1)} %get-tuple-element.103.slots_ref, s32[2]{0:T(128)S(1)} %pad_add_fusion.place_ref, bf16[1024,512]{1,0:T(8,128)(2,1)S(1)} %ask.1.q_ref, bf16[8192,128]{1,0:T(8,128)(2,1)S(1)} %constant_dynamic-update-slice_fusion.k_ref, ...), custom_call_target="tpu_custom_call" | custom-call | flops 1 | bytes 1 | tf_op jit(solution)/shard_map/attend/pallas_call | solution.py:237
  75.4 4.4 %collective-permute-done.14.near_ref = bf16[256,512]{1,0:T(8,128)(2,1)S(1)} collective-permute-done((bf16[256,512]{1,0:T(8,128)(2,1)S(1)}, bf16[256,512]{1,0:T(8,128)(2,1)S(1)}, u32[]{:S(2)}, u32[]{:S(2)}) %collective-permute-start.14) | collective-permute-done | bytes 262176 | tf_op jit(solution)/shard_map/ppermute | solution.py:53
  79.8 1.3 %multiply.4 = (bf16[256,512]{1,0:T(8,128)(2,1)S(1)}, bf16[256,512]{1,0:T(8,128)(2,1)S(1)}, f32[256,512]{1,0:T(8,128)S(1)}, f32[256,512]{1,0:T(8,128)S(1)}) custom-call(bf16[256,512]{1,0:T(8,128)(2,1)S(1)} %attend.4.mine_ref, bf16[256,512]{1,0:T(8,128)(2,1)S(1)} %collective-permute-done.14.near_ref, ...), custom_call_target="tpu_custom_call" | custom-call | flops 1 | bytes 1 | tf_op jit(solution)/shard_map/multiply/pallas_call | solution.py:286
  81.1 7.8 %collective-permute-start.18 = (bf16[256,512]{1,0:T(8,128)(2,1)S(1)}, bf16[256,512]{1,0:T(8,128)(2,1)S(1)}, u32[]{:S(2)}, u32[]{:S(2)}) collective-permute-start(bf16[256,512]{1,0:T(8,128)(2,1)S(1)} %get-tuple-element.100), channel_id=1, source_target_pairs={{0,32},{32,0},{64,96},{96,64},{1,33},{33,1},{65,97},{97,65},{2,34}... | collective-permute-start | bytes 786440 | tf_op jit(solution)/shard_map/ppermute | solution.py:53
  89.0 3.0 %attend.7.mine_ref = bf16[256,512]{1,0:T(8,128)(2,1)S(1)} custom-call(s32[8,128]{1,0:T(8,128)S(1)} %get-tuple-element.103.slots_ref, s32[2]{0:T(128)S(1)} %pad_add_fusion.place_ref, bf16[1024,512]{1,0:T(8,128)(2,1)S(1)} %ask.1.q_ref, bf16[8192,128]{1,0:T(8,128)(2,1)S(1)} %constant_dynamic-update-slice_fusion.k_ref, ...), custom_call_target="tpu_custom_call" | custom-call | flops 1 | bytes 1 | tf_op jit(solution)/shard_map/attend/pallas_call | solution.py:237
  92.0 1.3 %multiply.5 = (bf16[256,512]{1,0:T(8,128)(2,1)S(1)}, bf16[256,512]{1,0:T(8,128)(2,1)S(1)}, f32[256,512]{1,0:T(8,128)S(1)}, f32[256,512]{1,0:T(8,128)S(1)}) custom-call(bf16[256,512]{1,0:T(8,128)(2,1)S(1)} %attend.5.mine_ref, bf16[256,512]{1,0:T(8,128)(2,1)S(1)} %collective-permute-done.20.near_ref, ...), custom_call_target="tpu_custom_call" | custom-call | flops 1 | bytes 1 | tf_op jit(solution)/shard_map/multiply/pallas_call | solution.py:286
  93.3 0.4 collective-permute-start.22
  94.0 3.6 %collective-permute-start.19 = (bf16[256,512]{1,0:T(8,128)(2,1)S(1)}, bf16[256,512]{1,0:T(8,128)(2,1)S(1)}, u32[]{:S(2)}, u32[]{:S(2)}) collective-permute-start(bf16[256,512]{1,0:T(8,128)(2,1)S(1)} %add_convert_fusion.7), channel_id=1, source_target_pairs={{0,65},{32,97},{64,1},{96,33},{1,64},{33,96},{65,0},{97,32},{2,67}... | collective-permute-start | bytes 786440 | tf_op jit(solution)/shard_map/ppermute | solution.py:53
  97.6 0.6 collective-permute-start.21
  98.2 1.3 %multiply.6 = (bf16[256,512]{1,0:T(8,128)(2,1)S(1)}, bf16[256,512]{1,0:T(8,128)(2,1)S(1)}, f32[256,512]{1,0:T(8,128)S(1)}, f32[256,512]{1,0:T(8,128)S(1)}) custom-call(bf16[256,512]{1,0:T(8,128)(2,1)S(1)} %attend.6.mine_ref, bf16[256,512]{1,0:T(8,128)(2,1)S(1)} %collective-permute-done.24.near_ref, ...), custom_call_target="tpu_custom_call" | custom-call | flops 1 | bytes 1 | tf_op jit(solution)/shard_map/multiply/pallas_call | solution.py:286
  99.7 1.8 %collective-permute-start.23 = (bf16[256,512]{1,0:T(8,128)(2,1)S(1)}, bf16[256,512]{1,0:T(8,128)(2,1)S(1)}, u32[]{:S(2)}, u32[]{:S(2)}) collective-permute-start(bf16[256,512]{1,0:T(8,128)(2,1)S(1)} %add_convert_fusion.5), channel_id=1, source_target_pairs={{0,65},{32,97},{64,1},{96,33},{1,64},{33,96},{65,0},{97,32},{2,67}... | collective-permute-start | bytes 786440 | tf_op jit(solution)/shard_map/ppermute | solution.py:53
  101.5 2.5 %collective-permute-done.19 = bf16[256,512]{1,0:T(8,128)(2,1)S(1)} collective-permute-done((bf16[256,512]{1,0:T(8,128)(2,1)S(1)}, bf16[256,512]{1,0:T(8,128)(2,1)S(1)}, u32[]{:S(2)}, u32[]{:S(2)}) %collective-permute-start.19) | collective-permute-done | bytes 262176 | tf_op jit(solution)/shard_map/ppermute | solution.py:53
  104.0 1.3 %collective-permute-start.25 = (bf16[256,512]{1,0:T(8,128)(2,1)S(1)}, bf16[256,512]{1,0:T(8,128)(2,1)S(1)}, u32[]{:S(2)}, u32[]{:S(2)}) collective-permute-start(bf16[256,512]{1,0:T(8,128)(2,1)S(1)} %get-tuple-element.112), channel_id=1, source_target_pairs={{0,32},{32,0},{64,96},{96,64},{1,33},{33,1},{65,97},{97,65},{2,34}... | collective-permute-start | bytes 786440 | tf_op jit(solution)/shard_map/ppermute | solution.py:53
  105.4 1.3 %multiply.7 = (bf16[256,512]{1,0:T(8,128)(2,1)S(1)}, bf16[256,512]{1,0:T(8,128)(2,1)S(1)}, f32[256,512]{1,0:T(8,128)S(1)}, f32[256,512]{1,0:T(8,128)S(1)}) custom-call(bf16[256,512]{1,0:T(8,128)(2,1)S(1)} %attend.7.mine_ref, bf16[256,512]{1,0:T(8,128)(2,1)S(1)} %collective-permute-done.28.near_ref, ...), custom_call_target="tpu_custom_call" | custom-call | flops 1 | bytes 1 | tf_op jit(solution)/shard_map/multiply/pallas_call | solution.py:286
  106.7 0.9 collective-permute-start.29
  107.9 2.6 %collective-permute-start.27 = (bf16[256,512]{1,0:T(8,128)(2,1)S(1)}, bf16[256,512]{1,0:T(8,128)(2,1)S(1)}, u32[]{:S(2)}, u32[]{:S(2)}) collective-permute-start(bf16[256,512]{1,0:T(8,128)(2,1)S(1)} %add_convert_fusion.3), channel_id=1, source_target_pairs={{0,65},{32,97},{64,1},{96,33},{1,64},{33,96},{65,0},{97,32},{2,67}... | collective-permute-start | bytes 786440 | tf_op jit(solution)/shard_map/ppermute | solution.py:53
  110.7 1.5 %collective-permute-start.31 = (bf16[256,512]{1,0:T(8,128)(2,1)S(1)}, bf16[256,512]{1,0:T(8,128)(2,1)S(1)}, u32[]{:S(2)}, u32[]{:S(2)}) collective-permute-start(bf16[256,512]{1,0:T(8,128)(2,1)S(1)} %add_convert_fusion.1), channel_id=1, source_target_pairs={{0,65},{32,97},{64,1},{96,33},{1,64},{33,96},{65,0},{97,32},{2,67}... | collective-permute-start | bytes 786440 | tf_op jit(solution)/shard_map/ppermute | solution.py:53
  112.2 4.4 %collective-permute-done.27 = bf16[256,512]{1,0:T(8,128)(2,1)S(1)} collective-permute-done((bf16[256,512]{1,0:T(8,128)(2,1)S(1)}, bf16[256,512]{1,0:T(8,128)(2,1)S(1)}, u32[]{:S(2)}, u32[]{:S(2)}) %collective-permute-start.27) | collective-permute-done | bytes 262176 | tf_op jit(solution)/shard_map/ppermute | solution.py:53
  116.8 5.5 %collective-permute-done.31 = bf16[256,512]{1,0:T(8,128)(2,1)S(1)} collective-permute-done((bf16[256,512]{1,0:T(8,128)(2,1)S(1)}, bf16[256,512]{1,0:T(8,128)(2,1)S(1)}, u32[]{:S(2)}, u32[]{:S(2)}) %collective-permute-start.31) | collective-permute-done | bytes 262176 | tf_op jit(solution)/shard_map/ppermute | solution.py:53
  122.4 1.0 pad_maximum_fusion
  (68 shorter events, 3.0 us)
Async XLA Ops:
  0.0 0.7 copy-start.1
  5.4 15.2 %collective-permute-start.5 = (bf16[2064,128]{1,0:T(8,128)(2,1)S(1)}, bf16[2064,128]{1,0:T(8,128)(2,1)S(1)}, u32[]{:S(2)}, u32[]{:S(2)}) collective-permute-start(bf16[2064,128]{1,0:T(8,128)(2,1)S(1)} %get-tuple-element.75.refs_4_), channel_id=1, source_target_pairs={{0,2},{2,4},{4,6},{6,0},{8,10},{10,12},{12,14},{14,8},{16,18},{18,... | collective-permute-start | bytes 1585160 | tf_op jit(solution)/shard_map/ppermute | solution.py:41
  7.6 14.6 %collective-permute-start = (bf16[2064,128]{1,0:T(8,128)(2,1)S(1)}, bf16[2064,128]{1,0:T(8,128)(2,1)S(1)}, u32[]{:S(2)}, u32[]{:S(2)}) collective-permute-start(bf16[2064,128]{1,0:T(8,128)(2,1)S(1)} %get-tuple-element.73.refs_0_), channel_id=1, source_target_pairs={{0,8},{2,10},{4,12},{6,14},{8,16},{10,18},{12,20},{14,22},{16,24},... | collective-permute-start | bytes 1585160 | tf_op jit(solution)/shard_map/ppermute | solution.py:41
  8.8 27.7 %collective-permute-start.4 = (bf16[2064,128]{1,0:T(8,128)(2,1)S(1)}, bf16[2064,128]{1,0:T(8,128)(2,1)}, u32[]{:S(2)}, u32[]{:S(2)}) collective-permute-start(bf16[2064,128]{1,0:T(8,128)(2,1)S(1)} %get-tuple-element.75.refs_4_), channel_id=1, source_target_pairs={{0,6},{2,0},{4,2},{6,4},{8,14},{10,8},{12,10},{14,12},{16,22},{18,... | collective-permute-start | bytes 1585160 | tf_op jit(solution)/shard_map/ppermute | solution.py:41
  10.3 26.2 %collective-permute-start.2 = (bf16[2064,128]{1,0:T(8,128)(2,1)S(1)}, bf16[2064,128]{1,0:T(8,128)(2,1)}, u32[]{:S(2)}, u32[]{:S(2)}) collective-permute-start(bf16[2064,128]{1,0:T(8,128)(2,1)S(1)} %get-tuple-element.73.refs_0_), channel_id=1, source_target_pairs={{0,24},{2,26},{4,28},{6,30},{8,0},{10,2},{12,4},{14,6},{16,8},{18,... | collective-permute-start | bytes 1585160 | tf_op jit(solution)/shard_map/ppermute | solution.py:41
  11.8 14.7 %copy-start = (f32[4096]{0:T(1024)S(1)}, f32[4096]{0:T(1024)}, u32[]{:S(2)}) copy-start(f32[4096]{0:T(1024)} %param.9) | copy-start | bytes 49156
  14.9 0.8 copy-start.2
  15.7 0.8 copy-start.4
  16.5 0.8 copy-start.5
  20.6 15.9 %collective-permute-start.6 = (bf16[2064,128]{1,0:T(8,128)(2,1)S(1)}, bf16[2064,128]{1,0:T(8,128)(2,1)}, u32[]{:S(2)}, u32[]{:S(2)}) collective-permute-start(bf16[2064,128]{1,0:T(8,128)(2,1)S(1)} %get-tuple-element.75.refs_4_), channel_id=1, source_target_pairs={{0,4},{2,6},{4,0},{6,2},{8,12},{10,14},{12,8},{14,10},{16,20},{18,... | collective-permute-start | bytes 1585160 | tf_op jit(solution)/shard_map/ppermute | solution.py:41
  22.2 14.3 %collective-permute-start.3 = (bf16[2064,128]{1,0:T(8,128)(2,1)S(1)}, bf16[2064,128]{1,0:T(8,128)(2,1)}, u32[]{:S(2)}, u32[]{:S(2)}) collective-permute-start(bf16[2064,128]{1,0:T(8,128)(2,1)S(1)} %get-tuple-element.73.refs_0_), channel_id=1, source_target_pairs={{0,16},{2,18},{4,20},{6,22},{8,24},{10,26},{12,28},{14,30},{16,0},... | collective-permute-start | bytes 1585160 | tf_op jit(solution)/shard_map/ppermute | solution.py:41
  24.9 11.5 %collective-permute-start.1 = (bf16[64,2048]{1,0:T(8,128)(2,1)S(1)}, bf16[64,2048]{1,0:T(8,128)(2,1)}, u32[]{:S(2)}, u32[]{:S(2)}) collective-permute-start(bf16[64,2048]{1,0:T(8,128)(2,1)S(1)} %get-tuple-element.69), channel_id=1, source_target_pairs={{0,64},{32,96},{64,0},{96,32},{1,65},{33,97},{65,1},{97,33},{2,66}... | collective-permute-start | bytes 786440 | tf_op jit(solution)/shard_map/ppermute | solution.py:53
  36.4 14.2 %collective-permute-start.12 = (bf16[160,2048]{1,0:T(8,128)(2,1)}, bf16[160,2048]{1,0:T(8,128)(2,1)S(1)}, u32[]{:S(2)}, u32[]{:S(2)}) collective-permute-start(bf16[160,2048]{1,0:T(8,128)(2,1)} %copy-done.4), channel_id=1, source_target_pairs={{0,64},{32,96},{64,0},{96,32},{1,65},{33,97},{65,1},{97,33},{2,66}... | collective-permute-start | bytes 1966088 | tf_op jit(solution)/shard_map/ppermute | solution.py:53
  39.4 15.9 %collective-permute-start.7 = (bf16[2048,128]{1,0:T(8,128)(2,1)S(1)}, bf16[2048,128]{1,0:T(8,128)(2,1)S(1)}, u32[]{:S(2)}, u32[]{:S(2)}) collective-permute-start(bf16[2048,128]{1,0:T(8,128)(2,1)S(1)} %get-tuple-element.77), channel_id=1, source_target_pairs={{0,6},{2,0},{4,2},{6,4},{8,14},{10,8},{12,10},{14,12},{16,22},{18,... | collective-permute-start | bytes 1572872 | tf_op jit(solution)/shard_map/ppermute | solution.py:41
  40.2 13.4 %collective-permute-start.8 = (bf16[2048,128]{1,0:T(8,128)(2,1)S(1)}, bf16[2048,128]{1,0:T(8,128)(2,1)S(1)}, u32[]{:S(2)}, u32[]{:S(2)}) collective-permute-start(bf16[2048,128]{1,0:T(8,128)(2,1)S(1)} %get-tuple-element.79), channel_id=1, source_target_pairs={{0,2},{2,4},{4,6},{6,0},{8,10},{10,12},{12,14},{14,8},{16,18},{18,... | collective-permute-start | bytes 1572872 | tf_op jit(solution)/shard_map/ppermute | solution.py:41
  40.9 14.3 %collective-permute-start.10 = (bf16[2048,128]{1,0:T(8,128)(2,1)S(1)}, bf16[2048,128]{1,0:T(8,128)(2,1)S(1)}, u32[]{:S(2)}, u32[]{:S(2)}) collective-permute-start(bf16[2048,128]{1,0:T(8,128)(2,1)S(1)} %get-tuple-element.82), channel_id=1, source_target_pairs={{0,24},{2,26},{4,28},{6,30},{8,0},{10,2},{12,4},{14,6},{16,8},{18,... | collective-permute-start | bytes 1572872 | tf_op jit(solution)/shard_map/ppermute | solution.py:41
  42.4 11.1 %collective-permute-start.11 = (bf16[2048,128]{1,0:T(8,128)(2,1)S(1)}, bf16[2048,128]{1,0:T(8,128)(2,1)S(1)}, u32[]{:S(2)}, u32[]{:S(2)}) collective-permute-start(bf16[2048,128]{1,0:T(8,128)(2,1)S(1)} %get-tuple-element.84), channel_id=1, source_target_pairs={{0,8},{2,10},{4,12},{6,14},{8,16},{10,18},{12,20},{14,22},{16,24},... | collective-permute-start | bytes 1572872 | tf_op jit(solution)/shard_map/ppermute | solution.py:41
  45.5 5.2 %copy-start.3 = (bf16[160,2048]{1,0:T(8,128)(2,1)S(1)}, bf16[160,2048]{1,0:T(8,128)(2,1)}, u32[]{:S(2)}) copy-start(bf16[160,2048]{1,0:T(8,128)(2,1)} %copy-done.2) | copy-start | bytes 1966084
  45.8 18.1 %copy-start.6 = (bf16[128,2048]{1,0:T(8,128)(2,1)S(1)}, bf16[128,2048]{1,0:T(8,128)(2,1)}, u32[]{:S(2)}) copy-start(bf16[128,2048]{1,0:T(8,128)(2,1)} %copy-done.5) | copy-start | bytes 1572868
  50.6 13.2 %collective-permute-start.15 = (bf16[160,2048]{1,0:T(8,128)(2,1)S(1)}, bf16[160,2048]{1,0:T(8,128)(2,1)S(1)}, u32[]{:S(2)}, u32[]{:S(2)}) collective-permute-start(bf16[160,2048]{1,0:T(8,128)(2,1)S(1)} %copy-done.3), channel_id=1, source_target_pairs={{0,64},{32,96},{64,0},{96,32},{1,65},{33,97},{65,1},{97,33},{2,66}... | collective-permute-start | bytes 1966088 | tf_op jit(solution)/shard_map/ppermute | solution.py:53
  53.6 10.5 %collective-permute-start.13 = (bf16[2048,128]{1,0:T(8,128)(2,1)S(1)}, bf16[2048,128]{1,0:T(8,128)(2,1)S(1)}, u32[]{:S(2)}, u32[]{:S(2)}) collective-permute-start(bf16[2048,128]{1,0:T(8,128)(2,1)S(1)} %get-tuple-element.88), channel_id=1, source_target_pairs={{0,16},{2,18},{4,20},{6,22},{8,24},{10,26},{12,28},{14,30},{16,0},... | collective-permute-start | bytes 1572872 | tf_op jit(solution)/shard_map/ppermute | solution.py:41
  53.7 10.6 %collective-permute-start.9 = (bf16[2048,128]{1,0:T(8,128)(2,1)S(1)}, bf16[2048,128]{1,0:T(8,128)(2,1)S(1)}, u32[]{:S(2)}, u32[]{:S(2)}) collective-permute-start(bf16[2048,128]{1,0:T(8,128)(2,1)S(1)} %get-tuple-element.80), channel_id=1, source_target_pairs={{0,4},{2,6},{4,0},{6,2},{8,12},{10,14},{12,8},{14,10},{16,20},{18,... | collective-permute-start | bytes 1572872 | tf_op jit(solution)/shard_map/ppermute | solution.py:41
  63.8 11.5 %collective-permute-start.16 = (bf16[128,2048]{1,0:T(8,128)(2,1)S(1)}, bf16[128,2048]{1,0:T(8,128)(2,1)S(1)}, u32[]{:S(2)}, u32[]{:S(2)}) collective-permute-start(bf16[128,2048]{1,0:T(8,128)(2,1)S(1)} %copy-done.6), channel_id=1, source_target_pairs={{0,64},{32,96},{64,0},{96,32},{1,65},{33,97},{65,1},{97,33},{2,66}... | collective-permute-start | bytes 1572872 | tf_op jit(solution)/shard_map/ppermute | solution.py:53
  67.4 12.4 %collective-permute-start.14 = (bf16[256,512]{1,0:T(8,128)(2,1)S(1)}, bf16[256,512]{1,0:T(8,128)(2,1)S(1)}, u32[]{:S(2)}, u32[]{:S(2)}) collective-permute-start(bf16[256,512]{1,0:T(8,128)(2,1)S(1)} %attend.4.mine_ref), channel_id=1, source_target_pairs={{0,64},{32,96},{64,0},{96,32},{1,65},{33,97},{65,1},{97,33},{2,66}... | collective-permute-start | bytes 786440 | tf_op jit(solution)/shard_map/ppermute | solution.py:53
  72.3 19.7 %collective-permute-start.20 = (bf16[256,512]{1,0:T(8,128)(2,1)S(1)}, bf16[256,512]{1,0:T(8,128)(2,1)S(1)}, u32[]{:S(2)}, u32[]{:S(2)}) collective-permute-start(bf16[256,512]{1,0:T(8,128)(2,1)S(1)} %attend.5.mine_ref), channel_id=1, source_target_pairs={{0,64},{32,96},{64,0},{96,32},{1,65},{33,97},{65,1},{97,33},{2,66}... | collective-permute-start | bytes 786440 | tf_op jit(solution)/shard_map/ppermute | solution.py:53
  81.1 12.8 %collective-permute-start.18 = (bf16[256,512]{1,0:T(8,128)(2,1)S(1)}, bf16[256,512]{1,0:T(8,128)(2,1)S(1)}, u32[]{:S(2)}, u32[]{:S(2)}) collective-permute-start(bf16[256,512]{1,0:T(8,128)(2,1)S(1)} %get-tuple-element.100), channel_id=1, source_target_pairs={{0,32},{32,0},{64,96},{96,64},{1,33},{33,1},{65,97},{97,65},{2,34}... | collective-permute-start | bytes 786440 | tf_op jit(solution)/shard_map/ppermute | solution.py:53
  88.9 8.7 %collective-permute-start.24 = (bf16[256,512]{1,0:T(8,128)(2,1)S(1)}, bf16[256,512]{1,0:T(8,128)(2,1)S(1)}, u32[]{:S(2)}, u32[]{:S(2)}) collective-permute-start(bf16[256,512]{1,0:T(8,128)(2,1)S(1)} %attend.6.mine_ref), channel_id=1, source_target_pairs={{0,64},{32,96},{64,0},{96,32},{1,65},{33,97},{65,1},{97,33},{2,66}... | collective-permute-start | bytes 786440 | tf_op jit(solution)/shard_map/ppermute | solution.py:53
  93.3 6.2 %collective-permute-start.22 = (bf16[256,512]{1,0:T(8,128)(2,1)S(1)}, bf16[256,512]{1,0:T(8,128)(2,1)S(1)}, u32[]{:S(2)}, u32[]{:S(2)}) collective-permute-start(bf16[256,512]{1,0:T(8,128)(2,1)S(1)} %get-tuple-element.108), channel_id=1, source_target_pairs={{0,32},{32,0},{64,96},{96,64},{1,33},{33,1},{65,97},{97,65},{2,34}... | collective-permute-start | bytes 786440 | tf_op jit(solution)/shard_map/ppermute | solution.py:53
  93.8 6.0 %collective-permute-start.17 = (bf16[256,512]{1,0:T(8,128)(2,1)S(1)}, bf16[256,512]{1,0:T(8,128)(2,1)S(1)}, u32[]{:S(2)}, u32[]{:S(2)}) collective-permute-start(bf16[256,512]{1,0:T(8,128)(2,1)S(1)} %get-tuple-element.98), channel_id=1, source_target_pairs={{0,32},{32,0},{64,96},{96,64},{1,33},{33,1},{65,97},{97,65},{2,34}... | collective-permute-start | bytes 786440 | tf_op jit(solution)/shard_map/ppermute | solution.py:53
  94.0 10.0 %collective-permute-start.19 = (bf16[256,512]{1,0:T(8,128)(2,1)S(1)}, bf16[256,512]{1,0:T(8,128)(2,1)S(1)}, u32[]{:S(2)}, u32[]{:S(2)}) collective-permute-start(bf16[256,512]{1,0:T(8,128)(2,1)S(1)} %add_convert_fusion.7), channel_id=1, source_target_pairs={{0,65},{32,97},{64,1},{96,33},{1,64},{33,96},{65,0},{97,32},{2,67}... | collective-permute-start | bytes 786440 | tf_op jit(solution)/shard_map/ppermute | solution.py:53
  97.6 7.8 %collective-permute-start.28 = (bf16[256,512]{1,0:T(8,128)(2,1)S(1)}, bf16[256,512]{1,0:T(8,128)(2,1)S(1)}, u32[]{:S(2)}, u32[]{:S(2)}) collective-permute-start(bf16[256,512]{1,0:T(8,128)(2,1)S(1)} %attend.7.mine_ref), channel_id=1, source_target_pairs={{0,64},{32,96},{64,0},{96,32},{1,65},{33,97},{65,1},{97,33},{2,66}... | collective-permute-start | bytes 786440 | tf_op jit(solution)/shard_map/ppermute | solution.py:53
  97.6 10.3 %collective-permute-start.21 = (bf16[256,512]{1,0:T(8,128)(2,1)S(1)}, bf16[256,512]{1,0:T(8,128)(2,1)S(1)}, u32[]{:S(2)}, u32[]{:S(2)}) collective-permute-start(bf16[256,512]{1,0:T(8,128)(2,1)S(1)} %get-tuple-element.106), channel_id=1, source_target_pairs={{0,32},{32,0},{64,96},{96,64},{1,33},{33,1},{65,97},{97,65},{2,34}... | collective-permute-start | bytes 786440 | tf_op jit(solution)/shard_map/ppermute | solution.py:53
  99.5 8.1 %collective-permute-start.26 = (bf16[256,512]{1,0:T(8,128)(2,1)S(1)}, bf16[256,512]{1,0:T(8,128)(2,1)S(1)}, u32[]{:S(2)}, u32[]{:S(2)}) collective-permute-start(bf16[256,512]{1,0:T(8,128)(2,1)S(1)} %get-tuple-element.114), channel_id=1, source_target_pairs={{0,32},{32,0},{64,96},{96,64},{1,33},{33,1},{65,97},{97,65},{2,34}... | collective-permute-start | bytes 786440 | tf_op jit(solution)/shard_map/ppermute | solution.py:53
  99.7 10.8 %collective-permute-start.23 = (bf16[256,512]{1,0:T(8,128)(2,1)S(1)}, bf16[256,512]{1,0:T(8,128)(2,1)S(1)}, u32[]{:S(2)}, u32[]{:S(2)}) collective-permute-start(bf16[256,512]{1,0:T(8,128)(2,1)S(1)} %add_convert_fusion.5), channel_id=1, source_target_pairs={{0,65},{32,97},{64,1},{96,33},{1,64},{33,96},{65,0},{97,32},{2,67}... | collective-permute-start | bytes 786440 | tf_op jit(solution)/shard_map/ppermute | solution.py:53
  104.0 8.3 %collective-permute-start.25 = (bf16[256,512]{1,0:T(8,128)(2,1)S(1)}, bf16[256,512]{1,0:T(8,128)(2,1)S(1)}, u32[]{:S(2)}, u32[]{:S(2)}) collective-permute-start(bf16[256,512]{1,0:T(8,128)(2,1)S(1)} %get-tuple-element.112), channel_id=1, source_target_pairs={{0,32},{32,0},{64,96},{96,64},{1,33},{33,1},{65,97},{97,65},{2,34}... | collective-permute-start | bytes 786440 | tf_op jit(solution)/shard_map/ppermute | solution.py:53
  106.7 10.0 %collective-permute-start.29 = (bf16[256,512]{1,0:T(8,128)(2,1)S(1)}, bf16[256,512]{1,0:T(8,128)(2,1)S(1)}, u32[]{:S(2)}, u32[]{:S(2)}) collective-permute-start(bf16[256,512]{1,0:T(8,128)(2,1)S(1)} %get-tuple-element.119), channel_id=1, source_target_pairs={{0,32},{32,0},{64,96},{96,64},{1,33},{33,1},{65,97},{97,65},{2,34}... | collective-permute-start | bytes 786440 | tf_op jit(solution)/shard_map/ppermute | solution.py:53
  107.7 3.0 %collective-permute-start.30 = (bf16[256,512]{1,0:T(8,128)(2,1)S(1)}, bf16[256,512]{1,0:T(8,128)(2,1)S(1)}, u32[]{:S(2)}, u32[]{:S(2)}) collective-permute-start(bf16[256,512]{1,0:T(8,128)(2,1)S(1)} %get-tuple-element.121), channel_id=1, source_target_pairs={{0,32},{32,0},{64,96},{96,64},{1,33},{33,1},{65,97},{97,65},{2,34}... | collective-permute-start | bytes 786440 | tf_op jit(solution)/shard_map/ppermute | solution.py:53
  107.9 8.8 %collective-permute-start.27 = (bf16[256,512]{1,0:T(8,128)(2,1)S(1)}, bf16[256,512]{1,0:T(8,128)(2,1)S(1)}, u32[]{:S(2)}, u32[]{:S(2)}) collective-permute-start(bf16[256,512]{1,0:T(8,128)(2,1)S(1)} %add_convert_fusion.3), channel_id=1, source_target_pairs={{0,65},{32,97},{64,1},{96,33},{1,64},{33,96},{65,0},{97,32},{2,67}... | collective-permute-start | bytes 786440 | tf_op jit(solution)/shard_map/ppermute | solution.py:53
  110.7 11.5 %collective-permute-start.31 = (bf16[256,512]{1,0:T(8,128)(2,1)S(1)}, bf16[256,512]{1,0:T(8,128)(2,1)S(1)}, u32[]{:S(2)}, u32[]{:S(2)}) collective-permute-start(bf16[256,512]{1,0:T(8,128)(2,1)S(1)} %add_convert_fusion.1), channel_id=1, source_target_pairs={{0,65},{32,97},{64,1},{96,33},{1,64},{33,96},{65,0},{97,32},{2,67}... | collective-permute-start | bytes 786440 | tf_op jit(solution)/shard_map/ppermute | solution.py:53

commit v6 on v5

--- a/solution.py
+++ b/solution.py
@@ -19,7 +19,7 @@
 PICKS = SIDE * SIDE * CAP
 NOTE_ROWS = 16
 EPSILON = 1e-05
-NEAR_PIECES = (64, 160, 160, 128)
+NEAR_PIECES = (112, 144, 128, 128)
 CHUNKS = (2, 2, 2, 2)
 AHEAD = 3
 LAG = 2

time: 124 us -> 120 us (0.968)
  waiting for transfers between devices: 35.1 us -> 28.6 us
  starting transfers between devices: 40.5 us -> 42.3 us
    ppermute x20, waiting for transfers between devices: 29 us -> 18.2 us  [along_z(): return lax.ppermute(value, SECTION_HEAD, pairs)]
    ppermute x12, waiting for transfers between devices: 6.12 us -> 10.3 us  [along_seq(): return lax.ppermute(value, 'seq', pairs)]
    ppermute x20, starting transfers between devices: 25.1 us -> 27 us  [along_z(): return lax.ppermute(value, SECTION_HEAD, pairs)]
  transfers between devices with their start and end apart: 32 -> 32, of which waited for: 9 -> 9; matrix products, arithmetic and copies ran while one was open for 2% -> 2% of each run, Pallas kernels for 29% -> 31%
where the time goes in v6:
time: 120 us
  starting transfers between devices  42.3 us (35%)
  Pallas kernels  41.3 us (34%)
  waiting for transfers between devices  28.6 us (24%)
  local copies, waits for them, and re-layouts  5.06 us (4%)
  other arithmetic  2.04 us (2%)
    ppermute x20, starting transfers between devices, along_z(): return lax.ppermute(value, SECTION_HEAD, pairs)  27 us
    ppermute x20, waiting for transfers between devices, along_z(): return lax.ppermute(value, SECTION_HEAD, pairs)  18.2 us
    ppermute x12, starting transfers between devices, along_seq(): return lax.ppermute(value, 'seq', pairs)  15.4 us
    pallas_call x4, Pallas kernels, attend(): pl.pallas_call(functools.partial(attend_body, first_tile), in_specs=[SMEM...  11.9 us
    ppermute x12, waiting for transfers between devices, along_seq(): return lax.ppermute(value, 'seq', pairs)  10.3 us
    pallas_call x1, Pallas kernels, queries_of(): pl.pallas_call(ask_body, grid=(steps,), in_specs=[pl.BlockSpec((rows // s...  9.63 us
    pallas_call x2, Pallas kernels, pick(): pl.pallas_call(pick_body, grid_spec=pltpu.PrefetchScalarGridSpec(num_scal...  7.06 us
    pallas_call x4, Pallas kernels, multiply(): pl.pallas_call(multiply_body, in_specs=[VMEM_WHOLE] * 3, out_specs=[VMEM_...  5.2 us
  transfers between devices with their start and end apart: 32, of which 9 were waited for; matrix products, arithmetic and copies ran while one was open for 2% of the time, Pallas kernels for 31%

profile of v6, /device:TPU:1, one launch (start us, length us, event | category | flops | bytes accessed | tf_op | source)
XLA Modules:
  0.0 119.7 jit_solution(12430993973684340587)
XLA Ops:
  0.7 4.7 %project.1 = (bf16[2064,128]{1,0:T(8,128)(2,1)S(1)}, bf16[2064,128]{1,0:T(8,128)(2,1)S(1)}, s32[8,128]{1,0:T(8,128)S(1)}) custom-call(s32[8,16]{1,0:T(8,128)S(1)} %copy-done.1, bf16[2048,1024]{1,0:T(8,128)(2,1)} %x_ref.1, bf16[1024,128]{1,0:T(8,128)(2,1)} %wk_ref.1, bf16[1024,128]{1,0:T(8,128)(2,1)} %wv_ref.1), custom_call_target="tpu_custom_call" | custom-call | flops 1 | bytes 1 | tf_op jit(solution)/shard_map/project/pallas_call | solution.py:135
  5.4 2.2 %collective-permute-start.5 = (bf16[2064,128]{1,0:T(8,128)(2,1)S(1)}, bf16[2064,128]{1,0:T(8,128)(2,1)S(1)}, u32[]{:S(2)}, u32[]{:S(2)}) collective-permute-start(bf16[2064,128]{1,0:T(8,128)(2,1)S(1)} %get-tuple-element.75.refs_4_), channel_id=1, source_target_pairs={{0,2},{2,4},{4,6},{6,0},{8,10},{10,12},{12,14},{14,8},{16,18},{18,... | collective-permute-start | bytes 1585160 | tf_op jit(solution)/shard_map/ppermute | solution.py:41
  7.6 1.2 %collective-permute-start = (bf16[2064,128]{1,0:T(8,128)(2,1)S(1)}, bf16[2064,128]{1,0:T(8,128)(2,1)S(1)}, u32[]{:S(2)}, u32[]{:S(2)}) collective-permute-start(bf16[2064,128]{1,0:T(8,128)(2,1)S(1)} %get-tuple-element.73.refs_0_), channel_id=1, source_target_pairs={{0,8},{2,10},{4,12},{6,14},{8,16},{10,18},{12,20},{14,22},{16,24},... | collective-permute-start | bytes 1585160 | tf_op jit(solution)/shard_map/ppermute | solution.py:41
  8.8 1.5 %collective-permute-start.4 = (bf16[2064,128]{1,0:T(8,128)(2,1)S(1)}, bf16[2064,128]{1,0:T(8,128)(2,1)}, u32[]{:S(2)}, u32[]{:S(2)}) collective-permute-start(bf16[2064,128]{1,0:T(8,128)(2,1)S(1)} %get-tuple-element.75.refs_4_), channel_id=1, source_target_pairs={{0,6},{2,0},{4,2},{6,4},{8,14},{10,8},{12,10},{14,12},{16,22},{18,... | collective-permute-start | bytes 1585160 | tf_op jit(solution)/shard_map/ppermute | solution.py:41
  10.3 1.5 %collective-permute-start.2 = (bf16[2064,128]{1,0:T(8,128)(2,1)S(1)}, bf16[2064,128]{1,0:T(8,128)(2,1)}, u32[]{:S(2)}, u32[]{:S(2)}) collective-permute-start(bf16[2064,128]{1,0:T(8,128)(2,1)S(1)} %get-tuple-element.73.refs_0_), channel_id=1, source_target_pairs={{0,24},{2,26},{4,28},{6,30},{8,0},{10,2},{12,4},{14,6},{16,8},{18,... | collective-permute-start | bytes 1585160 | tf_op jit(solution)/shard_map/ppermute | solution.py:41
  11.8 4.0 %pick.2 = (bf16[112,2048]{1,0:T(8,128)(2,1)}, bf16[144,2048]{1,0:T(8,128)(2,1)S(1)}, bf16[128,2048]{1,0:T(8,128)(2,1)S(1)}, bf16[128,2048]{1,0:T(8,128)(2,1)S(1)}) custom-call(s32[4]{0:T(128)S(1)} %pad_add_fusion.1.places_ref, bf16[512,4096]{1,0:T(8,128)(2,1)} %w_ref.3), custom_call_target="tpu_custom_call" | custom-call | flops 1 | bytes 1 | tf_op jit(solution)/shard_map/pick/pallas_call | solution.py:258
  15.9 0.8 copy-done.2
  16.7 0.8 copy-done.3
  17.5 0.8 copy-done.5
  18.3 2.3 %collective-permute-done.5.refs_7_ = bf16[2064,128]{1,0:T(8,128)(2,1)S(1)} collective-permute-done((bf16[2064,128]{1,0:T(8,128)(2,1)S(1)}, bf16[2064,128]{1,0:T(8,128)(2,1)S(1)}, u32[]{:S(2)}, u32[]{:S(2)}) %collective-permute-start.5) | collective-permute-done | bytes 528416 | tf_op jit(solution)/shard_map/ppermute | solution.py:41
  20.6 1.6 %collective-permute-start.6 = (bf16[2064,128]{1,0:T(8,128)(2,1)S(1)}, bf16[2064,128]{1,0:T(8,128)(2,1)}, u32[]{:S(2)}, u32[]{:S(2)}) collective-permute-start(bf16[2064,128]{1,0:T(8,128)(2,1)S(1)} %get-tuple-element.75.refs_4_), channel_id=1, source_target_pairs={{0,4},{2,6},{4,0},{6,2},{8,12},{10,14},{12,8},{14,10},{16,20},{18,... | collective-permute-start | bytes 1585160 | tf_op jit(solution)/shard_map/ppermute | solution.py:41
  22.2 2.7 %collective-permute-start.3 = (bf16[2064,128]{1,0:T(8,128)(2,1)S(1)}, bf16[2064,128]{1,0:T(8,128)(2,1)}, u32[]{:S(2)}, u32[]{:S(2)}) collective-permute-start(bf16[2064,128]{1,0:T(8,128)(2,1)S(1)} %get-tuple-element.73.refs_0_), channel_id=1, source_target_pairs={{0,16},{2,18},{4,20},{6,22},{8,24},{10,26},{12,28},{14,30},{16,0},... | collective-permute-start | bytes 1585160 | tf_op jit(solution)/shard_map/ppermute | solution.py:41
  24.9 1.6 %collective-permute-start.1 = (bf16[112,2048]{1,0:T(8,128)(2,1)}, bf16[112,2048]{1,0:T(8,128)(2,1)}, u32[]{:S(2)}, u32[]{:S(2)}) collective-permute-start(bf16[112,2048]{1,0:T(8,128)(2,1)} %get-tuple-element.69), channel_id=1, source_target_pairs={{0,64},{32,96},{64,0},{96,32},{1,65},{33,97},{65,1},{97,33},{2,66}... | collective-permute-start | bytes 1376264 | tf_op jit(solution)/shard_map/ppermute | solution.py:53
  26.6 9.6 %ask.1.q_ref = bf16[1024,512]{1,0:T(8,128)(2,1)S(1)} custom-call(bf16[1024,4096]{1,0:T(8,128)(2,1)} %x_ref.2, f32[1,4096]{1,0:T(1,128)S(1)} %bitcast.11, bf16[4096,512]{1,0:T(8,128)(2,1)} %w_ref.1), custom_call_target="tpu_custom_call" | custom-call | flops 1 | bytes 1 | tf_op jit(solution)/shard_map/ask/pallas_call | solution.py:308
  36.9 2.8 %pack.1 = (bf16[2048,128]{1,0:T(8,128)(2,1)S(1)}, bf16[2048,128]{1,0:T(8,128)(2,1)S(1)}, bf16[2048,128]{1,0:T(8,128)(2,1)S(1)}, bf16[2048,128]{1,0:T(8,128)(2,1)...) custom-call(s32[2]{0:T(128)S(1)} %pad_add_fusion.place_ref, ...), custom_call_target="tpu_custom_call" | custom-call | flops 1 | bytes 1 | tf_op jit(solution)/shard_map/pack/pallas_call | solution.py:187
  39.8 0.8 collective-permute-start.7
  41.3 1.1 collective-permute-start.10
  42.8 3.0 %pick.3 = bf16[512,2048]{1,0:T(8,128)(2,1)S(1)} custom-call(s32[4]{0:T(128)S(1)} %pad_add_fusion.2.places_ref, bf16[512,4096]{1,0:T(8,128)(2,1)} %w_ref.3), custom_call_target="tpu_custom_call" | custom-call | flops 1 | bytes 1 | tf_op jit(solution)/shard_map/pick/pallas_call | solution.py:258
  46.1 1.1 constant_dynamic-update-slice_fusion.11
  47.2 2.0 %collective-permute-done.12 = bf16[144,2048]{1,0:T(8,128)(2,1)S(1)} collective-permute-done((bf16[144,2048]{1,0:T(8,128)(2,1)}, bf16[144,2048]{1,0:T(8,128)(2,1)S(1)}, u32[]{:S(2)}, u32[]{:S(2)}) %collective-permute-start.12) | collective-permute-done | bytes 589856 | tf_op jit(solution)/shard_map/ppermute | solution.py:53
  49.2 4.1 %collective-permute-done.11 = bf16[2048,128]{1,0:T(8,128)(2,1)S(1)} collective-permute-done((bf16[2048,128]{1,0:T(8,128)(2,1)S(1)}, bf16[2048,128]{1,0:T(8,128)(2,1)S(1)}, u32[]{:S(2)}, u32[]{:S(2)}) %collective-permute-start.11) | collective-permute-done | bytes 524320 | tf_op jit(solution)/shard_map/ppermute | solution.py:41
  53.4 1.7 %collective-permute-start.9 = (bf16[2048,128]{1,0:T(8,128)(2,1)S(1)}, bf16[2048,128]{1,0:T(8,128)(2,1)S(1)}, u32[]{:S(2)}, u32[]{:S(2)}) collective-permute-start(bf16[2048,128]{1,0:T(8,128)(2,1)S(1)} %get-tuple-element.80), channel_id=1, source_target_pairs={{0,4},{2,6},{4,0},{6,2},{8,12},{10,14},{12,8},{14,10},{16,20},{18,... | collective-permute-start | bytes 1572872 | tf_op jit(solution)/shard_map/ppermute | solution.py:41
  55.2 4.4 %collective-permute-done.15 = bf16[128,2048]{1,0:T(8,128)(2,1)S(1)} collective-permute-done((bf16[128,2048]{1,0:T(8,128)(2,1)S(1)}, bf16[128,2048]{1,0:T(8,128)(2,1)S(1)}, u32[]{:S(2)}, u32[]{:S(2)}) %collective-permute-start.15) | collective-permute-done | bytes 524320 | tf_op jit(solution)/shard_map/ppermute | solution.py:53
  59.6 4.0 %collective-permute-done.13 = bf16[2048,128]{1,0:T(8,128)(2,1)S(1)} collective-permute-done((bf16[2048,128]{1,0:T(8,128)(2,1)S(1)}, bf16[2048,128]{1,0:T(8,128)(2,1)S(1)}, u32[]{:S(2)}, u32[]{:S(2)}) %collective-permute-start.13) | collective-permute-done | bytes 524320 | tf_op jit(solution)/shard_map/ppermute | solution.py:41
  63.9 3.0 %attend.4.mine_ref = bf16[256,512]{1,0:T(8,128)(2,1)S(1)} custom-call(s32[8,128]{1,0:T(8,128)S(1)} %get-tuple-element.103.slots_ref, s32[2]{0:T(128)S(1)} %pad_add_fusion.place_ref, bf16[1024,512]{1,0:T(8,128)(2,1)S(1)} %ask.1.q_ref, bf16[8192,128]{1,0:T(8,128)(2,1)S(1)} %constant_dynamic-update-slice_fusion.k_ref, ...), custom_call_target="tpu_custom_call" | custom-call | flops 1 | bytes 1 | tf_op jit(solution)/shard_map/attend/pallas_call | solution.py:237
  66.9 2.4 %collective-permute-start.14 = (bf16[256,512]{1,0:T(8,128)(2,1)S(1)}, bf16[256,512]{1,0:T(8,128)(2,1)S(1)}, u32[]{:S(2)}, u32[]{:S(2)}) collective-permute-start(bf16[256,512]{1,0:T(8,128)(2,1)S(1)} %attend.4.mine_ref), channel_id=1, source_target_pairs={{0,64},{32,96},{64,0},{96,32},{1,65},{33,97},{65,1},{97,33},{2,66}... | collective-permute-start | bytes 786440 | tf_op jit(solution)/shard_map/ppermute | solution.py:53
  69.3 3.0 %attend.5.mine_ref = bf16[256,512]{1,0:T(8,128)(2,1)S(1)} custom-call(s32[8,128]{1,0:T(8,128)S(1)} %get-tuple-element.103.slots_ref, s32[2]{0:T(128)S(1)} %pad_add_fusion.place_ref, bf16[1024,512]{1,0:T(8,128)(2,1)S(1)} %ask.1.q_ref, bf16[8192,128]{1,0:T(8,128)(2,1)S(1)} %constant_dynamic-update-slice_fusion.k_ref, ...), custom_call_target="tpu_custom_call" | custom-call | flops 1 | bytes 1 | tf_op jit(solution)/shard_map/attend/pallas_call | solution.py:237
  72.4 3.0 %attend.6.mine_ref = bf16[256,512]{1,0:T(8,128)(2,1)S(1)} custom-call(s32[8,128]{1,0:T(8,128)S(1)} %get-tuple-element.103.slots_ref, s32[2]{0:T(128)S(1)} %pad_add_fusion.place_ref, bf16[1024,512]{1,0:T(8,128)(2,1)S(1)} %ask.1.q_ref, bf16[8192,128]{1,0:T(8,128)(2,1)S(1)} %constant_dynamic-update-slice_fusion.k_ref, ...), custom_call_target="tpu_custom_call" | custom-call | flops 1 | bytes 1 | tf_op jit(solution)/shard_map/attend/pallas_call | solution.py:237
  75.4 0.8 collective-permute-done.14.near_ref
  76.2 1.3 %multiply.4 = (bf16[256,512]{1,0:T(8,128)(2,1)S(1)}, bf16[256,512]{1,0:T(8,128)(2,1)S(1)}, f32[256,512]{1,0:T(8,128)S(1)}, f32[256,512]{1,0:T(8,128)S(1)}) custom-call(bf16[256,512]{1,0:T(8,128)(2,1)S(1)} %attend.4.mine_ref, bf16[256,512]{1,0:T(8,128)(2,1)S(1)} %collective-permute-done.14.near_ref, ...), custom_call_target="tpu_custom_call" | custom-call | flops 1 | bytes 1 | tf_op jit(solution)/shard_map/multiply/pallas_call | solution.py:286
  77.5 7.5 %collective-permute-start.18 = (bf16[256,512]{1,0:T(8,128)(2,1)S(1)}, bf16[256,512]{1,0:T(8,128)(2,1)S(1)}, u32[]{:S(2)}, u32[]{:S(2)}) collective-permute-start(bf16[256,512]{1,0:T(8,128)(2,1)S(1)} %get-tuple-element.100), channel_id=1, source_target_pairs={{0,32},{32,0},{64,96},{96,64},{1,33},{33,1},{65,97},{97,65},{2,34}... | collective-permute-start | bytes 786440 | tf_op jit(solution)/shard_map/ppermute | solution.py:53
  85.0 1.8 %collective-permute-start.24 = (bf16[256,512]{1,0:T(8,128)(2,1)S(1)}, bf16[256,512]{1,0:T(8,128)(2,1)S(1)}, u32[]{:S(2)}, u32[]{:S(2)}) collective-permute-start(bf16[256,512]{1,0:T(8,128)(2,1)S(1)} %attend.6.mine_ref), channel_id=1, source_target_pairs={{0,64},{32,96},{64,0},{96,32},{1,65},{33,97},{65,1},{97,33},{2,66}... | collective-permute-start | bytes 786440 | tf_op jit(solution)/shard_map/ppermute | solution.py:53
  86.7 3.0 %attend.7.mine_ref = bf16[256,512]{1,0:T(8,128)(2,1)S(1)} custom-call(s32[8,128]{1,0:T(8,128)S(1)} %get-tuple-element.103.slots_ref, s32[2]{0:T(128)S(1)} %pad_add_fusion.place_ref, bf16[1024,512]{1,0:T(8,128)(2,1)S(1)} %ask.1.q_ref, bf16[8192,128]{1,0:T(8,128)(2,1)S(1)} %constant_dynamic-update-slice_fusion.k_ref, ...), custom_call_target="tpu_custom_call" | custom-call | flops 1 | bytes 1 | tf_op jit(solution)/shard_map/attend/pallas_call | solution.py:237
  89.7 1.3 %multiply.5 = (bf16[256,512]{1,0:T(8,128)(2,1)S(1)}, bf16[256,512]{1,0:T(8,128)(2,1)S(1)}, f32[256,512]{1,0:T(8,128)S(1)}, f32[256,512]{1,0:T(8,128)S(1)}) custom-call(bf16[256,512]{1,0:T(8,128)(2,1)S(1)} %attend.5.mine_ref, bf16[256,512]{1,0:T(8,128)(2,1)S(1)} %collective-permute-done.20.near_ref, ...), custom_call_target="tpu_custom_call" | custom-call | flops 1 | bytes 1 | tf_op jit(solution)/shard_map/multiply/pallas_call | solution.py:286
  91.7 2.2 %collective-permute-start.19 = (bf16[256,512]{1,0:T(8,128)(2,1)S(1)}, bf16[256,512]{1,0:T(8,128)(2,1)S(1)}, u32[]{:S(2)}, u32[]{:S(2)}) collective-permute-start(bf16[256,512]{1,0:T(8,128)(2,1)S(1)} %add_convert_fusion.7), channel_id=1, source_target_pairs={{0,65},{32,97},{64,1},{96,33},{1,64},{33,96},{65,0},{97,32},{2,67}... | collective-permute-start | bytes 786440 | tf_op jit(solution)/shard_map/ppermute | solution.py:53
  93.9 0.8 collective-permute-start.28
  94.8 0.9 collective-permute-start.21
  95.7 1.3 %multiply.6 = (bf16[256,512]{1,0:T(8,128)(2,1)S(1)}, bf16[256,512]{1,0:T(8,128)(2,1)S(1)}, f32[256,512]{1,0:T(8,128)S(1)}, f32[256,512]{1,0:T(8,128)S(1)}) custom-call(bf16[256,512]{1,0:T(8,128)(2,1)S(1)} %attend.6.mine_ref, bf16[256,512]{1,0:T(8,128)(2,1)S(1)} %collective-permute-done.24.near_ref, ...), custom_call_target="tpu_custom_call" | custom-call | flops 1 | bytes 1 | tf_op jit(solution)/shard_map/multiply/pallas_call | solution.py:286
  97.2 2.0 %collective-permute-start.23 = (bf16[256,512]{1,0:T(8,128)(2,1)S(1)}, bf16[256,512]{1,0:T(8,128)(2,1)S(1)}, u32[]{:S(2)}, u32[]{:S(2)}) collective-permute-start(bf16[256,512]{1,0:T(8,128)(2,1)S(1)} %add_convert_fusion.5), channel_id=1, source_target_pairs={{0,65},{32,97},{64,1},{96,33},{1,64},{33,96},{65,0},{97,32},{2,67}... | collective-permute-start | bytes 786440 | tf_op jit(solution)/shard_map/ppermute | solution.py:53
  99.2 1.4 %collective-permute-done.19 = bf16[256,512]{1,0:T(8,128)(2,1)S(1)} collective-permute-done((bf16[256,512]{1,0:T(8,128)(2,1)S(1)}, bf16[256,512]{1,0:T(8,128)(2,1)S(1)}, u32[]{:S(2)}, u32[]{:S(2)}) %collective-permute-start.19) | collective-permute-done | bytes 262176 | tf_op jit(solution)/shard_map/ppermute | solution.py:53
  100.5 1.2 %collective-permute-start.25 = (bf16[256,512]{1,0:T(8,128)(2,1)S(1)}, bf16[256,512]{1,0:T(8,128)(2,1)S(1)}, u32[]{:S(2)}, u32[]{:S(2)}) collective-permute-start(bf16[256,512]{1,0:T(8,128)(2,1)S(1)} %get-tuple-element.112), channel_id=1, source_target_pairs={{0,32},{32,0},{64,96},{96,64},{1,33},{33,1},{65,97},{97,65},{2,34}... | collective-permute-start | bytes 786440 | tf_op jit(solution)/shard_map/ppermute | solution.py:53
  101.9 1.3 %multiply.7 = (bf16[256,512]{1,0:T(8,128)(2,1)S(1)}, bf16[256,512]{1,0:T(8,128)(2,1)S(1)}, f32[256,512]{1,0:T(8,128)S(1)}, f32[256,512]{1,0:T(8,128)S(1)}) custom-call(bf16[256,512]{1,0:T(8,128)(2,1)S(1)} %attend.7.mine_ref, bf16[256,512]{1,0:T(8,128)(2,1)S(1)} %collective-permute-done.28.near_ref, ...), custom_call_target="tpu_custom_call" | custom-call | flops 1 | bytes 1 | tf_op jit(solution)/shard_map/multiply/pallas_call | solution.py:286
  103.2 0.8 collective-permute-start.29
  104.2 2.1 %collective-permute-start.27 = (bf16[256,512]{1,0:T(8,128)(2,1)S(1)}, bf16[256,512]{1,0:T(8,128)(2,1)S(1)}, u32[]{:S(2)}, u32[]{:S(2)}) collective-permute-start(bf16[256,512]{1,0:T(8,128)(2,1)S(1)} %add_convert_fusion.3), channel_id=1, source_target_pairs={{0,65},{32,97},{64,1},{96,33},{1,64},{33,96},{65,0},{97,32},{2,67}... | collective-permute-start | bytes 786440 | tf_op jit(solution)/shard_map/ppermute | solution.py:53
  106.5 2.2 %collective-permute-start.31 = (bf16[256,512]{1,0:T(8,128)(2,1)S(1)}, bf16[256,512]{1,0:T(8,128)(2,1)S(1)}, u32[]{:S(2)}, u32[]{:S(2)}) collective-permute-start(bf16[256,512]{1,0:T(8,128)(2,1)S(1)} %add_convert_fusion.1), channel_id=1, source_target_pairs={{0,65},{32,97},{64,1},{96,33},{1,64},{33,96},{65,0},{97,32},{2,67}... | collective-permute-start | bytes 786440 | tf_op jit(solution)/shard_map/ppermute | solution.py:53
  108.8 4.2 %collective-permute-done.27 = bf16[256,512]{1,0:T(8,128)(2,1)S(1)} collective-permute-done((bf16[256,512]{1,0:T(8,128)(2,1)S(1)}, bf16[256,512]{1,0:T(8,128)(2,1)S(1)}, u32[]{:S(2)}, u32[]{:S(2)}) %collective-permute-start.27) | collective-permute-done | bytes 262176 | tf_op jit(solution)/shard_map/ppermute | solution.py:53
  113.1 5.5 %collective-permute-done.31 = bf16[256,512]{1,0:T(8,128)(2,1)S(1)} collective-permute-done((bf16[256,512]{1,0:T(8,128)(2,1)S(1)}, bf16[256,512]{1,0:T(8,128)(2,1)S(1)}, u32[]{:S(2)}, u32[]{:S(2)}) %collective-permute-start.31) | collective-permute-done | bytes 262176 | tf_op jit(solution)/shard_map/ppermute | solution.py:53
  118.7 1.0 pad_maximum_fusion
  (68 shorter events, 5.0 us)
Async XLA Ops:
  0.0 0.7 copy-start.1
  5.4 15.2 %collective-permute-start.5 = (bf16[2064,128]{1,0:T(8,128)(2,1)S(1)}, bf16[2064,128]{1,0:T(8,128)(2,1)S(1)}, u32[]{:S(2)}, u32[]{:S(2)}) collective-permute-start(bf16[2064,128]{1,0:T(8,128)(2,1)S(1)} %get-tuple-element.75.refs_4_), channel_id=1, source_target_pairs={{0,2},{2,4},{4,6},{6,0},{8,10},{10,12},{12,14},{14,8},{16,18},{18,... | collective-permute-start | bytes 1585160 | tf_op jit(solution)/shard_map/ppermute | solution.py:41
  7.6 14.6 %collective-permute-start = (bf16[2064,128]{1,0:T(8,128)(2,1)S(1)}, bf16[2064,128]{1,0:T(8,128)(2,1)S(1)}, u32[]{:S(2)}, u32[]{:S(2)}) collective-permute-start(bf16[2064,128]{1,0:T(8,128)(2,1)S(1)} %get-tuple-element.73.refs_0_), channel_id=1, source_target_pairs={{0,8},{2,10},{4,12},{6,14},{8,16},{10,18},{12,20},{14,22},{16,24},... | collective-permute-start | bytes 1585160 | tf_op jit(solution)/shard_map/ppermute | solution.py:41
  8.8 28.1 %collective-permute-start.4 = (bf16[2064,128]{1,0:T(8,128)(2,1)S(1)}, bf16[2064,128]{1,0:T(8,128)(2,1)}, u32[]{:S(2)}, u32[]{:S(2)}) collective-permute-start(bf16[2064,128]{1,0:T(8,128)(2,1)S(1)} %get-tuple-element.75.refs_4_), channel_id=1, source_target_pairs={{0,6},{2,0},{4,2},{6,4},{8,14},{10,8},{12,10},{14,12},{16,22},{18,... | collective-permute-start | bytes 1585160 | tf_op jit(solution)/shard_map/ppermute | solution.py:41
  10.3 26.6 %collective-permute-start.2 = (bf16[2064,128]{1,0:T(8,128)(2,1)S(1)}, bf16[2064,128]{1,0:T(8,128)(2,1)}, u32[]{:S(2)}, u32[]{:S(2)}) collective-permute-start(bf16[2064,128]{1,0:T(8,128)(2,1)S(1)} %get-tuple-element.73.refs_0_), channel_id=1, source_target_pairs={{0,24},{2,26},{4,28},{6,30},{8,0},{10,2},{12,4},{14,6},{16,8},{18,... | collective-permute-start | bytes 1585160 | tf_op jit(solution)/shard_map/ppermute | solution.py:41
  11.8 14.7 %copy-start = (f32[4096]{0:T(1024)S(1)}, f32[4096]{0:T(1024)}, u32[]{:S(2)}) copy-start(f32[4096]{0:T(1024)} %param.9) | copy-start | bytes 49156
  15.9 0.8 copy-start.2
  16.7 0.8 copy-start.3
  17.5 0.8 copy-start.5
  20.6 16.3 %collective-permute-start.6 = (bf16[2064,128]{1,0:T(8,128)(2,1)S(1)}, bf16[2064,128]{1,0:T(8,128)(2,1)}, u32[]{:S(2)}, u32[]{:S(2)}) collective-permute-start(bf16[2064,128]{1,0:T(8,128)(2,1)S(1)} %get-tuple-element.75.refs_4_), channel_id=1, source_target_pairs={{0,4},{2,6},{4,0},{6,2},{8,12},{10,14},{12,8},{14,10},{16,20},{18,... | collective-permute-start | bytes 1585160 | tf_op jit(solution)/shard_map/ppermute | solution.py:41
  22.2 14.7 %collective-permute-start.3 = (bf16[2064,128]{1,0:T(8,128)(2,1)S(1)}, bf16[2064,128]{1,0:T(8,128)(2,1)}, u32[]{:S(2)}, u32[]{:S(2)}) collective-permute-start(bf16[2064,128]{1,0:T(8,128)(2,1)S(1)} %get-tuple-element.73.refs_0_), channel_id=1, source_target_pairs={{0,16},{2,18},{4,20},{6,22},{8,24},{10,26},{12,28},{14,30},{16,0},... | collective-permute-start | bytes 1585160 | tf_op jit(solution)/shard_map/ppermute | solution.py:41
  24.9 11.5 %collective-permute-start.1 = (bf16[112,2048]{1,0:T(8,128)(2,1)}, bf16[112,2048]{1,0:T(8,128)(2,1)}, u32[]{:S(2)}, u32[]{:S(2)}) collective-permute-start(bf16[112,2048]{1,0:T(8,128)(2,1)} %get-tuple-element.69), channel_id=1, source_target_pairs={{0,64},{32,96},{64,0},{96,32},{1,65},{33,97},{65,1},{97,33},{2,66}... | collective-permute-start | bytes 1376264 | tf_op jit(solution)/shard_map/ppermute | solution.py:53
  36.4 12.8 %collective-permute-start.12 = (bf16[144,2048]{1,0:T(8,128)(2,1)}, bf16[144,2048]{1,0:T(8,128)(2,1)S(1)}, u32[]{:S(2)}, u32[]{:S(2)}) collective-permute-start(bf16[144,2048]{1,0:T(8,128)(2,1)} %copy-done.2), channel_id=1, source_target_pairs={{0,64},{32,96},{64,0},{96,32},{1,65},{33,97},{65,1},{97,33},{2,66}... | collective-permute-start | bytes 1769480 | tf_op jit(solution)/shard_map/ppermute | solution.py:53
  39.8 15.3 %collective-permute-start.7 = (bf16[2048,128]{1,0:T(8,128)(2,1)S(1)}, bf16[2048,128]{1,0:T(8,128)(2,1)S(1)}, u32[]{:S(2)}, u32[]{:S(2)}) collective-permute-start(bf16[2048,128]{1,0:T(8,128)(2,1)S(1)} %get-tuple-element.77), channel_id=1, source_target_pairs={{0,6},{2,0},{4,2},{6,4},{8,14},{10,8},{12,10},{14,12},{16,22},{18,... | collective-permute-start | bytes 1572872 | tf_op jit(solution)/shard_map/ppermute | solution.py:41
  40.6 12.7 %collective-permute-start.8 = (bf16[2048,128]{1,0:T(8,128)(2,1)S(1)}, bf16[2048,128]{1,0:T(8,128)(2,1)S(1)}, u32[]{:S(2)}, u32[]{:S(2)}) collective-permute-start(bf16[2048,128]{1,0:T(8,128)(2,1)S(1)} %get-tuple-element.79), channel_id=1, source_target_pairs={{0,2},{2,4},{4,6},{6,0},{8,10},{10,12},{12,14},{14,8},{16,18},{18,... | collective-permute-start | bytes 1572872 | tf_op jit(solution)/shard_map/ppermute | solution.py:41
  41.3 13.7 %collective-permute-start.10 = (bf16[2048,128]{1,0:T(8,128)(2,1)S(1)}, bf16[2048,128]{1,0:T(8,128)(2,1)S(1)}, u32[]{:S(2)}, u32[]{:S(2)}) collective-permute-start(bf16[2048,128]{1,0:T(8,128)(2,1)S(1)} %get-tuple-element.82), channel_id=1, source_target_pairs={{0,24},{2,26},{4,28},{6,30},{8,0},{10,2},{12,4},{14,6},{16,8},{18,... | collective-permute-start | bytes 1572872 | tf_op jit(solution)/shard_map/ppermute | solution.py:41
  42.4 10.9 %collective-permute-start.11 = (bf16[2048,128]{1,0:T(8,128)(2,1)S(1)}, bf16[2048,128]{1,0:T(8,128)(2,1)S(1)}, u32[]{:S(2)}, u32[]{:S(2)}) collective-permute-start(bf16[2048,128]{1,0:T(8,128)(2,1)S(1)} %get-tuple-element.84), channel_id=1, source_target_pairs={{0,8},{2,10},{4,12},{6,14},{8,16},{10,18},{12,20},{14,22},{16,24},... | collective-permute-start | bytes 1572872 | tf_op jit(solution)/shard_map/ppermute | solution.py:41
  45.8 3.4 %copy-start.6 = (bf16[128,2048]{1,0:T(8,128)(2,1)S(1)}, bf16[128,2048]{1,0:T(8,128)(2,1)}, u32[]{:S(2)}) copy-start(bf16[128,2048]{1,0:T(8,128)(2,1)} %copy-done.5) | copy-start | bytes 1572868
  46.1 13.5 %copy-start.4 = (bf16[128,2048]{1,0:T(8,128)(2,1)S(1)}, bf16[128,2048]{1,0:T(8,128)(2,1)}, u32[]{:S(2)}) copy-start(bf16[128,2048]{1,0:T(8,128)(2,1)} %copy-done.3) | copy-start | bytes 1572868
  49.2 10.4 %collective-permute-start.15 = (bf16[128,2048]{1,0:T(8,128)(2,1)S(1)}, bf16[128,2048]{1,0:T(8,128)(2,1)S(1)}, u32[]{:S(2)}, u32[]{:S(2)}) collective-permute-start(bf16[128,2048]{1,0:T(8,128)(2,1)S(1)} %copy-done.6), channel_id=1, source_target_pairs={{0,64},{32,96},{64,0},{96,32},{1,65},{33,97},{65,1},{97,33},{2,66}... | collective-permute-start | bytes 1572872 | tf_op jit(solution)/shard_map/ppermute | solution.py:53
  53.3 10.3 %collective-permute-start.13 = (bf16[2048,128]{1,0:T(8,128)(2,1)S(1)}, bf16[2048,128]{1,0:T(8,128)(2,1)S(1)}, u32[]{:S(2)}, u32[]{:S(2)}) collective-permute-start(bf16[2048,128]{1,0:T(8,128)(2,1)S(1)} %get-tuple-element.88), channel_id=1, source_target_pairs={{0,16},{2,18},{4,20},{6,22},{8,24},{10,26},{12,28},{14,30},{16,0},... | collective-permute-start | bytes 1572872 | tf_op jit(solution)/shard_map/ppermute | solution.py:41
  53.4 10.4 %collective-permute-start.9 = (bf16[2048,128]{1,0:T(8,128)(2,1)S(1)}, bf16[2048,128]{1,0:T(8,128)(2,1)S(1)}, u32[]{:S(2)}, u32[]{:S(2)}) collective-permute-start(bf16[2048,128]{1,0:T(8,128)(2,1)S(1)} %get-tuple-element.80), channel_id=1, source_target_pairs={{0,4},{2,6},{4,0},{6,2},{8,12},{10,14},{12,8},{14,10},{16,20},{18,... | collective-permute-start | bytes 1572872 | tf_op jit(solution)/shard_map/ppermute | solution.py:41
  59.6 15.7 %collective-permute-start.16 = (bf16[128,2048]{1,0:T(8,128)(2,1)S(1)}, bf16[128,2048]{1,0:T(8,128)(2,1)S(1)}, u32[]{:S(2)}, u32[]{:S(2)}) collective-permute-start(bf16[128,2048]{1,0:T(8,128)(2,1)S(1)} %copy-done.4), channel_id=1, source_target_pairs={{0,64},{32,96},{64,0},{96,32},{1,65},{33,97},{65,1},{97,33},{2,66}... | collective-permute-start | bytes 1572872 | tf_op jit(solution)/shard_map/ppermute | solution.py:53
  66.9 9.3 %collective-permute-start.14 = (bf16[256,512]{1,0:T(8,128)(2,1)S(1)}, bf16[256,512]{1,0:T(8,128)(2,1)S(1)}, u32[]{:S(2)}, u32[]{:S(2)}) collective-permute-start(bf16[256,512]{1,0:T(8,128)(2,1)S(1)} %attend.4.mine_ref), channel_id=1, source_target_pairs={{0,64},{32,96},{64,0},{96,32},{1,65},{33,97},{65,1},{97,33},{2,66}... | collective-permute-start | bytes 786440 | tf_op jit(solution)/shard_map/ppermute | solution.py:53
  72.3 17.4 %collective-permute-start.20 = (bf16[256,512]{1,0:T(8,128)(2,1)S(1)}, bf16[256,512]{1,0:T(8,128)(2,1)S(1)}, u32[]{:S(2)}, u32[]{:S(2)}) collective-permute-start(bf16[256,512]{1,0:T(8,128)(2,1)S(1)} %attend.5.mine_ref), channel_id=1, source_target_pairs={{0,64},{32,96},{64,0},{96,32},{1,65},{33,97},{65,1},{97,33},{2,66}... | collective-permute-start | bytes 786440 | tf_op jit(solution)/shard_map/ppermute | solution.py:53
  77.5 14.2 %collective-permute-start.18 = (bf16[256,512]{1,0:T(8,128)(2,1)S(1)}, bf16[256,512]{1,0:T(8,128)(2,1)S(1)}, u32[]{:S(2)}, u32[]{:S(2)}) collective-permute-start(bf16[256,512]{1,0:T(8,128)(2,1)S(1)} %get-tuple-element.100), channel_id=1, source_target_pairs={{0,32},{32,0},{64,96},{96,64},{1,33},{33,1},{65,97},{97,65},{2,34}... | collective-permute-start | bytes 786440 | tf_op jit(solution)/shard_map/ppermute | solution.py:53
  85.0 9.8 %collective-permute-start.24 = (bf16[256,512]{1,0:T(8,128)(2,1)S(1)}, bf16[256,512]{1,0:T(8,128)(2,1)S(1)}, u32[]{:S(2)}, u32[]{:S(2)}) collective-permute-start(bf16[256,512]{1,0:T(8,128)(2,1)S(1)} %attend.6.mine_ref), channel_id=1, source_target_pairs={{0,64},{32,96},{64,0},{96,32},{1,65},{33,97},{65,1},{97,33},{2,66}... | collective-permute-start | bytes 786440 | tf_op jit(solution)/shard_map/ppermute | solution.py:53
  91.0 6.0 %collective-permute-start.22 = (bf16[256,512]{1,0:T(8,128)(2,1)S(1)}, bf16[256,512]{1,0:T(8,128)(2,1)S(1)}, u32[]{:S(2)}, u32[]{:S(2)}) collective-permute-start(bf16[256,512]{1,0:T(8,128)(2,1)S(1)} %get-tuple-element.108), channel_id=1, source_target_pairs={{0,32},{32,0},{64,96},{96,64},{1,33},{33,1},{65,97},{97,65},{2,34}... | collective-permute-start | bytes 786440 | tf_op jit(solution)/shard_map/ppermute | solution.py:53
  91.5 5.7 %collective-permute-start.17 = (bf16[256,512]{1,0:T(8,128)(2,1)S(1)}, bf16[256,512]{1,0:T(8,128)(2,1)S(1)}, u32[]{:S(2)}, u32[]{:S(2)}) collective-permute-start(bf16[256,512]{1,0:T(8,128)(2,1)S(1)} %get-tuple-element.98), channel_id=1, source_target_pairs={{0,32},{32,0},{64,96},{96,64},{1,33},{33,1},{65,97},{97,65},{2,34}... | collective-permute-start | bytes 786440 | tf_op jit(solution)/shard_map/ppermute | solution.py:53
  91.7 8.8 %collective-permute-start.19 = (bf16[256,512]{1,0:T(8,128)(2,1)S(1)}, bf16[256,512]{1,0:T(8,128)(2,1)S(1)}, u32[]{:S(2)}, u32[]{:S(2)}) collective-permute-start(bf16[256,512]{1,0:T(8,128)(2,1)S(1)} %add_convert_fusion.7), channel_id=1, source_target_pairs={{0,65},{32,97},{64,1},{96,33},{1,64},{33,96},{65,0},{97,32},{2,67}... | collective-permute-start | bytes 786440 | tf_op jit(solution)/shard_map/ppermute | solution.py:53
  93.9 8.0 %collective-permute-start.28 = (bf16[256,512]{1,0:T(8,128)(2,1)S(1)}, bf16[256,512]{1,0:T(8,128)(2,1)S(1)}, u32[]{:S(2)}, u32[]{:S(2)}) collective-permute-start(bf16[256,512]{1,0:T(8,128)(2,1)S(1)} %attend.7.mine_ref), channel_id=1, source_target_pairs={{0,64},{32,96},{64,0},{96,32},{1,65},{33,97},{65,1},{97,33},{2,66}... | collective-permute-start | bytes 786440 | tf_op jit(solution)/shard_map/ppermute | solution.py:53
  94.8 9.4 %collective-permute-start.21 = (bf16[256,512]{1,0:T(8,128)(2,1)S(1)}, bf16[256,512]{1,0:T(8,128)(2,1)S(1)}, u32[]{:S(2)}, u32[]{:S(2)}) collective-permute-start(bf16[256,512]{1,0:T(8,128)(2,1)S(1)} %get-tuple-element.106), channel_id=1, source_target_pairs={{0,32},{32,0},{64,96},{96,64},{1,33},{33,1},{65,97},{97,65},{2,34}... | collective-permute-start | bytes 786440 | tf_op jit(solution)/shard_map/ppermute | solution.py:53
  97.0 7.0 %collective-permute-start.26 = (bf16[256,512]{1,0:T(8,128)(2,1)S(1)}, bf16[256,512]{1,0:T(8,128)(2,1)S(1)}, u32[]{:S(2)}, u32[]{:S(2)}) collective-permute-start(bf16[256,512]{1,0:T(8,128)(2,1)S(1)} %get-tuple-element.114), channel_id=1, source_target_pairs={{0,32},{32,0},{64,96},{96,64},{1,33},{33,1},{65,97},{97,65},{2,34}... | collective-permute-start | bytes 786440 | tf_op jit(solution)/shard_map/ppermute | solution.py:53
  97.2 9.1 %collective-permute-start.23 = (bf16[256,512]{1,0:T(8,128)(2,1)S(1)}, bf16[256,512]{1,0:T(8,128)(2,1)S(1)}, u32[]{:S(2)}, u32[]{:S(2)}) collective-permute-start(bf16[256,512]{1,0:T(8,128)(2,1)S(1)} %add_convert_fusion.5), channel_id=1, source_target_pairs={{0,65},{32,97},{64,1},{96,33},{1,64},{33,96},{65,0},{97,32},{2,67}... | collective-permute-start | bytes 786440 | tf_op jit(solution)/shard_map/ppermute | solution.py:53
  100.5 8.2 %collective-permute-start.25 = (bf16[256,512]{1,0:T(8,128)(2,1)S(1)}, bf16[256,512]{1,0:T(8,128)(2,1)S(1)}, u32[]{:S(2)}, u32[]{:S(2)}) collective-permute-start(bf16[256,512]{1,0:T(8,128)(2,1)S(1)} %get-tuple-element.112), channel_id=1, source_target_pairs={{0,32},{32,0},{64,96},{96,64},{1,33},{33,1},{65,97},{97,65},{2,34}... | collective-permute-start | bytes 786440 | tf_op jit(solution)/shard_map/ppermute | solution.py:53
  103.2 9.9 %collective-permute-start.29 = (bf16[256,512]{1,0:T(8,128)(2,1)S(1)}, bf16[256,512]{1,0:T(8,128)(2,1)S(1)}, u32[]{:S(2)}, u32[]{:S(2)}) collective-permute-start(bf16[256,512]{1,0:T(8,128)(2,1)S(1)} %get-tuple-element.119), channel_id=1, source_target_pairs={{0,32},{32,0},{64,96},{96,64},{1,33},{33,1},{65,97},{97,65},{2,34}... | collective-permute-start | bytes 786440 | tf_op jit(solution)/shard_map/ppermute | solution.py:53
  104.0 2.5 %collective-permute-start.30 = (bf16[256,512]{1,0:T(8,128)(2,1)S(1)}, bf16[256,512]{1,0:T(8,128)(2,1)S(1)}, u32[]{:S(2)}, u32[]{:S(2)}) collective-permute-start(bf16[256,512]{1,0:T(8,128)(2,1)S(1)} %get-tuple-element.121), channel_id=1, source_target_pairs={{0,32},{32,0},{64,96},{96,64},{1,33},{33,1},{65,97},{97,65},{2,34}... | collective-permute-start | bytes 786440 | tf_op jit(solution)/shard_map/ppermute | solution.py:53
  104.2 8.8 %collective-permute-start.27 = (bf16[256,512]{1,0:T(8,128)(2,1)S(1)}, bf16[256,512]{1,0:T(8,128)(2,1)S(1)}, u32[]{:S(2)}, u32[]{:S(2)}) collective-permute-start(bf16[256,512]{1,0:T(8,128)(2,1)S(1)} %add_convert_fusion.3), channel_id=1, source_target_pairs={{0,65},{32,97},{64,1},{96,33},{1,64},{33,96},{65,0},{97,32},{2,67}... | collective-permute-start | bytes 786440 | tf_op jit(solution)/shard_map/ppermute | solution.py:53
  106.5 12.0 %collective-permute-start.31 = (bf16[256,512]{1,0:T(8,128)(2,1)S(1)}, bf16[256,512]{1,0:T(8,128)(2,1)S(1)}, u32[]{:S(2)}, u32[]{:S(2)}) collective-permute-start(bf16[256,512]{1,0:T(8,128)(2,1)S(1)} %add_convert_fusion.1), channel_id=1, source_target_pairs={{0,65},{32,97},{64,1},{96,33},{1,64},{33,96},{65,0},{97,32},{2,67}... | collective-permute-start | bytes 786440 | tf_op jit(solution)/shard_map/ppermute | solution.py:53

commit v7 on v6

--- a/solution.py
+++ b/solution.py
@@ -412,7 +412,10 @@
         sent.append(send)
         total = keep_own + got_own.astype(jnp.float32) + far.astype(jnp.float32)
         outs.append(total.astype(jnp.bfloat16))
-    return jnp.concatenate(outs, axis=0)
+    whole = jnp.zeros((sum(CHUNKS) * TILE, outs[0].shape[1]), outs[0].dtype)
+    for start, part in zip(starts, outs):
+        whole = lax.dynamic_update_slice_in_dim(whole, part, start * TILE, 0)
+    return whole
 
 
 def solution(mesh):

time: 120 us -> 120 us (level)
    unnamed x24 -> x26, local copies, waits for them, and re-layouts: 4.88 us -> 4.88 us
where the time goes in v7:
time: 120 us; the launch traced here: 119 us
  starting transfers between devices  42.5 us (35%)
  Pallas kernels  41.3 us (34%)
  waiting for transfers between devices  28.6 us (24%)
  local copies, waits for them, and re-layouts  5.13 us (4%)
  other arithmetic  1.6 us (1%)
    ppermute x20, starting transfers between devices, along_z(): return lax.ppermute(value, SECTION_HEAD, pairs)  27.1 us
    ppermute x20, waiting for transfers between devices, along_z(): return lax.ppermute(value, SECTION_HEAD, pairs)  18 us
    ppermute x12, starting transfers between devices, along_seq(): return lax.ppermute(value, 'seq', pairs)  15.4 us
    pallas_call x4, Pallas kernels, attend(): pl.pallas_call(functools.partial(attend_body, first_tile), in_specs=[SMEM...  11.9 us
    ppermute x12, waiting for transfers between devices, along_seq(): return lax.ppermute(value, 'seq', pairs)  10.6 us
    pallas_call x1, Pallas kernels, queries_of(): pl.pallas_call(ask_body, grid=(steps,), in_specs=[pl.BlockSpec((rows // s...  9.63 us
    pallas_call x2, Pallas kernels, pick(): pl.pallas_call(pick_body, grid_spec=pltpu.PrefetchScalarGridSpec(num_scal...  7.07 us
    pallas_call x4, Pallas kernels, multiply(): pl.pallas_call(multiply_body, in_specs=[VMEM_WHOLE] * 3, out_specs=[VMEM_...  5.18 us
  transfers between devices with their start and end apart: 32, of which 9 were waited for; matrix products, arithmetic and copies ran while one was open for 2% of the time, Pallas kernels for 31%

profile of v7, /device:TPU:1, one launch (start us, length us, event | category | flops | bytes accessed | tf_op | source)
XLA Modules:
  0.0 119.5 jit_solution(16807852545300401300)
XLA Ops:
  0.7 4.7 %project.1 = (bf16[2064,128]{1,0:T(8,128)(2,1)S(1)}, bf16[2064,128]{1,0:T(8,128)(2,1)S(1)}, s32[8,128]{1,0:T(8,128)S(1)}) custom-call(s32[8,16]{1,0:T(8,128)S(1)} %copy-done.1, bf16[2048,1024]{1,0:T(8,128)(2,1)} %x_ref.1, bf16[1024,128]{1,0:T(8,128)(2,1)} %wk_ref.1, bf16[1024,128]{1,0:T(8,128)(2,1)} %wv_ref.1), custom_call_target="tpu_custom_call" | custom-call | flops 1 | bytes 1 | tf_op jit(solution)/shard_map/project/pallas_call | solution.py:135
  5.4 2.2 %collective-permute-start.5 = (bf16[2064,128]{1,0:T(8,128)(2,1)S(1)}, bf16[2064,128]{1,0:T(8,128)(2,1)S(1)}, u32[]{:S(2)}, u32[]{:S(2)}) collective-permute-start(bf16[2064,128]{1,0:T(8,128)(2,1)S(1)} %get-tuple-element.75.refs_4_), channel_id=1, source_target_pairs={{0,2},{2,4},{4,6},{6,0},{8,10},{10,12},{12,14},{14,8},{16,18},{18,... | collective-permute-start | bytes 1585160 | tf_op jit(solution)/shard_map/ppermute | solution.py:41
  7.6 1.2 %collective-permute-start = (bf16[2064,128]{1,0:T(8,128)(2,1)S(1)}, bf16[2064,128]{1,0:T(8,128)(2,1)S(1)}, u32[]{:S(2)}, u32[]{:S(2)}) collective-permute-start(bf16[2064,128]{1,0:T(8,128)(2,1)S(1)} %get-tuple-element.73.refs_0_), channel_id=1, source_target_pairs={{0,8},{2,10},{4,12},{6,14},{8,16},{10,18},{12,20},{14,22},{16,24},... | collective-permute-start | bytes 1585160 | tf_op jit(solution)/shard_map/ppermute | solution.py:41
  8.8 1.5 %collective-permute-start.4 = (bf16[2064,128]{1,0:T(8,128)(2,1)S(1)}, bf16[2064,128]{1,0:T(8,128)(2,1)}, u32[]{:S(2)}, u32[]{:S(2)}) collective-permute-start(bf16[2064,128]{1,0:T(8,128)(2,1)S(1)} %get-tuple-element.75.refs_4_), channel_id=1, source_target_pairs={{0,6},{2,0},{4,2},{6,4},{8,14},{10,8},{12,10},{14,12},{16,22},{18,... | collective-permute-start | bytes 1585160 | tf_op jit(solution)/shard_map/ppermute | solution.py:41
  10.3 1.5 %collective-permute-start.2 = (bf16[2064,128]{1,0:T(8,128)(2,1)S(1)}, bf16[2064,128]{1,0:T(8,128)(2,1)}, u32[]{:S(2)}, u32[]{:S(2)}) collective-permute-start(bf16[2064,128]{1,0:T(8,128)(2,1)S(1)} %get-tuple-element.73.refs_0_), channel_id=1, source_target_pairs={{0,24},{2,26},{4,28},{6,30},{8,0},{10,2},{12,4},{14,6},{16,8},{18,... | collective-permute-start | bytes 1585160 | tf_op jit(solution)/shard_map/ppermute | solution.py:41
  11.8 4.1 %pick.2 = (bf16[112,2048]{1,0:T(8,128)(2,1)}, bf16[144,2048]{1,0:T(8,128)(2,1)S(1)}, bf16[128,2048]{1,0:T(8,128)(2,1)S(1)}, bf16[128,2048]{1,0:T(8,128)(2,1)S(1)}) custom-call(s32[4]{0:T(128)S(1)} %get-tuple-element.125.places_ref, bf16[512,4096]{1,0:T(8,128)(2,1)} %w_ref.3), custom_call_target="tpu_custom_call" | custom-call | flops 1 | bytes 1 | tf_op jit(solution)/shard_map/pick/pallas_call | solution.py:258
  15.9 0.8 copy-done.2
  16.7 0.8 copy-done.3
  17.5 0.8 copy-done.5
  18.3 2.3 %collective-permute-done.5.refs_7_ = bf16[2064,128]{1,0:T(8,128)(2,1)S(1)} collective-permute-done((bf16[2064,128]{1,0:T(8,128)(2,1)S(1)}, bf16[2064,128]{1,0:T(8,128)(2,1)S(1)}, u32[]{:S(2)}, u32[]{:S(2)}) %collective-permute-start.5) | collective-permute-done | bytes 528416 | tf_op jit(solution)/shard_map/ppermute | solution.py:41
  20.6 1.6 %collective-permute-start.6 = (bf16[2064,128]{1,0:T(8,128)(2,1)S(1)}, bf16[2064,128]{1,0:T(8,128)(2,1)}, u32[]{:S(2)}, u32[]{:S(2)}) collective-permute-start(bf16[2064,128]{1,0:T(8,128)(2,1)S(1)} %get-tuple-element.75.refs_4_), channel_id=1, source_target_pairs={{0,4},{2,6},{4,0},{6,2},{8,12},{10,14},{12,8},{14,10},{16,20},{18,... | collective-permute-start | bytes 1585160 | tf_op jit(solution)/shard_map/ppermute | solution.py:41
  22.2 2.7 %collective-permute-start.3 = (bf16[2064,128]{1,0:T(8,128)(2,1)S(1)}, bf16[2064,128]{1,0:T(8,128)(2,1)}, u32[]{:S(2)}, u32[]{:S(2)}) collective-permute-start(bf16[2064,128]{1,0:T(8,128)(2,1)S(1)} %get-tuple-element.73.refs_0_), channel_id=1, source_target_pairs={{0,16},{2,18},{4,20},{6,22},{8,24},{10,26},{12,28},{14,30},{16,0},... | collective-permute-start | bytes 1585160 | tf_op jit(solution)/shard_map/ppermute | solution.py:41
  24.9 1.6 %collective-permute-start.1 = (bf16[112,2048]{1,0:T(8,128)(2,1)}, bf16[112,2048]{1,0:T(8,128)(2,1)}, u32[]{:S(2)}, u32[]{:S(2)}) collective-permute-start(bf16[112,2048]{1,0:T(8,128)(2,1)} %get-tuple-element.69), channel_id=1, source_target_pairs={{0,64},{32,96},{64,0},{96,32},{1,65},{33,97},{65,1},{97,33},{2,66}... | collective-permute-start | bytes 1376264 | tf_op jit(solution)/shard_map/ppermute | solution.py:53
  26.6 9.6 %ask.1.q_ref = bf16[1024,512]{1,0:T(8,128)(2,1)S(1)} custom-call(bf16[1024,4096]{1,0:T(8,128)(2,1)} %x_ref.2, f32[1,4096]{1,0:T(1,128)S(1)} %bitcast.11, bf16[4096,512]{1,0:T(8,128)(2,1)} %w_ref.1), custom_call_target="tpu_custom_call" | custom-call | flops 1 | bytes 1 | tf_op jit(solution)/shard_map/ask/pallas_call | solution.py:308
  36.9 2.8 %pack.1 = (bf16[2048,128]{1,0:T(8,128)(2,1)S(1)}, bf16[2048,128]{1,0:T(8,128)(2,1)S(1)}, bf16[2048,128]{1,0:T(8,128)(2,1)S(1)}, bf16[2048,128]{1,0:T(8,128)(2,1)...) custom-call(s32[2]{0:T(128)S(1)} %pad_add_fusion.place_ref, ...), custom_call_target="tpu_custom_call" | custom-call | flops 1 | bytes 1 | tf_op jit(solution)/shard_map/pack/pallas_call | solution.py:187
  39.8 0.8 collective-permute-start.7
  41.3 1.1 collective-permute-start.10
  42.8 3.0 %pick.3 = bf16[512,2048]{1,0:T(8,128)(2,1)S(1)} custom-call(s32[4]{0:T(128)S(1)} %get-tuple-element.126.places_ref, bf16[512,4096]{1,0:T(8,128)(2,1)} %w_ref.3), custom_call_target="tpu_custom_call" | custom-call | flops 1 | bytes 1 | tf_op jit(solution)/shard_map/pick/pallas_call | solution.py:258
  46.1 1.1 constant_dynamic-update-slice_fusion.11
  47.2 1.9 %collective-permute-done.12 = bf16[144,2048]{1,0:T(8,128)(2,1)S(1)} collective-permute-done((bf16[144,2048]{1,0:T(8,128)(2,1)}, bf16[144,2048]{1,0:T(8,128)(2,1)S(1)}, u32[]{:S(2)}, u32[]{:S(2)}) %collective-permute-start.12) | collective-permute-done | bytes 589856 | tf_op jit(solution)/shard_map/ppermute | solution.py:53
  49.1 4.2 %collective-permute-done.11 = bf16[2048,128]{1,0:T(8,128)(2,1)S(1)} collective-permute-done((bf16[2048,128]{1,0:T(8,128)(2,1)S(1)}, bf16[2048,128]{1,0:T(8,128)(2,1)S(1)}, u32[]{:S(2)}, u32[]{:S(2)}) %collective-permute-start.11) | collective-permute-done | bytes 524320 | tf_op jit(solution)/shard_map/ppermute | solution.py:41
  53.4 1.7 %collective-permute-start.9 = (bf16[2048,128]{1,0:T(8,128)(2,1)S(1)}, bf16[2048,128]{1,0:T(8,128)(2,1)S(1)}, u32[]{:S(2)}, u32[]{:S(2)}) collective-permute-start(bf16[2048,128]{1,0:T(8,128)(2,1)S(1)} %get-tuple-element.80), channel_id=1, source_target_pairs={{0,4},{2,6},{4,0},{6,2},{8,12},{10,14},{12,8},{14,10},{16,20},{18,... | collective-permute-start | bytes 1572872 | tf_op jit(solution)/shard_map/ppermute | solution.py:41
  55.2 4.3 %collective-permute-done.15 = bf16[128,2048]{1,0:T(8,128)(2,1)S(1)} collective-permute-done((bf16[128,2048]{1,0:T(8,128)(2,1)S(1)}, bf16[128,2048]{1,0:T(8,128)(2,1)S(1)}, u32[]{:S(2)}, u32[]{:S(2)}) %collective-permute-start.15) | collective-permute-done | bytes 524320 | tf_op jit(solution)/shard_map/ppermute | solution.py:53
  59.5 4.1 %collective-permute-done.13 = bf16[2048,128]{1,0:T(8,128)(2,1)S(1)} collective-permute-done((bf16[2048,128]{1,0:T(8,128)(2,1)S(1)}, bf16[2048,128]{1,0:T(8,128)(2,1)S(1)}, u32[]{:S(2)}, u32[]{:S(2)}) %collective-permute-start.13) | collective-permute-done | bytes 524320 | tf_op jit(solution)/shard_map/ppermute | solution.py:41
  63.9 3.0 %attend.4.mine_ref = bf16[256,512]{1,0:T(8,128)(2,1)S(1)} custom-call(s32[8,128]{1,0:T(8,128)S(1)} %get-tuple-element.103.slots_ref, s32[2]{0:T(128)S(1)} %pad_add_fusion.place_ref, bf16[1024,512]{1,0:T(8,128)(2,1)S(1)} %ask.1.q_ref, bf16[8192,128]{1,0:T(8,128)(2,1)S(1)} %constant_dynamic-update-slice_fusion.k_ref, ...), custom_call_target="tpu_custom_call" | custom-call | flops 1 | bytes 1 | tf_op jit(solution)/shard_map/attend/pallas_call | solution.py:237
  66.9 2.4 %collective-permute-start.14 = (bf16[256,512]{1,0:T(8,128)(2,1)S(1)}, bf16[256,512]{1,0:T(8,128)(2,1)S(1)}, u32[]{:S(2)}, u32[]{:S(2)}) collective-permute-start(bf16[256,512]{1,0:T(8,128)(2,1)S(1)} %attend.4.mine_ref), channel_id=1, source_target_pairs={{0,64},{32,96},{64,0},{96,32},{1,65},{33,97},{65,1},{97,33},{2,66}... | collective-permute-start | bytes 786440 | tf_op jit(solution)/shard_map/ppermute | solution.py:53
  69.3 3.0 %attend.5.mine_ref = bf16[256,512]{1,0:T(8,128)(2,1)S(1)} custom-call(s32[8,128]{1,0:T(8,128)S(1)} %get-tuple-element.103.slots_ref, s32[2]{0:T(128)S(1)} %pad_add_fusion.place_ref, bf16[1024,512]{1,0:T(8,128)(2,1)S(1)} %ask.1.q_ref, bf16[8192,128]{1,0:T(8,128)(2,1)S(1)} %constant_dynamic-update-slice_fusion.k_ref, ...), custom_call_target="tpu_custom_call" | custom-call | flops 1 | bytes 1 | tf_op jit(solution)/shard_map/attend/pallas_call | solution.py:237
  72.4 3.0 %attend.6.mine_ref = bf16[256,512]{1,0:T(8,128)(2,1)S(1)} custom-call(s32[8,128]{1,0:T(8,128)S(1)} %get-tuple-element.103.slots_ref, s32[2]{0:T(128)S(1)} %pad_add_fusion.place_ref, bf16[1024,512]{1,0:T(8,128)(2,1)S(1)} %ask.1.q_ref, bf16[8192,128]{1,0:T(8,128)(2,1)S(1)} %constant_dynamic-update-slice_fusion.k_ref, ...), custom_call_target="tpu_custom_call" | custom-call | flops 1 | bytes 1 | tf_op jit(solution)/shard_map/attend/pallas_call | solution.py:237
  75.4 0.8 collective-permute-done.14.near_ref
  76.2 1.3 %multiply.4 = (bf16[256,512]{1,0:T(8,128)(2,1)S(1)}, bf16[256,512]{1,0:T(8,128)(2,1)S(1)}, f32[256,512]{1,0:T(8,128)S(1)}, f32[256,512]{1,0:T(8,128)S(1)}) custom-call(bf16[256,512]{1,0:T(8,128)(2,1)S(1)} %attend.4.mine_ref, bf16[256,512]{1,0:T(8,128)(2,1)S(1)} %collective-permute-done.14.near_ref, ...), custom_call_target="tpu_custom_call" | custom-call | flops 1 | bytes 1 | tf_op jit(solution)/shard_map/multiply/pallas_call | solution.py:286
  77.5 7.5 %collective-permute-start.18 = (bf16[256,512]{1,0:T(8,128)(2,1)S(1)}, bf16[256,512]{1,0:T(8,128)(2,1)S(1)}, u32[]{:S(2)}, u32[]{:S(2)}) collective-permute-start(bf16[256,512]{1,0:T(8,128)(2,1)S(1)} %get-tuple-element.100), channel_id=1, source_target_pairs={{0,32},{32,0},{64,96},{96,64},{1,33},{33,1},{65,97},{97,65},{2,34}... | collective-permute-start | bytes 786440 | tf_op jit(solution)/shard_map/ppermute | solution.py:53
  85.0 1.8 %collective-permute-start.24 = (bf16[256,512]{1,0:T(8,128)(2,1)S(1)}, bf16[256,512]{1,0:T(8,128)(2,1)S(1)}, u32[]{:S(2)}, u32[]{:S(2)}) collective-permute-start(bf16[256,512]{1,0:T(8,128)(2,1)S(1)} %attend.6.mine_ref), channel_id=1, source_target_pairs={{0,64},{32,96},{64,0},{96,32},{1,65},{33,97},{65,1},{97,33},{2,66}... | collective-permute-start | bytes 786440 | tf_op jit(solution)/shard_map/ppermute | solution.py:53
  86.7 3.0 %attend.7.mine_ref = bf16[256,512]{1,0:T(8,128)(2,1)S(1)} custom-call(s32[8,128]{1,0:T(8,128)S(1)} %get-tuple-element.103.slots_ref, s32[2]{0:T(128)S(1)} %pad_add_fusion.place_ref, bf16[1024,512]{1,0:T(8,128)(2,1)S(1)} %ask.1.q_ref, bf16[8192,128]{1,0:T(8,128)(2,1)S(1)} %constant_dynamic-update-slice_fusion.k_ref, ...), custom_call_target="tpu_custom_call" | custom-call | flops 1 | bytes 1 | tf_op jit(solution)/shard_map/attend/pallas_call | solution.py:237
  89.7 1.3 %multiply.5 = (bf16[256,512]{1,0:T(8,128)(2,1)S(1)}, bf16[256,512]{1,0:T(8,128)(2,1)S(1)}, f32[256,512]{1,0:T(8,128)S(1)}, f32[256,512]{1,0:T(8,128)S(1)}) custom-call(bf16[256,512]{1,0:T(8,128)(2,1)S(1)} %attend.5.mine_ref, bf16[256,512]{1,0:T(8,128)(2,1)S(1)} %collective-permute-done.20.near_ref, ...), custom_call_target="tpu_custom_call" | custom-call | flops 1 | bytes 1 | tf_op jit(solution)/shard_map/multiply/pallas_call | solution.py:286
  91.7 2.2 %collective-permute-start.19 = (bf16[256,512]{1,0:T(8,128)(2,1)S(1)}, bf16[256,512]{1,0:T(8,128)(2,1)S(1)}, u32[]{:S(2)}, u32[]{:S(2)}) collective-permute-start(bf16[256,512]{1,0:T(8,128)(2,1)S(1)} %add_convert_fusion.7), channel_id=1, source_target_pairs={{0,65},{32,97},{64,1},{96,33},{1,64},{33,96},{65,0},{97,32},{2,67}... | collective-permute-start | bytes 786440 | tf_op jit(solution)/shard_map/ppermute | solution.py:53
  93.9 0.9 collective-permute-start.28
  94.8 0.9 collective-permute-start.21
  95.7 1.3 %multiply.6 = (bf16[256,512]{1,0:T(8,128)(2,1)S(1)}, bf16[256,512]{1,0:T(8,128)(2,1)S(1)}, f32[256,512]{1,0:T(8,128)S(1)}, f32[256,512]{1,0:T(8,128)S(1)}) custom-call(bf16[256,512]{1,0:T(8,128)(2,1)S(1)} %attend.6.mine_ref, bf16[256,512]{1,0:T(8,128)(2,1)S(1)} %collective-permute-done.24.near_ref, ...), custom_call_target="tpu_custom_call" | custom-call | flops 1 | bytes 1 | tf_op jit(solution)/shard_map/multiply/pallas_call | solution.py:286
  97.2 2.0 %collective-permute-start.23 = (bf16[256,512]{1,0:T(8,128)(2,1)S(1)}, bf16[256,512]{1,0:T(8,128)(2,1)S(1)}, u32[]{:S(2)}, u32[]{:S(2)}) collective-permute-start(bf16[256,512]{1,0:T(8,128)(2,1)S(1)} %add_convert_fusion.5), channel_id=1, source_target_pairs={{0,65},{32,97},{64,1},{96,33},{1,64},{33,96},{65,0},{97,32},{2,67}... | collective-permute-start | bytes 786440 | tf_op jit(solution)/shard_map/ppermute | solution.py:53
  99.1 1.4 %collective-permute-done.19 = bf16[256,512]{1,0:T(8,128)(2,1)S(1)} collective-permute-done((bf16[256,512]{1,0:T(8,128)(2,1)S(1)}, bf16[256,512]{1,0:T(8,128)(2,1)S(1)}, u32[]{:S(2)}, u32[]{:S(2)}) %collective-permute-start.19) | collective-permute-done | bytes 262176 | tf_op jit(solution)/shard_map/ppermute | solution.py:53
  100.5 1.3 %collective-permute-start.25 = (bf16[256,512]{1,0:T(8,128)(2,1)S(1)}, bf16[256,512]{1,0:T(8,128)(2,1)S(1)}, u32[]{:S(2)}, u32[]{:S(2)}) collective-permute-start(bf16[256,512]{1,0:T(8,128)(2,1)S(1)} %get-tuple-element.112), channel_id=1, source_target_pairs={{0,32},{32,0},{64,96},{96,64},{1,33},{33,1},{65,97},{97,65},{2,34}... | collective-permute-start | bytes 786440 | tf_op jit(solution)/shard_map/ppermute | solution.py:53
  101.9 1.3 %multiply.7 = (bf16[256,512]{1,0:T(8,128)(2,1)S(1)}, bf16[256,512]{1,0:T(8,128)(2,1)S(1)}, f32[256,512]{1,0:T(8,128)S(1)}, f32[256,512]{1,0:T(8,128)S(1)}) custom-call(bf16[256,512]{1,0:T(8,128)(2,1)S(1)} %attend.7.mine_ref, bf16[256,512]{1,0:T(8,128)(2,1)S(1)} %collective-permute-done.28.near_ref, ...), custom_call_target="tpu_custom_call" | custom-call | flops 1 | bytes 1 | tf_op jit(solution)/shard_map/multiply/pallas_call | solution.py:286
  103.3 0.8 collective-permute-start.29
  104.3 2.2 %collective-permute-start.27 = (bf16[256,512]{1,0:T(8,128)(2,1)S(1)}, bf16[256,512]{1,0:T(8,128)(2,1)S(1)}, u32[]{:S(2)}, u32[]{:S(2)}) collective-permute-start(bf16[256,512]{1,0:T(8,128)(2,1)S(1)} %add_convert_fusion.3), channel_id=1, source_target_pairs={{0,65},{32,97},{64,1},{96,33},{1,64},{33,96},{65,0},{97,32},{2,67}... | collective-permute-start | bytes 786440 | tf_op jit(solution)/shard_map/ppermute | solution.py:53
  106.6 2.2 %collective-permute-start.31 = (bf16[256,512]{1,0:T(8,128)(2,1)S(1)}, bf16[256,512]{1,0:T(8,128)(2,1)S(1)}, u32[]{:S(2)}, u32[]{:S(2)}) collective-permute-start(bf16[256,512]{1,0:T(8,128)(2,1)S(1)} %add_convert_fusion.1), channel_id=1, source_target_pairs={{0,65},{32,97},{64,1},{96,33},{1,64},{33,96},{65,0},{97,32},{2,67}... | collective-permute-start | bytes 786440 | tf_op jit(solution)/shard_map/ppermute | solution.py:53
  108.8 4.2 %collective-permute-done.27 = bf16[256,512]{1,0:T(8,128)(2,1)S(1)} collective-permute-done((bf16[256,512]{1,0:T(8,128)(2,1)S(1)}, bf16[256,512]{1,0:T(8,128)(2,1)S(1)}, u32[]{:S(2)}, u32[]{:S(2)}) %collective-permute-start.27) | collective-permute-done | bytes 262176 | tf_op jit(solution)/shard_map/ppermute | solution.py:53
  113.2 5.5 %collective-permute-done.31 = bf16[256,512]{1,0:T(8,128)(2,1)S(1)} collective-permute-done((bf16[256,512]{1,0:T(8,128)(2,1)S(1)}, bf16[256,512]{1,0:T(8,128)(2,1)S(1)}, u32[]{:S(2)}, u32[]{:S(2)}) %collective-permute-start.31) | collective-permute-done | bytes 262176 | tf_op jit(solution)/shard_map/ppermute | solution.py:53
  118.6 0.8 fusion.1
  (69 shorter events, 5.0 us)
Async XLA Ops:
  0.0 0.7 copy-start.1
  5.4 15.2 %collective-permute-start.5 = (bf16[2064,128]{1,0:T(8,128)(2,1)S(1)}, bf16[2064,128]{1,0:T(8,128)(2,1)S(1)}, u32[]{:S(2)}, u32[]{:S(2)}) collective-permute-start(bf16[2064,128]{1,0:T(8,128)(2,1)S(1)} %get-tuple-element.75.refs_4_), channel_id=1, source_target_pairs={{0,2},{2,4},{4,6},{6,0},{8,10},{10,12},{12,14},{14,8},{16,18},{18,... | collective-permute-start | bytes 1585160 | tf_op jit(solution)/shard_map/ppermute | solution.py:41
  7.6 14.6 %collective-permute-start = (bf16[2064,128]{1,0:T(8,128)(2,1)S(1)}, bf16[2064,128]{1,0:T(8,128)(2,1)S(1)}, u32[]{:S(2)}, u32[]{:S(2)}) collective-permute-start(bf16[2064,128]{1,0:T(8,128)(2,1)S(1)} %get-tuple-element.73.refs_0_), channel_id=1, source_target_pairs={{0,8},{2,10},{4,12},{6,14},{8,16},{10,18},{12,20},{14,22},{16,24},... | collective-permute-start | bytes 1585160 | tf_op jit(solution)/shard_map/ppermute | solution.py:41
  8.8 28.1 %collective-permute-start.4 = (bf16[2064,128]{1,0:T(8,128)(2,1)S(1)}, bf16[2064,128]{1,0:T(8,128)(2,1)}, u32[]{:S(2)}, u32[]{:S(2)}) collective-permute-start(bf16[2064,128]{1,0:T(8,128)(2,1)S(1)} %get-tuple-element.75.refs_4_), channel_id=1, source_target_pairs={{0,6},{2,0},{4,2},{6,4},{8,14},{10,8},{12,10},{14,12},{16,22},{18,... | collective-permute-start | bytes 1585160 | tf_op jit(solution)/shard_map/ppermute | solution.py:41
  10.3 26.6 %collective-permute-start.2 = (bf16[2064,128]{1,0:T(8,128)(2,1)S(1)}, bf16[2064,128]{1,0:T(8,128)(2,1)}, u32[]{:S(2)}, u32[]{:S(2)}) collective-permute-start(bf16[2064,128]{1,0:T(8,128)(2,1)S(1)} %get-tuple-element.73.refs_0_), channel_id=1, source_target_pairs={{0,24},{2,26},{4,28},{6,30},{8,0},{10,2},{12,4},{14,6},{16,8},{18,... | collective-permute-start | bytes 1585160 | tf_op jit(solution)/shard_map/ppermute | solution.py:41
  11.8 14.7 %copy-start = (f32[4096]{0:T(1024)S(1)}, f32[4096]{0:T(1024)}, u32[]{:S(2)}) copy-start(f32[4096]{0:T(1024)} %param.9) | copy-start | bytes 49156
  15.9 0.8 copy-start.2
  16.7 0.8 copy-start.3
  17.5 0.8 copy-start.5
  20.6 16.3 %collective-permute-start.6 = (bf16[2064,128]{1,0:T(8,128)(2,1)S(1)}, bf16[2064,128]{1,0:T(8,128)(2,1)}, u32[]{:S(2)}, u32[]{:S(2)}) collective-permute-start(bf16[2064,128]{1,0:T(8,128)(2,1)S(1)} %get-tuple-element.75.refs_4_), channel_id=1, source_target_pairs={{0,4},{2,6},{4,0},{6,2},{8,12},{10,14},{12,8},{14,10},{16,20},{18,... | collective-permute-start | bytes 1585160 | tf_op jit(solution)/shard_map/ppermute | solution.py:41
  22.2 14.7 %collective-permute-start.3 = (bf16[2064,128]{1,0:T(8,128)(2,1)S(1)}, bf16[2064,128]{1,0:T(8,128)(2,1)}, u32[]{:S(2)}, u32[]{:S(2)}) collective-permute-start(bf16[2064,128]{1,0:T(8,128)(2,1)S(1)} %get-tuple-element.73.refs_0_), channel_id=1, source_target_pairs={{0,16},{2,18},{4,20},{6,22},{8,24},{10,26},{12,28},{14,30},{16,0},... | collective-permute-start | bytes 1585160 | tf_op jit(solution)/shard_map/ppermute | solution.py:41
  24.9 11.4 %collective-permute-start.1 = (bf16[112,2048]{1,0:T(8,128)(2,1)}, bf16[112,2048]{1,0:T(8,128)(2,1)}, u32[]{:S(2)}, u32[]{:S(2)}) collective-permute-start(bf16[112,2048]{1,0:T(8,128)(2,1)} %get-tuple-element.69), channel_id=1, source_target_pairs={{0,64},{32,96},{64,0},{96,32},{1,65},{33,97},{65,1},{97,33},{2,66}... | collective-permute-start | bytes 1376264 | tf_op jit(solution)/shard_map/ppermute | solution.py:53
  36.3 12.8 %collective-permute-start.12 = (bf16[144,2048]{1,0:T(8,128)(2,1)}, bf16[144,2048]{1,0:T(8,128)(2,1)S(1)}, u32[]{:S(2)}, u32[]{:S(2)}) collective-permute-start(bf16[144,2048]{1,0:T(8,128)(2,1)} %copy-done.2), channel_id=1, source_target_pairs={{0,64},{32,96},{64,0},{96,32},{1,65},{33,97},{65,1},{97,33},{2,66}... | collective-permute-start | bytes 1769480 | tf_op jit(solution)/shard_map/ppermute | solution.py:53
  39.8 15.3 %collective-permute-start.7 = (bf16[2048,128]{1,0:T(8,128)(2,1)S(1)}, bf16[2048,128]{1,0:T(8,128)(2,1)S(1)}, u32[]{:S(2)}, u32[]{:S(2)}) collective-permute-start(bf16[2048,128]{1,0:T(8,128)(2,1)S(1)} %get-tuple-element.77), channel_id=1, source_target_pairs={{0,6},{2,0},{4,2},{6,4},{8,14},{10,8},{12,10},{14,12},{16,22},{18,... | collective-permute-start | bytes 1572872 | tf_op jit(solution)/shard_map/ppermute | solution.py:41
  40.6 12.7 %collective-permute-start.8 = (bf16[2048,128]{1,0:T(8,128)(2,1)S(1)}, bf16[2048,128]{1,0:T(8,128)(2,1)S(1)}, u32[]{:S(2)}, u32[]{:S(2)}) collective-permute-start(bf16[2048,128]{1,0:T(8,128)(2,1)S(1)} %get-tuple-element.79), channel_id=1, source_target_pairs={{0,2},{2,4},{4,6},{6,0},{8,10},{10,12},{12,14},{14,8},{16,18},{18,... | collective-permute-start | bytes 1572872 | tf_op jit(solution)/shard_map/ppermute | solution.py:41
  41.3 13.7 %collective-permute-start.10 = (bf16[2048,128]{1,0:T(8,128)(2,1)S(1)}, bf16[2048,128]{1,0:T(8,128)(2,1)S(1)}, u32[]{:S(2)}, u32[]{:S(2)}) collective-permute-start(bf16[2048,128]{1,0:T(8,128)(2,1)S(1)} %get-tuple-element.82), channel_id=1, source_target_pairs={{0,24},{2,26},{4,28},{6,30},{8,0},{10,2},{12,4},{14,6},{16,8},{18,... | collective-permute-start | bytes 1572872 | tf_op jit(solution)/shard_map/ppermute | solution.py:41
  42.4 10.9 %collective-permute-start.11 = (bf16[2048,128]{1,0:T(8,128)(2,1)S(1)}, bf16[2048,128]{1,0:T(8,128)(2,1)S(1)}, u32[]{:S(2)}, u32[]{:S(2)}) collective-permute-start(bf16[2048,128]{1,0:T(8,128)(2,1)S(1)} %get-tuple-element.84), channel_id=1, source_target_pairs={{0,8},{2,10},{4,12},{6,14},{8,16},{10,18},{12,20},{14,22},{16,24},... | collective-permute-start | bytes 1572872 | tf_op jit(solution)/shard_map/ppermute | solution.py:41
  45.8 3.3 %copy-start.6 = (bf16[128,2048]{1,0:T(8,128)(2,1)S(1)}, bf16[128,2048]{1,0:T(8,128)(2,1)}, u32[]{:S(2)}) copy-start(bf16[128,2048]{1,0:T(8,128)(2,1)} %copy-done.5) | copy-start | bytes 1572868
  46.1 13.4 %copy-start.4 = (bf16[128,2048]{1,0:T(8,128)(2,1)S(1)}, bf16[128,2048]{1,0:T(8,128)(2,1)}, u32[]{:S(2)}) copy-start(bf16[128,2048]{1,0:T(8,128)(2,1)} %copy-done.3) | copy-start | bytes 1572868
  49.1 10.4 %collective-permute-start.15 = (bf16[128,2048]{1,0:T(8,128)(2,1)S(1)}, bf16[128,2048]{1,0:T(8,128)(2,1)S(1)}, u32[]{:S(2)}, u32[]{:S(2)}) collective-permute-start(bf16[128,2048]{1,0:T(8,128)(2,1)S(1)} %copy-done.6), channel_id=1, source_target_pairs={{0,64},{32,96},{64,0},{96,32},{1,65},{33,97},{65,1},{97,33},{2,66}... | collective-permute-start | bytes 1572872 | tf_op jit(solution)/shard_map/ppermute | solution.py:53
  53.3 10.3 %collective-permute-start.13 = (bf16[2048,128]{1,0:T(8,128)(2,1)S(1)}, bf16[2048,128]{1,0:T(8,128)(2,1)S(1)}, u32[]{:S(2)}, u32[]{:S(2)}) collective-permute-start(bf16[2048,128]{1,0:T(8,128)(2,1)S(1)} %get-tuple-element.88), channel_id=1, source_target_pairs={{0,16},{2,18},{4,20},{6,22},{8,24},{10,26},{12,28},{14,30},{16,0},... | collective-permute-start | bytes 1572872 | tf_op jit(solution)/shard_map/ppermute | solution.py:41
  53.4 10.4 %collective-permute-start.9 = (bf16[2048,128]{1,0:T(8,128)(2,1)S(1)}, bf16[2048,128]{1,0:T(8,128)(2,1)S(1)}, u32[]{:S(2)}, u32[]{:S(2)}) collective-permute-start(bf16[2048,128]{1,0:T(8,128)(2,1)S(1)} %get-tuple-element.80), channel_id=1, source_target_pairs={{0,4},{2,6},{4,0},{6,2},{8,12},{10,14},{12,8},{14,10},{16,20},{18,... | collective-permute-start | bytes 1572872 | tf_op jit(solution)/shard_map/ppermute | solution.py:41
  59.5 15.9 %collective-permute-start.16 = (bf16[128,2048]{1,0:T(8,128)(2,1)S(1)}, bf16[128,2048]{1,0:T(8,128)(2,1)S(1)}, u32[]{:S(2)}, u32[]{:S(2)}) collective-permute-start(bf16[128,2048]{1,0:T(8,128)(2,1)S(1)} %copy-done.4), channel_id=1, source_target_pairs={{0,64},{32,96},{64,0},{96,32},{1,65},{33,97},{65,1},{97,33},{2,66}... | collective-permute-start | bytes 1572872 | tf_op jit(solution)/shard_map/ppermute | solution.py:53
  66.9 9.3 %collective-permute-start.14 = (bf16[256,512]{1,0:T(8,128)(2,1)S(1)}, bf16[256,512]{1,0:T(8,128)(2,1)S(1)}, u32[]{:S(2)}, u32[]{:S(2)}) collective-permute-start(bf16[256,512]{1,0:T(8,128)(2,1)S(1)} %attend.4.mine_ref), channel_id=1, source_target_pairs={{0,64},{32,96},{64,0},{96,32},{1,65},{33,97},{65,1},{97,33},{2,66}... | collective-permute-start | bytes 786440 | tf_op jit(solution)/shard_map/ppermute | solution.py:53
  72.3 17.4 %collective-permute-start.20 = (bf16[256,512]{1,0:T(8,128)(2,1)S(1)}, bf16[256,512]{1,0:T(8,128)(2,1)S(1)}, u32[]{:S(2)}, u32[]{:S(2)}) collective-permute-start(bf16[256,512]{1,0:T(8,128)(2,1)S(1)} %attend.5.mine_ref), channel_id=1, source_target_pairs={{0,64},{32,96},{64,0},{96,32},{1,65},{33,97},{65,1},{97,33},{2,66}... | collective-permute-start | bytes 786440 | tf_op jit(solution)/shard_map/ppermute | solution.py:53
  77.5 14.1 %collective-permute-start.18 = (bf16[256,512]{1,0:T(8,128)(2,1)S(1)}, bf16[256,512]{1,0:T(8,128)(2,1)S(1)}, u32[]{:S(2)}, u32[]{:S(2)}) collective-permute-start(bf16[256,512]{1,0:T(8,128)(2,1)S(1)} %get-tuple-element.100), channel_id=1, source_target_pairs={{0,32},{32,0},{64,96},{96,64},{1,33},{33,1},{65,97},{97,65},{2,34}... | collective-permute-start | bytes 786440 | tf_op jit(solution)/shard_map/ppermute | solution.py:53
  85.0 9.8 %collective-permute-start.24 = (bf16[256,512]{1,0:T(8,128)(2,1)S(1)}, bf16[256,512]{1,0:T(8,128)(2,1)S(1)}, u32[]{:S(2)}, u32[]{:S(2)}) collective-permute-start(bf16[256,512]{1,0:T(8,128)(2,1)S(1)} %attend.6.mine_ref), channel_id=1, source_target_pairs={{0,64},{32,96},{64,0},{96,32},{1,65},{33,97},{65,1},{97,33},{2,66}... | collective-permute-start | bytes 786440 | tf_op jit(solution)/shard_map/ppermute | solution.py:53
  91.0 6.0 %collective-permute-start.22 = (bf16[256,512]{1,0:T(8,128)(2,1)S(1)}, bf16[256,512]{1,0:T(8,128)(2,1)S(1)}, u32[]{:S(2)}, u32[]{:S(2)}) collective-permute-start(bf16[256,512]{1,0:T(8,128)(2,1)S(1)} %get-tuple-element.108), channel_id=1, source_target_pairs={{0,32},{32,0},{64,96},{96,64},{1,33},{33,1},{65,97},{97,65},{2,34}... | collective-permute-start | bytes 786440 | tf_op jit(solution)/shard_map/ppermute | solution.py:53
  91.5 5.7 %collective-permute-start.17 = (bf16[256,512]{1,0:T(8,128)(2,1)S(1)}, bf16[256,512]{1,0:T(8,128)(2,1)S(1)}, u32[]{:S(2)}, u32[]{:S(2)}) collective-permute-start(bf16[256,512]{1,0:T(8,128)(2,1)S(1)} %get-tuple-element.98), channel_id=1, source_target_pairs={{0,32},{32,0},{64,96},{96,64},{1,33},{33,1},{65,97},{97,65},{2,34}... | collective-permute-start | bytes 786440 | tf_op jit(solution)/shard_map/ppermute | solution.py:53
  91.7 8.8 %collective-permute-start.19 = (bf16[256,512]{1,0:T(8,128)(2,1)S(1)}, bf16[256,512]{1,0:T(8,128)(2,1)S(1)}, u32[]{:S(2)}, u32[]{:S(2)}) collective-permute-start(bf16[256,512]{1,0:T(8,128)(2,1)S(1)} %add_convert_fusion.7), channel_id=1, source_target_pairs={{0,65},{32,97},{64,1},{96,33},{1,64},{33,96},{65,0},{97,32},{2,67}... | collective-permute-start | bytes 786440 | tf_op jit(solution)/shard_map/ppermute | solution.py:53
  93.9 8.0 %collective-permute-start.28 = (bf16[256,512]{1,0:T(8,128)(2,1)S(1)}, bf16[256,512]{1,0:T(8,128)(2,1)S(1)}, u32[]{:S(2)}, u32[]{:S(2)}) collective-permute-start(bf16[256,512]{1,0:T(8,128)(2,1)S(1)} %attend.7.mine_ref), channel_id=1, source_target_pairs={{0,64},{32,96},{64,0},{96,32},{1,65},{33,97},{65,1},{97,33},{2,66}... | collective-permute-start | bytes 786440 | tf_op jit(solution)/shard_map/ppermute | solution.py:53
  94.8 9.5 %collective-permute-start.21 = (bf16[256,512]{1,0:T(8,128)(2,1)S(1)}, bf16[256,512]{1,0:T(8,128)(2,1)S(1)}, u32[]{:S(2)}, u32[]{:S(2)}) collective-permute-start(bf16[256,512]{1,0:T(8,128)(2,1)S(1)} %get-tuple-element.106), channel_id=1, source_target_pairs={{0,32},{32,0},{64,96},{96,64},{1,33},{33,1},{65,97},{97,65},{2,34}... | collective-permute-start | bytes 786440 | tf_op jit(solution)/shard_map/ppermute | solution.py:53
  97.0 7.1 %collective-permute-start.26 = (bf16[256,512]{1,0:T(8,128)(2,1)S(1)}, bf16[256,512]{1,0:T(8,128)(2,1)S(1)}, u32[]{:S(2)}, u32[]{:S(2)}) collective-permute-start(bf16[256,512]{1,0:T(8,128)(2,1)S(1)} %get-tuple-element.114), channel_id=1, source_target_pairs={{0,32},{32,0},{64,96},{96,64},{1,33},{33,1},{65,97},{97,65},{2,34}... | collective-permute-start | bytes 786440 | tf_op jit(solution)/shard_map/ppermute | solution.py:53
  97.2 9.2 %collective-permute-start.23 = (bf16[256,512]{1,0:T(8,128)(2,1)S(1)}, bf16[256,512]{1,0:T(8,128)(2,1)S(1)}, u32[]{:S(2)}, u32[]{:S(2)}) collective-permute-start(bf16[256,512]{1,0:T(8,128)(2,1)S(1)} %add_convert_fusion.5), channel_id=1, source_target_pairs={{0,65},{32,97},{64,1},{96,33},{1,64},{33,96},{65,0},{97,32},{2,67}... | collective-permute-start | bytes 786440 | tf_op jit(solution)/shard_map/ppermute | solution.py:53
  100.5 8.3 %collective-permute-start.25 = (bf16[256,512]{1,0:T(8,128)(2,1)S(1)}, bf16[256,512]{1,0:T(8,128)(2,1)S(1)}, u32[]{:S(2)}, u32[]{:S(2)}) collective-permute-start(bf16[256,512]{1,0:T(8,128)(2,1)S(1)} %get-tuple-element.112), channel_id=1, source_target_pairs={{0,32},{32,0},{64,96},{96,64},{1,33},{33,1},{65,97},{97,65},{2,34}... | collective-permute-start | bytes 786440 | tf_op jit(solution)/shard_map/ppermute | solution.py:53
  103.3 9.9 %collective-permute-start.29 = (bf16[256,512]{1,0:T(8,128)(2,1)S(1)}, bf16[256,512]{1,0:T(8,128)(2,1)S(1)}, u32[]{:S(2)}, u32[]{:S(2)}) collective-permute-start(bf16[256,512]{1,0:T(8,128)(2,1)S(1)} %get-tuple-element.119), channel_id=1, source_target_pairs={{0,32},{32,0},{64,96},{96,64},{1,33},{33,1},{65,97},{97,65},{2,34}... | collective-permute-start | bytes 786440 | tf_op jit(solution)/shard_map/ppermute | solution.py:53
  104.1 2.5 %collective-permute-start.30 = (bf16[256,512]{1,0:T(8,128)(2,1)S(1)}, bf16[256,512]{1,0:T(8,128)(2,1)S(1)}, u32[]{:S(2)}, u32[]{:S(2)}) collective-permute-start(bf16[256,512]{1,0:T(8,128)(2,1)S(1)} %get-tuple-element.121), channel_id=1, source_target_pairs={{0,32},{32,0},{64,96},{96,64},{1,33},{33,1},{65,97},{97,65},{2,34}... | collective-permute-start | bytes 786440 | tf_op jit(solution)/shard_map/ppermute | solution.py:53
  104.3 8.8 %collective-permute-start.27 = (bf16[256,512]{1,0:T(8,128)(2,1)S(1)}, bf16[256,512]{1,0:T(8,128)(2,1)S(1)}, u32[]{:S(2)}, u32[]{:S(2)}) collective-permute-start(bf16[256,512]{1,0:T(8,128)(2,1)S(1)} %add_convert_fusion.3), channel_id=1, source_target_pairs={{0,65},{32,97},{64,1},{96,33},{1,64},{33,96},{65,0},{97,32},{2,67}... | collective-permute-start | bytes 786440 | tf_op jit(solution)/shard_map/ppermute | solution.py:53
  106.6 12.0 %collective-permute-start.31 = (bf16[256,512]{1,0:T(8,128)(2,1)S(1)}, bf16[256,512]{1,0:T(8,128)(2,1)S(1)}, u32[]{:S(2)}, u32[]{:S(2)}) collective-permute-start(bf16[256,512]{1,0:T(8,128)(2,1)S(1)} %add_convert_fusion.1), channel_id=1, source_target_pairs={{0,65},{32,97},{64,1},{96,33},{1,64},{33,96},{65,0},{97,32},{2,67}... | collective-permute-start | bytes 786440 | tf_op jit(solution)/shard_map/ppermute | solution.py:53
  113.1 5.5 %copy-start.7 = (bf16[1024,512]{1,0:T(8,128)(2,1)}, bf16[1024,512]{1,0:T(8,128)(2,1)S(1)}, u32[]{:S(2)}) copy-start(bf16[1024,512]{1,0:T(8,128)(2,1)S(1)} %fusion) | copy-start | bytes 3145732

commit v8 on v6

--- a/solution.py
+++ b/solution.py
@@ -19,7 +19,7 @@
 PICKS = SIDE * SIDE * CAP
 NOTE_ROWS = 16
 EPSILON = 1e-05
-NEAR_PIECES = (112, 144, 128, 128)
+NEAR_PIECES = (96, 144, 144, 128)
 CHUNKS = (2, 2, 2, 2)
 AHEAD = 3
 LAG = 2
@@ -304,7 +304,7 @@
 
 def queries_of(text_hidden, norm_gain, query_weight):
     (rows, depth), width = text_hidden.shape, query_weight.shape[1]
-    steps = 4
+    steps = 8
     return pl.pallas_call(
         ask_body,
         grid=(steps,),

time: 120 us -> 123 us (1.025)
  waiting for transfers between devices: 28.6 us -> 31.6 us
  starting transfers between devices: 42.3 us -> 40.2 us
  Pallas kernels: 41.3 us -> 42.8 us
    ppermute x20, waiting for transfers between devices: 18.2 us -> 22.7 us  [along_z(): return lax.ppermute(value, SECTION_HEAD, pairs)]
    ppermute x20, starting transfers between devices: 27 us -> 24.9 us  [along_z(): return lax.ppermute(value, SECTION_HEAD, pairs)]
    pallas_call x1, Pallas kernels: 9.63 us -> 11.3 us  [queries_of(): pl.pallas_call(ask_body, grid=(steps,), in_specs=[pl.BlockSpec((rows // s...]
    ppermute x12, waiting for transfers between devices: 10.3 us -> 8.91 us  [along_seq(): return lax.ppermute(value, 'seq', pairs)]
where the time goes in v8:
time: 123 us; the launch traced here: 122 us
  Pallas kernels  42.8 us (35%)
  starting transfers between devices  40.2 us (33%)
  waiting for transfers between devices  31.6 us (26%)
  local copies, waits for them, and re-layouts  5.06 us (4%)
  other arithmetic  2.04 us (2%)
    ppermute x20, starting transfers between devices, along_z(): return lax.ppermute(value, SECTION_HEAD, pairs)  24.9 us
    ppermute x20, waiting for transfers between devices, along_z(): return lax.ppermute(value, SECTION_HEAD, pairs)  22.7 us
    ppermute x12, starting transfers between devices, along_seq(): return lax.ppermute(value, 'seq', pairs)  15.3 us
    pallas_call x4, Pallas kernels, attend(): pl.pallas_call(functools.partial(attend_body, first_tile), in_specs=[SMEM...  11.9 us
    pallas_call x1, Pallas kernels, queries_of(): pl.pallas_call(ask_body, grid=(steps,), in_specs=[pl.BlockSpec((rows // s...  11.3 us
    ppermute x12, waiting for transfers between devices, along_seq(): return lax.ppermute(value, 'seq', pairs)  8.91 us
    pallas_call x2, Pallas kernels, pick(): pl.pallas_call(pick_body, grid_spec=pltpu.PrefetchScalarGridSpec(num_scal...  7.04 us
    pallas_call x4, Pallas kernels, multiply(): pl.pallas_call(multiply_body, in_specs=[VMEM_WHOLE] * 3, out_specs=[VMEM_...  5.18 us
  transfers between devices with their start and end apart: 32, of which 9 were waited for; matrix products, arithmetic and copies ran while one was open for 2% of the time, Pallas kernels for 31%

profile of v8, /device:TPU:1, one launch (start us, length us, event | category | flops | bytes accessed | tf_op | source)
XLA Modules:
  0.0 122.2 jit_solution(15053639826145170823)
XLA Ops:
  0.0 0.7 copy-done.1
  0.7 4.7 %project.1 = (bf16[2064,128]{1,0:T(8,128)(2,1)S(1)}, bf16[2064,128]{1,0:T(8,128)(2,1)S(1)}, s32[8,128]{1,0:T(8,128)S(1)}) custom-call(s32[8,16]{1,0:T(8,128)S(1)} %copy-done.1, bf16[2048,1024]{1,0:T(8,128)(2,1)} %x_ref.1, bf16[1024,128]{1,0:T(8,128)(2,1)} %wk_ref.1, bf16[1024,128]{1,0:T(8,128)(2,1)} %wv_ref.1), custom_call_target="tpu_custom_call" | custom-call | flops 1 | bytes 1 | tf_op jit(solution)/shard_map/project/pallas_call | solution.py:135
  5.4 2.2 %collective-permute-start.5 = (bf16[2064,128]{1,0:T(8,128)(2,1)S(1)}, bf16[2064,128]{1,0:T(8,128)(2,1)S(1)}, u32[]{:S(2)}, u32[]{:S(2)}) collective-permute-start(bf16[2064,128]{1,0:T(8,128)(2,1)S(1)} %get-tuple-element.75.refs_4_), channel_id=1, source_target_pairs={{0,2},{2,4},{4,6},{6,0},{8,10},{10,12},{12,14},{14,8},{16,18},{18,... | collective-permute-start | bytes 1585160 | tf_op jit(solution)/shard_map/ppermute | solution.py:41
  7.6 1.2 collective-permute-start
  8.8 1.5 %collective-permute-start.4 = (bf16[2064,128]{1,0:T(8,128)(2,1)S(1)}, bf16[2064,128]{1,0:T(8,128)(2,1)}, u32[]{:S(2)}, u32[]{:S(2)}) collective-permute-start(bf16[2064,128]{1,0:T(8,128)(2,1)S(1)} %get-tuple-element.75.refs_4_), channel_id=1, source_target_pairs={{0,6},{2,0},{4,2},{6,4},{8,14},{10,8},{12,10},{14,12},{16,22},{18,... | collective-permute-start | bytes 1585160 | tf_op jit(solution)/shard_map/ppermute | solution.py:41
  10.3 1.5 %collective-permute-start.2 = (bf16[2064,128]{1,0:T(8,128)(2,1)S(1)}, bf16[2064,128]{1,0:T(8,128)(2,1)}, u32[]{:S(2)}, u32[]{:S(2)}) collective-permute-start(bf16[2064,128]{1,0:T(8,128)(2,1)S(1)} %get-tuple-element.73.refs_0_), channel_id=1, source_target_pairs={{0,24},{2,26},{4,28},{6,30},{8,0},{10,2},{12,4},{14,6},{16,8},{18,... | collective-permute-start | bytes 1585160 | tf_op jit(solution)/shard_map/ppermute | solution.py:41
  11.8 4.0 %pick.2 = (bf16[96,2048]{1,0:T(8,128)(2,1)}, bf16[144,2048]{1,0:T(8,128)(2,1)S(1)}, bf16[144,2048]{1,0:T(8,128)(2,1)S(1)}, bf16[128,2048]{1,0:T(8,128)(2,1)S(1)}) custom-call(s32[4]{0:T(128)S(1)} %pad_add_fusion.1.places_ref, bf16[512,4096]{1,0:T(8,128)(2,1)} %w_ref.3), custom_call_target="tpu_custom_call" | custom-call | flops 1 | bytes 1 | tf_op jit(solution)/shard_map/pick/pallas_call | solution.py:258
  15.9 0.8 copy-done.2
  16.7 0.8 copy-done.4
  17.5 0.8 copy-done.5
  18.3 2.3 %collective-permute-done.5.refs_7_ = bf16[2064,128]{1,0:T(8,128)(2,1)S(1)} collective-permute-done((bf16[2064,128]{1,0:T(8,128)(2,1)S(1)}, bf16[2064,128]{1,0:T(8,128)(2,1)S(1)}, u32[]{:S(2)}, u32[]{:S(2)}) %collective-permute-start.5) | collective-permute-done | bytes 528416 | tf_op jit(solution)/shard_map/ppermute | solution.py:41
  20.6 1.6 %collective-permute-start.6 = (bf16[2064,128]{1,0:T(8,128)(2,1)S(1)}, bf16[2064,128]{1,0:T(8,128)(2,1)}, u32[]{:S(2)}, u32[]{:S(2)}) collective-permute-start(bf16[2064,128]{1,0:T(8,128)(2,1)S(1)} %get-tuple-element.75.refs_4_), channel_id=1, source_target_pairs={{0,4},{2,6},{4,0},{6,2},{8,12},{10,14},{12,8},{14,10},{16,20},{18,... | collective-permute-start | bytes 1585160 | tf_op jit(solution)/shard_map/ppermute | solution.py:41
  22.2 2.7 %collective-permute-start.3 = (bf16[2064,128]{1,0:T(8,128)(2,1)S(1)}, bf16[2064,128]{1,0:T(8,128)(2,1)}, u32[]{:S(2)}, u32[]{:S(2)}) collective-permute-start(bf16[2064,128]{1,0:T(8,128)(2,1)S(1)} %get-tuple-element.73.refs_0_), channel_id=1, source_target_pairs={{0,16},{2,18},{4,20},{6,22},{8,24},{10,26},{12,28},{14,30},{16,0},... | collective-permute-start | bytes 1585160 | tf_op jit(solution)/shard_map/ppermute | solution.py:41
  24.9 1.6 %collective-permute-start.1 = (bf16[96,2048]{1,0:T(8,128)(2,1)}, bf16[96,2048]{1,0:T(8,128)(2,1)}, u32[]{:S(2)}, u32[]{:S(2)}) collective-permute-start(bf16[96,2048]{1,0:T(8,128)(2,1)} %get-tuple-element.69), channel_id=1, source_target_pairs={{0,64},{32,96},{64,0},{96,32},{1,65},{33,97},{65,1},{97,33},{2,66}... | collective-permute-start | bytes 1179656 | tf_op jit(solution)/shard_map/ppermute | solution.py:53
  26.6 11.3 %ask.1.q_ref = bf16[1024,512]{1,0:T(8,128)(2,1)S(1)} custom-call(bf16[1024,4096]{1,0:T(8,128)(2,1)} %x_ref.2, f32[1,4096]{1,0:T(1,128)S(1)} %bitcast.11, bf16[4096,512]{1,0:T(8,128)(2,1)} %w_ref.1), custom_call_target="tpu_custom_call" | custom-call | flops 1 | bytes 1 | tf_op jit(solution)/shard_map/ask/pallas_call | solution.py:308
  38.2 2.8 %pack.1 = (bf16[2048,128]{1,0:T(8,128)(2,1)S(1)}, bf16[2048,128]{1,0:T(8,128)(2,1)S(1)}, bf16[2048,128]{1,0:T(8,128)(2,1)S(1)}, bf16[2048,128]{1,0:T(8,128)(2,1)...) custom-call(s32[2]{0:T(128)S(1)} %pad_add_fusion.place_ref, ...), custom_call_target="tpu_custom_call" | custom-call | flops 1 | bytes 1 | tf_op jit(solution)/shard_map/pack/pallas_call | solution.py:187
  41.0 0.8 collective-permute-start.7
  41.9 0.7 collective-permute-start.8
  42.5 0.9 collective-permute-start.10
  44.0 3.0 %pick.3 = bf16[512,2048]{1,0:T(8,128)(2,1)S(1)} custom-call(s32[4]{0:T(128)S(1)} %pad_add_fusion.2.places_ref, bf16[512,4096]{1,0:T(8,128)(2,1)} %w_ref.3), custom_call_target="tpu_custom_call" | custom-call | flops 1 | bytes 1 | tf_op jit(solution)/shard_map/pick/pallas_call | solution.py:258
  47.3 1.1 constant_dynamic-update-slice_fusion.11
  48.4 2.4 %collective-permute-done.12 = bf16[144,2048]{1,0:T(8,128)(2,1)S(1)} collective-permute-done((bf16[144,2048]{1,0:T(8,128)(2,1)}, bf16[144,2048]{1,0:T(8,128)(2,1)S(1)}, u32[]{:S(2)}, u32[]{:S(2)}) %collective-permute-start.12) | collective-permute-done | bytes 589856 | tf_op jit(solution)/shard_map/ppermute | solution.py:53
  51.0 3.8 %collective-permute-done.11 = bf16[2048,128]{1,0:T(8,128)(2,1)S(1)} collective-permute-done((bf16[2048,128]{1,0:T(8,128)(2,1)S(1)}, bf16[2048,128]{1,0:T(8,128)(2,1)S(1)}, u32[]{:S(2)}, u32[]{:S(2)}) %collective-permute-start.11) | collective-permute-done | bytes 524320 | tf_op jit(solution)/shard_map/ppermute | solution.py:41
  54.9 1.5 %collective-permute-start.9 = (bf16[2048,128]{1,0:T(8,128)(2,1)S(1)}, bf16[2048,128]{1,0:T(8,128)(2,1)S(1)}, u32[]{:S(2)}, u32[]{:S(2)}) collective-permute-start(bf16[2048,128]{1,0:T(8,128)(2,1)S(1)} %get-tuple-element.80), channel_id=1, source_target_pairs={{0,4},{2,6},{4,0},{6,2},{8,12},{10,14},{12,8},{14,10},{16,20},{18,... | collective-permute-start | bytes 1572872 | tf_op jit(solution)/shard_map/ppermute | solution.py:41
  56.6 6.0 %collective-permute-done.15 = bf16[144,2048]{1,0:T(8,128)(2,1)S(1)} collective-permute-done((bf16[144,2048]{1,0:T(8,128)(2,1)S(1)}, bf16[144,2048]{1,0:T(8,128)(2,1)S(1)}, u32[]{:S(2)}, u32[]{:S(2)}) %collective-permute-start.15) | collective-permute-done | bytes 589856 | tf_op jit(solution)/shard_map/ppermute | solution.py:53
  62.8 2.8 %collective-permute-done.13 = bf16[2048,128]{1,0:T(8,128)(2,1)S(1)} collective-permute-done((bf16[2048,128]{1,0:T(8,128)(2,1)S(1)}, bf16[2048,128]{1,0:T(8,128)(2,1)S(1)}, u32[]{:S(2)}, u32[]{:S(2)}) %collective-permute-start.13) | collective-permute-done | bytes 524320 | tf_op jit(solution)/shard_map/ppermute | solution.py:41
  65.9 3.0 %attend.4.mine_ref = bf16[256,512]{1,0:T(8,128)(2,1)S(1)} custom-call(s32[8,128]{1,0:T(8,128)S(1)} %get-tuple-element.103.slots_ref, s32[2]{0:T(128)S(1)} %pad_add_fusion.place_ref, bf16[1024,512]{1,0:T(8,128)(2,1)S(1)} %ask.1.q_ref, bf16[8192,128]{1,0:T(8,128)(2,1)S(1)} %constant_dynamic-update-slice_fusion.k_ref, ...), custom_call_target="tpu_custom_call" | custom-call | flops 1 | bytes 1 | tf_op jit(solution)/shard_map/attend/pallas_call | solution.py:237
  68.9 1.3 %collective-permute-start.14 = (bf16[256,512]{1,0:T(8,128)(2,1)S(1)}, bf16[256,512]{1,0:T(8,128)(2,1)S(1)}, u32[]{:S(2)}, u32[]{:S(2)}) collective-permute-start(bf16[256,512]{1,0:T(8,128)(2,1)S(1)} %attend.4.mine_ref), channel_id=1, source_target_pairs={{0,64},{32,96},{64,0},{96,32},{1,65},{33,97},{65,1},{97,33},{2,66}... | collective-permute-start | bytes 786440 | tf_op jit(solution)/shard_map/ppermute | solution.py:53
  70.3 3.0 %attend.5.mine_ref = bf16[256,512]{1,0:T(8,128)(2,1)S(1)} custom-call(s32[8,128]{1,0:T(8,128)S(1)} %get-tuple-element.103.slots_ref, s32[2]{0:T(128)S(1)} %pad_add_fusion.place_ref, bf16[1024,512]{1,0:T(8,128)(2,1)S(1)} %ask.1.q_ref, bf16[8192,128]{1,0:T(8,128)(2,1)S(1)} %constant_dynamic-update-slice_fusion.k_ref, ...), custom_call_target="tpu_custom_call" | custom-call | flops 1 | bytes 1 | tf_op jit(solution)/shard_map/attend/pallas_call | solution.py:237
  73.7 3.0 %attend.6.mine_ref = bf16[256,512]{1,0:T(8,128)(2,1)S(1)} custom-call(s32[8,128]{1,0:T(8,128)S(1)} %get-tuple-element.103.slots_ref, s32[2]{0:T(128)S(1)} %pad_add_fusion.place_ref, bf16[1024,512]{1,0:T(8,128)(2,1)S(1)} %ask.1.q_ref, bf16[8192,128]{1,0:T(8,128)(2,1)S(1)} %constant_dynamic-update-slice_fusion.k_ref, ...), custom_call_target="tpu_custom_call" | custom-call | flops 1 | bytes 1 | tf_op jit(solution)/shard_map/attend/pallas_call | solution.py:237
  76.8 1.9 %collective-permute-done.14.near_ref = bf16[256,512]{1,0:T(8,128)(2,1)S(1)} collective-permute-done((bf16[256,512]{1,0:T(8,128)(2,1)S(1)}, bf16[256,512]{1,0:T(8,128)(2,1)S(1)}, u32[]{:S(2)}, u32[]{:S(2)}) %collective-permute-start.14) | collective-permute-done | bytes 262176 | tf_op jit(solution)/shard_map/ppermute | solution.py:53
  78.6 1.3 %multiply.4 = (bf16[256,512]{1,0:T(8,128)(2,1)S(1)}, bf16[256,512]{1,0:T(8,128)(2,1)S(1)}, f32[256,512]{1,0:T(8,128)S(1)}, f32[256,512]{1,0:T(8,128)S(1)}) custom-call(bf16[256,512]{1,0:T(8,128)(2,1)S(1)} %attend.4.mine_ref, bf16[256,512]{1,0:T(8,128)(2,1)S(1)} %collective-permute-done.14.near_ref, ...), custom_call_target="tpu_custom_call" | custom-call | flops 1 | bytes 1 | tf_op jit(solution)/shard_map/multiply/pallas_call | solution.py:286
  79.9 7.8 %collective-permute-start.18 = (bf16[256,512]{1,0:T(8,128)(2,1)S(1)}, bf16[256,512]{1,0:T(8,128)(2,1)S(1)}, u32[]{:S(2)}, u32[]{:S(2)}) collective-permute-start(bf16[256,512]{1,0:T(8,128)(2,1)S(1)} %get-tuple-element.100), channel_id=1, source_target_pairs={{0,32},{32,0},{64,96},{96,64},{1,33},{33,1},{65,97},{97,65},{2,34}... | collective-permute-start | bytes 786440 | tf_op jit(solution)/shard_map/ppermute | solution.py:53
  87.8 3.0 %attend.7.mine_ref = bf16[256,512]{1,0:T(8,128)(2,1)S(1)} custom-call(s32[8,128]{1,0:T(8,128)S(1)} %get-tuple-element.103.slots_ref, s32[2]{0:T(128)S(1)} %pad_add_fusion.place_ref, bf16[1024,512]{1,0:T(8,128)(2,1)S(1)} %ask.1.q_ref, bf16[8192,128]{1,0:T(8,128)(2,1)S(1)} %constant_dynamic-update-slice_fusion.k_ref, ...), custom_call_target="tpu_custom_call" | custom-call | flops 1 | bytes 1 | tf_op jit(solution)/shard_map/attend/pallas_call | solution.py:237
  90.8 1.3 %multiply.5 = (bf16[256,512]{1,0:T(8,128)(2,1)S(1)}, bf16[256,512]{1,0:T(8,128)(2,1)S(1)}, f32[256,512]{1,0:T(8,128)S(1)}, f32[256,512]{1,0:T(8,128)S(1)}) custom-call(bf16[256,512]{1,0:T(8,128)(2,1)S(1)} %attend.5.mine_ref, bf16[256,512]{1,0:T(8,128)(2,1)S(1)} %collective-permute-done.20.near_ref, ...), custom_call_target="tpu_custom_call" | custom-call | flops 1 | bytes 1 | tf_op jit(solution)/shard_map/multiply/pallas_call | solution.py:286
  92.8 3.6 %collective-permute-start.19 = (bf16[256,512]{1,0:T(8,128)(2,1)S(1)}, bf16[256,512]{1,0:T(8,128)(2,1)S(1)}, u32[]{:S(2)}, u32[]{:S(2)}) collective-permute-start(bf16[256,512]{1,0:T(8,128)(2,1)S(1)} %add_convert_fusion.7), channel_id=1, source_target_pairs={{0,65},{32,97},{64,1},{96,33},{1,64},{33,96},{65,0},{97,32},{2,67}... | collective-permute-start | bytes 786440 | tf_op jit(solution)/shard_map/ppermute | solution.py:53
  96.4 0.6 collective-permute-start.21
  97.0 1.3 %multiply.6 = (bf16[256,512]{1,0:T(8,128)(2,1)S(1)}, bf16[256,512]{1,0:T(8,128)(2,1)S(1)}, f32[256,512]{1,0:T(8,128)S(1)}, f32[256,512]{1,0:T(8,128)S(1)}) custom-call(bf16[256,512]{1,0:T(8,128)(2,1)S(1)} %attend.6.mine_ref, bf16[256,512]{1,0:T(8,128)(2,1)S(1)} %collective-permute-done.24.near_ref, ...), custom_call_target="tpu_custom_call" | custom-call | flops 1 | bytes 1 | tf_op jit(solution)/shard_map/multiply/pallas_call | solution.py:286
  98.5 1.8 %collective-permute-start.23 = (bf16[256,512]{1,0:T(8,128)(2,1)S(1)}, bf16[256,512]{1,0:T(8,128)(2,1)S(1)}, u32[]{:S(2)}, u32[]{:S(2)}) collective-permute-start(bf16[256,512]{1,0:T(8,128)(2,1)S(1)} %add_convert_fusion.5), channel_id=1, source_target_pairs={{0,65},{32,97},{64,1},{96,33},{1,64},{33,96},{65,0},{97,32},{2,67}... | collective-permute-start | bytes 786440 | tf_op jit(solution)/shard_map/ppermute | solution.py:53
  100.3 2.5 %collective-permute-done.19 = bf16[256,512]{1,0:T(8,128)(2,1)S(1)} collective-permute-done((bf16[256,512]{1,0:T(8,128)(2,1)S(1)}, bf16[256,512]{1,0:T(8,128)(2,1)S(1)}, u32[]{:S(2)}, u32[]{:S(2)}) %collective-permute-start.19) | collective-permute-done | bytes 262176 | tf_op jit(solution)/shard_map/ppermute | solution.py:53
  102.8 1.3 %collective-permute-start.25 = (bf16[256,512]{1,0:T(8,128)(2,1)S(1)}, bf16[256,512]{1,0:T(8,128)(2,1)S(1)}, u32[]{:S(2)}, u32[]{:S(2)}) collective-permute-start(bf16[256,512]{1,0:T(8,128)(2,1)S(1)} %get-tuple-element.112), channel_id=1, source_target_pairs={{0,32},{32,0},{64,96},{96,64},{1,33},{33,1},{65,97},{97,65},{2,34}... | collective-permute-start | bytes 786440 | tf_op jit(solution)/shard_map/ppermute | solution.py:53
  104.2 1.3 %multiply.7 = (bf16[256,512]{1,0:T(8,128)(2,1)S(1)}, bf16[256,512]{1,0:T(8,128)(2,1)S(1)}, f32[256,512]{1,0:T(8,128)S(1)}, f32[256,512]{1,0:T(8,128)S(1)}) custom-call(bf16[256,512]{1,0:T(8,128)(2,1)S(1)} %attend.7.mine_ref, bf16[256,512]{1,0:T(8,128)(2,1)S(1)} %collective-permute-done.28.near_ref, ...), custom_call_target="tpu_custom_call" | custom-call | flops 1 | bytes 1 | tf_op jit(solution)/shard_map/multiply/pallas_call | solution.py:286
  105.5 0.9 collective-permute-start.29
  106.7 2.6 %collective-permute-start.27 = (bf16[256,512]{1,0:T(8,128)(2,1)S(1)}, bf16[256,512]{1,0:T(8,128)(2,1)S(1)}, u32[]{:S(2)}, u32[]{:S(2)}) collective-permute-start(bf16[256,512]{1,0:T(8,128)(2,1)S(1)} %add_convert_fusion.3), channel_id=1, source_target_pairs={{0,65},{32,97},{64,1},{96,33},{1,64},{33,96},{65,0},{97,32},{2,67}... | collective-permute-start | bytes 786440 | tf_op jit(solution)/shard_map/ppermute | solution.py:53
  109.5 1.5 %collective-permute-start.31 = (bf16[256,512]{1,0:T(8,128)(2,1)S(1)}, bf16[256,512]{1,0:T(8,128)(2,1)S(1)}, u32[]{:S(2)}, u32[]{:S(2)}) collective-permute-start(bf16[256,512]{1,0:T(8,128)(2,1)S(1)} %add_convert_fusion.1), channel_id=1, source_target_pairs={{0,65},{32,97},{64,1},{96,33},{1,64},{33,96},{65,0},{97,32},{2,67}... | collective-permute-start | bytes 786440 | tf_op jit(solution)/shard_map/ppermute | solution.py:53
  111.0 4.4 %collective-permute-done.27 = bf16[256,512]{1,0:T(8,128)(2,1)S(1)} collective-permute-done((bf16[256,512]{1,0:T(8,128)(2,1)S(1)}, bf16[256,512]{1,0:T(8,128)(2,1)S(1)}, u32[]{:S(2)}, u32[]{:S(2)}) %collective-permute-start.27) | collective-permute-done | bytes 262176 | tf_op jit(solution)/shard_map/ppermute | solution.py:53
  115.6 5.5 %collective-permute-done.31 = bf16[256,512]{1,0:T(8,128)(2,1)S(1)} collective-permute-done((bf16[256,512]{1,0:T(8,128)(2,1)S(1)}, bf16[256,512]{1,0:T(8,128)(2,1)S(1)}, u32[]{:S(2)}, u32[]{:S(2)}) %collective-permute-start.31) | collective-permute-done | bytes 262176 | tf_op jit(solution)/shard_map/ppermute | solution.py:53
  121.2 1.0 pad_maximum_fusion
  (68 shorter events, 4.3 us)
Async XLA Ops:
  0.0 0.7 copy-start.1
  5.4 15.2 %collective-permute-start.5 = (bf16[2064,128]{1,0:T(8,128)(2,1)S(1)}, bf16[2064,128]{1,0:T(8,128)(2,1)S(1)}, u32[]{:S(2)}, u32[]{:S(2)}) collective-permute-start(bf16[2064,128]{1,0:T(8,128)(2,1)S(1)} %get-tuple-element.75.refs_4_), channel_id=1, source_target_pairs={{0,2},{2,4},{4,6},{6,0},{8,10},{10,12},{12,14},{14,8},{16,18},{18,... | collective-permute-start | bytes 1585160 | tf_op jit(solution)/shard_map/ppermute | solution.py:41
  7.6 14.6 %collective-permute-start = (bf16[2064,128]{1,0:T(8,128)(2,1)S(1)}, bf16[2064,128]{1,0:T(8,128)(2,1)S(1)}, u32[]{:S(2)}, u32[]{:S(2)}) collective-permute-start(bf16[2064,128]{1,0:T(8,128)(2,1)S(1)} %get-tuple-element.73.refs_0_), channel_id=1, source_target_pairs={{0,8},{2,10},{4,12},{6,14},{8,16},{10,18},{12,20},{14,22},{16,24},... | collective-permute-start | bytes 1585160 | tf_op jit(solution)/shard_map/ppermute | solution.py:41
  8.8 29.3 %collective-permute-start.4 = (bf16[2064,128]{1,0:T(8,128)(2,1)S(1)}, bf16[2064,128]{1,0:T(8,128)(2,1)}, u32[]{:S(2)}, u32[]{:S(2)}) collective-permute-start(bf16[2064,128]{1,0:T(8,128)(2,1)S(1)} %get-tuple-element.75.refs_4_), channel_id=1, source_target_pairs={{0,6},{2,0},{4,2},{6,4},{8,14},{10,8},{12,10},{14,12},{16,22},{18,... | collective-permute-start | bytes 1585160 | tf_op jit(solution)/shard_map/ppermute | solution.py:41
  10.3 27.8 %collective-permute-start.2 = (bf16[2064,128]{1,0:T(8,128)(2,1)S(1)}, bf16[2064,128]{1,0:T(8,128)(2,1)}, u32[]{:S(2)}, u32[]{:S(2)}) collective-permute-start(bf16[2064,128]{1,0:T(8,128)(2,1)S(1)} %get-tuple-element.73.refs_0_), channel_id=1, source_target_pairs={{0,24},{2,26},{4,28},{6,30},{8,0},{10,2},{12,4},{14,6},{16,8},{18,... | collective-permute-start | bytes 1585160 | tf_op jit(solution)/shard_map/ppermute | solution.py:41
  11.8 14.7 %copy-start = (f32[4096]{0:T(1024)S(1)}, f32[4096]{0:T(1024)}, u32[]{:S(2)}) copy-start(f32[4096]{0:T(1024)} %param.9) | copy-start | bytes 49156
  15.9 0.8 copy-start.2
  16.7 0.8 copy-start.4
  17.5 0.8 copy-start.5
  20.6 17.5 %collective-permute-start.6 = (bf16[2064,128]{1,0:T(8,128)(2,1)S(1)}, bf16[2064,128]{1,0:T(8,128)(2,1)}, u32[]{:S(2)}, u32[]{:S(2)}) collective-permute-start(bf16[2064,128]{1,0:T(8,128)(2,1)S(1)} %get-tuple-element.75.refs_4_), channel_id=1, source_target_pairs={{0,4},{2,6},{4,0},{6,2},{8,12},{10,14},{12,8},{14,10},{16,20},{18,... | collective-permute-start | bytes 1585160 | tf_op jit(solution)/shard_map/ppermute | solution.py:41
  22.2 16.0 %collective-permute-start.3 = (bf16[2064,128]{1,0:T(8,128)(2,1)S(1)}, bf16[2064,128]{1,0:T(8,128)(2,1)}, u32[]{:S(2)}, u32[]{:S(2)}) collective-permute-start(bf16[2064,128]{1,0:T(8,128)(2,1)S(1)} %get-tuple-element.73.refs_0_), channel_id=1, source_target_pairs={{0,16},{2,18},{4,20},{6,22},{8,24},{10,26},{12,28},{14,30},{16,0},... | collective-permute-start | bytes 1585160 | tf_op jit(solution)/shard_map/ppermute | solution.py:41
  24.9 13.2 %collective-permute-start.1 = (bf16[96,2048]{1,0:T(8,128)(2,1)}, bf16[96,2048]{1,0:T(8,128)(2,1)}, u32[]{:S(2)}, u32[]{:S(2)}) collective-permute-start(bf16[96,2048]{1,0:T(8,128)(2,1)} %get-tuple-element.69), channel_id=1, source_target_pairs={{0,64},{32,96},{64,0},{96,32},{1,65},{33,97},{65,1},{97,33},{2,66}... | collective-permute-start | bytes 1179656 | tf_op jit(solution)/shard_map/ppermute | solution.py:53
  38.1 12.8 %collective-permute-start.12 = (bf16[144,2048]{1,0:T(8,128)(2,1)}, bf16[144,2048]{1,0:T(8,128)(2,1)S(1)}, u32[]{:S(2)}, u32[]{:S(2)}) collective-permute-start(bf16[144,2048]{1,0:T(8,128)(2,1)} %copy-done.4), channel_id=1, source_target_pairs={{0,64},{32,96},{64,0},{96,32},{1,65},{33,97},{65,1},{97,33},{2,66}... | collective-permute-start | bytes 1769480 | tf_op jit(solution)/shard_map/ppermute | solution.py:53
  41.0 15.5 %collective-permute-start.7 = (bf16[2048,128]{1,0:T(8,128)(2,1)S(1)}, bf16[2048,128]{1,0:T(8,128)(2,1)S(1)}, u32[]{:S(2)}, u32[]{:S(2)}) collective-permute-start(bf16[2048,128]{1,0:T(8,128)(2,1)S(1)} %get-tuple-element.77), channel_id=1, source_target_pairs={{0,6},{2,0},{4,2},{6,4},{8,14},{10,8},{12,10},{14,12},{16,22},{18,... | collective-permute-start | bytes 1572872 | tf_op jit(solution)/shard_map/ppermute | solution.py:41
  41.9 13.0 %collective-permute-start.8 = (bf16[2048,128]{1,0:T(8,128)(2,1)S(1)}, bf16[2048,128]{1,0:T(8,128)(2,1)S(1)}, u32[]{:S(2)}, u32[]{:S(2)}) collective-permute-start(bf16[2048,128]{1,0:T(8,128)(2,1)S(1)} %get-tuple-element.79), channel_id=1, source_target_pairs={{0,2},{2,4},{4,6},{6,0},{8,10},{10,12},{12,14},{14,8},{16,18},{18,... | collective-permute-start | bytes 1572872 | tf_op jit(solution)/shard_map/ppermute | solution.py:41
  42.5 13.9 %collective-permute-start.10 = (bf16[2048,128]{1,0:T(8,128)(2,1)S(1)}, bf16[2048,128]{1,0:T(8,128)(2,1)S(1)}, u32[]{:S(2)}, u32[]{:S(2)}) collective-permute-start(bf16[2048,128]{1,0:T(8,128)(2,1)S(1)} %get-tuple-element.82), channel_id=1, source_target_pairs={{0,24},{2,26},{4,28},{6,30},{8,0},{10,2},{12,4},{14,6},{16,8},{18,... | collective-permute-start | bytes 1572872 | tf_op jit(solution)/shard_map/ppermute | solution.py:41
  43.4 11.4 %collective-permute-start.11 = (bf16[2048,128]{1,0:T(8,128)(2,1)S(1)}, bf16[2048,128]{1,0:T(8,128)(2,1)S(1)}, u32[]{:S(2)}, u32[]{:S(2)}) collective-permute-start(bf16[2048,128]{1,0:T(8,128)(2,1)S(1)} %get-tuple-element.84), channel_id=1, source_target_pairs={{0,8},{2,10},{4,12},{6,14},{8,16},{10,18},{12,20},{14,22},{16,24},... | collective-permute-start | bytes 1572872 | tf_op jit(solution)/shard_map/ppermute | solution.py:41
  47.0 3.8 %copy-start.3 = (bf16[144,2048]{1,0:T(8,128)(2,1)S(1)}, bf16[144,2048]{1,0:T(8,128)(2,1)}, u32[]{:S(2)}) copy-start(bf16[144,2048]{1,0:T(8,128)(2,1)} %copy-done.2) | copy-start | bytes 1769476
  47.3 15.3 %copy-start.6 = (bf16[128,2048]{1,0:T(8,128)(2,1)S(1)}, bf16[128,2048]{1,0:T(8,128)(2,1)}, u32[]{:S(2)}) copy-start(bf16[128,2048]{1,0:T(8,128)(2,1)} %copy-done.5) | copy-start | bytes 1572868
  50.8 11.8 %collective-permute-start.15 = (bf16[144,2048]{1,0:T(8,128)(2,1)S(1)}, bf16[144,2048]{1,0:T(8,128)(2,1)S(1)}, u32[]{:S(2)}, u32[]{:S(2)}) collective-permute-start(bf16[144,2048]{1,0:T(8,128)(2,1)S(1)} %copy-done.3), channel_id=1, source_target_pairs={{0,64},{32,96},{64,0},{96,32},{1,65},{33,97},{65,1},{97,33},{2,66}... | collective-permute-start | bytes 1769480 | tf_op jit(solution)/shard_map/ppermute | solution.py:53
  54.8 10.8 %collective-permute-start.13 = (bf16[2048,128]{1,0:T(8,128)(2,1)S(1)}, bf16[2048,128]{1,0:T(8,128)(2,1)S(1)}, u32[]{:S(2)}, u32[]{:S(2)}) collective-permute-start(bf16[2048,128]{1,0:T(8,128)(2,1)S(1)} %get-tuple-element.88), channel_id=1, source_target_pairs={{0,16},{2,18},{4,20},{6,22},{8,24},{10,26},{12,28},{14,30},{16,0},... | collective-permute-start | bytes 1572872 | tf_op jit(solution)/shard_map/ppermute | solution.py:41
  54.9 10.8 %collective-permute-start.9 = (bf16[2048,128]{1,0:T(8,128)(2,1)S(1)}, bf16[2048,128]{1,0:T(8,128)(2,1)S(1)}, u32[]{:S(2)}, u32[]{:S(2)}) collective-permute-start(bf16[2048,128]{1,0:T(8,128)(2,1)S(1)} %get-tuple-element.80), channel_id=1, source_target_pairs={{0,4},{2,6},{4,0},{6,2},{8,12},{10,14},{12,8},{14,10},{16,20},{18,... | collective-permute-start | bytes 1572872 | tf_op jit(solution)/shard_map/ppermute | solution.py:41
  62.6 14.1 %collective-permute-start.16 = (bf16[128,2048]{1,0:T(8,128)(2,1)S(1)}, bf16[128,2048]{1,0:T(8,128)(2,1)S(1)}, u32[]{:S(2)}, u32[]{:S(2)}) collective-permute-start(bf16[128,2048]{1,0:T(8,128)(2,1)S(1)} %copy-done.6), channel_id=1, source_target_pairs={{0,64},{32,96},{64,0},{96,32},{1,65},{33,97},{65,1},{97,33},{2,66}... | collective-permute-start | bytes 1572872 | tf_op jit(solution)/shard_map/ppermute | solution.py:53
  68.9 9.7 %collective-permute-start.14 = (bf16[256,512]{1,0:T(8,128)(2,1)S(1)}, bf16[256,512]{1,0:T(8,128)(2,1)S(1)}, u32[]{:S(2)}, u32[]{:S(2)}) collective-permute-start(bf16[256,512]{1,0:T(8,128)(2,1)S(1)} %attend.4.mine_ref), channel_id=1, source_target_pairs={{0,64},{32,96},{64,0},{96,32},{1,65},{33,97},{65,1},{97,33},{2,66}... | collective-permute-start | bytes 786440 | tf_op jit(solution)/shard_map/ppermute | solution.py:53
  73.2 17.6 %collective-permute-start.20 = (bf16[256,512]{1,0:T(8,128)(2,1)S(1)}, bf16[256,512]{1,0:T(8,128)(2,1)S(1)}, u32[]{:S(2)}, u32[]{:S(2)}) collective-permute-start(bf16[256,512]{1,0:T(8,128)(2,1)S(1)} %attend.5.mine_ref), channel_id=1, source_target_pairs={{0,64},{32,96},{64,0},{96,32},{1,65},{33,97},{65,1},{97,33},{2,66}... | collective-permute-start | bytes 786440 | tf_op jit(solution)/shard_map/ppermute | solution.py:53
  79.9 12.8 %collective-permute-start.18 = (bf16[256,512]{1,0:T(8,128)(2,1)S(1)}, bf16[256,512]{1,0:T(8,128)(2,1)S(1)}, u32[]{:S(2)}, u32[]{:S(2)}) collective-permute-start(bf16[256,512]{1,0:T(8,128)(2,1)S(1)} %get-tuple-element.100), channel_id=1, source_target_pairs={{0,32},{32,0},{64,96},{96,64},{1,33},{33,1},{65,97},{97,65},{2,34}... | collective-permute-start | bytes 786440 | tf_op jit(solution)/shard_map/ppermute | solution.py:53
  87.7 8.7 %collective-permute-start.24 = (bf16[256,512]{1,0:T(8,128)(2,1)S(1)}, bf16[256,512]{1,0:T(8,128)(2,1)S(1)}, u32[]{:S(2)}, u32[]{:S(2)}) collective-permute-start(bf16[256,512]{1,0:T(8,128)(2,1)S(1)} %attend.6.mine_ref), channel_id=1, source_target_pairs={{0,64},{32,96},{64,0},{96,32},{1,65},{33,97},{65,1},{97,33},{2,66}... | collective-permute-start | bytes 786440 | tf_op jit(solution)/shard_map/ppermute | solution.py:53
  92.1 6.2 %collective-permute-start.22 = (bf16[256,512]{1,0:T(8,128)(2,1)S(1)}, bf16[256,512]{1,0:T(8,128)(2,1)S(1)}, u32[]{:S(2)}, u32[]{:S(2)}) collective-permute-start(bf16[256,512]{1,0:T(8,128)(2,1)S(1)} %get-tuple-element.108), channel_id=1, source_target_pairs={{0,32},{32,0},{64,96},{96,64},{1,33},{33,1},{65,97},{97,65},{2,34}... | collective-permute-start | bytes 786440 | tf_op jit(solution)/shard_map/ppermute | solution.py:53
  92.6 6.0 %collective-permute-start.17 = (bf16[256,512]{1,0:T(8,128)(2,1)S(1)}, bf16[256,512]{1,0:T(8,128)(2,1)S(1)}, u32[]{:S(2)}, u32[]{:S(2)}) collective-permute-start(bf16[256,512]{1,0:T(8,128)(2,1)S(1)} %get-tuple-element.98), channel_id=1, source_target_pairs={{0,32},{32,0},{64,96},{96,64},{1,33},{33,1},{65,97},{97,65},{2,34}... | collective-permute-start | bytes 786440 | tf_op jit(solution)/shard_map/ppermute | solution.py:53
  92.8 10.0 %collective-permute-start.19 = (bf16[256,512]{1,0:T(8,128)(2,1)S(1)}, bf16[256,512]{1,0:T(8,128)(2,1)S(1)}, u32[]{:S(2)}, u32[]{:S(2)}) collective-permute-start(bf16[256,512]{1,0:T(8,128)(2,1)S(1)} %add_convert_fusion.7), channel_id=1, source_target_pairs={{0,65},{32,97},{64,1},{96,33},{1,64},{33,96},{65,0},{97,32},{2,67}... | collective-permute-start | bytes 786440 | tf_op jit(solution)/shard_map/ppermute | solution.py:53
  96.4 7.9 %collective-permute-start.28 = (bf16[256,512]{1,0:T(8,128)(2,1)S(1)}, bf16[256,512]{1,0:T(8,128)(2,1)S(1)}, u32[]{:S(2)}, u32[]{:S(2)}) collective-permute-start(bf16[256,512]{1,0:T(8,128)(2,1)S(1)} %attend.7.mine_ref), channel_id=1, source_target_pairs={{0,64},{32,96},{64,0},{96,32},{1,65},{33,97},{65,1},{97,33},{2,66}... | collective-permute-start | bytes 786440 | tf_op jit(solution)/shard_map/ppermute | solution.py:53
  96.4 10.3 %collective-permute-start.21 = (bf16[256,512]{1,0:T(8,128)(2,1)S(1)}, bf16[256,512]{1,0:T(8,128)(2,1)S(1)}, u32[]{:S(2)}, u32[]{:S(2)}) collective-permute-start(bf16[256,512]{1,0:T(8,128)(2,1)S(1)} %get-tuple-element.106), channel_id=1, source_target_pairs={{0,32},{32,0},{64,96},{96,64},{1,33},{33,1},{65,97},{97,65},{2,34}... | collective-permute-start | bytes 786440 | tf_op jit(solution)/shard_map/ppermute | solution.py:53
  98.3 8.1 %collective-permute-start.26 = (bf16[256,512]{1,0:T(8,128)(2,1)S(1)}, bf16[256,512]{1,0:T(8,128)(2,1)S(1)}, u32[]{:S(2)}, u32[]{:S(2)}) collective-permute-start(bf16[256,512]{1,0:T(8,128)(2,1)S(1)} %get-tuple-element.114), channel_id=1, source_target_pairs={{0,32},{32,0},{64,96},{96,64},{1,33},{33,1},{65,97},{97,65},{2,34}... | collective-permute-start | bytes 786440 | tf_op jit(solution)/shard_map/ppermute | solution.py:53
  98.5 10.8 %collective-permute-start.23 = (bf16[256,512]{1,0:T(8,128)(2,1)S(1)}, bf16[256,512]{1,0:T(8,128)(2,1)S(1)}, u32[]{:S(2)}, u32[]{:S(2)}) collective-permute-start(bf16[256,512]{1,0:T(8,128)(2,1)S(1)} %add_convert_fusion.5), channel_id=1, source_target_pairs={{0,65},{32,97},{64,1},{96,33},{1,64},{33,96},{65,0},{97,32},{2,67}... | collective-permute-start | bytes 786440 | tf_op jit(solution)/shard_map/ppermute | solution.py:53
  102.8 8.3 %collective-permute-start.25 = (bf16[256,512]{1,0:T(8,128)(2,1)S(1)}, bf16[256,512]{1,0:T(8,128)(2,1)S(1)}, u32[]{:S(2)}, u32[]{:S(2)}) collective-permute-start(bf16[256,512]{1,0:T(8,128)(2,1)S(1)} %get-tuple-element.112), channel_id=1, source_target_pairs={{0,32},{32,0},{64,96},{96,64},{1,33},{33,1},{65,97},{97,65},{2,34}... | collective-permute-start | bytes 786440 | tf_op jit(solution)/shard_map/ppermute | solution.py:53
  105.5 10.0 %collective-permute-start.29 = (bf16[256,512]{1,0:T(8,128)(2,1)S(1)}, bf16[256,512]{1,0:T(8,128)(2,1)S(1)}, u32[]{:S(2)}, u32[]{:S(2)}) collective-permute-start(bf16[256,512]{1,0:T(8,128)(2,1)S(1)} %get-tuple-element.119), channel_id=1, source_target_pairs={{0,32},{32,0},{64,96},{96,64},{1,33},{33,1},{65,97},{97,65},{2,34}... | collective-permute-start | bytes 786440 | tf_op jit(solution)/shard_map/ppermute | solution.py:53
  106.5 3.0 %collective-permute-start.30 = (bf16[256,512]{1,0:T(8,128)(2,1)S(1)}, bf16[256,512]{1,0:T(8,128)(2,1)S(1)}, u32[]{:S(2)}, u32[]{:S(2)}) collective-permute-start(bf16[256,512]{1,0:T(8,128)(2,1)S(1)} %get-tuple-element.121), channel_id=1, source_target_pairs={{0,32},{32,0},{64,96},{96,64},{1,33},{33,1},{65,97},{97,65},{2,34}... | collective-permute-start | bytes 786440 | tf_op jit(solution)/shard_map/ppermute | solution.py:53
  106.7 8.8 %collective-permute-start.27 = (bf16[256,512]{1,0:T(8,128)(2,1)S(1)}, bf16[256,512]{1,0:T(8,128)(2,1)S(1)}, u32[]{:S(2)}, u32[]{:S(2)}) collective-permute-start(bf16[256,512]{1,0:T(8,128)(2,1)S(1)} %add_convert_fusion.3), channel_id=1, source_target_pairs={{0,65},{32,97},{64,1},{96,33},{1,64},{33,96},{65,0},{97,32},{2,67}... | collective-permute-start | bytes 786440 | tf_op jit(solution)/shard_map/ppermute | solution.py:53
  109.5 11.5 %collective-permute-start.31 = (bf16[256,512]{1,0:T(8,128)(2,1)S(1)}, bf16[256,512]{1,0:T(8,128)(2,1)S(1)}, u32[]{:S(2)}, u32[]{:S(2)}) collective-permute-start(bf16[256,512]{1,0:T(8,128)(2,1)S(1)} %add_convert_fusion.1), channel_id=1, source_target_pairs={{0,65},{32,97},{64,1},{96,33},{1,64},{33,96},{65,0},{97,32},{2,67}... | collective-permute-start | bytes 786440 | tf_op jit(solution)/shard_map/ppermute | solution.py:53
